TPU v7x, 32 devices: a whole 2x2x4 slice. The times are simulated.
32 devices in a mesh: sub: 8 (over z, y), grp: 4 (over x, core).
Axes of the slice: x: 2, y: 2, z: 4, core: 2. Of those that a mesh axis runs over, the one named last changes fastest.
Arguments:
- schur: bfloat16 [8, 2048, 2048], P('sub', 'grp'), may hold values from -0.125 to 0.125
- rhs: float32 [8, 2048, 192], P('sub', 'grp'), may hold values from -6 to 6
- start: float32 [8, 2048, 192], P('sub', 'grp'), may hold values from -6 to 6
- project: bfloat16 [8, 32, 4096], P('sub', 'grp'), may hold values from -0.75 to 0.75
- coarse_basis: bfloat16 [8, 8, 2048], P('sub', None, 'grp'), may hold values from -0.375 to 0.375
- owner_of_face: int32 [8, 32, 1], replicated, may hold values from 0 to 4; in each aligned block of 32 rows (0 to 31, 32 to 63, ..., all dimensions but the last counted through in order) at most 8 rows name the same one
- mortar_of_face: int32 [8, 32], replicated, may hold values from 0 to 15
- mortar_order: int32 [8, 16], replicated, may hold values from 3 to 7
- subdomain_map: int32 [8], replicated, may hold values from 0 to 7, each once
- vertex_ids: int32 [8, 8], replicated, may hold values from 0 to 15, all different within a row
Outputs:
- solution: float32 [8, 2048, 192], P('sub', 'grp')
Inputs may be any that keep to these rules, and one draw needn't show every extreme that they name: `owner_of_face`: the 32 faces of one subdomain name one offset at most 8 times. `mortar_of_face`: faces with the same owner and the same number lie on one mortar. `mortar_order`: row o holds the orders of the mortars owned by index o. `subdomain_map`: each subdomain once. `vertex_ids`: the 8 vertices of a subdomain differ; every vertex belongs to some subdomain.
All inputs are finite; a program needn't handle non-finite values.
Results may differ from a plain program's by a relative error of at most 0.0031.
Values may be sent and summed in bfloat16 or wider, within the bound.
No kernel may reach another device: no remote copies, remote signals or barrier semaphores. Data moves between devices by JAX's collectives and lax.ppermute only.
A program may use at most 64 MiB of HBM per device.

v0:
```python
import jax
import jax.numpy as jnp
from jax import lax
from jax.sharding import PartitionSpec as P

DEG = 8
FPTS = 64
MODES = 64
MORT_OWN = 16
ITERS = 2
REACH = 2
CAP = 8


relax_weight = 0.5
coarse_weight = 0.5


def passed_along(value, axis, steps):
    count = lax.axis_size(axis)
    pairs = [(source, (source + steps) % count) for source in range(count)]
    return lax.ppermute(value, axis, pairs)


def body(
    schur,
    rhs,
    start,
    project,
    coarse_basis,
    owner_of_face,
    mortar_of_face,
    mortar_order,
    subdomain_map,
    vertex_ids,
):
    highest = lax.Precision.HIGHEST
    contract_first = (((0,), (0,)), ((), ()))
    sub_count = lax.axis_size("sub")
    position = lax.axis_index("sub")
    all_faces = owner_of_face.shape[1]
    own_faces = project.shape[1]
    own_rows = schur.shape[1]
    neighbours = 2 * REACH + 1
    capacity = CAP
    vertices = 2 * sub_count
    held = jnp.take(owner_of_face[:, :, 0], subdomain_map, axis=0)
    mortar_local = jnp.take(mortar_of_face, subdomain_map, axis=0)
    face_index = jnp.arange(all_faces, dtype=jnp.int32)
    earlier = face_index[None, :] < face_index[:, None]
    ranks = jnp.sum(
        ((held[:, :, None] == held[:, None, :]) & earlier[None, :, :]).astype(jnp.int32), axis=2
    )
    my_held = lax.dynamic_index_in_dim(held, position, 0, keepdims=False)
    my_ranks = lax.dynamic_index_in_dim(ranks, position, 0, keepdims=False)
    slot_ids = my_held * capacity + my_ranks
    send_table = (
        jnp.arange(neighbours * capacity, dtype=jnp.int32)[:, None] == slot_ids[None, :]
    ).astype(jnp.bfloat16)
    links = jnp.arange(neighbours, dtype=jnp.int32)
    senders = jnp.mod(position - links + REACH, sub_count)
    from_held = jnp.take(held, senders, axis=0)
    from_mortar = jnp.take(mortar_local, senders, axis=0)
    from_ranks = jnp.take(ranks, senders, axis=0)
    incoming = (from_held == links[:, None]).astype(jnp.float32)
    mortar_hot = (
        from_mortar[:, :, None] == jnp.arange(MORT_OWN, dtype=jnp.int32)[None, None, :]
    ).astype(jnp.float32)
    rank_hot = (
        from_ranks[:, :, None] == jnp.arange(capacity, dtype=jnp.int32)[None, None, :]
    ).astype(jnp.float32)
    counts = jnp.einsum("jfk,jf->k", mortar_hot, incoming)
    degree = jnp.arange(MODES, dtype=jnp.int32)
    orders = lax.dynamic_index_in_dim(mortar_order, position, 0, keepdims=False)[:, None]
    keep_mask = ((degree[None, :] // DEG <= orders) & (degree[None, :] % DEG <= orders)).astype(
        jnp.float32
    )
    divisor = jnp.maximum(counts, 1.0)
    joined = jnp.einsum("jfk,jfc->kjc", mortar_hot * incoming[:, :, None], rank_hot)
    owner_table = joined.reshape(MORT_OWN, neighbours * capacity).astype(jnp.bfloat16)
    my_corners = lax.dynamic_index_in_dim(
        jnp.take(vertex_ids, subdomain_map, axis=0), position, 0, keepdims=False
    )
    corner_hot = (my_corners[:, None] == jnp.arange(vertices, dtype=jnp.int32)[None, :]).astype(
        jnp.float32
    )
    coarse_wide = coarse_basis[0].astype(jnp.float32)
    tables = project[0].reshape(own_faces, MODES, FPTS)
    matrix = schur[0]
    target = rhs[0]
    traces = start[0]
    for repeat in range(ITERS):
        trace_b = traces.astype(jnp.bfloat16)
        product = jnp.dot(
            matrix,
            lax.all_gather(trace_b, "grp", axis=0, tiled=True),
            preferred_element_type=jnp.float32,
        )
        residual = (product - target).astype(jnp.bfloat16)
        face_res = residual.reshape(own_faces, FPTS, -1)
        coeffs = jnp.einsum(
            "fmp,fpr->fmr", tables, face_res, preferred_element_type=jnp.float32
        ).astype(jnp.bfloat16)
        grouped = lax.all_to_all(coeffs, "grp", split_axis=2, concat_axis=0, tiled=True)
        part_rhs = grouped.shape[2]
        payload = grouped.reshape(all_faces, MODES * part_rhs)
        outgoing = jnp.dot(send_table, payload, preferred_element_type=jnp.float32).astype(
            jnp.bfloat16
        )
        blocks = outgoing.reshape(neighbours, capacity, -1)
        arrivals = []
        for link in range(neighbours):
            arrivals.append(passed_along(blocks[link], "sub", link - REACH))
        arrived = jnp.concatenate(arrivals, axis=0)
        mortar_sums = jnp.dot(owner_table, arrived, preferred_element_type=jnp.float32)
        shaped = mortar_sums.reshape(MORT_OWN, MODES, part_rhs) / divisor[:, None, None]
        shaped = shaped * keep_mask[:, :, None]
        averages = shaped.reshape(MORT_OWN, MODES * part_rhs).astype(jnp.bfloat16)
        replies = lax.dot_general(
            owner_table, averages, contract_first, preferred_element_type=jnp.float32
        ).astype(jnp.bfloat16)
        reply_blocks = replies.reshape(neighbours, capacity, -1)
        answers = []
        for link in range(neighbours):
            answers.append(passed_along(reply_blocks[link], "sub", REACH - link))
        answered = jnp.concatenate(answers, axis=0)
        own_back = lax.dot_general(
            send_table, answered, contract_first, preferred_element_type=jnp.float32
        ).astype(jnp.bfloat16)
        returned = lax.all_to_all(
            own_back.reshape(all_faces, MODES, part_rhs),
            "grp",
            split_axis=0,
            concat_axis=2,
            tiled=True,
        )
        lifted = jnp.einsum(
            "fmp,fmr->fpr", tables, returned, preferred_element_type=jnp.float32
        ).reshape(own_rows, -1)
        partial_value = jnp.dot(coarse_wide, lifted, precision=highest)
        spread = lax.dot_general(corner_hot, partial_value, contract_first, precision=highest)
        vertex = lax.psum(spread, ("sub", "grp"))
        picked = jnp.dot(corner_hot, vertex, precision=highest)
        coarse_corr = lax.dot_general(coarse_wide, picked, contract_first, precision=highest)
        traces = traces - relax_weight * lifted - coarse_weight * coarse_corr
    return traces[None]


def solution(mesh):
    return jax.shard_map(
        body,
        mesh=mesh,
        in_specs=(
            P("sub", "grp", None),
            P("sub", "grp", None),
            P("sub", "grp", None),
            P("sub", "grp", None),
            P("sub", None, "grp"),
            P(),
            P(),
            P(),
            P(),
            P(),
        ),
        out_specs=P("sub", "grp", None),
        check_vma=False,
    )
```

profile of v0, /device:TPU:0, one launch (start us, length us, event | category | flops | bytes accessed | tf_op | source)
XLA Modules:
  0.0 198.5 jit_solution(15513312980948887110)
XLA Ops:
  0.0 1.2 reshape_squeeze.3
  1.2 1.0 bitcast_convert_fusion
  2.2 10.1 %all_gather.6 = bf16[2048,192]{0,1:T(8,128)(2,1)S(1)} all-gather(bf16[512,192]{0,1:T(8,128)(2,1)S(1)} %bitcast_convert_fusion), channel_id=1, replica_groups=mesh['sub'=8,'grp'=4] {'grp'}, dimensions={0}, use_global_device_ids=true | all-gather | bytes 983040 | tf_op jit(solution)/shard_map/all_gather | solution.py:96
  12.3 1.8 fusion.20
  14.8 1.0 reshape.310
  15.8 3.4 %all-to-all-start = ((bf16[4,2,12288]{2,1,0:T(2,128)(2,1)}), bf16[4,2,12288]{2,1,0:T(2,128)(2,1)S(1)}, u32[]{:S(2)}, u32[]{:S(2)}) async-start(bf16[4,2,12288]{2,1,0:T(2,128)(2,1)} %reshape.310), calls=%async_computation | async-start | bytes 393216 | tf_op jit(solution)/shard_map/all_to_all | solution.py:104
  19.3 0.6 gather_fusion.3
  19.8 0.6 gather_fusion.1
  20.8 0.6 gather_fusion.5
  21.3 0.6 gather_fusion.2
  21.9 0.6 gather_fusion.4
  22.5 0.7 fusion.62
  23.5 0.9 all-to-all-done
  25.0 0.8 reshape.235
  26.1 3.6 %collective-permute-start = (bf16[8,3072]{1,0:T(8,128)(2,1)S(1)}, bf16[8,3072]{1,0:T(8,128)(2,1)S(1)}, u32[]{:S(2)}, u32[]{:S(2)}) collective-permute-start(bf16[8,3072]{1,0:T(8,128)(2,1)S(1)} %get-tuple-element.28), channel_id=1, source_target_pairs={{0,24},{4,28},{8,0},{12,4},{16,8},{20,12},{24,16},{28,20},{1,25},{... | collective-permute-start | bytes 147464 | tf_op jit(solution)/shard_map/ppermute | solution.py:22
  29.9 1.6 collective-permute-start.3
  31.4 3.3 %collective-permute-start.1 = (bf16[8,3072]{1,0:T(8,128)(2,1)S(1)}, bf16[8,3072]{1,0:T(8,128)(2,1)S(1)}, u32[]{:S(2)}, u32[]{:S(2)}) collective-permute-start(bf16[8,3072]{1,0:T(8,128)(2,1)S(1)} %get-tuple-element.27), channel_id=1, source_target_pairs={{0,28},{4,0},{8,4},{12,8},{16,12},{20,16},{24,20},{28,24},{1,29},{... | collective-permute-start | bytes 147464 | tf_op jit(solution)/shard_map/ppermute | solution.py:22
  34.7 1.7 collective-permute-done.1
  36.5 0.8 collective-permute-done.3
  37.3 0.7 dot_general.91
  39.5 0.6 gather_fusion
  40.0 3.9 %collective-permute-start.9 = (bf16[8,3072]{1,0:T(8,128)(2,1)S(1)}, bf16[8,3072]{1,0:T(8,128)(2,1)S(1)}, u32[]{:S(2)}, u32[]{:S(2)}) collective-permute-start(bf16[8,3072]{1,0:T(8,128)(2,1)S(1)} %get-tuple-element.19), channel_id=1, source_target_pairs={{0,24},{4,28},{8,0},{12,4},{16,8},{20,12},{24,16},{28,20},{1,25},{... | collective-permute-start | bytes 147464 | tf_op jit(solution)/shard_map/ppermute | solution.py:22
  43.9 2.5 %collective-permute-start.8 = (bf16[8,3072]{1,0:T(8,128)(2,1)S(1)}, bf16[8,3072]{1,0:T(8,128)(2,1)S(1)}, u32[]{:S(2)}, u32[]{:S(2)}) collective-permute-start(bf16[8,3072]{1,0:T(8,128)(2,1)S(1)} %get-tuple-element.20), channel_id=1, source_target_pairs={{0,28},{4,0},{8,4},{12,8},{16,12},{20,16},{24,20},{28,24},{1,29},{... | collective-permute-start | bytes 147464 | tf_op jit(solution)/shard_map/ppermute | solution.py:22
  46.4 6.8 %collective-permute-done.6 = bf16[8,3072]{1,0:T(8,128)(2,1)S(1)} collective-permute-done((bf16[8,3072]{1,0:T(8,128)(2,1)S(1)}, bf16[8,3072]{1,0:T(8,128)(2,1)S(1)}, u32[]{:S(2)}, u32[]{:S(2)}) %collective-permute-start.6) | collective-permute-done | bytes 49184 | tf_op jit(solution)/shard_map/ppermute | solution.py:22
  53.5 0.5 reshape.236
  54.3 1.0 reshape.312
  55.3 3.4 %all-to-all-start.1 = ((bf16[4,2,12288]{2,1,0:T(2,128)(2,1)}), bf16[4,2,12288]{2,1,0:T(2,128)(2,1)S(1)}, u32[]{:S(2)}, u32[]{:S(2)}) async-start(bf16[4,2,12288]{2,1,0:T(2,128)(2,1)} %reshape.312), calls=%async_computation.1 | async-start | bytes 393216 | tf_op jit(solution)/shard_map/all_to_all | solution.py:130
  58.7 0.8 broadcast_select_fusion.4
  59.5 4.5 %all-to-all-done.1 = bf16[4,2,12288]{2,1,0:T(2,128)(2,1)S(1)} async-done(((bf16[4,2,12288]{2,1,0:T(2,128)(2,1)}), bf16[4,2,12288]{2,1,0:T(2,128)(2,1)S(1)}, u32[]{:S(2)}, u32[]{:S(2)}) %all-to-all-start.1) | async-done | bytes 196640 | tf_op jit(solution)/shard_map/all_to_all | solution.py:130
  65.4 36.9 %psum.14 = f32[16,192]{1,0:T(8,128)S(1)} all-reduce(f32[16,192]{1,0:T(8,128)S(1)} %fusion.55), channel_id=1, replica_groups=mesh['sub'=8,'grp'=4] {'sub','grp'}, use_global_device_ids=true, to_apply=%region_1.0 | all-reduce | flops 3072 | bytes 24576 | tf_op jit(solution)/shard_map/psum | solution.py:142
  102.5 1.1 fusion.72
  103.6 9.4 %all_gather.7 = bf16[2048,192]{0,1:T(8,128)(2,1)S(1)} all-gather(bf16[512,192]{0,1:T(8,128)(2,1)S(1)} %get-tuple-element.33), channel_id=1, replica_groups=mesh['sub'=8,'grp'=4] {'grp'}, dimensions={0}, use_global_device_ids=true | all-gather | bytes 983040 | tf_op jit(solution)/shard_map/all_gather | solution.py:96
  113.0 0.8 fusion.23
  114.8 7.7 %all_to_all.66 = bf16[4,2,12288]{2,1,0:T(2,128)(2,1)S(1)} all-to-all(bf16[4,2,12288]{2,1,0:T(2,128)(2,1)S(1)} %reshape.314), channel_id=1, replica_groups=mesh['sub'=8,'grp'=4] {'grp'}, dimensions={0} | all-to-all | bytes 393216 | tf_op jit(solution)/shard_map/all_to_all | solution.py:104
  123.1 0.8 reshape.239
  124.1 2.3 %collective-permute-start.10 = (bf16[8,3072]{1,0:T(8,128)(2,1)S(1)}, bf16[8,3072]{1,0:T(8,128)(2,1)S(1)}, u32[]{:S(2)}, u32[]{:S(2)}) collective-permute-start(bf16[8,3072]{1,0:T(8,128)(2,1)S(1)} %get-tuple-element.18), channel_id=1, source_target_pairs={{0,24},{4,28},{8,0},{12,4},{16,8},{20,12},{24,16},{28,20},{1,25},{... | collective-permute-start | bytes 147464 | tf_op jit(solution)/shard_map/ppermute | solution.py:22
  126.5 0.6 collective-permute-start.14
  127.1 0.8 collective-permute-start.13
  127.9 4.0 %collective-permute-start.11 = (bf16[8,3072]{1,0:T(8,128)(2,1)S(1)}, bf16[8,3072]{1,0:T(8,128)(2,1)S(1)}, u32[]{:S(2)}, u32[]{:S(2)}) collective-permute-start(bf16[8,3072]{1,0:T(8,128)(2,1)S(1)} %get-tuple-element.17), channel_id=1, source_target_pairs={{0,28},{4,0},{8,4},{12,8},{16,12},{20,16},{24,20},{28,24},{1,29},{... | collective-permute-start | bytes 147464 | tf_op jit(solution)/shard_map/ppermute | solution.py:22
  131.8 1.7 collective-permute-done.11
  133.9 0.7 dot_general.107
  136.0 0.7 collective-permute-start.15
  136.7 3.2 %collective-permute-start.19 = (bf16[8,3072]{1,0:T(8,128)(2,1)S(1)}, bf16[8,3072]{1,0:T(8,128)(2,1)S(1)}, u32[]{:S(2)}, u32[]{:S(2)}) collective-permute-start(bf16[8,3072]{1,0:T(8,128)(2,1)S(1)} %get-tuple-element.9), channel_id=1, source_target_pairs={{0,24},{4,28},{8,0},{12,4},{16,8},{20,12},{24,16},{28,20},{1,25},{... | collective-permute-start | bytes 147464 | tf_op jit(solution)/shard_map/ppermute | solution.py:22
  139.9 3.0 %collective-permute-start.18 = (bf16[8,3072]{1,0:T(8,128)(2,1)S(1)}, bf16[8,3072]{1,0:T(8,128)(2,1)S(1)}, u32[]{:S(2)}, u32[]{:S(2)}) collective-permute-start(bf16[8,3072]{1,0:T(8,128)(2,1)S(1)} %get-tuple-element.10), channel_id=1, source_target_pairs={{0,28},{4,0},{8,4},{12,8},{16,12},{20,16},{24,20},{28,24},{1,29},{... | collective-permute-start | bytes 147464 | tf_op jit(solution)/shard_map/ppermute | solution.py:22
  142.9 6.8 %collective-permute-done.16 = bf16[8,3072]{1,0:T(8,128)(2,1)S(1)} collective-permute-done((bf16[8,3072]{1,0:T(8,128)(2,1)S(1)}, bf16[8,3072]{1,0:T(8,128)(2,1)S(1)}, u32[]{:S(2)}, u32[]{:S(2)}) %collective-permute-start.16) | collective-permute-done | bytes 49184 | tf_op jit(solution)/shard_map/ppermute | solution.py:22
  151.1 7.7 %all_to_all.67 = bf16[4,2,12288]{2,1,0:T(2,128)(2,1)S(1)} all-to-all(bf16[4,2,12288]{2,1,0:T(2,128)(2,1)S(1)} %reshape.316), channel_id=1, replica_groups=mesh['sub'=8,'grp'=4] {'grp'}, dimensions={0} | all-to-all | bytes 393216 | tf_op jit(solution)/shard_map/all_to_all | solution.py:130
  160.3 36.9 %psum.15 = f32[16,192]{1,0:T(8,128)S(1)} all-reduce(f32[16,192]{1,0:T(8,128)S(1)} %fusion.53), channel_id=1, replica_groups=mesh['sub'=8,'grp'=4] {'sub','grp'}, use_global_device_ids=true, to_apply=%region_2.5 | all-reduce | flops 3072 | bytes 24576 | tf_op jit(solution)/shard_map/psum | solution.py:142
  197.3 1.1 fusion.6
  (138 shorter events, 12.5 us)
Async XLA Ops:
  0.0 12.3 %copy-start = (bf16[1,512,2048]{2,1,0:T(8,128)(2,1)S(1)}, bf16[1,512,2048]{2,1,0:T(8,128)(2,1)}, u32[]{:S(2)}) copy-start(bf16[1,512,2048]{2,1,0:T(8,128)(2,1)} %param.14) | copy-start | bytes 6291460
  14.1 5.0 %copy-start.13 = (s32[8]{0:T(128)S(1)}, s32[8]{0:T(128)}, u32[]{:S(2)}) copy-start(s32[8]{0:T(128)} %param.22) | copy-start | bytes 100
  14.1 5.1 %copy-start.4 = (s32[8,32]{1,0:T(8,128)S(1)}, s32[8,32]{1,0:T(8,128)}, u32[]{:S(2)}) copy-start(s32[8,32]{1,0:T(8,128)} %param.20) | copy-start | bytes 3076
  14.2 5.7 %copy-start.5 = (s32[8,32,1]{1,2,0:T(1,128)S(1)}, s32[8,32,1]{1,2,0:T(1,128)}, u32[]{:S(2)}) copy-start(s32[8,32,1]{1,2,0:T(1,128)} %param.19) | copy-start | bytes 3076
  15.8 8.6 %all-to-all-start = ((bf16[4,2,12288]{2,1,0:T(2,128)(2,1)}), bf16[4,2,12288]{2,1,0:T(2,128)(2,1)S(1)}, u32[]{:S(2)}, u32[]{:S(2)}) async-start(bf16[4,2,12288]{2,1,0:T(2,128)(2,1)} %reshape.310), calls=%async_computation | async-start | bytes 393216 | tf_op jit(solution)/shard_map/all_to_all | solution.py:104
  19.2 5.5 %copy-start.12 = (pred[8]{0:T(512)(128)(4,1)}, pred[8]{0:T(512)(128)(4,1)S(1)}, u32[]{:S(2)}) copy-start(pred[8]{0:T(512)(128)(4,1)S(1)} %compare_and_fusion.1) | copy-start | bytes 28
  23.4 15.7 %copy-start.8 = (bf16[5,8,16]{2,1,0:T(8,128)(2,1)}, bf16[5,8,16]{2,1,0:T(8,128)(2,1)S(1)}, u32[]{:S(2)}) copy-start(bf16[5,8,16]{2,1,0:T(8,128)(2,1)S(1)} %convolution_convert_fusion.8) | copy-start | bytes 3844
  23.5 14.8 %copy-start.10 = (f32[16,64]{1,0:T(8,128)}, f32[16,64]{1,0:T(8,128)S(1)}, u32[]{:S(2)}) copy-start(f32[16,64]{1,0:T(8,128)S(1)} %and_convert_fusion) | copy-start | bytes 12292
  26.1 8.6 %collective-permute-start = (bf16[8,3072]{1,0:T(8,128)(2,1)S(1)}, bf16[8,3072]{1,0:T(8,128)(2,1)S(1)}, u32[]{:S(2)}, u32[]{:S(2)}) collective-permute-start(bf16[8,3072]{1,0:T(8,128)(2,1)S(1)} %get-tuple-element.28), channel_id=1, source_target_pairs={{0,24},{4,28},{8,0},{12,4},{16,8},{20,12},{24,16},{28,20},{1,25},{... | collective-permute-start | bytes 147464 | tf_op jit(solution)/shard_map/ppermute | solution.py:22
  29.9 9.0 %copy-start.14 = (f32[16]{0:T(128)}, f32[16]{0:T(128)S(1)}, u32[]{:S(2)}) copy-start(f32[16]{0:T(128)S(1)} %fusion.30) | copy-start | bytes 196
  29.9 7.4 %collective-permute-start.4 = (bf16[8,3072]{1,0:T(8,128)(2,1)S(1)}, bf16[8,3072]{1,0:T(8,128)(2,1)S(1)}, u32[]{:S(2)}, u32[]{:S(2)}) collective-permute-start(bf16[8,3072]{1,0:T(8,128)(2,1)S(1)} %get-tuple-element.24), channel_id=1, source_target_pairs={{0,8},{4,12},{8,16},{12,20},{16,24},{20,28},{24,0},{28,4},{1,9},{5... | collective-permute-start | bytes 147464 | tf_op jit(solution)/shard_map/ppermute | solution.py:22
  29.9 7.4 %collective-permute-start.3 = (bf16[8,3072]{1,0:T(8,128)(2,1)S(1)}, bf16[8,3072]{1,0:T(8,128)(2,1)S(1)}, u32[]{:S(2)}, u32[]{:S(2)}) collective-permute-start(bf16[8,3072]{1,0:T(8,128)(2,1)S(1)} %get-tuple-element.25), channel_id=1, source_target_pairs={{0,4},{4,8},{8,12},{12,16},{16,20},{20,24},{24,28},{28,0},{1,5},{5... | collective-permute-start | bytes 147464 | tf_op jit(solution)/shard_map/ppermute | solution.py:22
  31.4 5.1 %collective-permute-start.2 = (bf16[8,3072]{1,0:T(8,128)(2,1)S(1)}, bf16[8,3072]{1,0:T(8,128)(2,1)S(1)}, u32[]{:S(2)}, u32[]{:S(2)}) collective-permute-start(bf16[8,3072]{1,0:T(8,128)(2,1)S(1)} %get-tuple-element.26), channel_id=1, source_target_pairs={{0,0},{4,4},{8,8},{12,12},{16,16},{20,20},{24,24},{28,28},{1,1},{5... | collective-permute-start | bytes 147464 | tf_op jit(solution)/shard_map/ppermute | solution.py:22
  31.4 5.0 %collective-permute-start.1 = (bf16[8,3072]{1,0:T(8,128)(2,1)S(1)}, bf16[8,3072]{1,0:T(8,128)(2,1)S(1)}, u32[]{:S(2)}, u32[]{:S(2)}) collective-permute-start(bf16[8,3072]{1,0:T(8,128)(2,1)S(1)} %get-tuple-element.27), channel_id=1, source_target_pairs={{0,28},{4,0},{8,4},{12,8},{16,12},{20,16},{24,20},{28,24},{1,29},{... | collective-permute-start | bytes 147464 | tf_op jit(solution)/shard_map/ppermute | solution.py:22
  37.9 1.5 copy-start.6
  39.4 7.0 %collective-permute-start.5 = (bf16[8,3072]{1,0:T(8,128)(2,1)S(1)}, bf16[8,3072]{1,0:T(8,128)(2,1)S(1)}, u32[]{:S(2)}, u32[]{:S(2)}) collective-permute-start(bf16[8,3072]{1,0:T(8,128)(2,1)S(1)} %get-tuple-element.23), channel_id=1, source_target_pairs={{0,8},{4,12},{8,16},{12,20},{16,24},{20,28},{24,0},{28,4},{1,9},{5... | collective-permute-start | bytes 147464 | tf_op jit(solution)/shard_map/ppermute | solution.py:22
  40.0 13.2 %collective-permute-start.9 = (bf16[8,3072]{1,0:T(8,128)(2,1)S(1)}, bf16[8,3072]{1,0:T(8,128)(2,1)S(1)}, u32[]{:S(2)}, u32[]{:S(2)}) collective-permute-start(bf16[8,3072]{1,0:T(8,128)(2,1)S(1)} %get-tuple-element.19), channel_id=1, source_target_pairs={{0,24},{4,28},{8,0},{12,4},{16,8},{20,12},{24,16},{28,20},{1,25},{... | collective-permute-start | bytes 147464 | tf_op jit(solution)/shard_map/ppermute | solution.py:22
  43.9 9.3 %collective-permute-start.8 = (bf16[8,3072]{1,0:T(8,128)(2,1)S(1)}, bf16[8,3072]{1,0:T(8,128)(2,1)S(1)}, u32[]{:S(2)}, u32[]{:S(2)}) collective-permute-start(bf16[8,3072]{1,0:T(8,128)(2,1)S(1)} %get-tuple-element.20), channel_id=1, source_target_pairs={{0,28},{4,0},{8,4},{12,8},{16,12},{20,16},{24,20},{28,24},{1,29},{... | collective-permute-start | bytes 147464 | tf_op jit(solution)/shard_map/ppermute | solution.py:22
  46.4 6.8 %collective-permute-start.7 = (bf16[8,3072]{1,0:T(8,128)(2,1)S(1)}, bf16[8,3072]{1,0:T(8,128)(2,1)S(1)}, u32[]{:S(2)}, u32[]{:S(2)}) collective-permute-start(bf16[8,3072]{1,0:T(8,128)(2,1)S(1)} %get-tuple-element.21), channel_id=1, source_target_pairs={{0,0},{4,4},{8,8},{12,12},{16,16},{20,20},{24,24},{28,28},{1,1},{5... | collective-permute-start | bytes 147464 | tf_op jit(solution)/shard_map/ppermute | solution.py:22
  46.4 6.8 %collective-permute-start.6 = (bf16[8,3072]{1,0:T(8,128)(2,1)S(1)}, bf16[8,3072]{1,0:T(8,128)(2,1)S(1)}, u32[]{:S(2)}, u32[]{:S(2)}) collective-permute-start(bf16[8,3072]{1,0:T(8,128)(2,1)S(1)} %get-tuple-element.22), channel_id=1, source_target_pairs={{0,4},{4,8},{8,12},{12,16},{16,20},{20,24},{24,28},{28,0},{1,5},{5... | collective-permute-start | bytes 147464 | tf_op jit(solution)/shard_map/ppermute | solution.py:22
  54.3 10.6 %copy-start.7 = (bf16[1,8,512]{2,1,0:T(8,128)(2,1)S(1)}, bf16[1,8,512]{2,1,0:T(8,128)(2,1)}, u32[]{:S(2)}) copy-start(bf16[1,8,512]{2,1,0:T(8,128)(2,1)} %param.18) | copy-start | bytes 24580
  55.3 8.6 %all-to-all-start.1 = ((bf16[4,2,12288]{2,1,0:T(2,128)(2,1)}), bf16[4,2,12288]{2,1,0:T(2,128)(2,1)S(1)}, u32[]{:S(2)}, u32[]{:S(2)}) async-start(bf16[4,2,12288]{2,1,0:T(2,128)(2,1)} %reshape.312), calls=%async_computation.1 | async-start | bytes 393216 | tf_op jit(solution)/shard_map/all_to_all | solution.py:130
  58.7 43.8 %copy-start.1 = (f32[1,512,192]{1,2,0:T(8,128)S(1)}, f32[1,512,192]{1,2,0:T(8,128)}, u32[]{:S(2)}) copy-start(f32[1,512,192]{1,2,0:T(8,128)} %param.16) | copy-start | bytes 1179652
  102.3 10.7 %copy-start.3 = (f32[1,512,192]{1,2,0:T(8,128)S(1)}, f32[1,512,192]{1,2,0:T(8,128)}, u32[]{:S(2)}) copy-start(f32[1,512,192]{1,2,0:T(8,128)} %param.15) | copy-start | bytes 1179652
  123.1 11.9 %copy-start.9 = (bf16[5,8,16]{2,1,0:T(8,128)(2,1)S(1)}, bf16[5,8,16]{2,1,0:T(8,128)(2,1)}, u32[]{:S(2)}) copy-start(bf16[5,8,16]{2,1,0:T(8,128)(2,1)} %copy-done.8) | copy-start | bytes 3844
  123.1 11.9 %copy-start.11 = (f32[16,64]{1,0:T(8,128)S(1)}, f32[16,64]{1,0:T(8,128)}, u32[]{:S(2)}) copy-start(f32[16,64]{1,0:T(8,128)} %copy-done.10) | copy-start | bytes 12292
  123.1 11.9 %copy-start.15 = (f32[16]{0:T(128)S(1)}, f32[16]{0:T(128)}, u32[]{:S(2)}) copy-start(f32[16]{0:T(128)} %copy-done.14) | copy-start | bytes 196
  124.1 7.7 %collective-permute-start.10 = (bf16[8,3072]{1,0:T(8,128)(2,1)S(1)}, bf16[8,3072]{1,0:T(8,128)(2,1)S(1)}, u32[]{:S(2)}, u32[]{:S(2)}) collective-permute-start(bf16[8,3072]{1,0:T(8,128)(2,1)S(1)} %get-tuple-element.18), channel_id=1, source_target_pairs={{0,24},{4,28},{8,0},{12,4},{16,8},{20,12},{24,16},{28,20},{1,25},{... | collective-permute-start | bytes 147464 | tf_op jit(solution)/shard_map/ppermute | solution.py:22
  126.5 7.4 %collective-permute-start.14 = (bf16[8,3072]{1,0:T(8,128)(2,1)S(1)}, bf16[8,3072]{1,0:T(8,128)(2,1)S(1)}, u32[]{:S(2)}, u32[]{:S(2)}) collective-permute-start(bf16[8,3072]{1,0:T(8,128)(2,1)S(1)} %get-tuple-element.14), channel_id=1, source_target_pairs={{0,8},{4,12},{8,16},{12,20},{16,24},{20,28},{24,0},{28,4},{1,9},{5... | collective-permute-start | bytes 147464 | tf_op jit(solution)/shard_map/ppermute | solution.py:22
  127.1 6.8 %collective-permute-start.13 = (bf16[8,3072]{1,0:T(8,128)(2,1)S(1)}, bf16[8,3072]{1,0:T(8,128)(2,1)S(1)}, u32[]{:S(2)}, u32[]{:S(2)}) collective-permute-start(bf16[8,3072]{1,0:T(8,128)(2,1)S(1)} %get-tuple-element.15), channel_id=1, source_target_pairs={{0,4},{4,8},{8,12},{12,16},{16,20},{20,24},{24,28},{28,0},{1,5},{5... | collective-permute-start | bytes 147464 | tf_op jit(solution)/shard_map/ppermute | solution.py:22
  127.9 5.7 %collective-permute-start.12 = (bf16[8,3072]{1,0:T(8,128)(2,1)S(1)}, bf16[8,3072]{1,0:T(8,128)(2,1)S(1)}, u32[]{:S(2)}, u32[]{:S(2)}) collective-permute-start(bf16[8,3072]{1,0:T(8,128)(2,1)S(1)} %get-tuple-element.16), channel_id=1, source_target_pairs={{0,0},{4,4},{8,8},{12,12},{16,16},{20,20},{24,24},{28,28},{1,1},{5... | collective-permute-start | bytes 147464 | tf_op jit(solution)/shard_map/ppermute | solution.py:22
  127.9 5.7 %collective-permute-start.11 = (bf16[8,3072]{1,0:T(8,128)(2,1)S(1)}, bf16[8,3072]{1,0:T(8,128)(2,1)S(1)}, u32[]{:S(2)}, u32[]{:S(2)}) collective-permute-start(bf16[8,3072]{1,0:T(8,128)(2,1)S(1)} %get-tuple-element.17), channel_id=1, source_target_pairs={{0,28},{4,0},{8,4},{12,8},{16,12},{20,16},{24,20},{28,24},{1,29},{... | collective-permute-start | bytes 147464 | tf_op jit(solution)/shard_map/ppermute | solution.py:22
  136.0 6.9 %collective-permute-start.15 = (bf16[8,3072]{1,0:T(8,128)(2,1)S(1)}, bf16[8,3072]{1,0:T(8,128)(2,1)S(1)}, u32[]{:S(2)}, u32[]{:S(2)}) collective-permute-start(bf16[8,3072]{1,0:T(8,128)(2,1)S(1)} %get-tuple-element.13), channel_id=1, source_target_pairs={{0,8},{4,12},{8,16},{12,20},{16,24},{20,28},{24,0},{28,4},{1,9},{5... | collective-permute-start | bytes 147464 | tf_op jit(solution)/shard_map/ppermute | solution.py:22
  136.7 13.0 %collective-permute-start.19 = (bf16[8,3072]{1,0:T(8,128)(2,1)S(1)}, bf16[8,3072]{1,0:T(8,128)(2,1)S(1)}, u32[]{:S(2)}, u32[]{:S(2)}) collective-permute-start(bf16[8,3072]{1,0:T(8,128)(2,1)S(1)} %get-tuple-element.9), channel_id=1, source_target_pairs={{0,24},{4,28},{8,0},{12,4},{16,8},{20,12},{24,16},{28,20},{1,25},{... | collective-permute-start | bytes 147464 | tf_op jit(solution)/shard_map/ppermute | solution.py:22
  139.9 9.8 %collective-permute-start.18 = (bf16[8,3072]{1,0:T(8,128)(2,1)S(1)}, bf16[8,3072]{1,0:T(8,128)(2,1)S(1)}, u32[]{:S(2)}, u32[]{:S(2)}) collective-permute-start(bf16[8,3072]{1,0:T(8,128)(2,1)S(1)} %get-tuple-element.10), channel_id=1, source_target_pairs={{0,28},{4,0},{8,4},{12,8},{16,12},{20,16},{24,20},{28,24},{1,29},{... | collective-permute-start | bytes 147464 | tf_op jit(solution)/shard_map/ppermute | solution.py:22
  142.9 6.8 %collective-permute-start.17 = (bf16[8,3072]{1,0:T(8,128)(2,1)S(1)}, bf16[8,3072]{1,0:T(8,128)(2,1)S(1)}, u32[]{:S(2)}, u32[]{:S(2)}) collective-permute-start(bf16[8,3072]{1,0:T(8,128)(2,1)S(1)} %get-tuple-element.11), channel_id=1, source_target_pairs={{0,0},{4,4},{8,8},{12,12},{16,16},{20,20},{24,24},{28,28},{1,1},{5... | collective-permute-start | bytes 147464 | tf_op jit(solution)/shard_map/ppermute | solution.py:22
  142.9 6.8 %collective-permute-start.16 = (bf16[8,3072]{1,0:T(8,128)(2,1)S(1)}, bf16[8,3072]{1,0:T(8,128)(2,1)S(1)}, u32[]{:S(2)}, u32[]{:S(2)}) collective-permute-start(bf16[8,3072]{1,0:T(8,128)(2,1)S(1)} %get-tuple-element.12), channel_id=1, source_target_pairs={{0,4},{4,8},{8,12},{12,16},{16,20},{20,24},{24,28},{28,0},{1,5},{5... | collective-permute-start | bytes 147464 | tf_op jit(solution)/shard_map/ppermute | solution.py:22
  158.8 38.5 %copy-start.2 = (f32[512,192]{0,1:T(8,128)S(1)}, f32[512,192]{0,1:T(8,128)}, u32[]{:S(2)}) copy-start(f32[512,192]{0,1:T(8,128)} %get-tuple-element.34) | copy-start | bytes 1179652
where the time goes:
time: 200 us; the launch traced here: 198 us
  blocking collectives  109 us (54%)
  starting transfers between devices  36.2 us (18%)
  waiting for transfers between devices  23.5 us (12%)
  local copies, waits for them, and re-layouts  17.4 us (9%)
  matrix products  9.64 us (5%)
  other arithmetic  2.44 us (1%)
    psum x2, blocking collectives, body(): vertex = lax.psum(spread, ('sub', 'grp'))  73.8 us
    ppermute x20, starting transfers between devices, passed_along(): return lax.ppermute(value, axis, pairs)  29.5 us
    all_gather x2, blocking collectives, body(): lax.all_gather(trace_b, 'grp', axis=0, tiled=True)  19.4 us
    ppermute x20, waiting for transfers between devices, passed_along(): return lax.ppermute(value, axis, pairs)  18.1 us
    all_to_all x1, blocking collectives, body(): lax.all_to_all(coeffs, 'grp', split_axis=2, concat_axis=0, tiled=True)  7.67 us
    all_to_all x1, blocking collectives, body(): lax.all_to_all(own_back.reshape(all_faces, MODES, part_rhs), 'grp', split...  7.67 us
    all_to_all x1, waiting for transfers between devices, body(): lax.all_to_all(own_back.reshape(all_faces, MODES, part_rhs), 'grp', split...  4.49 us
  transfers between devices with their start and end apart: 22, of which 8 were waited for; matrix products, arithmetic and copies ran while one was open for 3% of the time, Pallas kernels for 0%

commit v1 on v0

v1 whole, which is shorter than its diff:
```python
import functools

import jax
import jax.numpy as jnp
from jax import lax
from jax.experimental import pallas as pl
from jax.experimental.pallas import tpu as pltpu
from jax.sharding import PartitionSpec as P

DEG = 8
MODES = 64
FPTS = 64
MORT_OWN = 16
REACH = 2
CAP = 8
LINKS = 2 * REACH + 1
SLOTS = LINKS * CAP

relax_weight = 0.5
coarse_weight = 0.5

BF = jnp.bfloat16
F32 = jnp.float32
CONTRACT_FIRST = (((0,), (0,)), ((), ()))
VMEM = pl.BlockSpec(memory_space=pltpu.VMEM)
SMEM = pl.BlockSpec(memory_space=pltpu.SMEM)


def split_two(value):
    high = value.astype(BF)
    return high, (value - high.astype(F32)).astype(BF)


class Sizes:
    def __init__(self, subs, grps, schur, project, coarse_basis, rhs):
        self.subs = subs
        self.grps = grps
        self.rows = schur.shape[1]
        self.all_rows = schur.shape[2]
        self.own = project.shape[1]
        self.faces = self.own * grps
        self.corners = coarse_basis.shape[1]
        self.rhs = rhs.shape[2]
        self.vertices = 2 * subs
        self.share = MODES // grps
        self.wide = -(-(self.rhs + self.vertices) // 128) * 128
        self.lanes = self.rhs // 128 * 128
        self.tail = self.rhs - self.lanes
        self.near = self.vertices == self.share and LINKS <= subs <= 2 * LINKS
        self.extra = 2 if self.near else 0
        self.t_src = 0
        self.t_arr = SLOTS
        self.t_slot = 2 * SLOTS
        self.t_count = self.t_slot + self.faces
        self.t_order = self.t_count + MORT_OWN
        self.t_corner = self.t_order + MORT_OWN
        self.t_end = self.t_corner + self.corners


def call(kernel, sizes, ins, outs, args, scratch=()):
    return pl.pallas_call(
        functools.partial(kernel, sizes),
        out_shape=outs,
        in_specs=ins,
        out_specs=jax.tree.map(lambda _: VMEM, outs),
        scratch_shapes=list(scratch),
    )(*args)


def table_kernel(z, ids, owner, mortar, order, smap, vids, table, used, names):
    s = ids[0]
    g = ids[1]
    d = smap[s]
    for i in range(SLOTS):
        table[z.t_src + i] = 0
    for i in range(LINKS):
        used[i] = 0
    for i in range(MORT_OWN):
        table[z.t_count + i] = 0
        table[z.t_order + i] = order[s * MORT_OWN + i]
    for i in range(z.corners):
        table[z.t_corner + i] = vids[d * z.corners + i]
    for f in range(z.faces):
        o = owner[d * z.faces + f]
        r = used[o]
        used[o] = r + 1
        slot = o * CAP + r
        table[z.t_slot + f] = slot
        table[z.t_src + slot] = ((f // z.own) ^ g) * z.own + f % z.own
    for link in range(LINKS):
        dd = smap[lax.rem(s - link + REACH + z.subs, z.subs)]
        r = jnp.int32(0)
        for f in range(z.faces):
            hit = (owner[dd * z.faces + f] == link).astype(jnp.int32)
            m = mortar[dd * z.faces + f]
            names[r] = m
            table[z.t_count + m] = table[z.t_count + m] + hit
            r = r + hit
        for i in range(CAP):
            table[z.t_arr + link * CAP + i] = jnp.where(i < r, names[i], MORT_OWN)


def narrow_kernel(z, start, out):
    half = z.rows // 2
    value = start[...].astype(BF)
    out[: z.rows, :] = value[:, : z.lanes]
    out[z.rows :, : z.tail] = value[:half, z.lanes :]
    out[z.rows :, z.tail :] = value[half:, z.lanes :]


def first_kernel(z, ids, schur, b0, b1, b2, b3, rhs, tables, cext, o0, o1, o2, o3, res_out, gathered, held, coeffs):
    g = ids[1]
    half = z.rows // 2
    for j, b in enumerate((b0, b1, b2, b3)):
        off = pl.multiple_of((g ^ j) * z.rows, z.rows)
        gathered[pl.ds(off, z.rows), : z.lanes] = b[: z.rows, :]
        gathered[pl.ds(off, half), z.lanes :] = b[z.rows :, : z.tail]
        gathered[pl.ds(off + half, half), z.lanes :] = b[z.rows :, z.tail :]
    product = jnp.dot(schur[...], gathered[...], preferred_element_type=F32)
    residual = product - rhs[...]
    res_out[...] = residual
    held[:, : z.rhs] = residual.astype(BF)
    held[:, z.rhs :] = cext[...]
    for f in range(z.own):
        coeffs[f] = jnp.dot(tables[f, :MODES, :], held[f * FPTS : (f + 1) * FPTS, :], preferred_element_type=F32).astype(BF)
    for j, o in enumerate((o0, o1, o2, o3)):
        at = pl.multiple_of((g ^ j) * z.share, z.share)
        for f in range(z.own):
            o[f] = coeffs[f, pl.ds(at, z.share), :]


def pack_kernel(z, table, c0, c1, c2, c3, o0, o1, o2, o3, o4, data):
    for j, c in enumerate((c0, c1, c2, c3)):
        data[j * z.own : (j + 1) * z.own] = c[...]
    for link, o in enumerate((o0, o1, o2, o3, o4)):
        for i in range(CAP):
            o[i] = data[table[z.t_src + link * CAP + i]]


def average_body(z, ids, table, arrivals, total, held):
    g = ids[1]
    total[...] = jnp.zeros_like(total)
    for link, a in enumerate(arrivals):
        for i in range(CAP):
            m = table[z.t_arr + link * CAP + i]
            total[m] = total[m] + a[i].astype(F32)
    mode = g * z.share + lax.broadcasted_iota(jnp.int32, (z.share, z.rhs), 0)
    degree_a = mode // DEG
    degree_b = mode % DEG
    degree = jnp.maximum(degree_a, degree_b)
    for k in range(MORT_OWN):
        divisor = jnp.maximum(table[z.t_count + k], 1).astype(F32)
        kept = jnp.where(degree <= table[z.t_order + k], 1.0, 0.0)
        value = total[k, :, : z.rhs] / divisor * kept
        held[k] = value.astype(BF)
    held[MORT_OWN] = jnp.zeros_like(held[MORT_OWN])


def reply_body(z, table, held, g_high, g_low, replies, vertex):
    flat = held[:MORT_OWN].reshape(MORT_OWN * z.share, z.rhs)
    value = lax.dot_general(g_high, flat, CONTRACT_FIRST, preferred_element_type=F32)
    value = value + lax.dot_general(g_low, flat, CONTRACT_FIRST, preferred_element_type=F32)
    if z.near:
        high, low = split_two(value)
        vertex[0] = high
        vertex[1] = low
    else:
        vertex[...] = value
    for link, o in enumerate(replies):
        for i in range(CAP):
            o[i] = held[table[z.t_arr + link * CAP + i]]
        if z.near:
            o[CAP] = high
            o[CAP + 1] = low


def average_first(z, ids, table, a0, a1, a2, a3, a4, o0, o1, o2, o3, o4, vertex, g_high, g_low, total, held):
    average_body(z, ids, table, (a0, a1, a2, a3, a4), total, held)
    wide = total[:MORT_OWN, :, z.rhs : z.rhs + z.vertices].reshape(MORT_OWN * z.share, z.vertices)
    high, low = split_two(wide)
    g_high[...] = high
    g_low[...] = low
    reply_body(z, table, held, high, low, (o0, o1, o2, o3, o4), vertex)


def average_second(z, ids, table, a0, a1, a2, a3, a4, g_high, g_low, o0, o1, o2, o3, o4, vertex, total, held):
    average_body(z, ids, table, (a0, a1, a2, a3, a4), total, held)
    reply_body(z, table, held, g_high[...], g_low[...], (o0, o1, o2, o3, o4), vertex)


def near_sum(z, blocks, fars):
    value = None
    for b, at in [(b, CAP) for b in blocks] + [(b, 0) for b in fars]:
        one = b[at].astype(F32) + b[at + 1].astype(F32)
        value = one if value is None else value + one
    return split_two(value)


def spread_first(z, table, *refs):
    fars = refs[LINKS:-2]
    blocks, out, data = refs[:LINKS], refs[-2], refs[-1]
    for link, b in enumerate(blocks):
        data[link * CAP : (link + 1) * CAP] = b[:CAP]
    quarter = z.own // 2
    for f in range(z.faces):
        out[f] = data[table[z.t_slot + f], :, : z.lanes]
    for member in range(z.grps):
        for i in range(quarter):
            f = member * z.own + i
            left = data[table[z.t_slot + f], :, z.lanes :]
            right = data[table[z.t_slot + f + quarter], :, z.lanes :]
            out[z.faces + member * quarter + i] = jnp.concatenate([left, right], axis=1)
    if z.near:
        high, low = near_sum(z, blocks, fars)
        at = z.faces + z.faces // 2
        out[at] = high[:, : z.lanes]
        out[at + 1] = low[:, : z.lanes]
        out[at + 2] = jnp.concatenate([high[:, z.lanes :], low[:, z.lanes :]], axis=1)


def spread_second(z, ids, table, *refs):
    fars = refs[LINKS : -1 - z.grps]
    blocks, outs, data = refs[:LINKS], refs[-1 - z.grps : -1], refs[-1]
    g = ids[1]
    for link, b in enumerate(blocks):
        data[link * CAP : (link + 1) * CAP] = b[:CAP]
    for j, o in enumerate(outs):
        for i in range(z.own):
            o[i] = data[table[z.t_slot + (g ^ j) * z.own + i]]
    if z.near:
        high, low = near_sum(z, blocks, fars)
        for o in outs:
            o[z.own] = high
            o[z.own + 1] = low


def picked_rows(z, table, whole):
    rows = [whole[pl.ds(table[z.t_corner + i], 1), :] for i in range(z.corners)]
    high, low = split_two(jnp.concatenate(rows, axis=0))
    return jnp.concatenate([high.astype(F32), low.astype(F32)], axis=0).astype(BF)


def second_kernel(z, ids, table, schur, *refs):
    n = z.grps
    shares, refs = refs[:n], refs[n:]
    exts, refs = refs[:n], refs[n:]
    vertex_in, resid, refs = refs[0], refs[1], refs[2:]
    outs, refs = refs[:n], refs[n:]
    own_out, averages, gathered, whole, held, coeffs = refs
    g = ids[1]
    quarter = z.own // 2
    if z.near:
        at = z.faces + z.faces // 2
        for j, a in enumerate(shares):
            main = a[at].astype(F32) + a[at + 1].astype(F32)
            both = a[at + 2].astype(F32)
            tail = both[:, : z.tail] + both[:, z.tail :]
            if j:
                main = main + whole[:, : z.lanes]
                tail = tail + whole[:, z.lanes :]
            whole[:, : z.lanes] = main
            whole[:, z.lanes :] = tail
    else:
        whole[...] = vertex_in[...]
    picked = picked_rows(z, table, whole)
    for j, e in enumerate(exts):
        member = g ^ j
        for i in range(z.own):
            f = member * z.own + i
            for jj, a in enumerate(shares):
                rows = pl.ds(pl.multiple_of((g ^ jj) * z.share, z.share), z.share)
                averages[f, rows, : z.lanes] = a[f]
                low = (i // quarter) * z.tail
                averages[f, rows, z.lanes :] = a[z.faces + member * quarter + i % quarter, :, low : low + z.tail]
            averages[f, MODES:, :] = picked
            lifted = lax.dot_general(e[i], averages[f], CONTRACT_FIRST, preferred_element_type=F32)
            gathered[pl.ds(pl.multiple_of(f * FPTS, FPTS), FPTS), :] = lifted.astype(BF)
            if j == 0:
                own_out[i] = averages[f]
    product = jnp.dot(schur[...], gathered[...], preferred_element_type=F32)
    held[...] = (resid[...] - 0.5 * product).astype(BF)
    for f in range(z.own):
        coeffs[f] = jnp.dot(exts[0][f, :MODES, :], held[f * FPTS : (f + 1) * FPTS, :], preferred_element_type=F32).astype(BF)
    for j, o in enumerate(outs):
        at = pl.multiple_of((g ^ j) * z.share, z.share)
        for f in range(z.own):
            o[f] = coeffs[f, pl.ds(at, z.share), :]


def last_kernel(z, ids, table, *refs):
    n = z.grps
    shares, refs = refs[:n], refs[n:]
    ext, vertex_in, earlier, start, out, averages, whole = refs
    g = ids[1]
    if z.near:
        value = None
        for c in shares:
            one = c[z.own].astype(F32) + c[z.own + 1].astype(F32)
            value = one if value is None else value + one
        whole[...] = value
    else:
        whole[...] = vertex_in[...]
    picked = picked_rows(z, table, whole)
    for i in range(z.own):
        for j, c in enumerate(shares):
            rows = pl.ds(pl.multiple_of((g ^ j) * z.share, z.share), z.share)
            averages[i, rows, :] = c[i]
        averages[i, MODES:, :] = picked
        both = lax.dot_general(ext[i], averages[i], CONTRACT_FIRST, preferred_element_type=F32)
        both = both + lax.dot_general(ext[i], earlier[i], CONTRACT_FIRST, preferred_element_type=F32)
        rows = slice(i * FPTS, (i + 1) * FPTS)
        out[rows, :] = start[rows, :] - 0.5 * both


def passed_along(value, steps):
    count = lax.axis_size("sub")
    return lax.ppermute(value, "sub", [(s, (s + steps) % count) for s in range(count)])


def swapped(value, mask):
    count = lax.axis_size("grp")
    return lax.ppermute(value, "grp", [(s, s ^ mask) for s in range(count)])


def hypercube(value):
    two = swapped(value, 2)
    one = swapped(value, 1)
    return [value, one, two, swapped(two, 1)]


def exchanged(blocks):
    return [blocks[0]] + [swapped(blocks[j], j) for j in range(1, len(blocks))]


def along_links(blocks, sign):
    return [b if link == REACH else passed_along(b, sign * (link - REACH)) for link, b in enumerate(blocks)]


def body(schur, rhs, start, project, coarse_basis, owner_of_face, mortar_of_face, mortar_order, subdomain_map, vertex_ids):
    subs, grps = lax.axis_size("sub"), lax.axis_size("grp")
    z = Sizes(subs, grps, schur, project, coarse_basis, rhs)
    ids = jnp.stack([lax.axis_index("sub"), lax.axis_index("grp")]).astype(jnp.int32)
    shape = jax.ShapeDtypeStruct
    matrix, target, first = schur[0], rhs[0], start[0]

    packed_rows = z.rows + z.rows * z.tail // z.lanes
    trace_b = call(narrow_kernel, z, [VMEM], shape((packed_rows, z.lanes), BF), (first,))
    blocks = hypercube(trace_b)

    table = pl.pallas_call(
        functools.partial(table_kernel, z),
        out_shape=shape((z.t_end,), jnp.int32),
        in_specs=[SMEM] * 6,
        out_specs=SMEM,
        scratch_shapes=[pltpu.SMEM((LINKS,), jnp.int32), pltpu.SMEM((z.faces + 1,), jnp.int32)],
    )(ids, owner_of_face.reshape(-1), mortar_of_face.reshape(-1), mortar_order.reshape(-1), subdomain_map, vertex_ids.reshape(-1))

    joined = jnp.concatenate([project[0], coarse_basis[0]], axis=1) if z.own == z.corners else None
    assert joined is not None

    def extended(value):
        tables = value[:, : MODES * FPTS].reshape(z.own, MODES, FPTS)
        coarse = value[:, MODES * FPTS :].reshape(z.corners, z.own, FPTS).transpose(1, 0, 2)
        return jnp.concatenate([tables, coarse, coarse], axis=1)

    ext_own = extended(joined)
    exts = [ext_own] + [extended(v) for v in hypercube(joined)[1:]]

    my_corners = lax.dynamic_index_in_dim(
        vertex_ids, lax.dynamic_index_in_dim(subdomain_map, lax.axis_index("sub"), 0, False), 0, False
    )
    corner_hot = (my_corners[:, None] == jnp.arange(z.wide - z.rhs, dtype=jnp.int32)[None, :]).astype(BF)
    cext = lax.dot_general(coarse_basis[0], corner_hot, CONTRACT_FIRST, preferred_element_type=F32).astype(BF)

    part = shape((z.own, z.share, z.wide), BF)
    thin = shape((z.own, z.share, z.rhs), BF)
    link_wide = [shape((CAP, z.share, z.wide), BF)] * LINKS
    link_thin = [shape((CAP, z.share, z.rhs), BF)] * LINKS
    reply = [shape((CAP + z.extra, z.share, z.rhs), BF)] * LINKS
    vertex_shape = shape((2, z.vertices, z.rhs), BF) if z.near else shape((z.vertices, z.rhs), F32)
    g_shape = [shape((MORT_OWN * z.share, z.vertices), BF)] * 2

    def far(vertex):
        if not z.near:
            return []
        return [passed_along(vertex, off) for off in range(REACH + 1, subs - REACH)]

    def summed(vertex):
        if z.near:
            return jnp.zeros((8, 128), F32)
        return lax.psum(vertex, ("sub", "grp"))

    *parts, resid = call(
        first_kernel,
        z,
        [SMEM] + [VMEM] * 8,
        [part] * grps + [shape((z.rows, z.rhs), F32)],
        (ids, matrix, *blocks, target, ext_own, cext),
        (
            pltpu.VMEM((z.all_rows, z.rhs), BF),
            pltpu.VMEM((z.rows, z.wide), BF),
            pltpu.VMEM((z.own, MODES, z.wide), BF),
        ),
    )
    parts = exchanged(parts)
    outgoing = call(pack_kernel, z, [SMEM] + [VMEM] * 4, link_wide, (table, *parts), (pltpu.VMEM((z.faces, z.share, z.wide), BF),))
    arrived = along_links(outgoing, 1)
    *replies, vertex, g_high, g_low = call(
        average_first,
        z,
        [SMEM] * 2 + [VMEM] * LINKS,
        reply + [vertex_shape] + g_shape,
        (ids, table, *arrived),
        (pltpu.VMEM((MORT_OWN + 1, z.share, z.wide), F32), pltpu.VMEM((MORT_OWN + 1, z.share, z.rhs), BF)),
    )
    answered = along_links(replies, -1)
    fars = far(vertex)
    count = z.faces + z.faces // 2 + (3 if z.near else 0)
    spread = call(
        spread_first,
        z,
        [SMEM] + [VMEM] * (LINKS + len(fars)),
        shape((count, z.share, z.lanes), BF),
        (table, *answered, *fars),
        (pltpu.VMEM((SLOTS, z.share, z.rhs), BF),),
    )
    shares = hypercube(spread)
    *parts, earlier = call(
        second_kernel,
        z,
        [SMEM] * 2 + [VMEM] * (1 + 2 * grps + 2),
        [thin] * grps + [shape((z.own, MODES + 2 * z.corners, z.rhs), BF)],
        (ids, table, matrix, *shares, *exts, summed(vertex), resid),
        (
            pltpu.VMEM((z.faces, MODES + 2 * z.corners, z.rhs), BF),
            pltpu.VMEM((z.all_rows, z.rhs), BF),
            pltpu.VMEM((z.vertices, z.rhs), F32),
            pltpu.VMEM((z.rows, z.rhs), BF),
            pltpu.VMEM((z.own, MODES, z.rhs), BF),
        ),
    )
    parts = exchanged(parts)
    outgoing = call(pack_kernel, z, [SMEM] + [VMEM] * 4, link_thin, (table, *parts), (pltpu.VMEM((z.faces, z.share, z.rhs), BF),))
    arrived = along_links(outgoing, 1)
    *replies, vertex = call(
        average_second,
        z,
        [SMEM] * 2 + [VMEM] * (LINKS + 2),
        reply + [vertex_shape],
        (ids, table, *arrived, g_high, g_low),
        (pltpu.VMEM((MORT_OWN + 1, z.share, z.rhs), F32), pltpu.VMEM((MORT_OWN + 1, z.share, z.rhs), BF)),
    )
    answered = along_links(replies, -1)
    fars = far(vertex)
    outs = call(
        spread_second,
        z,
        [SMEM] * 2 + [VMEM] * (LINKS + len(fars)),
        [shape((z.own + z.extra, z.share, z.rhs), BF)] * grps,
        (ids, table, *answered, *fars),
        (pltpu.VMEM((SLOTS, z.share, z.rhs), BF),),
    )
    shares = exchanged(outs)
    result = call(
        last_kernel,
        z,
        [SMEM] * 2 + [VMEM] * (grps + 4),
        shape((z.rows, z.rhs), F32),
        (ids, table, *shares, ext_own, summed(vertex), earlier, first),
        (
            pltpu.VMEM((z.own, MODES + 2 * z.corners, z.rhs), BF),
            pltpu.VMEM((z.vertices, z.rhs), F32),
        ),
    )
    return result[None]


def solution(mesh):
    return jax.shard_map(
        body,
        mesh=mesh,
        in_specs=(
            P("sub", "grp", None),
            P("sub", "grp", None),
            P("sub", "grp", None),
            P("sub", "grp", None),
            P("sub", None, "grp"),
            P(),
            P(),
            P(),
            P(),
            P(),
        ),
        out_specs=P("sub", "grp", None),
        check_vma=False,
    )
```

time: 200 us -> 147 us (0.73)
  blocking collectives: 109 us -> 0 us
  waiting for transfers between devices: 23.5 us -> 54.6 us
  Pallas kernels: 0 us -> 27.1 us
  matrix products: 9.64 us -> 0.97 us
  starting transfers between devices: 36.2 us -> 38.6 us
  local copies, waits for them, and re-layouts: 17.4 us -> 19.4 us
    psum x2 -> x0, blocking collectives: 73.8 us -> none  [body(): vertex = lax.psum(spread, ('sub', 'grp'))]
    ppermute x20 -> x40, waiting for transfers between devices: 18.1 us -> 54.6 us  [the longest x22 41.7 us: passed_along(): lax.ppermute(value, 'sub', [(s, (s + steps) % count) for s in range(count)])]
    pallas_call x0 -> x11, Pallas kernels: none -> 27.1 us  [the longest x10 24.8 us: call(): pl.pallas_call(functools.partial(kernel, sizes), out_shape=outs, in_specs...]
    all_gather x2 -> x0, blocking collectives: 19.4 us -> none  [body(): lax.all_gather(trace_b, 'grp', axis=0, tiled=True)]
    all_to_all x2 -> x0, blocking collectives: 15.3 us -> none  [the longest x1 7.67 us: body(): lax.all_to_all(coeffs, 'grp', split_axis=2, concat_axis=0, tiled=True)]
    ppermute x20 -> x40, starting transfers between devices: 29.5 us -> 38.6 us  [the longest x22 26.7 us: passed_along(): lax.ppermute(value, 'sub', [(s, (s + steps) % count) for s in range(count)])]
    dot_general x24 -> x1, matrix products: 9.64 us -> 0.97 us  [body(): lax.dot_general(coarse_basis[0], corner_hot, CONTRACT_FIRST, preferred_el...]
    all_to_all x2 -> x0, starting transfers between devices: 6.73 us -> none  [the longest x1 3.37 us: body(): lax.all_to_all(coeffs, 'grp', split_axis=2, concat_axis=0, tiled=True)]
  transfers between devices with their start and end apart: 22 -> 40, of which waited for: 8 -> 16; matrix products, arithmetic and copies ran while one was open for 3% -> 9% of each run, Pallas kernels for 0% -> 2%
where the time goes in v1:
time: 147 us; the launch traced here: 146 us
  waiting for transfers between devices  54.6 us (37%)
  starting transfers between devices  38.6 us (26%)
  Pallas kernels  27.1 us (18%)
  local copies, waits for them, and re-layouts  19.4 us (13%)
  other arithmetic  3.49 us (2%)
  between operations  2.29 us (2%)
    ppermute x22, waiting for transfers between devices, passed_along(): lax.ppermute(value, 'sub', [(s, (s + steps) % count) for s in range(count)])  41.7 us
    ppermute x22, starting transfers between devices, passed_along(): lax.ppermute(value, 'sub', [(s, (s + steps) % count) for s in range(count)])  26.7 us
    pallas_call x10, Pallas kernels, call(): pl.pallas_call(functools.partial(kernel, sizes), out_shape=outs, in_specs...  24.8 us
    ppermute x18, waiting for transfers between devices, swapped(): return lax.ppermute(value, 'grp', [(s, s ^ mask) for s in range(count)])  12.9 us
    ppermute x18, starting transfers between devices, swapped(): return lax.ppermute(value, 'grp', [(s, s ^ mask) for s in range(count)])  11.9 us
    unnamed x91, local copies, waits for them, and re-layouts  8.9 us
  transfers between devices with their start and end apart: 40, of which 16 were waited for; matrix products, arithmetic and copies ran while one was open for 9% of the time, Pallas kernels for 2%

profile of v1, /device:TPU:0, one launch (start us, length us, event | category | flops | bytes accessed | tf_op | source)
XLA Modules:
  0.0 146.4 jit_solution(12603791385447987241)
XLA Ops:
  0.0 2.1 %copy.23 = f32[1,512,192]{2,1,0:T(8,128)} copy(f32[1,512,192]{1,2,0:T(8,128)} %param.12) | data formatting | bytes 786432 | tf_op args[2]
  2.1 1.8 %shard_map.101.b0 = bf16[768,128]{1,0:T(8,128)(2,1)} custom-call(f32[512,192]{1,0:T(8,128)} %bitcast.29), custom_call_target="tpu_custom_call" | custom-call | tf_op jit(solution)/shard_map/pallas_call | solution.py:61
  3.9 3.0 %collective-permute-start.1 = (bf16[768,128]{1,0:T(8,128)(2,1)}, bf16[768,128]{1,0:T(8,128)(2,1)S(1)}, u32[]{:S(2)}, u32[]{:S(2)}) collective-permute-start(bf16[768,128]{1,0:T(8,128)(2,1)} %shard_map.101.b0), channel_id=1, source_target_pairs={{0,2},{1,3},{2,0},{3,1},{4,6},{5,7},{6,4},{7,5},{8,10},{9,11},{10,... | collective-permute-start | bytes 589832 | tf_op jit(solution)/shard_map/ppermute | solution.py:322
  6.8 1.3 dynamic_slice.8
  11.4 1.0 convolution_convert_fusion
  13.2 1.0 reshape_squeeze.6
  14.2 1.0 copy.24
  17.9 4.2 %shard_map.102 = (bf16[8,16,256]{2,1,0:T(8,128)(2,1)}, bf16[8,16,256]{2,1,0:T(8,128)(2,1)}, bf16[8,16,256]{2,1,0:T(8,128)(2,1)}, bf16[8,16,256]{2,1,0:T(8,128)(2,1)}, f32[512,192]{1,0:T(8,128)}) custom-call(s32[2]{0:T(128)} %pad_add_fusion.ids, bf16[512,2048]{1,0:T(8,128)(2,1)} %bitcast.27, bf16[768,128]{1,0:T(8,128)(2,1)} %shard_map.101.b0, ...), custom_call_target="tpu_custom_call" | custom-call | tf_op jit(solution)/shard_map/pallas_call | solution.py:61
  22.2 1.8 %collective-permute-start.5 = (bf16[8,16,256]{2,1,0:T(8,128)(2,1)}, bf16[8,16,256]{2,1,0:T(8,128)(2,1)S(1)}, u32[]{:S(2)}, u32[]{:S(2)}) collective-permute-start(bf16[8,16,256]{2,1,0:T(8,128)(2,1)} %get-tuple-element.46), channel_id=1, source_target_pairs={{0,3},{1,2},{2,1},{3,0},{4,7},{5,6},{6,5},{7,4},{8,11},{9,10},{10,... | collective-permute-start | bytes 196616 | tf_op jit(solution)/shard_map/ppermute | solution.py:322
  27.7 2.3 %shard_map.100.table = s32[152]{0:T(256)} custom-call(s32[2]{0:T(128)} %pad_add_fusion.ids, s32[256]{0:T(256)} %reshape.32.owner, s32[256]{0:T(256)} %reshape.33.mortar, s32[128]{0:T(128)} %reshape.34.order, s32[8]{0:T(128)} %smap.1, s32[64]{0:T(128)} %reshape.35.vids), custom_call_target="tpu_custom_call" | custom-call | tf_op jit(solution)/shard_map/pallas_call | solution.py:350
  30.7 1.7 %shard_map.103 = (bf16[8,16,256]{2,1,0:T(8,128)(2,1)}, bf16[8,16,256]{2,1,0:T(8,128)(2,1)}, bf16[8,16,256]{2,1,0:T(8,128)(2,1)}, bf16[8,16,256]{2,1,0:T(8,128)(2,1)}, bf16[8,16,256]{2,1,0:T(8,128)(2,1)}) custom-call(s32[152]{0:T(256)} %shard_map.100.table, bf16[8,16,256]{2,1,0:T(8,128)(2,1)} %get-tuple-element.43.c0, bf16[8,16,256]{2,1,0:T(8,128)(2,1)} %copy-done.24, ...), custom_call_target="tpu_custom_call" | custom-call | tf_op jit(solution)/shard_map/pallas_call | solution.py:61
  32.4 3.6 %collective-permute-start.6 = (bf16[8,16,256]{2,1,0:T(8,128)(2,1)}, bf16[8,16,256]{2,1,0:T(8,128)(2,1)S(1)}, u32[]{:S(2)}, u32[]{:S(2)}) collective-permute-start(bf16[8,16,256]{2,1,0:T(8,128)(2,1)} %get-tuple-element.47), channel_id=1, source_target_pairs={{0,24},{4,28},{8,0},{12,4},{16,8},{20,12},{24,16},{28,20},{1,25},{... | collective-permute-start | bytes 196616 | tf_op jit(solution)/shard_map/ppermute | solution.py:317
  36.0 1.4 collective-permute-start.7
  38.0 1.0 collective-permute-start.9
  39.0 1.5 %collective-permute-done.7.a1 = bf16[8,16,256]{2,1,0:T(8,128)(2,1)S(1)} collective-permute-done((bf16[8,16,256]{2,1,0:T(8,128)(2,1)}, bf16[8,16,256]{2,1,0:T(8,128)(2,1)S(1)}, u32[]{:S(2)}, u32[]{:S(2)}) %collective-permute-start.7) | collective-permute-done | bytes 65568 | tf_op jit(solution)/shard_map/ppermute | solution.py:317
  40.5 4.7 %collective-permute-done.8.a3 = bf16[8,16,256]{2,1,0:T(8,128)(2,1)S(1)} collective-permute-done((bf16[8,16,256]{2,1,0:T(8,128)(2,1)}, bf16[8,16,256]{2,1,0:T(8,128)(2,1)S(1)}, u32[]{:S(2)}, u32[]{:S(2)}) %collective-permute-start.8) | collective-permute-done | bytes 65568 | tf_op jit(solution)/shard_map/ppermute | solution.py:317
  45.8 2.2 %shard_map.104 = (bf16[10,16,192]{2,1,0:T(8,128)(2,1)}, bf16[10,16,192]{2,1,0:T(8,128)(2,1)}, bf16[10,16,192]{2,1,0:T(8,128)(2,1)}, bf16[10,16,192]{2,1,0:T(8,12...) custom-call(s32[2]{0:T(128)} %pad_add_fusion.ids, ...), custom_call_target="tpu_custom_call" | custom-call | tf_op jit(solution)/shard_map/pallas_call | solution.py:61
  48.0 1.6 %collective-permute-start.11 = (bf16[10,16,192]{2,1,0:T(8,128)(2,1)}, bf16[10,16,192]{2,1,0:T(8,128)(2,1)S(1)}, u32[]{:S(2)}, u32[]{:S(2)}) collective-permute-start(bf16[10,16,192]{2,1,0:T(8,128)(2,1)} %get-tuple-element.53), channel_id=1, source_target_pairs={{0,4},{4,8},{8,12},{12,16},{16,20},{20,24},{24,28},{28,0},{1,5},{5... | collective-permute-start | bytes 184328 | tf_op jit(solution)/shard_map/ppermute | solution.py:317
  49.6 3.2 %collective-permute-start.12 = (bf16[10,16,192]{2,1,0:T(8,128)(2,1)}, bf16[10,16,192]{2,1,0:T(8,128)(2,1)S(1)}, u32[]{:S(2)}, u32[]{:S(2)}) collective-permute-start(bf16[10,16,192]{2,1,0:T(8,128)(2,1)} %get-tuple-element.55), channel_id=1, source_target_pairs={{0,28},{4,0},{8,4},{12,8},{16,12},{20,16},{24,20},{28,24},{1,29},{... | collective-permute-start | bytes 184328 | tf_op jit(solution)/shard_map/ppermute | solution.py:317
  52.8 1.9 %collective-permute-start.13 = (bf16[10,16,192]{2,1,0:T(8,128)(2,1)}, bf16[10,16,192]{2,1,0:T(8,128)(2,1)S(1)}, u32[]{:S(2)}, u32[]{:S(2)}) collective-permute-start(bf16[10,16,192]{2,1,0:T(8,128)(2,1)} %get-tuple-element.56), channel_id=1, source_target_pairs={{0,24},{4,28},{8,0},{12,4},{16,8},{20,12},{24,16},{28,20},{1,25},{... | collective-permute-start | bytes 184328 | tf_op jit(solution)/shard_map/ppermute | solution.py:317
  54.8 5.7 %collective-permute-done.14.refs_5_ = bf16[2,16,192]{2,1,0:T(8,128)(2,1)S(1)} collective-permute-done((bf16[2,16,192]{2,1,0:T(8,128)(2,1)}, bf16[2,16,192]{2,1,0:T(8,128)(2,1)S(1)}, u32[]{:S(2)}, u32[]{:S(2)}) %collective-permute-start.14) | collective-permute-done | bytes 12320 | tf_op jit(solution)/shard_map/ppermute | solution.py:317
  60.7 4.7 %collective-permute-done.15.refs_6_ = bf16[2,16,192]{2,1,0:T(8,128)(2,1)S(1)} collective-permute-done((bf16[2,16,192]{2,1,0:T(8,128)(2,1)}, bf16[2,16,192]{2,1,0:T(8,128)(2,1)S(1)}, u32[]{:S(2)}, u32[]{:S(2)}) %collective-permute-start.15) | collective-permute-done | bytes 12320 | tf_op jit(solution)/shard_map/ppermute | solution.py:317
  65.3 1.0 collective-permute-start.16
  66.4 3.8 %collective-permute-done.16.refs_7_ = bf16[2,16,192]{2,1,0:T(8,128)(2,1)S(1)} collective-permute-done((bf16[2,16,192]{2,1,0:T(8,128)(2,1)}, bf16[2,16,192]{2,1,0:T(8,128)(2,1)S(1)}, u32[]{:S(2)}, u32[]{:S(2)}) %collective-permute-start.16) | collective-permute-done | bytes 12320 | tf_op jit(solution)/shard_map/ppermute | solution.py:317
  70.9 1.9 %shard_map.105.refs_0_ = bf16[51,16,128]{2,1,0:T(8,128)(2,1)} custom-call(s32[152]{0:T(256)} %shard_map.100.table, bf16[10,16,192]{2,1,0:T(8,128)(2,1)} %copy-done.12, bf16[10,16,192]{2,1,0:T(8,128)(2,1)} %copy-done.13, bf16[10,16,192]{2,1,0:T(8,128)(2,1)} %get-tuple-element.54.refs_2_, bf16[10,16,192]{2,1,0:T(8,128)(2,1)} %copy-done.14, ...), custom_call_target="tpu_custom_call" | custom-call | tf_op jit(solution)/shard_map/pallas_call | solution.py:61
  73.3 1.5 %collective-permute-start.21 = (bf16[8,4608]{1,0:T(8,128)(2,1)S(1)}, bf16[8,4608]{1,0:T(8,128)(2,1)S(1)}, u32[]{:S(2)}, u32[]{:S(2)}) collective-permute-start(bf16[8,4608]{1,0:T(8,128)(2,1)S(1)} %pad_maximum_fusion.4), channel_id=1, source_target_pairs={{0,2},{1,3},{2,0},{3,1},{4,6},{5,7},{6,4},{7,5},{8,10},{9,11},{10,... | collective-permute-start | bytes 221192 | tf_op jit(solution)/shard_map/ppermute | solution.py:322
  74.9 4.7 %collective-permute-done.21 = bf16[8,4608]{1,0:T(8,128)(2,1)S(1)} collective-permute-done((bf16[8,4608]{1,0:T(8,128)(2,1)S(1)}, bf16[8,4608]{1,0:T(8,128)(2,1)S(1)}, u32[]{:S(2)}, u32[]{:S(2)}) %collective-permute-start.21) | collective-permute-done | bytes 73760 | tf_op jit(solution)/shard_map/ppermute | solution.py:322
  83.4 4.7 %shard_map.106 = (bf16[8,16,192]{2,1,0:T(8,128)(2,1)}, bf16[8,16,192]{2,1,0:T(8,128)(2,1)}, bf16[8,16,192]{2,1,0:T(8,128)(2,1)}, bf16[8,16,192]{2,1,0:T(8,128)(2,1)}, bf16[8,80,192]{2,1,0:T(8,128)(2,1)}) custom-call(s32[2]{0:T(128)} %pad_add_fusion.ids, s32[152]{0:T(256)} %shard_map.100.table, bf16[512,2048]{1,0:T(8,128)(2,1)} %bitcast.28, ...), custom_call_target="tpu_custom_call" | custom-call | tf_op jit(solution)/shard_map/pallas_call | solution.py:61
  89.1 0.9 collective-permute-start.25
  90.0 3.7 %collective-permute-done.24.c2 = bf16[8,16,192]{2,1,0:T(8,128)(2,1)S(1)} collective-permute-done((bf16[8,16,192]{2,1,0:T(8,128)(2,1)}, bf16[8,16,192]{2,1,0:T(8,128)(2,1)S(1)}, u32[]{:S(2)}, u32[]{:S(2)}) %collective-permute-start.24) | collective-permute-done | bytes 49184 | tf_op jit(solution)/shard_map/ppermute | solution.py:322
  94.4 1.7 %shard_map.107 = (bf16[8,16,192]{2,1,0:T(8,128)(2,1)}, bf16[8,16,192]{2,1,0:T(8,128)(2,1)}, bf16[8,16,192]{2,1,0:T(8,128)(2,1)}, bf16[8,16,192]{2,1,0:T(8,128)(2,1)}, bf16[8,16,192]{2,1,0:T(8,128)(2,1)}) custom-call(s32[152]{0:T(256)} %shard_map.100.table, bf16[8,16,192]{2,1,0:T(8,128)(2,1)} %get-tuple-element.59.c0, bf16[8,16,192]{2,1,0:T(8,128)(2,1)} %copy-done.31, ...), custom_call_target="tpu_custom_call" | custom-call | tf_op jit(solution)/shard_map/pallas_call | solution.py:61
  96.1 3.0 %collective-permute-start.26 = (bf16[8,16,192]{2,1,0:T(8,128)(2,1)}, bf16[8,16,192]{2,1,0:T(8,128)(2,1)S(1)}, u32[]{:S(2)}, u32[]{:S(2)}) collective-permute-start(bf16[8,16,192]{2,1,0:T(8,128)(2,1)} %get-tuple-element.63), channel_id=1, source_target_pairs={{0,24},{4,28},{8,0},{12,4},{16,8},{20,12},{24,16},{28,20},{1,25},{... | collective-permute-start | bytes 147464 | tf_op jit(solution)/shard_map/ppermute | solution.py:317
  99.5 1.6 %collective-permute-start.28 = (bf16[8,16,192]{2,1,0:T(8,128)(2,1)}, bf16[8,16,192]{2,1,0:T(8,128)(2,1)S(1)}, u32[]{:S(2)}, u32[]{:S(2)}) collective-permute-start(bf16[8,16,192]{2,1,0:T(8,128)(2,1)} %get-tuple-element.66), channel_id=1, source_target_pairs={{0,4},{4,8},{8,12},{12,16},{16,20},{20,24},{24,28},{28,0},{1,5},{5... | collective-permute-start | bytes 147464 | tf_op jit(solution)/shard_map/ppermute | solution.py:317
  101.9 1.7 %collective-permute-done.27.a1 = bf16[8,16,192]{2,1,0:T(8,128)(2,1)S(1)} collective-permute-done((bf16[8,16,192]{2,1,0:T(8,128)(2,1)}, bf16[8,16,192]{2,1,0:T(8,128)(2,1)S(1)}, u32[]{:S(2)}, u32[]{:S(2)}) %collective-permute-start.27) | collective-permute-done | bytes 49184 | tf_op jit(solution)/shard_map/ppermute | solution.py:317
  103.5 3.5 %collective-permute-done.28.a3 = bf16[8,16,192]{2,1,0:T(8,128)(2,1)S(1)} collective-permute-done((bf16[8,16,192]{2,1,0:T(8,128)(2,1)}, bf16[8,16,192]{2,1,0:T(8,128)(2,1)S(1)}, u32[]{:S(2)}, u32[]{:S(2)}) %collective-permute-start.28) | collective-permute-done | bytes 49184 | tf_op jit(solution)/shard_map/ppermute | solution.py:317
  108.0 2.2 %shard_map.108 = (bf16[10,16,192]{2,1,0:T(8,128)(2,1)}, bf16[10,16,192]{2,1,0:T(8,128)(2,1)}, bf16[10,16,192]{2,1,0:T(8,128)(2,1)}, bf16[10,16,192]{2,1,0:T(8,12...) custom-call(s32[2]{0:T(128)} %pad_add_fusion.ids, s32[152]{0:T(256)} %shard_map.100.table, ...), custom_call_target="tpu_custom_call" | custom-call | tf_op jit(solution)/shard_map/pallas_call | solution.py:61
  110.2 1.0 collective-permute-start.31
  111.2 3.8 %collective-permute-start.32 = (bf16[10,16,192]{2,1,0:T(8,128)(2,1)}, bf16[10,16,192]{2,1,0:T(8,128)(2,1)S(1)}, u32[]{:S(2)}, u32[]{:S(2)}) collective-permute-start(bf16[10,16,192]{2,1,0:T(8,128)(2,1)} %get-tuple-element.73), channel_id=1, source_target_pairs={{0,28},{4,0},{8,4},{12,8},{16,12},{20,16},{24,20},{28,24},{1,29},{... | collective-permute-start | bytes 184328 | tf_op jit(solution)/shard_map/ppermute | solution.py:317
  115.0 2.0 %collective-permute-start.33 = (bf16[10,16,192]{2,1,0:T(8,128)(2,1)}, bf16[10,16,192]{2,1,0:T(8,128)(2,1)S(1)}, u32[]{:S(2)}, u32[]{:S(2)}) collective-permute-start(bf16[10,16,192]{2,1,0:T(8,128)(2,1)} %get-tuple-element.74), channel_id=1, source_target_pairs={{0,24},{4,28},{8,0},{12,4},{16,8},{20,12},{24,16},{28,20},{1,25},{... | collective-permute-start | bytes 184328 | tf_op jit(solution)/shard_map/ppermute | solution.py:317
  117.0 5.7 %collective-permute-done.34.refs_5_ = bf16[2,16,192]{2,1,0:T(8,128)(2,1)S(1)} collective-permute-done((bf16[2,16,192]{2,1,0:T(8,128)(2,1)}, bf16[2,16,192]{2,1,0:T(8,128)(2,1)S(1)}, u32[]{:S(2)}, u32[]{:S(2)}) %collective-permute-start.34) | collective-permute-done | bytes 12320 | tf_op jit(solution)/shard_map/ppermute | solution.py:317
  122.7 4.8 %collective-permute-done.35.refs_6_ = bf16[2,16,192]{2,1,0:T(8,128)(2,1)S(1)} collective-permute-done((bf16[2,16,192]{2,1,0:T(8,128)(2,1)}, bf16[2,16,192]{2,1,0:T(8,128)(2,1)S(1)}, u32[]{:S(2)}, u32[]{:S(2)}) %collective-permute-start.35) | collective-permute-done | bytes 12320 | tf_op jit(solution)/shard_map/ppermute | solution.py:317
  128.0 4.4 %collective-permute-done.36.refs_7_ = bf16[2,16,192]{2,1,0:T(8,128)(2,1)S(1)} collective-permute-done((bf16[2,16,192]{2,1,0:T(8,128)(2,1)}, bf16[2,16,192]{2,1,0:T(8,128)(2,1)S(1)}, u32[]{:S(2)}, u32[]{:S(2)}) %collective-permute-start.36) | collective-permute-done | bytes 12320 | tf_op jit(solution)/shard_map/ppermute | solution.py:317
  133.1 1.8 %shard_map.109 = (bf16[10,16,192]{2,1,0:T(8,128)(2,1)}, bf16[10,16,192]{2,1,0:T(8,128)(2,1)}, bf16[10,16,192]{2,1,0:T(8,128)(2,1)}, bf16[10,16,192]{2,1,0:T(8,128)(2,1)}) custom-call(s32[2]{0:T(128)} %pad_add_fusion.ids, s32[152]{0:T(256)} %shard_map.100.table, bf16[10,16,192]{2,1,0:T(8,128)(2,1)} %copy-done.8, bf16[10,16,192]{2,1,0:T(8,128)(2,1)} %copy-done.9, ...), custom_call_target="tpu_custom_call" | custom-call | tf_op jit(solution)/shard_map/pallas_call | solution.py:61
  135.0 0.9 collective-permute-start.38
  135.9 0.9 collective-permute-start.39
  136.8 3.7 %collective-permute-done.38.refs_2_ = bf16[10,16,192]{2,1,0:T(8,128)(2,1)S(1)} collective-permute-done((bf16[10,16,192]{2,1,0:T(8,128)(2,1)}, bf16[10,16,192]{2,1,0:T(8,128)(2,1)S(1)}, u32[]{:S(2)}, u32[]{:S(2)}) %collective-permute-start.38) | collective-permute-done | bytes 61472 | tf_op jit(solution)/shard_map/ppermute | solution.py:322
  141.9 2.6 %shard_map.110 = f32[512,192]{1,0:T(8,128)} custom-call(s32[2]{0:T(128)} %pad_add_fusion.ids, s32[152]{0:T(256)} %shard_map.100.table, bf16[10,16,192]{2,1,0:T(8,128)(2,1)} %get-tuple-element.76.refs_0_, bf16[10,16,192]{2,1,0:T(8,128)(2,1)} %copy-done.16, bf16[10,16,192]{2,1,0:T(8,128)(2,1)} %copy-done.17, bf16[10,16,192]{2,1,0:T(8,128)(2,1)} %copy-done.18, ...), custom_call_target="tpu_custom_call" | custom-call | tf_op jit(solution)/shard_map/pallas_call | solution.py:61
  144.5 2.0 %copy.30 = f32[1,512,192]{1,2,0:T(8,128)} copy(f32[1,512,192]{2,1,0:T(8,128)} %bitcast.32) | data formatting | bytes 786432 | tf_op jit(solution)/shard_map/broadcast_in_dim | solution.py:475
  (168 shorter events, 22.0 us)
Async XLA Ops:
  0.0 14.2 %copy-start = (f32[1,512,192]{1,2,0:T(8,128)S(1)}, f32[1,512,192]{1,2,0:T(8,128)}, u32[]{:S(2)}) copy-start(f32[1,512,192]{1,2,0:T(8,128)} %param.11) | copy-start | bytes 1179652
  3.9 11.4 %collective-permute-start.1 = (bf16[768,128]{1,0:T(8,128)(2,1)}, bf16[768,128]{1,0:T(8,128)(2,1)S(1)}, u32[]{:S(2)}, u32[]{:S(2)}) collective-permute-start(bf16[768,128]{1,0:T(8,128)(2,1)} %shard_map.101.b0), channel_id=1, source_target_pairs={{0,2},{1,3},{2,0},{3,1},{4,6},{5,7},{6,4},{7,5},{8,10},{9,11},{10,... | collective-permute-start | bytes 589832 | tf_op jit(solution)/shard_map/ppermute | solution.py:322
  6.8 10.3 %collective-permute-start = (bf16[768,128]{1,0:T(8,128)(2,1)}, bf16[768,128]{1,0:T(8,128)(2,1)S(1)}, u32[]{:S(2)}, u32[]{:S(2)}) collective-permute-start(bf16[768,128]{1,0:T(8,128)(2,1)} %shard_map.101.b0), channel_id=1, source_target_pairs={{0,1},{1,0},{2,3},{3,2},{4,5},{5,4},{6,7},{7,6},{8,9},{9,8},{10,11... | collective-permute-start | bytes 589832 | tf_op jit(solution)/shard_map/ppermute | solution.py:322
  15.2 9.9 %copy-start.43 = (s32[8,32,1]{1,2,0:T(1,128)S(1)}, s32[8,32,1]{1,2,0:T(1,128)}, u32[]{:S(2)}) copy-start(s32[8,32,1]{1,2,0:T(1,128)} %param.15) | copy-start | bytes 3076
  15.2 11.2 %copy-start.40 = (s32[8,32]{1,0:T(8,128)S(1)}, s32[8,32]{1,0:T(8,128)}, u32[]{:S(2)}) copy-start(s32[8,32]{1,0:T(8,128)} %param.16) | copy-start | bytes 3076
  15.2 11.9 %copy-start.42 = (s32[8,16]{1,0:T(8,128)S(1)}, s32[8,16]{1,0:T(8,128)}, u32[]{:S(2)}) copy-start(s32[8,16]{1,0:T(8,128)} %param.17) | copy-start | bytes 1540
  15.3 1.9 %collective-permute-start.2 = (bf16[768,128]{1,0:T(8,128)(2,1)S(1)}, bf16[768,128]{1,0:T(8,128)(2,1)S(1)}, u32[]{:S(2)}, u32[]{:S(2)}) collective-permute-start(bf16[768,128]{1,0:T(8,128)(2,1)S(1)} %collective-permute-done.1.b2), channel_id=1, source_target_pairs={{0,1},{1,0},{2,3},{3,2},{4,5},{5,4},{6,7},{7,6},{8,9},{9,8},{10,11... | collective-permute-start | bytes 589832 | tf_op jit(solution)/shard_map/ppermute | solution.py:322
  17.9 55.4 %copy-start.1 = (bf16[1,8,4096]{2,1,0:T(8,128)(2,1)S(1)}, bf16[1,8,4096]{2,1,0:T(8,128)(2,1)}, u32[]{:S(2)}) copy-start(bf16[1,8,4096]{2,1,0:T(8,128)(2,1)} %param.13) | copy-start | bytes 196612
  17.9 55.4 %copy-start.19 = (bf16[1,8,512]{2,1,0:T(8,128)(2,1)S(1)}, bf16[1,8,512]{2,1,0:T(8,128)(2,1)}, u32[]{:S(2)}) copy-start(bf16[1,8,512]{2,1,0:T(8,128)(2,1)} %param.14) | copy-start | bytes 24580
  22.1 7.9 %collective-permute-start.3 = (bf16[8,16,256]{2,1,0:T(8,128)(2,1)}, bf16[8,16,256]{2,1,0:T(8,128)(2,1)S(1)}, u32[]{:S(2)}, u32[]{:S(2)}) collective-permute-start(bf16[8,16,256]{2,1,0:T(8,128)(2,1)} %get-tuple-element.44), channel_id=1, source_target_pairs={{0,1},{1,0},{2,3},{3,2},{4,5},{5,4},{6,7},{7,6},{8,9},{9,8},{10,11... | collective-permute-start | bytes 196616 | tf_op jit(solution)/shard_map/ppermute | solution.py:322
  22.2 7.9 %collective-permute-start.4 = (bf16[8,16,256]{2,1,0:T(8,128)(2,1)}, bf16[8,16,256]{2,1,0:T(8,128)(2,1)S(1)}, u32[]{:S(2)}, u32[]{:S(2)}) collective-permute-start(bf16[8,16,256]{2,1,0:T(8,128)(2,1)} %get-tuple-element.45), channel_id=1, source_target_pairs={{0,2},{1,3},{2,0},{3,1},{4,6},{5,7},{6,4},{7,5},{8,10},{9,11},{10,... | collective-permute-start | bytes 196616 | tf_op jit(solution)/shard_map/ppermute | solution.py:322
  22.2 7.9 %collective-permute-start.5 = (bf16[8,16,256]{2,1,0:T(8,128)(2,1)}, bf16[8,16,256]{2,1,0:T(8,128)(2,1)S(1)}, u32[]{:S(2)}, u32[]{:S(2)}) collective-permute-start(bf16[8,16,256]{2,1,0:T(8,128)(2,1)} %get-tuple-element.46), channel_id=1, source_target_pairs={{0,3},{1,2},{2,1},{3,0},{4,7},{5,6},{6,5},{7,4},{8,11},{9,10},{10,... | collective-permute-start | bytes 196616 | tf_op jit(solution)/shard_map/ppermute | solution.py:322
  32.4 6.6 %collective-permute-start.6 = (bf16[8,16,256]{2,1,0:T(8,128)(2,1)}, bf16[8,16,256]{2,1,0:T(8,128)(2,1)S(1)}, u32[]{:S(2)}, u32[]{:S(2)}) collective-permute-start(bf16[8,16,256]{2,1,0:T(8,128)(2,1)} %get-tuple-element.47), channel_id=1, source_target_pairs={{0,24},{4,28},{8,0},{12,4},{16,8},{20,12},{24,16},{28,20},{1,25},{... | collective-permute-start | bytes 196616 | tf_op jit(solution)/shard_map/ppermute | solution.py:317
  36.0 4.5 %collective-permute-start.7 = (bf16[8,16,256]{2,1,0:T(8,128)(2,1)}, bf16[8,16,256]{2,1,0:T(8,128)(2,1)S(1)}, u32[]{:S(2)}, u32[]{:S(2)}) collective-permute-start(bf16[8,16,256]{2,1,0:T(8,128)(2,1)} %get-tuple-element.48), channel_id=1, source_target_pairs={{0,28},{4,0},{8,4},{12,8},{16,12},{20,16},{24,20},{28,24},{1,29},{... | collective-permute-start | bytes 196616 | tf_op jit(solution)/shard_map/ppermute | solution.py:317
  37.4 7.8 %collective-permute-start.8 = (bf16[8,16,256]{2,1,0:T(8,128)(2,1)}, bf16[8,16,256]{2,1,0:T(8,128)(2,1)S(1)}, u32[]{:S(2)}, u32[]{:S(2)}) collective-permute-start(bf16[8,16,256]{2,1,0:T(8,128)(2,1)} %get-tuple-element.50), channel_id=1, source_target_pairs={{0,4},{4,8},{8,12},{12,16},{16,20},{20,24},{24,28},{28,0},{1,5},{5... | collective-permute-start | bytes 196616 | tf_op jit(solution)/shard_map/ppermute | solution.py:317
  38.0 7.1 %collective-permute-start.9 = (bf16[8,16,256]{2,1,0:T(8,128)(2,1)}, bf16[8,16,256]{2,1,0:T(8,128)(2,1)S(1)}, u32[]{:S(2)}, u32[]{:S(2)}) collective-permute-start(bf16[8,16,256]{2,1,0:T(8,128)(2,1)} %get-tuple-element.51), channel_id=1, source_target_pairs={{0,8},{4,12},{8,16},{12,20},{16,24},{20,28},{24,0},{28,4},{1,9},{5... | collective-permute-start | bytes 196616 | tf_op jit(solution)/shard_map/ppermute | solution.py:317
  48.0 22.2 %collective-permute-start.10 = (bf16[10,16,192]{2,1,0:T(8,128)(2,1)}, bf16[10,16,192]{2,1,0:T(8,128)(2,1)S(1)}, u32[]{:S(2)}, u32[]{:S(2)}) collective-permute-start(bf16[10,16,192]{2,1,0:T(8,128)(2,1)} %get-tuple-element.52), channel_id=1, source_target_pairs={{0,8},{4,12},{8,16},{12,20},{16,24},{20,28},{24,0},{28,4},{1,9},{5... | collective-permute-start | bytes 184328 | tf_op jit(solution)/shard_map/ppermute | solution.py:317
  48.0 22.2 %collective-permute-start.11 = (bf16[10,16,192]{2,1,0:T(8,128)(2,1)}, bf16[10,16,192]{2,1,0:T(8,128)(2,1)S(1)}, u32[]{:S(2)}, u32[]{:S(2)}) collective-permute-start(bf16[10,16,192]{2,1,0:T(8,128)(2,1)} %get-tuple-element.53), channel_id=1, source_target_pairs={{0,4},{4,8},{8,12},{12,16},{16,20},{20,24},{24,28},{28,0},{1,5},{5... | collective-permute-start | bytes 184328 | tf_op jit(solution)/shard_map/ppermute | solution.py:317
  49.6 20.6 %collective-permute-start.12 = (bf16[10,16,192]{2,1,0:T(8,128)(2,1)}, bf16[10,16,192]{2,1,0:T(8,128)(2,1)S(1)}, u32[]{:S(2)}, u32[]{:S(2)}) collective-permute-start(bf16[10,16,192]{2,1,0:T(8,128)(2,1)} %get-tuple-element.55), channel_id=1, source_target_pairs={{0,28},{4,0},{8,4},{12,8},{16,12},{20,16},{24,20},{28,24},{1,29},{... | collective-permute-start | bytes 184328 | tf_op jit(solution)/shard_map/ppermute | solution.py:317
  52.8 17.4 %collective-permute-start.13 = (bf16[10,16,192]{2,1,0:T(8,128)(2,1)}, bf16[10,16,192]{2,1,0:T(8,128)(2,1)S(1)}, u32[]{:S(2)}, u32[]{:S(2)}) collective-permute-start(bf16[10,16,192]{2,1,0:T(8,128)(2,1)} %get-tuple-element.56), channel_id=1, source_target_pairs={{0,24},{4,28},{8,0},{12,4},{16,8},{20,12},{24,16},{28,20},{1,25},{... | collective-permute-start | bytes 184328 | tf_op jit(solution)/shard_map/ppermute | solution.py:317
  54.7 5.7 %collective-permute-start.14 = (bf16[2,16,192]{2,1,0:T(8,128)(2,1)}, bf16[2,16,192]{2,1,0:T(8,128)(2,1)S(1)}, u32[]{:S(2)}, u32[]{:S(2)}) collective-permute-start(bf16[2,16,192]{2,1,0:T(8,128)(2,1)} %get-tuple-element.57), channel_id=1, source_target_pairs={{0,12},{4,16},{8,20},{12,24},{16,28},{20,0},{24,4},{28,8},{1,13},{... | collective-permute-start | bytes 36872 | tf_op jit(solution)/shard_map/ppermute | solution.py:317
  60.5 9.8 %copy-start.37 = (bf16[2,16,192]{2,1,0:T(8,128)(2,1)}, bf16[2,16,192]{2,1,0:T(8,128)(2,1)S(1)}, u32[]{:S(2)}) copy-start(bf16[2,16,192]{2,1,0:T(8,128)(2,1)S(1)} %collective-permute-done.14.refs_5_) | copy-start | bytes 36868
  60.5 4.8 %collective-permute-start.15 = (bf16[2,16,192]{2,1,0:T(8,128)(2,1)}, bf16[2,16,192]{2,1,0:T(8,128)(2,1)S(1)}, u32[]{:S(2)}, u32[]{:S(2)}) collective-permute-start(bf16[2,16,192]{2,1,0:T(8,128)(2,1)} %get-tuple-element.57), channel_id=1, source_target_pairs={{0,16},{4,20},{8,24},{12,28},{16,0},{20,4},{24,8},{28,12},{1,17},{... | collective-permute-start | bytes 36872 | tf_op jit(solution)/shard_map/ppermute | solution.py:317
  65.3 4.8 %collective-permute-start.16 = (bf16[2,16,192]{2,1,0:T(8,128)(2,1)}, bf16[2,16,192]{2,1,0:T(8,128)(2,1)S(1)}, u32[]{:S(2)}, u32[]{:S(2)}) collective-permute-start(bf16[2,16,192]{2,1,0:T(8,128)(2,1)} %get-tuple-element.57), channel_id=1, source_target_pairs={{0,20},{4,24},{8,28},{12,0},{16,4},{20,8},{24,12},{28,16},{1,21},{... | collective-permute-start | bytes 36872 | tf_op jit(solution)/shard_map/ppermute | solution.py:317
  72.8 8.0 %collective-permute-start.18 = (bf16[51,16,128]{2,1,0:T(8,128)(2,1)}, bf16[51,16,128]{2,1,0:T(8,128)(2,1)S(1)}, u32[]{:S(2)}, u32[]{:S(2)}) collective-permute-start(bf16[51,16,128]{2,1,0:T(8,128)(2,1)} %shard_map.105.refs_0_), channel_id=1, source_target_pairs={{0,2},{1,3},{2,0},{3,1},{4,6},{5,7},{6,4},{7,5},{8,10},{9,11},{10,... | collective-permute-start | bytes 626696 | tf_op jit(solution)/shard_map/ppermute | solution.py:322
  73.3 6.2 %collective-permute-start.21 = (bf16[8,4608]{1,0:T(8,128)(2,1)S(1)}, bf16[8,4608]{1,0:T(8,128)(2,1)S(1)}, u32[]{:S(2)}, u32[]{:S(2)}) collective-permute-start(bf16[8,4608]{1,0:T(8,128)(2,1)S(1)} %pad_maximum_fusion.4), channel_id=1, source_target_pairs={{0,2},{1,3},{2,0},{3,1},{4,6},{5,7},{6,4},{7,5},{8,10},{9,11},{10,... | collective-permute-start | bytes 221192 | tf_op jit(solution)/shard_map/ppermute | solution.py:322
  74.9 5.0 %collective-permute-start.20 = (bf16[8,4608]{1,0:T(8,128)(2,1)S(1)}, bf16[8,4608]{1,0:T(8,128)(2,1)S(1)}, u32[]{:S(2)}, u32[]{:S(2)}) collective-permute-start(bf16[8,4608]{1,0:T(8,128)(2,1)S(1)} %pad_maximum_fusion.4), channel_id=1, source_target_pairs={{0,1},{1,0},{2,3},{3,2},{4,5},{5,4},{6,7},{7,6},{8,9},{9,8},{10,11... | collective-permute-start | bytes 221192 | tf_op jit(solution)/shard_map/ppermute | solution.py:322
  80.2 1.5 %collective-permute-start.22 = (bf16[8,4608]{1,0:T(8,128)(2,1)S(1)}, bf16[8,4608]{1,0:T(8,128)(2,1)S(1)}, u32[]{:S(2)}, u32[]{:S(2)}) collective-permute-start(bf16[8,4608]{1,0:T(8,128)(2,1)S(1)} %collective-permute-done.21), channel_id=1, source_target_pairs={{0,1},{1,0},{2,3},{3,2},{4,5},{5,4},{6,7},{7,6},{8,9},{9,8},{10,11... | collective-permute-start | bytes 221192 | tf_op jit(solution)/shard_map/ppermute | solution.py:322
  80.3 2.4 %collective-permute-start.17 = (bf16[51,16,128]{2,1,0:T(8,128)(2,1)}, bf16[51,16,128]{2,1,0:T(8,128)(2,1)S(1)}, u32[]{:S(2)}, u32[]{:S(2)}) collective-permute-start(bf16[51,16,128]{2,1,0:T(8,128)(2,1)} %shard_map.105.refs_0_), channel_id=1, source_target_pairs={{0,1},{1,0},{2,3},{3,2},{4,5},{5,4},{6,7},{7,6},{8,9},{9,8},{10,11... | collective-permute-start | bytes 626696 | tf_op jit(solution)/shard_map/ppermute | solution.py:322
  80.8 1.9 %collective-permute-start.19 = (bf16[51,16,128]{2,1,0:T(8,128)(2,1)S(1)}, bf16[51,16,128]{2,1,0:T(8,128)(2,1)S(1)}, u32[]{:S(2)}, u32[]{:S(2)}) collective-permute-start(bf16[51,16,128]{2,1,0:T(8,128)(2,1)S(1)} %collective-permute-done.18.refs_2_), channel_id=1, source_target_pairs={{0,1},{1,0},{2,3},{3,2},{4,5},{5,4},{6,7},{7,6},{8,9},{9,8},{10,11... | collective-permute-start | bytes 626696 | tf_op jit(solution)/shard_map/ppermute | solution.py:322
  88.2 1.9 %collective-permute-start.23 = (bf16[8,16,192]{2,1,0:T(8,128)(2,1)}, bf16[8,16,192]{2,1,0:T(8,128)(2,1)S(1)}, u32[]{:S(2)}, u32[]{:S(2)}) collective-permute-start(bf16[8,16,192]{2,1,0:T(8,128)(2,1)} %get-tuple-element.60), channel_id=1, source_target_pairs={{0,1},{1,0},{2,3},{3,2},{4,5},{5,4},{6,7},{7,6},{8,9},{9,8},{10,11... | collective-permute-start | bytes 147464 | tf_op jit(solution)/shard_map/ppermute | solution.py:322
  88.6 5.2 %collective-permute-start.24 = (bf16[8,16,192]{2,1,0:T(8,128)(2,1)}, bf16[8,16,192]{2,1,0:T(8,128)(2,1)S(1)}, u32[]{:S(2)}, u32[]{:S(2)}) collective-permute-start(bf16[8,16,192]{2,1,0:T(8,128)(2,1)} %get-tuple-element.61), channel_id=1, source_target_pairs={{0,2},{1,3},{2,0},{3,1},{4,6},{5,7},{6,4},{7,5},{8,10},{9,11},{10,... | collective-permute-start | bytes 147464 | tf_op jit(solution)/shard_map/ppermute | solution.py:322
  89.1 4.6 %collective-permute-start.25 = (bf16[8,16,192]{2,1,0:T(8,128)(2,1)}, bf16[8,16,192]{2,1,0:T(8,128)(2,1)S(1)}, u32[]{:S(2)}, u32[]{:S(2)}) collective-permute-start(bf16[8,16,192]{2,1,0:T(8,128)(2,1)} %get-tuple-element.62), channel_id=1, source_target_pairs={{0,3},{1,2},{2,1},{3,0},{4,7},{5,6},{6,5},{7,4},{8,11},{9,10},{10,... | collective-permute-start | bytes 147464 | tf_op jit(solution)/shard_map/ppermute | solution.py:322
  96.1 5.8 %collective-permute-start.26 = (bf16[8,16,192]{2,1,0:T(8,128)(2,1)}, bf16[8,16,192]{2,1,0:T(8,128)(2,1)S(1)}, u32[]{:S(2)}, u32[]{:S(2)}) collective-permute-start(bf16[8,16,192]{2,1,0:T(8,128)(2,1)} %get-tuple-element.63), channel_id=1, source_target_pairs={{0,24},{4,28},{8,0},{12,4},{16,8},{20,12},{24,16},{28,20},{1,25},{... | collective-permute-start | bytes 147464 | tf_op jit(solution)/shard_map/ppermute | solution.py:317
  99.1 4.5 %collective-permute-start.27 = (bf16[8,16,192]{2,1,0:T(8,128)(2,1)}, bf16[8,16,192]{2,1,0:T(8,128)(2,1)S(1)}, u32[]{:S(2)}, u32[]{:S(2)}) collective-permute-start(bf16[8,16,192]{2,1,0:T(8,128)(2,1)} %get-tuple-element.64), channel_id=1, source_target_pairs={{0,28},{4,0},{8,4},{12,8},{16,12},{20,16},{24,20},{28,24},{1,29},{... | collective-permute-start | bytes 147464 | tf_op jit(solution)/shard_map/ppermute | solution.py:317
  99.5 7.5 %collective-permute-start.28 = (bf16[8,16,192]{2,1,0:T(8,128)(2,1)}, bf16[8,16,192]{2,1,0:T(8,128)(2,1)S(1)}, u32[]{:S(2)}, u32[]{:S(2)}) collective-permute-start(bf16[8,16,192]{2,1,0:T(8,128)(2,1)} %get-tuple-element.66), channel_id=1, source_target_pairs={{0,4},{4,8},{8,12},{12,16},{16,20},{20,24},{24,28},{28,0},{1,5},{5... | collective-permute-start | bytes 147464 | tf_op jit(solution)/shard_map/ppermute | solution.py:317
  101.1 6.3 %collective-permute-start.29 = (bf16[8,16,192]{2,1,0:T(8,128)(2,1)}, bf16[8,16,192]{2,1,0:T(8,128)(2,1)S(1)}, u32[]{:S(2)}, u32[]{:S(2)}) collective-permute-start(bf16[8,16,192]{2,1,0:T(8,128)(2,1)} %get-tuple-element.67), channel_id=1, source_target_pairs={{0,8},{4,12},{8,16},{12,20},{16,24},{20,28},{24,0},{28,4},{1,9},{5... | collective-permute-start | bytes 147464 | tf_op jit(solution)/shard_map/ppermute | solution.py:317
  110.2 22.2 %collective-permute-start.30 = (bf16[10,16,192]{2,1,0:T(8,128)(2,1)}, bf16[10,16,192]{2,1,0:T(8,128)(2,1)S(1)}, u32[]{:S(2)}, u32[]{:S(2)}) collective-permute-start(bf16[10,16,192]{2,1,0:T(8,128)(2,1)} %get-tuple-element.70), channel_id=1, source_target_pairs={{0,8},{4,12},{8,16},{12,20},{16,24},{20,28},{24,0},{28,4},{1,9},{5... | collective-permute-start | bytes 184328 | tf_op jit(solution)/shard_map/ppermute | solution.py:317
  110.2 22.2 %collective-permute-start.31 = (bf16[10,16,192]{2,1,0:T(8,128)(2,1)}, bf16[10,16,192]{2,1,0:T(8,128)(2,1)S(1)}, u32[]{:S(2)}, u32[]{:S(2)}) collective-permute-start(bf16[10,16,192]{2,1,0:T(8,128)(2,1)} %get-tuple-element.71), channel_id=1, source_target_pairs={{0,4},{4,8},{8,12},{12,16},{16,20},{20,24},{24,28},{28,0},{1,5},{5... | collective-permute-start | bytes 184328 | tf_op jit(solution)/shard_map/ppermute | solution.py:317
  111.2 21.2 %collective-permute-start.32 = (bf16[10,16,192]{2,1,0:T(8,128)(2,1)}, bf16[10,16,192]{2,1,0:T(8,128)(2,1)S(1)}, u32[]{:S(2)}, u32[]{:S(2)}) collective-permute-start(bf16[10,16,192]{2,1,0:T(8,128)(2,1)} %get-tuple-element.73), channel_id=1, source_target_pairs={{0,28},{4,0},{8,4},{12,8},{16,12},{20,16},{24,20},{28,24},{1,29},{... | collective-permute-start | bytes 184328 | tf_op jit(solution)/shard_map/ppermute | solution.py:317
  115.0 17.5 %collective-permute-start.33 = (bf16[10,16,192]{2,1,0:T(8,128)(2,1)}, bf16[10,16,192]{2,1,0:T(8,128)(2,1)S(1)}, u32[]{:S(2)}, u32[]{:S(2)}) collective-permute-start(bf16[10,16,192]{2,1,0:T(8,128)(2,1)} %get-tuple-element.74), channel_id=1, source_target_pairs={{0,24},{4,28},{8,0},{12,4},{16,8},{20,12},{24,16},{28,20},{1,25},{... | collective-permute-start | bytes 184328 | tf_op jit(solution)/shard_map/ppermute | solution.py:317
  117.0 5.7 %collective-permute-start.34 = (bf16[2,16,192]{2,1,0:T(8,128)(2,1)}, bf16[2,16,192]{2,1,0:T(8,128)(2,1)S(1)}, u32[]{:S(2)}, u32[]{:S(2)}) collective-permute-start(bf16[2,16,192]{2,1,0:T(8,128)(2,1)} %get-tuple-element.75), channel_id=1, source_target_pairs={{0,12},{4,16},{8,20},{12,24},{16,28},{20,0},{24,4},{28,8},{1,13},{... | collective-permute-start | bytes 36872 | tf_op jit(solution)/shard_map/ppermute | solution.py:317
  122.7 9.8 %copy-start.34 = (bf16[2,16,192]{2,1,0:T(8,128)(2,1)}, bf16[2,16,192]{2,1,0:T(8,128)(2,1)S(1)}, u32[]{:S(2)}) copy-start(bf16[2,16,192]{2,1,0:T(8,128)(2,1)S(1)} %collective-permute-done.34.refs_5_) | copy-start | bytes 36868
  122.7 4.8 %collective-permute-start.35 = (bf16[2,16,192]{2,1,0:T(8,128)(2,1)}, bf16[2,16,192]{2,1,0:T(8,128)(2,1)S(1)}, u32[]{:S(2)}, u32[]{:S(2)}) collective-permute-start(bf16[2,16,192]{2,1,0:T(8,128)(2,1)} %get-tuple-element.75), channel_id=1, source_target_pairs={{0,16},{4,20},{8,24},{12,28},{16,0},{20,4},{24,8},{28,12},{1,17},{... | collective-permute-start | bytes 36872 | tf_op jit(solution)/shard_map/ppermute | solution.py:317
  127.6 4.8 %collective-permute-start.36 = (bf16[2,16,192]{2,1,0:T(8,128)(2,1)}, bf16[2,16,192]{2,1,0:T(8,128)(2,1)S(1)}, u32[]{:S(2)}, u32[]{:S(2)}) collective-permute-start(bf16[2,16,192]{2,1,0:T(8,128)(2,1)} %get-tuple-element.75), channel_id=1, source_target_pairs={{0,20},{4,24},{8,28},{12,0},{16,4},{20,8},{24,12},{28,16},{1,21},{... | collective-permute-start | bytes 36872 | tf_op jit(solution)/shard_map/ppermute | solution.py:317
  135.0 1.9 %collective-permute-start.37 = (bf16[10,16,192]{2,1,0:T(8,128)(2,1)}, bf16[10,16,192]{2,1,0:T(8,128)(2,1)S(1)}, u32[]{:S(2)}, u32[]{:S(2)}) collective-permute-start(bf16[10,16,192]{2,1,0:T(8,128)(2,1)} %get-tuple-element.77), channel_id=1, source_target_pairs={{0,1},{1,0},{2,3},{3,2},{4,5},{5,4},{6,7},{7,6},{8,9},{9,8},{10,11... | collective-permute-start | bytes 184328 | tf_op jit(solution)/shard_map/ppermute | solution.py:322
  135.0 5.6 %collective-permute-start.38 = (bf16[10,16,192]{2,1,0:T(8,128)(2,1)}, bf16[10,16,192]{2,1,0:T(8,128)(2,1)S(1)}, u32[]{:S(2)}, u32[]{:S(2)}) collective-permute-start(bf16[10,16,192]{2,1,0:T(8,128)(2,1)} %get-tuple-element.78), channel_id=1, source_target_pairs={{0,2},{1,3},{2,0},{3,1},{4,6},{5,7},{6,4},{7,5},{8,10},{9,11},{10,... | collective-permute-start | bytes 184328 | tf_op jit(solution)/shard_map/ppermute | solution.py:322
  135.9 5.3 %collective-permute-start.39 = (bf16[10,16,192]{2,1,0:T(8,128)(2,1)}, bf16[10,16,192]{2,1,0:T(8,128)(2,1)S(1)}, u32[]{:S(2)}, u32[]{:S(2)}) collective-permute-start(bf16[10,16,192]{2,1,0:T(8,128)(2,1)} %get-tuple-element.79), channel_id=1, source_target_pairs={{0,3},{1,2},{2,1},{3,0},{4,7},{5,6},{6,5},{7,4},{8,11},{9,10},{10,... | collective-permute-start | bytes 184328 | tf_op jit(solution)/shard_map/ppermute | solution.py:322
  (36 other events, 67.8 us)

commit v2 on v1

v2 whole, which is shorter than its diff:
```python
import functools

import jax
import jax.numpy as jnp
from jax import lax
from jax.experimental import pallas as pl
from jax.experimental.pallas import tpu as pltpu
from jax.sharding import PartitionSpec as P

DEG = 8
MODES = 64
FPTS = 64
MORT_OWN = 16
REACH = 2
CAP = 8
LINKS = 2 * REACH + 1
SLOTS = LINKS * CAP

BF = jnp.bfloat16
F32 = jnp.float32
CONTRACT_FIRST = (((0,), (0,)), ((), ()))
CONTRACT_LAST = (((1,), (1,)), ((), ()))
VMEM = pl.BlockSpec(memory_space=pltpu.VMEM)
SMEM = pl.BlockSpec(memory_space=pltpu.SMEM)
HBM = pl.BlockSpec(memory_space=pltpu.HBM)


def split_two(value):
    high = value.astype(BF)
    return high, (value - high.astype(F32)).astype(BF)


class Sizes:
    def __init__(self, subs, grps, schur, project, coarse_basis, rhs):
        self.subs = subs
        self.grps = grps
        self.rows = schur.shape[1]
        self.all_rows = schur.shape[2]
        self.own = project.shape[1]
        self.faces = self.own * grps
        self.corners = coarse_basis.shape[1]
        self.rhs = rhs.shape[2]
        self.vertices = 2 * subs
        self.share = MODES // grps
        self.wide = -(-(self.rhs + self.vertices) // 128) * 128
        self.lanes = self.rhs // 128 * 128
        self.tail = self.rhs - self.lanes
        self.near = self.vertices == self.share and LINKS <= subs <= 2 * LINKS
        self.extra = 2 if self.near else 0
        self.t_src = 0
        self.t_arr = SLOTS
        self.t_slot = 2 * SLOTS
        self.t_count = self.t_slot + self.faces
        self.t_order = self.t_count + MORT_OWN
        self.t_corner = self.t_order + MORT_OWN
        self.t_end = self.t_corner + self.corners


def call(kernel, sizes, outs, args, scratch=()):
    single = not isinstance(outs, list)
    outs = [outs] if single else outs
    ins = [SMEM if a.dtype == jnp.int32 else VMEM for a in args]
    args = [
        pltpu.with_memory_space_constraint(a, pltpu.SMEM if a.dtype == jnp.int32 else pltpu.VMEM) for a in args
    ]
    results = pl.pallas_call(
        functools.partial(kernel, sizes),
        out_shape=[pltpu.VMEM(o.shape, o.dtype) for o in outs],
        in_specs=ins,
        out_specs=[VMEM for _ in outs],
        scratch_shapes=list(scratch),
        compiler_params=pltpu.CompilerParams(vmem_limit_bytes=16 << 20),
    )(*args)
    return results[0] if single else results


def table_kernel(z, owner, mortar, order, smap, vids, table, used, names):
    s = lax.axis_index("sub")
    g = lax.axis_index("grp")
    d = smap[s]
    for i in range(SLOTS):
        table[z.t_src + i] = 0
    for i in range(LINKS):
        used[i] = 0
    for i in range(MORT_OWN):
        table[z.t_count + i] = 0
        table[z.t_order + i] = order[s, i]
    for i in range(z.corners):
        table[z.t_corner + i] = vids[d, i]
    for f in range(z.faces):
        o = owner[d, 0, f]
        r = used[o]
        used[o] = r + 1
        slot = o * CAP + r
        table[z.t_slot + f] = slot
        table[z.t_src + slot] = ((f // z.own) ^ g) * z.own + f % z.own
    for link in range(LINKS):
        dd = smap[lax.rem(s - link + REACH + z.subs, z.subs)]
        r = jnp.int32(0)
        for f in range(z.faces):
            hit = (owner[dd, 0, f] == link).astype(jnp.int32)
            m = mortar[dd, f]
            names[r] = m
            table[z.t_count + m] = table[z.t_count + m] + hit
            r = r + hit
        for i in range(CAP):
            table[z.t_arr + link * CAP + i] = jnp.where(i < r, names[i], MORT_OWN)


def narrow_kernel(z, start, out):
    out[...] = start[...].astype(BF)


def load_kernel(schur, rhs, schur_out, rhs_out, sems):
    copies = [
        pltpu.make_async_copy(schur, schur_out, sems.at[0]),
        pltpu.make_async_copy(rhs, rhs_out, sems.at[1]),
    ]
    for c in copies:
        c.start()
    for c in copies:
        c.wait()


def join_kernel(z, tables, coarse, out):
    half = MODES // 2
    for f in range(z.own):
        out[f, :half, :] = jnp.concatenate([tables[f, :half, :], tables[f, half:, :]], axis=1)
        one = coarse[:, f * FPTS : (f + 1) * FPTS].astype(F32)
        two = jnp.concatenate([one, one], axis=0).astype(BF)
        out[f, half:, :] = jnp.concatenate([two, two], axis=1)


def tables_of(ext):
    half = MODES // 2
    return jnp.concatenate([ext[:half, :FPTS], ext[:half, FPTS:]], axis=0)


def lifting(ext):
    half = MODES // 2
    return jnp.concatenate([ext[:, :FPTS], ext[:half, FPTS:]], axis=0)


def share_rows(z, member):
    at = member * z.share
    gap = 2 * z.corners
    return pl.ds(pl.multiple_of(jnp.where(at < MODES // 2, at, at + gap), z.share), z.share)


def coarse_rows(z):
    return slice(MODES // 2, MODES // 2 + 2 * z.corners)


def first_kernel(z, table, schur, b0, b1, b2, b3, rhs, tables, coarse, o0, o1, o2, o3, res_out, gathered, held, coeffs):
    g = lax.axis_index("grp")
    for j, b in enumerate((b0, b1, b2, b3)):
        gathered[:, pl.ds(pl.multiple_of((g ^ j) * z.rows, z.rows), z.rows)] = b[...]
    product = lax.dot_general(schur[...], gathered[...], CONTRACT_LAST, preferred_element_type=F32)
    residual = product - rhs[...].T
    res_out[...] = residual
    held[:, : z.rhs] = residual.astype(BF)
    column = lax.broadcasted_iota(jnp.int32, (1, z.wide - z.rhs), 1)
    hot = jnp.concatenate(
        [jnp.where(column == table[z.t_corner + i], 1.0, 0.0) for i in range(z.corners)], axis=0
    ).astype(BF)
    held[:, z.rhs :] = lax.dot_general(coarse[...], hot, CONTRACT_FIRST, preferred_element_type=F32).astype(BF)
    for f in range(z.own):
        coeffs[f] = jnp.dot(tables_of(tables[f]), held[f * FPTS : (f + 1) * FPTS, :], preferred_element_type=F32).astype(BF)
    for j, o in enumerate((o0, o1, o2, o3)):
        at = pl.multiple_of((g ^ j) * z.share, z.share)
        for f in range(z.own):
            o[f] = coeffs[f, pl.ds(at, z.share), :]


def pack_kernel(z, table, c0, c1, c2, c3, o0, o1, o2, o3, o4, data):
    for j, c in enumerate((c0, c1, c2, c3)):
        data[j * z.own : (j + 1) * z.own] = c[...]
    for link, o in enumerate((o0, o1, o2, o3, o4)):
        for i in range(CAP):
            o[i] = data[table[z.t_src + link * CAP + i]]


def average_body(z, table, arrivals, total, held):
    g = lax.axis_index("grp")
    total[...] = jnp.zeros_like(total)
    for link, a in enumerate(arrivals):
        for i in range(CAP):
            m = table[z.t_arr + link * CAP + i]
            total[m] = total[m] + a[i].astype(F32)
    mode = g * z.share + lax.broadcasted_iota(jnp.int32, (z.share, z.rhs), 0)
    degree_a = mode // DEG
    degree_b = mode % DEG
    degree = jnp.maximum(degree_a, degree_b)
    for k in range(MORT_OWN):
        divisor = jnp.maximum(table[z.t_count + k], 1).astype(F32)
        kept = jnp.where(degree <= table[z.t_order + k], 1.0, 0.0)
        value = total[k, :, : z.rhs] / divisor * kept
        held[k] = value.astype(BF)
    held[MORT_OWN] = jnp.zeros_like(held[MORT_OWN])


def reply_body(z, table, held, g_high, g_low, replies, vertex):
    flat = held[:MORT_OWN].reshape(MORT_OWN * z.share, z.rhs)
    value = lax.dot_general(g_high, flat, CONTRACT_FIRST, preferred_element_type=F32)
    value = value + lax.dot_general(g_low, flat, CONTRACT_FIRST, preferred_element_type=F32)
    if z.near:
        high, low = split_two(value)
        vertex[0] = high
        vertex[1] = low
    else:
        vertex[...] = value
    for link, o in enumerate(replies):
        for i in range(CAP):
            o[i] = held[table[z.t_arr + link * CAP + i]]
        if z.near:
            o[CAP] = high
            o[CAP + 1] = low


def average_first(z, table, a0, a1, a2, a3, a4, o0, o1, o2, o3, o4, vertex, g_high, g_low, total, held):
    average_body(z, table, (a0, a1, a2, a3, a4), total, held)
    wide = total[:MORT_OWN, :, z.rhs : z.rhs + z.vertices].reshape(MORT_OWN * z.share, z.vertices)
    high, low = split_two(wide)
    g_high[...] = high
    g_low[...] = low
    reply_body(z, table, held, high, low, (o0, o1, o2, o3, o4), vertex)


def average_second(z, table, a0, a1, a2, a3, a4, g_high, g_low, o0, o1, o2, o3, o4, vertex, total, held):
    average_body(z, table, (a0, a1, a2, a3, a4), total, held)
    reply_body(z, table, held, g_high[...], g_low[...], (o0, o1, o2, o3, o4), vertex)


def near_sum(blocks, fars):
    value = None
    for b, at in [(b, CAP) for b in blocks] + [(b, 0) for b in fars]:
        one = b[at].astype(F32) + b[at + 1].astype(F32)
        value = one if value is None else value + one
    return split_two(value)


def spread_first(z, table, *refs):
    fars = refs[LINKS:-2]
    blocks, out, data = refs[:LINKS], refs[-2], refs[-1]
    for link, b in enumerate(blocks):
        data[link * CAP : (link + 1) * CAP] = b[:CAP]
    quarter = z.own // 2
    for f in range(z.faces):
        out[f] = data[table[z.t_slot + f], :, : z.lanes]
    for member in range(z.grps):
        for i in range(quarter):
            f = member * z.own + i
            left = data[table[z.t_slot + f], :, z.lanes :]
            right = data[table[z.t_slot + f + quarter], :, z.lanes :]
            out[z.faces + member * quarter + i] = jnp.concatenate([left, right], axis=1)
    if z.near:
        high, low = near_sum(blocks, fars)
        at = z.faces + z.faces // 2
        out[at] = high[:, : z.lanes]
        out[at + 1] = low[:, : z.lanes]
        out[at + 2] = jnp.concatenate([high[:, z.lanes :], low[:, z.lanes :]], axis=1)


def spread_second(z, table, *refs):
    fars = refs[LINKS : -1 - z.grps]
    blocks, outs, data = refs[:LINKS], refs[-1 - z.grps : -1], refs[-1]
    g = lax.axis_index("grp")
    for link, b in enumerate(blocks):
        data[link * CAP : (link + 1) * CAP] = b[:CAP]
    for j, o in enumerate(outs):
        for i in range(z.own):
            o[i] = data[table[z.t_slot + (g ^ j) * z.own + i]]
    if z.near:
        high, low = near_sum(blocks, fars)
        for o in outs:
            o[z.own] = high
            o[z.own + 1] = low


def picked_rows(z, table, whole):
    rows = [whole[pl.ds(table[z.t_corner + i], 1), :] for i in range(z.corners)]
    high, low = split_two(jnp.concatenate(rows, axis=0))
    return jnp.concatenate([high.astype(F32), low.astype(F32)], axis=0).astype(BF)


def second_kernel(z, table, schur, *refs):
    n = z.grps
    shares, refs = refs[:n], refs[n:]
    exts, refs = refs[:n], refs[n:]
    vertex_in, resid, refs = refs[0], refs[1], refs[2:]
    outs, refs = refs[:n], refs[n:]
    own_out, averages, gathered, whole, held, coeffs = refs
    g = lax.axis_index("grp")
    quarter = z.own // 2
    if z.near:
        at = z.faces + z.faces // 2
        for j, a in enumerate(shares):
            main = a[at].astype(F32) + a[at + 1].astype(F32)
            both = a[at + 2].astype(F32)
            tail = both[:, : z.tail] + both[:, z.tail :]
            if j:
                main = main + whole[:, : z.lanes]
                tail = tail + whole[:, z.lanes :]
            whole[:, : z.lanes] = main
            whole[:, z.lanes :] = tail
    else:
        whole[...] = vertex_in[...]
    picked = picked_rows(z, table, whole)
    for j, e in enumerate(exts):
        member = g ^ j
        for i in range(z.own):
            f = member * z.own + i
            for jj, a in enumerate(shares):
                rows = share_rows(z, g ^ jj)
                averages[f, rows, : z.lanes] = a[f]
                low = (i // quarter) * z.tail
                averages[f, rows, z.lanes :] = a[z.faces + member * quarter + i % quarter, :, low : low + z.tail]
            averages[f, coarse_rows(z), :] = picked
            lifted = lax.dot_general(lifting(e[i]), averages[f], CONTRACT_FIRST, preferred_element_type=F32)
            gathered[pl.ds(pl.multiple_of(f * FPTS, FPTS), FPTS), :] = lifted.astype(BF)
            if j == 0:
                own_out[i] = averages[f]
    product = jnp.dot(schur[...], gathered[...], preferred_element_type=F32)
    held[...] = (resid[...] - 0.5 * product).astype(BF)
    for f in range(z.own):
        coeffs[f] = jnp.dot(tables_of(exts[0][f]), held[f * FPTS : (f + 1) * FPTS, :], preferred_element_type=F32).astype(BF)
    for j, o in enumerate(outs):
        at = pl.multiple_of((g ^ j) * z.share, z.share)
        for f in range(z.own):
            o[f] = coeffs[f, pl.ds(at, z.share), :]


def last_kernel(z, table, *refs):
    n = z.grps
    shares, refs = refs[:n], refs[n:]
    ext, vertex_in, earlier, start, out, averages, whole, whole_change = refs
    g = lax.axis_index("grp")
    if z.near:
        value = None
        for c in shares:
            one = c[z.own].astype(F32) + c[z.own + 1].astype(F32)
            value = one if value is None else value + one
        whole[...] = value
    else:
        whole[...] = vertex_in[...]
    picked = picked_rows(z, table, whole)
    for i in range(z.own):
        for j, c in enumerate(shares):
            averages[i, share_rows(z, g ^ j), :] = c[i]
        averages[i, coarse_rows(z), :] = picked
        lift = lifting(ext[i])
        both = lax.dot_general(lift, averages[i], CONTRACT_FIRST, preferred_element_type=F32)
        both = both + lax.dot_general(lift, earlier[i], CONTRACT_FIRST, preferred_element_type=F32)
        whole_change[i * FPTS : (i + 1) * FPTS, :] = both
    out[...] = start[...] - 0.5 * whole_change[...].T


def passed_along(value, steps):
    count = lax.axis_size("sub")
    return lax.ppermute(value, "sub", [(s, (s + steps) % count) for s in range(count)])


def swapped(value, mask):
    count = lax.axis_size("grp")
    return lax.ppermute(value, "grp", [(s, s ^ mask) for s in range(count)])


def hypercube(value):
    two = swapped(value, 2)
    one = swapped(value, 1)
    return [value, one, two, swapped(two, 1)]


def exchanged(blocks):
    return [blocks[0]] + [swapped(blocks[j], j) for j in range(1, len(blocks))]


def along_links(blocks, sign):
    return [b if link == REACH else passed_along(b, sign * (link - REACH)) for link, b in enumerate(blocks)]


def run(schur, rhs, start, project, coarse_basis, owner_of_face, mortar_of_face, mortar_order, subdomain_map, vertex_ids):
    subs, grps = lax.axis_size("sub"), lax.axis_size("grp")
    z = Sizes(subs, grps, schur, project, coarse_basis, rhs)
    shape = jax.ShapeDtypeStruct
    matrix, target, first = schur[0], rhs[0].T, start[0].T

    trace_b = call(narrow_kernel, z, shape((z.rhs, z.rows), BF), (first,))
    block_two = swapped(trace_b, 2)
    block_one = swapped(trace_b, 1)

    table = pl.pallas_call(
        functools.partial(table_kernel, z),
        out_shape=pltpu.SMEM((z.t_end,), jnp.int32),
        in_specs=[SMEM] * 5,
        out_specs=SMEM,
        scratch_shapes=[pltpu.SMEM((LINKS,), jnp.int32), pltpu.SMEM((z.faces + 1,), jnp.int32)],
    )(owner_of_face.transpose(0, 2, 1), mortar_of_face, mortar_order, subdomain_map, vertex_ids)
    matrix, target = pl.pallas_call(
        load_kernel,
        out_shape=[pltpu.VMEM(matrix.shape, BF), pltpu.VMEM(target.shape, F32)],
        in_specs=[HBM] * 2,
        out_specs=[VMEM] * 2,
        scratch_shapes=[pltpu.SemaphoreType.DMA((2,))],
        compiler_params=pltpu.CompilerParams(vmem_limit_bytes=16 << 20),
    )(*[pltpu.with_memory_space_constraint(a, pltpu.HBM) for a in (matrix, target)])
    assert z.own == z.corners
    ext_shape = shape((z.own, MODES // 2 + 2 * z.corners, 2 * FPTS), BF)
    ext_own = call(join_kernel, z, ext_shape, (project[0].reshape(z.own, MODES, FPTS), coarse_basis[0]))
    ext_two = swapped(ext_own, 2)
    block_three = swapped(block_two, 1)
    blocks = [trace_b, block_one, block_two, block_three]

    part = shape((z.own, z.share, z.wide), BF)
    thin = shape((z.own, z.share, z.rhs), BF)
    link_wide = [shape((CAP, z.share, z.wide), BF)] * LINKS
    link_thin = [shape((CAP, z.share, z.rhs), BF)] * LINKS
    reply = [shape((CAP + z.extra, z.share, z.rhs), BF)] * LINKS
    vertex_shape = shape((2, z.vertices, z.rhs), BF) if z.near else shape((z.vertices, z.rhs), F32)
    g_shape = [shape((MORT_OWN * z.share, z.vertices), BF)] * 2

    def far(vertex):
        if not z.near:
            return []
        return [passed_along(vertex, off) for off in range(REACH + 1, subs - REACH)]

    def summed(vertex):
        if z.near:
            return jnp.zeros((8, 128), F32)
        return lax.psum(vertex, ("sub", "grp"))

    *parts, resid = call(
        first_kernel,
        z,
        [part] * grps + [shape((z.rows, z.rhs), F32)],
        (table, matrix, *blocks, target, ext_own, coarse_basis[0]),
        (
            pltpu.VMEM((z.rhs, z.all_rows), BF),
            pltpu.VMEM((z.rows, z.wide), BF),
            pltpu.VMEM((z.own, MODES, z.wide), BF),
        ),
    )
    parts, ext_two = lax.optimization_barrier((parts, ext_two))
    parts = exchanged(parts)
    exts = [ext_own, swapped(ext_own, 1), ext_two, swapped(ext_two, 1)]
    parts, exts = lax.optimization_barrier((parts, exts))
    outgoing = call(pack_kernel, z, link_wide, (table, *parts), (pltpu.VMEM((z.faces, z.share, z.wide), BF),))
    arrived = along_links(outgoing, 1)
    *replies, vertex, g_high, g_low = call(
        average_first,
        z,
        reply + [vertex_shape] + g_shape,
        (table, *arrived),
        (pltpu.VMEM((MORT_OWN + 1, z.share, z.wide), F32), pltpu.VMEM((MORT_OWN + 1, z.share, z.rhs), BF)),
    )
    answered = along_links(replies, -1)
    fars = far(vertex)
    count = z.faces + z.faces // 2 + (3 if z.near else 0)
    spread = call(
        spread_first,
        z,
        shape((count, z.share, z.lanes), BF),
        (table, *answered, *fars),
        (pltpu.VMEM((SLOTS, z.share, z.rhs), BF),),
    )
    shares = hypercube(spread)
    *parts, earlier = call(
        second_kernel,
        z,
        [thin] * grps + [shape((z.own, MODES + 2 * z.corners, z.rhs), BF)],
        (table, matrix, *shares, *exts, summed(vertex), resid),
        (
            pltpu.VMEM((z.faces, MODES + 2 * z.corners, z.rhs), BF),
            pltpu.VMEM((z.all_rows, z.rhs), BF),
            pltpu.VMEM((z.vertices, z.rhs), F32),
            pltpu.VMEM((z.rows, z.rhs), BF),
            pltpu.VMEM((z.own, MODES, z.rhs), BF),
        ),
    )
    parts = exchanged(parts)
    outgoing = call(pack_kernel, z, link_thin, (table, *parts), (pltpu.VMEM((z.faces, z.share, z.rhs), BF),))
    arrived = along_links(outgoing, 1)
    *replies, vertex = call(
        average_second,
        z,
        reply + [vertex_shape],
        (table, *arrived, g_high, g_low),
        (pltpu.VMEM((MORT_OWN + 1, z.share, z.rhs), F32), pltpu.VMEM((MORT_OWN + 1, z.share, z.rhs), BF)),
    )
    answered = along_links(replies, -1)
    fars = far(vertex)
    outs = call(
        spread_second,
        z,
        [shape((z.own + z.extra, z.share, z.rhs), BF)] * grps,
        (table, *answered, *fars),
        (pltpu.VMEM((SLOTS, z.share, z.rhs), BF),),
    )
    shares = exchanged(outs)
    result = call(
        last_kernel,
        z,
        shape((z.rhs, z.rows), F32),
        (table, *shares, ext_own, summed(vertex), earlier, first),
        (
            pltpu.VMEM((z.own, MODES + 2 * z.corners, z.rhs), BF),
            pltpu.VMEM((z.vertices, z.rhs), F32),
            pltpu.VMEM((z.rows, z.rhs), F32),
        ),
    )
    return result.T[None]


def solution(mesh):
    return jax.shard_map(
        run,
        mesh=mesh,
        in_specs=(
            P("sub", "grp", None),
            P("sub", "grp", None),
            P("sub", "grp", None),
            P("sub", "grp", None),
            P("sub", None, "grp"),
            P(),
            P(),
            P(),
            P(),
            P(),
        ),
        out_specs=P("sub", "grp", None),
        check_vma=False,
    )
```

time: 147 us -> 114 us (0.78)
  Pallas kernels: 27.1 us -> 9.39 us
  local copies, waits for them, and re-layouts: 19.4 us -> 3.47 us
  waiting for transfers between devices: 54.6 us -> 62.4 us
  other arithmetic: 3.49 us -> 0 us
  between operations: 2.29 us -> 0.22 us
    pallas_call x11 -> x13, Pallas kernels: 27.1 us -> 9.39 us  [the longest x11 5.85 us: call(): pl.pallas_call(functools.partial(kernel, sizes), out_shape=[pltpu.VMEM(o....]
    ppermute x18, waiting for transfers between devices: 12.9 us -> 22.1 us  [swapped(): return lax.ppermute(value, 'grp', [(s, s ^ mask) for s in range(count)])]
    unnamed x91 -> x9, local copies, waits for them, and re-layouts: 8.9 us -> 2.44 us
    reshape x13 -> x0, local copies, waits for them, and re-layouts: 3.36 us -> none  [the longest x1 0.66 us: body(): mortar_of_face.reshape(-1)]
    concatenate x4 -> x0, other arithmetic: 2.21 us -> none  [the longest x3 2.21 us: extended(): return jnp.concatenate([tables, coarse, coarse], axis=1)]
    broadcast_in_dim x1 -> x0, local copies, waits for them, and re-layouts: 1.97 us -> none  [body(): return result[None]]
  transfers between devices with their start and end apart: 40 -> 40, of which waited for: 16 -> 19; matrix products, arithmetic and copies ran while one was open for 9% -> 1% of each run, Pallas kernels for 2% -> 4%
where the time goes in v2:
time: 114 us
  waiting for transfers between devices  62.4 us (55%)
  starting transfers between devices  38.2 us (34%)
  Pallas kernels  9.39 us (8%)
  local copies, waits for them, and re-layouts  3.47 us (3%)
    ppermute x22, waiting for transfers between devices, passed_along(): lax.ppermute(value, 'sub', [(s, (s + steps) % count) for s in range(count)])  40.3 us
    ppermute x22, starting transfers between devices, passed_along(): lax.ppermute(value, 'sub', [(s, (s + steps) % count) for s in range(count)])  25.7 us
    ppermute x18, waiting for transfers between devices, swapped(): return lax.ppermute(value, 'grp', [(s, s ^ mask) for s in range(count)])  22.1 us
    ppermute x18, starting transfers between devices, swapped(): return lax.ppermute(value, 'grp', [(s, s ^ mask) for s in range(count)])  12.6 us
    pallas_call x11, Pallas kernels, call(): pl.pallas_call(functools.partial(kernel, sizes), out_shape=[pltpu.VMEM(o....  5.85 us
    unnamed x9, local copies, waits for them, and re-layouts  2.44 us
  transfers between devices with their start and end apart: 40, of which 19 were waited for; matrix products, arithmetic and copies ran while one was open for 1% of the time, Pallas kernels for 4%

profile of v2, /device:TPU:0, one launch (start us, length us, event | category | flops | bytes accessed | tf_op | source)
XLA Modules:
  0.0 113.8 jit_solution(254014136543994564)
XLA Ops:
  0.0 1.0 copy-done
  1.0 3.0 %collective-permute-start.1 = (bf16[192,512]{1,0:T(8,128)(2,1)S(1)}, bf16[192,512]{1,0:T(8,128)(2,1)S(1)}, u32[]{:S(2)}, u32[]{:S(2)}) collective-permute-start(bf16[192,512]{1,0:T(8,128)(2,1)S(1)} %shard_map.102.b0), channel_id=1, source_target_pairs={{0,2},{1,3},{2,0},{3,1},{4,6},{5,7},{6,4},{7,5},{8,10},{9,11},{10,... | collective-permute-start | bytes 589832 | tf_op jit(solution)/shard_map/ppermute | solution.py:365
  4.1 4.9 %collective-permute-done.1.b2 = bf16[192,512]{1,0:T(8,128)(2,1)S(1)} collective-permute-done((bf16[192,512]{1,0:T(8,128)(2,1)S(1)}, bf16[192,512]{1,0:T(8,128)(2,1)S(1)}, u32[]{:S(2)}, u32[]{:S(2)}) %collective-permute-start.1) | collective-permute-done | bytes 196640 | tf_op jit(solution)/shard_map/ppermute | solution.py:365
  9.0 1.0 reshape_squeeze.3.tables
  10.0 0.7 copy-done.2
  10.8 1.8 %collective-permute-start.3 = (bf16[8,48,128]{2,1,0:T(8,128)(2,1)S(1)}, bf16[8,48,128]{2,1,0:T(8,128)(2,1)S(1)}, u32[]{:S(2)}, u32[]{:S(2)}) collective-permute-start(bf16[8,48,128]{2,1,0:T(8,128)(2,1)S(1)} %shard_map.103.tables.refs_4_), channel_id=1, source_target_pairs={{0,2},{1,3},{2,0},{3,1},{4,6},{5,7},{6,4},{7,5},{8,10},{9,11},{10,... | collective-permute-start | bytes 294920 | tf_op jit(solution)/shard_map/ppermute | solution.py:365
  12.8 1.6 %shard_map.101 = (bf16[512,2048]{1,0:T(8,128)(2,1)S(1)}, f32[192,512]{1,0:T(8,128)S(1)}) custom-call(bf16[512,2048]{1,0:T(8,128)(2,1)} %bitcast.17, f32[192,512]{1,0:T(8,128)} %bitcast.18), custom_call_target="tpu_custom_call" | custom-call | tf_op jit(solution)/shard_map/pallas_call | solution.py:399
  14.5 1.9 %shard_map.100.table = s32[152]{0:T(256)S(4)} custom-call(s32[8,1,32]{2,1,0:T(1,128)} %bitcast.19, s32[8,32]{1,0:T(8,128)} %mortar.1, s32[8,16]{1,0:T(8,128)} %order.1, s32[8]{0:T(128)} %smap.1, s32[8,8]{1,0:T(8,128)} %vids.1), custom_call_target="tpu_custom_call" | custom-call | tf_op jit(solution)/shard_map/pallas_call | solution.py:392
  16.4 1.1 shard_map.104
  18.5 1.3 %collective-permute-start.6 = (bf16[8,16,256]{2,1,0:T(8,128)(2,1)S(1)}, bf16[8,16,256]{2,1,0:T(8,128)(2,1)S(1)}, u32[]{:S(2)}, u32[]{:S(2)}) collective-permute-start(bf16[8,16,256]{2,1,0:T(8,128)(2,1)S(1)} %get-tuple-element.67), channel_id=1, source_target_pairs={{0,3},{1,2},{2,1},{3,0},{4,7},{5,6},{6,5},{7,4},{8,11},{9,10},{10,... | collective-permute-start | bytes 196616 | tf_op jit(solution)/shard_map/ppermute | solution.py:365
  19.7 3.3 %collective-permute-done.5.c2 = bf16[8,16,256]{2,1,0:T(8,128)(2,1)S(1)} collective-permute-done((bf16[8,16,256]{2,1,0:T(8,128)(2,1)S(1)}, bf16[8,16,256]{2,1,0:T(8,128)(2,1)S(1)}, u32[]{:S(2)}, u32[]{:S(2)}) %collective-permute-start.5) | collective-permute-done | bytes 65568 | tf_op jit(solution)/shard_map/ppermute | solution.py:365
  23.2 3.7 %collective-permute-start.9 = (bf16[8,16,256]{2,1,0:T(8,128)(2,1)S(1)}, bf16[8,16,256]{2,1,0:T(8,128)(2,1)S(1)}, u32[]{:S(2)}, u32[]{:S(2)}) collective-permute-start(bf16[8,16,256]{2,1,0:T(8,128)(2,1)S(1)} %get-tuple-element.73), channel_id=1, source_target_pairs={{0,24},{4,28},{8,0},{12,4},{16,8},{20,12},{24,16},{28,20},{1,25},{... | collective-permute-start | bytes 196616 | tf_op jit(solution)/shard_map/ppermute | solution.py:360
  26.8 1.4 %collective-permute-start.10 = (bf16[8,16,256]{2,1,0:T(8,128)(2,1)S(1)}, bf16[8,16,256]{2,1,0:T(8,128)(2,1)S(1)}, u32[]{:S(2)}, u32[]{:S(2)}) collective-permute-start(bf16[8,16,256]{2,1,0:T(8,128)(2,1)S(1)} %get-tuple-element.74), channel_id=1, source_target_pairs={{0,28},{4,0},{8,4},{12,8},{16,12},{20,16},{24,20},{28,24},{1,29},{... | collective-permute-start | bytes 196616 | tf_op jit(solution)/shard_map/ppermute | solution.py:360
  28.2 0.6 collective-permute-start.11
  28.8 0.9 collective-permute-start.12
  29.8 1.3 %collective-permute-done.10.a1 = bf16[8,16,256]{2,1,0:T(8,128)(2,1)S(1)} collective-permute-done((bf16[8,16,256]{2,1,0:T(8,128)(2,1)S(1)}, bf16[8,16,256]{2,1,0:T(8,128)(2,1)S(1)}, u32[]{:S(2)}, u32[]{:S(2)}) %collective-permute-start.10) | collective-permute-done | bytes 65568 | tf_op jit(solution)/shard_map/ppermute | solution.py:360
  31.1 4.5 %collective-permute-done.11.a3 = bf16[8,16,256]{2,1,0:T(8,128)(2,1)S(1)} collective-permute-done((bf16[8,16,256]{2,1,0:T(8,128)(2,1)S(1)}, bf16[8,16,256]{2,1,0:T(8,128)(2,1)S(1)}, u32[]{:S(2)}, u32[]{:S(2)}) %collective-permute-start.11) | collective-permute-done | bytes 65568 | tf_op jit(solution)/shard_map/ppermute | solution.py:360
  35.6 0.5 shard_map.106
  36.2 1.7 %collective-permute-start.14 = (bf16[10,16,192]{2,1,0:T(8,128)(2,1)S(1)}, bf16[10,16,192]{2,1,0:T(8,128)(2,1)S(1)}, u32[]{:S(2)}, u32[]{:S(2)}) collective-permute-start(bf16[10,16,192]{2,1,0:T(8,128)(2,1)S(1)} %get-tuple-element.79), channel_id=1, source_target_pairs={{0,4},{4,8},{8,12},{12,16},{16,20},{20,24},{24,28},{28,0},{1,5},{5... | collective-permute-start | bytes 184328 | tf_op jit(solution)/shard_map/ppermute | solution.py:360
  38.0 3.2 %collective-permute-start.15 = (bf16[10,16,192]{2,1,0:T(8,128)(2,1)S(1)}, bf16[10,16,192]{2,1,0:T(8,128)(2,1)S(1)}, u32[]{:S(2)}, u32[]{:S(2)}) collective-permute-start(bf16[10,16,192]{2,1,0:T(8,128)(2,1)S(1)} %get-tuple-element.81), channel_id=1, source_target_pairs={{0,28},{4,0},{8,4},{12,8},{16,12},{20,16},{24,20},{28,24},{1,29},{... | collective-permute-start | bytes 184328 | tf_op jit(solution)/shard_map/ppermute | solution.py:360
  41.2 1.8 %collective-permute-start.16 = (bf16[10,16,192]{2,1,0:T(8,128)(2,1)S(1)}, bf16[10,16,192]{2,1,0:T(8,128)(2,1)S(1)}, u32[]{:S(2)}, u32[]{:S(2)}) collective-permute-start(bf16[10,16,192]{2,1,0:T(8,128)(2,1)S(1)} %get-tuple-element.82), channel_id=1, source_target_pairs={{0,24},{4,28},{8,0},{12,4},{16,8},{20,12},{24,16},{28,20},{1,25},{... | collective-permute-start | bytes 184328 | tf_op jit(solution)/shard_map/ppermute | solution.py:360
  43.0 4.6 %collective-permute-done.19.refs_7_ = bf16[2,16,192]{2,1,0:T(8,128)(2,1)S(1)} collective-permute-done((bf16[2,16,192]{2,1,0:T(8,128)(2,1)S(1)}, bf16[2,16,192]{2,1,0:T(8,128)(2,1)S(1)}, u32[]{:S(2)}, u32[]{:S(2)}) %collective-permute-start.19) | collective-permute-done | bytes 12320 | tf_op jit(solution)/shard_map/ppermute | solution.py:360
  47.6 4.6 %collective-permute-done.18.refs_6_ = bf16[2,16,192]{2,1,0:T(8,128)(2,1)S(1)} collective-permute-done((bf16[2,16,192]{2,1,0:T(8,128)(2,1)S(1)}, bf16[2,16,192]{2,1,0:T(8,128)(2,1)S(1)}, u32[]{:S(2)}, u32[]{:S(2)}) %collective-permute-start.18) | collective-permute-done | bytes 12320 | tf_op jit(solution)/shard_map/ppermute | solution.py:360
  52.5 5.2 %collective-permute-done.17.refs_5_ = bf16[2,16,192]{2,1,0:T(8,128)(2,1)S(1)} collective-permute-done((bf16[2,16,192]{2,1,0:T(8,128)(2,1)S(1)}, bf16[2,16,192]{2,1,0:T(8,128)(2,1)S(1)}, u32[]{:S(2)}, u32[]{:S(2)}) %collective-permute-start.17) | collective-permute-done | bytes 12320 | tf_op jit(solution)/shard_map/ppermute | solution.py:360
  57.9 1.4 %collective-permute-start.21 = (bf16[51,16,128]{2,1,0:T(8,128)(2,1)S(1)}, bf16[51,16,128]{2,1,0:T(8,128)(2,1)S(1)}, u32[]{:S(2)}, u32[]{:S(2)}) collective-permute-start(bf16[51,16,128]{2,1,0:T(8,128)(2,1)S(1)} %shard_map.107.refs_0_), channel_id=1, source_target_pairs={{0,2},{1,3},{2,0},{3,1},{4,6},{5,7},{6,4},{7,5},{8,10},{9,11},{10,... | collective-permute-start | bytes 626696 | tf_op jit(solution)/shard_map/ppermute | solution.py:365
  59.4 4.4 %collective-permute-done.21.refs_2_ = bf16[51,16,128]{2,1,0:T(8,128)(2,1)S(1)} collective-permute-done((bf16[51,16,128]{2,1,0:T(8,128)(2,1)S(1)}, bf16[51,16,128]{2,1,0:T(8,128)(2,1)S(1)}, u32[]{:S(2)}, u32[]{:S(2)}) %collective-permute-start.21) | collective-permute-done | bytes 208928 | tf_op jit(solution)/shard_map/ppermute | solution.py:365
  63.8 1.5 %collective-permute-done.22.refs_3_ = bf16[51,16,128]{2,1,0:T(8,128)(2,1)S(1)} collective-permute-done((bf16[51,16,128]{2,1,0:T(8,128)(2,1)S(1)}, bf16[51,16,128]{2,1,0:T(8,128)(2,1)S(1)}, u32[]{:S(2)}, u32[]{:S(2)}) %collective-permute-start.22) | collective-permute-done | bytes 208928 | tf_op jit(solution)/shard_map/ppermute | solution.py:365
  65.3 2.9 %shard_map.108 = (bf16[8,16,192]{2,1,0:T(8,128)(2,1)S(1)}, bf16[8,16,192]{2,1,0:T(8,128)(2,1)S(1)}, bf16[8,16,192]{2,1,0:T(8,128)(2,1)S(1)}, bf16[8,16,192]{2,1,0:T(8,128)(2,1)S(1)}, bf16[8,80,192]{2,1,0:T(8,128)(2,1)S(1)}) custom-call(s32[152]{0:T(256)S(4)} %shard_map.100.table, bf16[512,2048]{1,0:T(8,128)(2,1)S(1)} %get-tuple-element.58.schur, ...), custom_call_target="tpu_custom_call" | custom-call | tf_op jit(solution)/shard_map/pallas_call | solution.py:66
  68.4 1.4 %collective-permute-start.24 = (bf16[8,16,192]{2,1,0:T(8,128)(2,1)S(1)}, bf16[8,16,192]{2,1,0:T(8,128)(2,1)S(1)}, u32[]{:S(2)}, u32[]{:S(2)}) collective-permute-start(bf16[8,16,192]{2,1,0:T(8,128)(2,1)S(1)} %get-tuple-element.91), channel_id=1, source_target_pairs={{0,2},{1,3},{2,0},{3,1},{4,6},{5,7},{6,4},{7,5},{8,10},{9,11},{10,... | collective-permute-start | bytes 147464 | tf_op jit(solution)/shard_map/ppermute | solution.py:365
  70.1 2.6 %collective-permute-done.24.c2 = bf16[8,16,192]{2,1,0:T(8,128)(2,1)S(1)} collective-permute-done((bf16[8,16,192]{2,1,0:T(8,128)(2,1)S(1)}, bf16[8,16,192]{2,1,0:T(8,128)(2,1)S(1)}, u32[]{:S(2)}, u32[]{:S(2)}) %collective-permute-start.24) | collective-permute-done | bytes 49184 | tf_op jit(solution)/shard_map/ppermute | solution.py:365
  72.8 1.1 collective-permute-done.25.c3
  74.0 2.2 %collective-permute-start.26 = (bf16[8,16,192]{2,1,0:T(8,128)(2,1)S(1)}, bf16[8,16,192]{2,1,0:T(8,128)(2,1)S(1)}, u32[]{:S(2)}, u32[]{:S(2)}) collective-permute-start(bf16[8,16,192]{2,1,0:T(8,128)(2,1)S(1)} %get-tuple-element.93), channel_id=1, source_target_pairs={{0,24},{4,28},{8,0},{12,4},{16,8},{20,12},{24,16},{28,20},{1,25},{... | collective-permute-start | bytes 147464 | tf_op jit(solution)/shard_map/ppermute | solution.py:360
  76.4 1.7 %collective-permute-start.28 = (bf16[8,16,192]{2,1,0:T(8,128)(2,1)S(1)}, bf16[8,16,192]{2,1,0:T(8,128)(2,1)S(1)}, u32[]{:S(2)}, u32[]{:S(2)}) collective-permute-start(bf16[8,16,192]{2,1,0:T(8,128)(2,1)S(1)} %get-tuple-element.96), channel_id=1, source_target_pairs={{0,4},{4,8},{8,12},{12,16},{16,20},{20,24},{24,28},{28,0},{1,5},{5... | collective-permute-start | bytes 147464 | tf_op jit(solution)/shard_map/ppermute | solution.py:360
  78.2 0.6 collective-permute-start.29
  78.8 1.6 %collective-permute-done.27.a1 = bf16[8,16,192]{2,1,0:T(8,128)(2,1)S(1)} collective-permute-done((bf16[8,16,192]{2,1,0:T(8,128)(2,1)S(1)}, bf16[8,16,192]{2,1,0:T(8,128)(2,1)S(1)}, u32[]{:S(2)}, u32[]{:S(2)}) %collective-permute-start.27) | collective-permute-done | bytes 49184 | tf_op jit(solution)/shard_map/ppermute | solution.py:360
  80.4 3.2 %collective-permute-done.28.a3 = bf16[8,16,192]{2,1,0:T(8,128)(2,1)S(1)} collective-permute-done((bf16[8,16,192]{2,1,0:T(8,128)(2,1)S(1)}, bf16[8,16,192]{2,1,0:T(8,128)(2,1)S(1)}, u32[]{:S(2)}, u32[]{:S(2)}) %collective-permute-start.28) | collective-permute-done | bytes 49184 | tf_op jit(solution)/shard_map/ppermute | solution.py:360
  83.6 0.6 collective-permute-done.29.a4
  84.7 1.8 %collective-permute-start.31 = (bf16[10,16,192]{2,1,0:T(8,128)(2,1)S(1)}, bf16[10,16,192]{2,1,0:T(8,128)(2,1)S(1)}, u32[]{:S(2)}, u32[]{:S(2)}) collective-permute-start(bf16[10,16,192]{2,1,0:T(8,128)(2,1)S(1)} %get-tuple-element.101), channel_id=1, source_target_pairs={{0,4},{4,8},{8,12},{12,16},{16,20},{20,24},{24,28},{28,0},{1,5},{5... | collective-permute-start | bytes 184328 | tf_op jit(solution)/shard_map/ppermute | solution.py:360
  86.5 3.1 %collective-permute-start.32 = (bf16[10,16,192]{2,1,0:T(8,128)(2,1)S(1)}, bf16[10,16,192]{2,1,0:T(8,128)(2,1)S(1)}, u32[]{:S(2)}, u32[]{:S(2)}) collective-permute-start(bf16[10,16,192]{2,1,0:T(8,128)(2,1)S(1)} %get-tuple-element.103), channel_id=1, source_target_pairs={{0,28},{4,0},{8,4},{12,8},{16,12},{20,16},{24,20},{28,24},{1,29},{... | collective-permute-start | bytes 184328 | tf_op jit(solution)/shard_map/ppermute | solution.py:360
  89.6 1.9 %collective-permute-start.33 = (bf16[10,16,192]{2,1,0:T(8,128)(2,1)S(1)}, bf16[10,16,192]{2,1,0:T(8,128)(2,1)S(1)}, u32[]{:S(2)}, u32[]{:S(2)}) collective-permute-start(bf16[10,16,192]{2,1,0:T(8,128)(2,1)S(1)} %get-tuple-element.104), channel_id=1, source_target_pairs={{0,24},{4,28},{8,0},{12,4},{16,8},{20,12},{24,16},{28,20},{1,25},{... | collective-permute-start | bytes 184328 | tf_op jit(solution)/shard_map/ppermute | solution.py:360
  91.4 4.6 %collective-permute-done.36.refs_7_ = bf16[2,16,192]{2,1,0:T(8,128)(2,1)S(1)} collective-permute-done((bf16[2,16,192]{2,1,0:T(8,128)(2,1)S(1)}, bf16[2,16,192]{2,1,0:T(8,128)(2,1)S(1)}, u32[]{:S(2)}, u32[]{:S(2)}) %collective-permute-start.36) | collective-permute-done | bytes 12320 | tf_op jit(solution)/shard_map/ppermute | solution.py:360
  96.1 4.6 %collective-permute-done.35.refs_6_ = bf16[2,16,192]{2,1,0:T(8,128)(2,1)S(1)} collective-permute-done((bf16[2,16,192]{2,1,0:T(8,128)(2,1)S(1)}, bf16[2,16,192]{2,1,0:T(8,128)(2,1)S(1)}, u32[]{:S(2)}, u32[]{:S(2)}) %collective-permute-start.35) | collective-permute-done | bytes 12320 | tf_op jit(solution)/shard_map/ppermute | solution.py:360
  101.0 5.2 %collective-permute-done.34.refs_5_ = bf16[2,16,192]{2,1,0:T(8,128)(2,1)S(1)} collective-permute-done((bf16[2,16,192]{2,1,0:T(8,128)(2,1)S(1)}, bf16[2,16,192]{2,1,0:T(8,128)(2,1)S(1)}, u32[]{:S(2)}, u32[]{:S(2)}) %collective-permute-start.34) | collective-permute-done | bytes 12320 | tf_op jit(solution)/shard_map/ppermute | solution.py:360
  106.4 0.9 collective-permute-start.38
  107.3 1.0 collective-permute-start.39
  108.3 3.5 %collective-permute-done.38.refs_2_ = bf16[10,16,192]{2,1,0:T(8,128)(2,1)S(1)} collective-permute-done((bf16[10,16,192]{2,1,0:T(8,128)(2,1)S(1)}, bf16[10,16,192]{2,1,0:T(8,128)(2,1)S(1)}, u32[]{:S(2)}, u32[]{:S(2)}) %collective-permute-start.38) | collective-permute-done | bytes 61472 | tf_op jit(solution)/shard_map/ppermute | solution.py:365
  111.8 0.7 collective-permute-done.39.refs_3_
  113.0 0.7 copy.11
  (56 shorter events, 4.2 us)
Async XLA Ops:
  0.0 1.0 copy-start
  1.0 15.4 %copy-start.3 = (bf16[1,8,512]{2,1,0:T(8,128)(2,1)S(1)}, bf16[1,8,512]{2,1,0:T(8,128)(2,1)}, u32[]{:S(2)}) copy-start(bf16[1,8,512]{2,1,0:T(8,128)(2,1)} %param.14) | copy-start | bytes 24580
  1.0 7.9 %collective-permute-start.1 = (bf16[192,512]{1,0:T(8,128)(2,1)S(1)}, bf16[192,512]{1,0:T(8,128)(2,1)S(1)}, u32[]{:S(2)}, u32[]{:S(2)}) collective-permute-start(bf16[192,512]{1,0:T(8,128)(2,1)S(1)} %shard_map.102.b0), channel_id=1, source_target_pairs={{0,2},{1,3},{2,0},{3,1},{4,6},{5,7},{6,4},{7,5},{8,10},{9,11},{10,... | collective-permute-start | bytes 589832 | tf_op jit(solution)/shard_map/ppermute | solution.py:365
  4.1 12.3 %collective-permute-start = (bf16[192,512]{1,0:T(8,128)(2,1)S(1)}, bf16[192,512]{1,0:T(8,128)(2,1)S(1)}, u32[]{:S(2)}, u32[]{:S(2)}) collective-permute-start(bf16[192,512]{1,0:T(8,128)(2,1)S(1)} %shard_map.102.b0), channel_id=1, source_target_pairs={{0,1},{1,0},{2,3},{3,2},{4,5},{5,4},{6,7},{7,6},{8,9},{9,8},{10,11... | collective-permute-start | bytes 589832 | tf_op jit(solution)/shard_map/ppermute | solution.py:365
  9.0 7.4 %collective-permute-start.2 = (bf16[192,512]{1,0:T(8,128)(2,1)S(1)}, bf16[192,512]{1,0:T(8,128)(2,1)S(1)}, u32[]{:S(2)}, u32[]{:S(2)}) collective-permute-start(bf16[192,512]{1,0:T(8,128)(2,1)S(1)} %collective-permute-done.1.b2), channel_id=1, source_target_pairs={{0,1},{1,0},{2,3},{3,2},{4,5},{5,4},{6,7},{7,6},{8,9},{9,8},{10,11... | collective-permute-start | bytes 589832 | tf_op jit(solution)/shard_map/ppermute | solution.py:365
  10.0 0.7 copy-start.2
  10.8 6.7 %collective-permute-start.3 = (bf16[8,48,128]{2,1,0:T(8,128)(2,1)S(1)}, bf16[8,48,128]{2,1,0:T(8,128)(2,1)S(1)}, u32[]{:S(2)}, u32[]{:S(2)}) collective-permute-start(bf16[8,48,128]{2,1,0:T(8,128)(2,1)S(1)} %shard_map.103.tables.refs_4_), channel_id=1, source_target_pairs={{0,2},{1,3},{2,0},{3,1},{4,6},{5,7},{6,4},{7,5},{8,10},{9,11},{10,... | collective-permute-start | bytes 294920 | tf_op jit(solution)/shard_map/ppermute | solution.py:365
  12.6 7.1 %collective-permute-start.7 = (bf16[8,48,128]{2,1,0:T(8,128)(2,1)S(1)}, bf16[8,48,128]{2,1,0:T(8,128)(2,1)}, u32[]{:S(2)}, u32[]{:S(2)}) collective-permute-start(bf16[8,48,128]{2,1,0:T(8,128)(2,1)S(1)} %shard_map.103.tables.refs_4_), channel_id=1, source_target_pairs={{0,1},{1,0},{2,3},{3,2},{4,5},{5,4},{6,7},{7,6},{8,9},{9,8},{10,11... | collective-permute-start | bytes 294920 | tf_op jit(solution)/shard_map/ppermute | solution.py:365
  17.5 5.6 %collective-permute-start.8 = (bf16[8,48,128]{2,1,0:T(8,128)(2,1)S(1)}, bf16[8,48,128]{2,1,0:T(8,128)(2,1)S(1)}, u32[]{:S(2)}, u32[]{:S(2)}) collective-permute-start(bf16[8,48,128]{2,1,0:T(8,128)(2,1)S(1)} %collective-permute-done.3.refs_6_), channel_id=1, source_target_pairs={{0,1},{1,0},{2,3},{3,2},{4,5},{5,4},{6,7},{7,6},{8,9},{9,8},{10,11... | collective-permute-start | bytes 294920 | tf_op jit(solution)/shard_map/ppermute | solution.py:365
  17.9 1.9 %collective-permute-start.4 = (bf16[8,16,256]{2,1,0:T(8,128)(2,1)S(1)}, bf16[8,16,256]{2,1,0:T(8,128)(2,1)S(1)}, u32[]{:S(2)}, u32[]{:S(2)}) collective-permute-start(bf16[8,16,256]{2,1,0:T(8,128)(2,1)S(1)} %get-tuple-element.65), channel_id=1, source_target_pairs={{0,1},{1,0},{2,3},{3,2},{4,5},{5,4},{6,7},{7,6},{8,9},{9,8},{10,11... | collective-permute-start | bytes 196616 | tf_op jit(solution)/shard_map/ppermute | solution.py:365
  18.1 5.0 %collective-permute-start.5 = (bf16[8,16,256]{2,1,0:T(8,128)(2,1)S(1)}, bf16[8,16,256]{2,1,0:T(8,128)(2,1)S(1)}, u32[]{:S(2)}, u32[]{:S(2)}) collective-permute-start(bf16[8,16,256]{2,1,0:T(8,128)(2,1)S(1)} %get-tuple-element.66), channel_id=1, source_target_pairs={{0,2},{1,3},{2,0},{3,1},{4,6},{5,7},{6,4},{7,5},{8,10},{9,11},{10,... | collective-permute-start | bytes 196616 | tf_op jit(solution)/shard_map/ppermute | solution.py:365
  18.5 4.6 %collective-permute-start.6 = (bf16[8,16,256]{2,1,0:T(8,128)(2,1)S(1)}, bf16[8,16,256]{2,1,0:T(8,128)(2,1)S(1)}, u32[]{:S(2)}, u32[]{:S(2)}) collective-permute-start(bf16[8,16,256]{2,1,0:T(8,128)(2,1)S(1)} %get-tuple-element.67), channel_id=1, source_target_pairs={{0,3},{1,2},{2,1},{3,0},{4,7},{5,6},{6,5},{7,4},{8,11},{9,10},{10,... | collective-permute-start | bytes 196616 | tf_op jit(solution)/shard_map/ppermute | solution.py:365
  23.2 6.6 %collective-permute-start.9 = (bf16[8,16,256]{2,1,0:T(8,128)(2,1)S(1)}, bf16[8,16,256]{2,1,0:T(8,128)(2,1)S(1)}, u32[]{:S(2)}, u32[]{:S(2)}) collective-permute-start(bf16[8,16,256]{2,1,0:T(8,128)(2,1)S(1)} %get-tuple-element.73), channel_id=1, source_target_pairs={{0,24},{4,28},{8,0},{12,4},{16,8},{20,12},{24,16},{28,20},{1,25},{... | collective-permute-start | bytes 196616 | tf_op jit(solution)/shard_map/ppermute | solution.py:360
  26.8 4.3 %collective-permute-start.10 = (bf16[8,16,256]{2,1,0:T(8,128)(2,1)S(1)}, bf16[8,16,256]{2,1,0:T(8,128)(2,1)S(1)}, u32[]{:S(2)}, u32[]{:S(2)}) collective-permute-start(bf16[8,16,256]{2,1,0:T(8,128)(2,1)S(1)} %get-tuple-element.74), channel_id=1, source_target_pairs={{0,28},{4,0},{8,4},{12,8},{16,12},{20,16},{24,20},{28,24},{1,29},{... | collective-permute-start | bytes 196616 | tf_op jit(solution)/shard_map/ppermute | solution.py:360
  28.2 7.4 %collective-permute-start.11 = (bf16[8,16,256]{2,1,0:T(8,128)(2,1)S(1)}, bf16[8,16,256]{2,1,0:T(8,128)(2,1)S(1)}, u32[]{:S(2)}, u32[]{:S(2)}) collective-permute-start(bf16[8,16,256]{2,1,0:T(8,128)(2,1)S(1)} %get-tuple-element.76), channel_id=1, source_target_pairs={{0,4},{4,8},{8,12},{12,16},{16,20},{20,24},{24,28},{28,0},{1,5},{5... | collective-permute-start | bytes 196616 | tf_op jit(solution)/shard_map/ppermute | solution.py:360
  28.8 6.8 %collective-permute-start.12 = (bf16[8,16,256]{2,1,0:T(8,128)(2,1)S(1)}, bf16[8,16,256]{2,1,0:T(8,128)(2,1)S(1)}, u32[]{:S(2)}, u32[]{:S(2)}) collective-permute-start(bf16[8,16,256]{2,1,0:T(8,128)(2,1)S(1)} %get-tuple-element.77), channel_id=1, source_target_pairs={{0,8},{4,12},{8,16},{12,20},{16,24},{20,28},{24,0},{28,4},{1,9},{5... | collective-permute-start | bytes 196616 | tf_op jit(solution)/shard_map/ppermute | solution.py:360
  36.2 21.6 %collective-permute-start.13 = (bf16[10,16,192]{2,1,0:T(8,128)(2,1)S(1)}, bf16[10,16,192]{2,1,0:T(8,128)(2,1)S(1)}, u32[]{:S(2)}, u32[]{:S(2)}) collective-permute-start(bf16[10,16,192]{2,1,0:T(8,128)(2,1)S(1)} %get-tuple-element.78), channel_id=1, source_target_pairs={{0,8},{4,12},{8,16},{12,20},{16,24},{20,28},{24,0},{28,4},{1,9},{5... | collective-permute-start | bytes 184328 | tf_op jit(solution)/shard_map/ppermute | solution.py:360
  36.2 21.6 %collective-permute-start.14 = (bf16[10,16,192]{2,1,0:T(8,128)(2,1)S(1)}, bf16[10,16,192]{2,1,0:T(8,128)(2,1)S(1)}, u32[]{:S(2)}, u32[]{:S(2)}) collective-permute-start(bf16[10,16,192]{2,1,0:T(8,128)(2,1)S(1)} %get-tuple-element.79), channel_id=1, source_target_pairs={{0,4},{4,8},{8,12},{12,16},{16,20},{20,24},{24,28},{28,0},{1,5},{5... | collective-permute-start | bytes 184328 | tf_op jit(solution)/shard_map/ppermute | solution.py:360
  38.0 19.8 %collective-permute-start.15 = (bf16[10,16,192]{2,1,0:T(8,128)(2,1)S(1)}, bf16[10,16,192]{2,1,0:T(8,128)(2,1)S(1)}, u32[]{:S(2)}, u32[]{:S(2)}) collective-permute-start(bf16[10,16,192]{2,1,0:T(8,128)(2,1)S(1)} %get-tuple-element.81), channel_id=1, source_target_pairs={{0,28},{4,0},{8,4},{12,8},{16,12},{20,16},{24,20},{28,24},{1,29},{... | collective-permute-start | bytes 184328 | tf_op jit(solution)/shard_map/ppermute | solution.py:360
  41.2 16.6 %collective-permute-start.16 = (bf16[10,16,192]{2,1,0:T(8,128)(2,1)S(1)}, bf16[10,16,192]{2,1,0:T(8,128)(2,1)S(1)}, u32[]{:S(2)}, u32[]{:S(2)}) collective-permute-start(bf16[10,16,192]{2,1,0:T(8,128)(2,1)S(1)} %get-tuple-element.82), channel_id=1, source_target_pairs={{0,24},{4,28},{8,0},{12,4},{16,8},{20,12},{24,16},{28,20},{1,25},{... | collective-permute-start | bytes 184328 | tf_op jit(solution)/shard_map/ppermute | solution.py:360
  43.0 4.6 %collective-permute-start.19 = (bf16[2,16,192]{2,1,0:T(8,128)(2,1)S(1)}, bf16[2,16,192]{2,1,0:T(8,128)(2,1)S(1)}, u32[]{:S(2)}, u32[]{:S(2)}) collective-permute-start(bf16[2,16,192]{2,1,0:T(8,128)(2,1)S(1)} %get-tuple-element.83), channel_id=1, source_target_pairs={{0,20},{4,24},{8,28},{12,0},{16,4},{20,8},{24,12},{28,16},{1,21},{... | collective-permute-start | bytes 36872 | tf_op jit(solution)/shard_map/ppermute | solution.py:360
  47.6 4.6 %collective-permute-start.18 = (bf16[2,16,192]{2,1,0:T(8,128)(2,1)S(1)}, bf16[2,16,192]{2,1,0:T(8,128)(2,1)S(1)}, u32[]{:S(2)}, u32[]{:S(2)}) collective-permute-start(bf16[2,16,192]{2,1,0:T(8,128)(2,1)S(1)} %get-tuple-element.83), channel_id=1, source_target_pairs={{0,16},{4,20},{8,24},{12,28},{16,0},{20,4},{24,8},{28,12},{1,17},{... | collective-permute-start | bytes 36872 | tf_op jit(solution)/shard_map/ppermute | solution.py:360
  52.2 5.5 %collective-permute-start.17 = (bf16[2,16,192]{2,1,0:T(8,128)(2,1)S(1)}, bf16[2,16,192]{2,1,0:T(8,128)(2,1)S(1)}, u32[]{:S(2)}, u32[]{:S(2)}) collective-permute-start(bf16[2,16,192]{2,1,0:T(8,128)(2,1)S(1)} %get-tuple-element.83), channel_id=1, source_target_pairs={{0,12},{4,16},{8,20},{12,24},{16,28},{20,0},{24,4},{28,8},{1,13},{... | collective-permute-start | bytes 36872 | tf_op jit(solution)/shard_map/ppermute | solution.py:360
  57.9 5.9 %collective-permute-start.21 = (bf16[51,16,128]{2,1,0:T(8,128)(2,1)S(1)}, bf16[51,16,128]{2,1,0:T(8,128)(2,1)S(1)}, u32[]{:S(2)}, u32[]{:S(2)}) collective-permute-start(bf16[51,16,128]{2,1,0:T(8,128)(2,1)S(1)} %shard_map.107.refs_0_), channel_id=1, source_target_pairs={{0,2},{1,3},{2,0},{3,1},{4,6},{5,7},{6,4},{7,5},{8,10},{9,11},{10,... | collective-permute-start | bytes 626696 | tf_op jit(solution)/shard_map/ppermute | solution.py:365
  59.4 4.4 %collective-permute-start.20 = (bf16[51,16,128]{2,1,0:T(8,128)(2,1)S(1)}, bf16[51,16,128]{2,1,0:T(8,128)(2,1)S(1)}, u32[]{:S(2)}, u32[]{:S(2)}) collective-permute-start(bf16[51,16,128]{2,1,0:T(8,128)(2,1)S(1)} %shard_map.107.refs_0_), channel_id=1, source_target_pairs={{0,1},{1,0},{2,3},{3,2},{4,5},{5,4},{6,7},{7,6},{8,9},{9,8},{10,11... | collective-permute-start | bytes 626696 | tf_op jit(solution)/shard_map/ppermute | solution.py:365
  63.8 1.5 %collective-permute-start.22 = (bf16[51,16,128]{2,1,0:T(8,128)(2,1)S(1)}, bf16[51,16,128]{2,1,0:T(8,128)(2,1)S(1)}, u32[]{:S(2)}, u32[]{:S(2)}) collective-permute-start(bf16[51,16,128]{2,1,0:T(8,128)(2,1)S(1)} %collective-permute-done.21.refs_2_), channel_id=1, source_target_pairs={{0,1},{1,0},{2,3},{3,2},{4,5},{5,4},{6,7},{7,6},{8,9},{9,8},{10,11... | collective-permute-start | bytes 626696 | tf_op jit(solution)/shard_map/ppermute | solution.py:365
  65.3 47.2 %copy-start.1 = (f32[1,512,192]{1,2,0:T(8,128)S(1)}, f32[1,512,192]{1,2,0:T(8,128)}, u32[]{:S(2)}) copy-start(f32[1,512,192]{1,2,0:T(8,128)} %param.12) | copy-start | bytes 1179652
  68.2 1.9 %collective-permute-start.23 = (bf16[8,16,192]{2,1,0:T(8,128)(2,1)S(1)}, bf16[8,16,192]{2,1,0:T(8,128)(2,1)S(1)}, u32[]{:S(2)}, u32[]{:S(2)}) collective-permute-start(bf16[8,16,192]{2,1,0:T(8,128)(2,1)S(1)} %get-tuple-element.90), channel_id=1, source_target_pairs={{0,1},{1,0},{2,3},{3,2},{4,5},{5,4},{6,7},{7,6},{8,9},{9,8},{10,11... | collective-permute-start | bytes 147464 | tf_op jit(solution)/shard_map/ppermute | solution.py:365
  68.4 4.4 %collective-permute-start.24 = (bf16[8,16,192]{2,1,0:T(8,128)(2,1)S(1)}, bf16[8,16,192]{2,1,0:T(8,128)(2,1)S(1)}, u32[]{:S(2)}, u32[]{:S(2)}) collective-permute-start(bf16[8,16,192]{2,1,0:T(8,128)(2,1)S(1)} %get-tuple-element.91), channel_id=1, source_target_pairs={{0,2},{1,3},{2,0},{3,1},{4,6},{5,7},{6,4},{7,5},{8,10},{9,11},{10,... | collective-permute-start | bytes 147464 | tf_op jit(solution)/shard_map/ppermute | solution.py:365
  69.8 4.1 %collective-permute-start.25 = (bf16[8,16,192]{2,1,0:T(8,128)(2,1)S(1)}, bf16[8,16,192]{2,1,0:T(8,128)(2,1)S(1)}, u32[]{:S(2)}, u32[]{:S(2)}) collective-permute-start(bf16[8,16,192]{2,1,0:T(8,128)(2,1)S(1)} %get-tuple-element.92), channel_id=1, source_target_pairs={{0,3},{1,2},{2,1},{3,0},{4,7},{5,6},{6,5},{7,4},{8,11},{9,10},{10,... | collective-permute-start | bytes 147464 | tf_op jit(solution)/shard_map/ppermute | solution.py:365
  74.0 4.9 %collective-permute-start.26 = (bf16[8,16,192]{2,1,0:T(8,128)(2,1)S(1)}, bf16[8,16,192]{2,1,0:T(8,128)(2,1)S(1)}, u32[]{:S(2)}, u32[]{:S(2)}) collective-permute-start(bf16[8,16,192]{2,1,0:T(8,128)(2,1)S(1)} %get-tuple-element.93), channel_id=1, source_target_pairs={{0,24},{4,28},{8,0},{12,4},{16,8},{20,12},{24,16},{28,20},{1,25},{... | collective-permute-start | bytes 147464 | tf_op jit(solution)/shard_map/ppermute | solution.py:360
  76.1 4.3 %collective-permute-start.27 = (bf16[8,16,192]{2,1,0:T(8,128)(2,1)S(1)}, bf16[8,16,192]{2,1,0:T(8,128)(2,1)S(1)}, u32[]{:S(2)}, u32[]{:S(2)}) collective-permute-start(bf16[8,16,192]{2,1,0:T(8,128)(2,1)S(1)} %get-tuple-element.94), channel_id=1, source_target_pairs={{0,28},{4,0},{8,4},{12,8},{16,12},{20,16},{24,20},{28,24},{1,29},{... | collective-permute-start | bytes 147464 | tf_op jit(solution)/shard_map/ppermute | solution.py:360
  76.4 7.2 %collective-permute-start.28 = (bf16[8,16,192]{2,1,0:T(8,128)(2,1)S(1)}, bf16[8,16,192]{2,1,0:T(8,128)(2,1)S(1)}, u32[]{:S(2)}, u32[]{:S(2)}) collective-permute-start(bf16[8,16,192]{2,1,0:T(8,128)(2,1)S(1)} %get-tuple-element.96), channel_id=1, source_target_pairs={{0,4},{4,8},{8,12},{12,16},{16,20},{20,24},{24,28},{28,0},{1,5},{5... | collective-permute-start | bytes 147464 | tf_op jit(solution)/shard_map/ppermute | solution.py:360
  78.2 6.1 %collective-permute-start.29 = (bf16[8,16,192]{2,1,0:T(8,128)(2,1)S(1)}, bf16[8,16,192]{2,1,0:T(8,128)(2,1)S(1)}, u32[]{:S(2)}, u32[]{:S(2)}) collective-permute-start(bf16[8,16,192]{2,1,0:T(8,128)(2,1)S(1)} %get-tuple-element.97), channel_id=1, source_target_pairs={{0,8},{4,12},{8,16},{12,20},{16,24},{20,28},{24,0},{28,4},{1,9},{5... | collective-permute-start | bytes 147464 | tf_op jit(solution)/shard_map/ppermute | solution.py:360
  84.6 21.6 %collective-permute-start.30 = (bf16[10,16,192]{2,1,0:T(8,128)(2,1)S(1)}, bf16[10,16,192]{2,1,0:T(8,128)(2,1)S(1)}, u32[]{:S(2)}, u32[]{:S(2)}) collective-permute-start(bf16[10,16,192]{2,1,0:T(8,128)(2,1)S(1)} %get-tuple-element.100), channel_id=1, source_target_pairs={{0,8},{4,12},{8,16},{12,20},{16,24},{20,28},{24,0},{28,4},{1,9},{5... | collective-permute-start | bytes 184328 | tf_op jit(solution)/shard_map/ppermute | solution.py:360
  84.7 21.6 %collective-permute-start.31 = (bf16[10,16,192]{2,1,0:T(8,128)(2,1)S(1)}, bf16[10,16,192]{2,1,0:T(8,128)(2,1)S(1)}, u32[]{:S(2)}, u32[]{:S(2)}) collective-permute-start(bf16[10,16,192]{2,1,0:T(8,128)(2,1)S(1)} %get-tuple-element.101), channel_id=1, source_target_pairs={{0,4},{4,8},{8,12},{12,16},{16,20},{20,24},{24,28},{28,0},{1,5},{5... | collective-permute-start | bytes 184328 | tf_op jit(solution)/shard_map/ppermute | solution.py:360
  86.5 19.8 %collective-permute-start.32 = (bf16[10,16,192]{2,1,0:T(8,128)(2,1)S(1)}, bf16[10,16,192]{2,1,0:T(8,128)(2,1)S(1)}, u32[]{:S(2)}, u32[]{:S(2)}) collective-permute-start(bf16[10,16,192]{2,1,0:T(8,128)(2,1)S(1)} %get-tuple-element.103), channel_id=1, source_target_pairs={{0,28},{4,0},{8,4},{12,8},{16,12},{20,16},{24,20},{28,24},{1,29},{... | collective-permute-start | bytes 184328 | tf_op jit(solution)/shard_map/ppermute | solution.py:360
  89.6 16.7 %collective-permute-start.33 = (bf16[10,16,192]{2,1,0:T(8,128)(2,1)S(1)}, bf16[10,16,192]{2,1,0:T(8,128)(2,1)S(1)}, u32[]{:S(2)}, u32[]{:S(2)}) collective-permute-start(bf16[10,16,192]{2,1,0:T(8,128)(2,1)S(1)} %get-tuple-element.104), channel_id=1, source_target_pairs={{0,24},{4,28},{8,0},{12,4},{16,8},{20,12},{24,16},{28,20},{1,25},{... | collective-permute-start | bytes 184328 | tf_op jit(solution)/shard_map/ppermute | solution.py:360
  91.4 4.6 %collective-permute-start.36 = (bf16[2,16,192]{2,1,0:T(8,128)(2,1)S(1)}, bf16[2,16,192]{2,1,0:T(8,128)(2,1)S(1)}, u32[]{:S(2)}, u32[]{:S(2)}) collective-permute-start(bf16[2,16,192]{2,1,0:T(8,128)(2,1)S(1)} %get-tuple-element.105), channel_id=1, source_target_pairs={{0,20},{4,24},{8,28},{12,0},{16,4},{20,8},{24,12},{28,16},{1,21},{... | collective-permute-start | bytes 36872 | tf_op jit(solution)/shard_map/ppermute | solution.py:360
  96.1 4.6 %collective-permute-start.35 = (bf16[2,16,192]{2,1,0:T(8,128)(2,1)S(1)}, bf16[2,16,192]{2,1,0:T(8,128)(2,1)S(1)}, u32[]{:S(2)}, u32[]{:S(2)}) collective-permute-start(bf16[2,16,192]{2,1,0:T(8,128)(2,1)S(1)} %get-tuple-element.105), channel_id=1, source_target_pairs={{0,16},{4,20},{8,24},{12,28},{16,0},{20,4},{24,8},{28,12},{1,17},{... | collective-permute-start | bytes 36872 | tf_op jit(solution)/shard_map/ppermute | solution.py:360
  100.7 5.5 %collective-permute-start.34 = (bf16[2,16,192]{2,1,0:T(8,128)(2,1)S(1)}, bf16[2,16,192]{2,1,0:T(8,128)(2,1)S(1)}, u32[]{:S(2)}, u32[]{:S(2)}) collective-permute-start(bf16[2,16,192]{2,1,0:T(8,128)(2,1)S(1)} %get-tuple-element.105), channel_id=1, source_target_pairs={{0,12},{4,16},{8,20},{12,24},{16,28},{20,0},{24,4},{28,8},{1,13},{... | collective-permute-start | bytes 36872 | tf_op jit(solution)/shard_map/ppermute | solution.py:360
  106.3 1.9 %collective-permute-start.37 = (bf16[10,16,192]{2,1,0:T(8,128)(2,1)S(1)}, bf16[10,16,192]{2,1,0:T(8,128)(2,1)S(1)}, u32[]{:S(2)}, u32[]{:S(2)}) collective-permute-start(bf16[10,16,192]{2,1,0:T(8,128)(2,1)S(1)} %get-tuple-element.107), channel_id=1, source_target_pairs={{0,1},{1,0},{2,3},{3,2},{4,5},{5,4},{6,7},{7,6},{8,9},{9,8},{10,11... | collective-permute-start | bytes 184328 | tf_op jit(solution)/shard_map/ppermute | solution.py:365
  106.4 5.4 %collective-permute-start.38 = (bf16[10,16,192]{2,1,0:T(8,128)(2,1)S(1)}, bf16[10,16,192]{2,1,0:T(8,128)(2,1)S(1)}, u32[]{:S(2)}, u32[]{:S(2)}) collective-permute-start(bf16[10,16,192]{2,1,0:T(8,128)(2,1)S(1)} %get-tuple-element.108), channel_id=1, source_target_pairs={{0,2},{1,3},{2,0},{3,1},{4,6},{5,7},{6,4},{7,5},{8,10},{9,11},{10,... | collective-permute-start | bytes 184328 | tf_op jit(solution)/shard_map/ppermute | solution.py:365
  107.3 5.2 %collective-permute-start.39 = (bf16[10,16,192]{2,1,0:T(8,128)(2,1)S(1)}, bf16[10,16,192]{2,1,0:T(8,128)(2,1)S(1)}, u32[]{:S(2)}, u32[]{:S(2)}) collective-permute-start(bf16[10,16,192]{2,1,0:T(8,128)(2,1)S(1)} %get-tuple-element.109), channel_id=1, source_target_pairs={{0,3},{1,2},{2,1},{3,0},{4,7},{5,6},{6,5},{7,4},{8,11},{9,10},{10,... | collective-permute-start | bytes 184328 | tf_op jit(solution)/shard_map/ppermute | solution.py:365

commit v3 on v2

v3 whole, which is shorter than its diff:
```python
import functools

import jax
import jax.numpy as jnp
from jax import lax
from jax.experimental import pallas as pl
from jax.experimental.pallas import tpu as pltpu
from jax.sharding import PartitionSpec as P

DEG = 8
MODES = 64
FPTS = 64
MORT_OWN = 16
REACH = 2
CAP = 8
LINKS = 2 * REACH + 1
SLOTS = LINKS * CAP

BF = jnp.bfloat16
F32 = jnp.float32
CONTRACT_FIRST = (((0,), (0,)), ((), ()))
CONTRACT_LAST = (((1,), (1,)), ((), ()))
VMEM = pl.BlockSpec(memory_space=pltpu.VMEM)
SMEM = pl.BlockSpec(memory_space=pltpu.SMEM)
HBM = pl.BlockSpec(memory_space=pltpu.HBM)


def split_two(value):
    high = value.astype(BF)
    return high, (value - high.astype(F32)).astype(BF)


class Sizes:
    def __init__(self, subs, grps, schur, project, coarse_basis, rhs):
        self.subs = subs
        self.grps = grps
        self.rows = schur.shape[1]
        self.all_rows = schur.shape[2]
        self.own = project.shape[1]
        self.faces = self.own * grps
        self.corners = coarse_basis.shape[1]
        self.rhs = rhs.shape[2]
        self.vertices = 2 * subs
        self.share = MODES // grps
        self.extra = 2 * self.vertices
        self.wide = -(-(self.rhs + self.extra) // 128) * 128
        self.lanes = self.rhs // 128 * 128
        self.tail = self.rhs - self.lanes
        self.missing = range(REACH + 1, subs - REACH)
        self.near = self.vertices == self.share and LINKS <= subs and len(self.missing) <= 3
        self.more = 3 if self.near else 0
        self.dense = self.share * self.rhs // self.lanes
        self.pieces = max(1, 128 // self.extra)
        self.slabs = max(1, self.extra // 128)
        self.head = self.faces + self.faces * self.tail // self.lanes
        self.packed = self.head + self.faces * self.slabs // self.pieces
        self.t_src = 0
        self.t_arr = SLOTS
        self.t_slot = 2 * SLOTS
        self.t_count = self.t_slot + self.faces
        self.t_order = self.t_count + MORT_OWN
        self.t_corner = self.t_order + MORT_OWN
        self.t_end = self.t_corner + self.corners


def call(kernel, sizes, outs, args, scratch=(), static=()):
    single = not isinstance(outs, list)
    outs = [outs] if single else outs
    ins = [SMEM if a.dtype == jnp.int32 else VMEM for a in args]
    args = [
        pltpu.with_memory_space_constraint(a, pltpu.SMEM if a.dtype == jnp.int32 else pltpu.VMEM) for a in args
    ]
    results = pl.pallas_call(
        functools.partial(kernel, sizes, *static),
        out_shape=[pltpu.VMEM(o.shape, o.dtype) for o in outs],
        in_specs=ins,
        out_specs=[VMEM for _ in outs],
        scratch_shapes=list(scratch),
        compiler_params=pltpu.CompilerParams(vmem_limit_bytes=16 << 20),
    )(*args)
    return results[0] if single else results


def meeting_of(link, s):
    odd, high = s % 2 == 1, (s // 2) % 2 == 1
    if link == REACH:
        return 4
    if abs(link - REACH) == 1:
        return jnp.where(odd == (link < REACH), 0, 3)
    return jnp.where(high == (link < REACH), 1, 2)


def table_kernel(z, owner, mortar, order, smap, vids, table, used, names, met):
    s = lax.axis_index("sub")
    g = lax.axis_index("grp")
    d = smap[s]
    for i in range(SLOTS):
        table[z.t_src + i] = 0
    for i in range(LINKS):
        used[i] = 0
        met[i] = jnp.int32(meeting_of(i, s))
    for i in range(MORT_OWN):
        table[z.t_count + i] = 0
        table[z.t_order + i] = order[s, i]
    for i in range(z.corners):
        table[z.t_corner + i] = vids[d, i]
    for f in range(z.faces):
        o = owner[d, 0, f]
        r = used[o]
        used[o] = r + 1
        slot = met[o] * CAP + r
        table[z.t_slot + f] = slot
        table[z.t_src + slot] = ((f // z.own) ^ g) * z.own + f % z.own
    for link in range(LINKS):
        dd = smap[lax.rem(s - link + REACH + z.subs, z.subs)]
        r = jnp.int32(0)
        for f in range(z.faces):
            hit = (owner[dd, 0, f] == link).astype(jnp.int32)
            m = mortar[dd, f]
            names[r] = m
            table[z.t_count + m] = table[z.t_count + m] + hit
            r = r + hit
        for i in range(CAP):
            table[z.t_arr + met[2 * REACH - link] * CAP + i] = jnp.where(i < r, names[i], MORT_OWN)


def narrow_kernel(z, start, coarse, out, held, basis, sems):
    pieces = 4
    size = z.rhs // pieces
    copies = [
        pltpu.make_async_copy(start.at[pl.ds(i * size, size)], held.at[pl.ds(i * size, size)], sems.at[i])
        for i in range(pieces)
    ]
    copies.append(pltpu.make_async_copy(coarse, basis, sems.at[pieces]))
    for c in copies:
        c.start()
    for i in range(pieces):
        copies[i].wait()
        out[i * size : (i + 1) * size, :] = held[i * size : (i + 1) * size, :].astype(BF)
    copies[pieces].wait()
    out[z.rhs :, :] = basis[...]


def unpack_kernel(z, p0, p1, p2, p3, out):
    for j, p in enumerate((p0, p1, p2, p3)):
        for i in range(z.own):
            out[j * z.own + i] = tables_of(p[i])


def load_kernel(schur, rhs, schur_out, rhs_out, sems):
    copies = [
        pltpu.make_async_copy(schur, schur_out, sems.at[0]),
        pltpu.make_async_copy(rhs, rhs_out, sems.at[1]),
    ]
    for c in copies:
        c.start()
    for c in copies:
        c.wait()


def join_kernel(z, tables, out):
    half = MODES // 2
    for f in range(z.own):
        out[f] = jnp.concatenate([tables[f, :half, :], tables[f, half:, :]], axis=1)


def tables_of(pair):
    return jnp.concatenate([pair[:, :FPTS], pair[:, FPTS:]], axis=0)


def share_rows(z, member):
    return pl.ds(pl.multiple_of(member * z.share, z.share), z.share)


def hot_rows(z, table, width, shift):
    column = lax.broadcasted_iota(jnp.int32, (1, width), 1)
    rows = [jnp.where(column == table[z.t_corner + i] + shift, 1.0, 0.0) for i in range(z.corners)]
    return jnp.concatenate(rows, axis=0).astype(BF)


def first_kernel(z, table, schur, b0, b1, b2, b3, rhs, tables, coarse, o0, o1, o2, o3, res_out, ext_out, gathered, held, coeffs):
    g = lax.axis_index("grp")
    for j, b in enumerate((b0, b1, b2, b3)):
        gathered[:, pl.ds(pl.multiple_of((g ^ j) * z.rows, z.rows), z.rows)] = b[...]
    product = lax.dot_general(schur[...], gathered[...], CONTRACT_LAST, preferred_element_type=F32)
    residual = product[:, : z.rhs] - rhs[...].T
    res_out[...] = residual
    held[:, : z.rhs] = residual.astype(BF)
    width = z.wide - z.rhs
    basis = lax.dot_general(coarse[...], hot_rows(z, table, width, 0), CONTRACT_FIRST, preferred_element_type=F32)
    image = jnp.dot(
        product[:, z.rhs :].astype(BF), hot_rows(z, table, width, z.vertices), preferred_element_type=F32
    )
    held[:, z.rhs :] = (basis + image).astype(BF)
    for f in range(z.own):
        coeffs[f] = jnp.dot(tables_of(tables[f]), held[f * FPTS : (f + 1) * FPTS, :], preferred_element_type=F32).astype(BF)
    ext_out[...] = coeffs[:, :, z.rhs :]
    for j, o in enumerate((o0, o1, o2, o3)):
        for f in range(z.own):
            o[f] = coeffs[f, share_rows(z, g ^ j), :]


def pack_kernel(z, sums, table, c0, c1, c2, c3, o0, o1, o2, o3, o4, data):
    parts = (c0, c1, c2, c3)
    for j, c in enumerate(parts):
        data[j * z.own : (j + 1) * z.own] = c[: z.own]
    for k, o in enumerate((o0, o1, o2, o3, o4)):
        for i in range(CAP):
            o[i] = data[table[z.t_src + k * CAP + i]]
    if sums:
        value = sum((c[z.own :].astype(F32) for c in parts[1:]), parts[0][z.own :].astype(F32)).astype(BF)
        for o in (o0, o1, o2, o3, o4):
            o[CAP:] = value


def average_kernel(z, dense, table, *refs):
    arrivals, refs = refs[:LINKS], refs[LINKS:]
    replies, refs = refs[:LINKS], refs[LINKS:]
    near, total, held = refs if dense and z.near else (None, *refs)
    g = lax.axis_index("grp")
    total[...] = jnp.zeros_like(total)
    for k, a in enumerate(arrivals):
        for i in range(CAP):
            m = table[z.t_arr + k * CAP + i]
            total[m] = total[m] + a[i].astype(F32)
    shape = total.shape[1:]
    row = lax.broadcasted_iota(jnp.int32, shape, 0)
    if dense:
        column = lax.broadcasted_iota(jnp.int32, shape, 1)
        half = z.share // 2
        row = jnp.where(row < z.share, row, row - z.share + jnp.where(column < z.tail, 0, half))
    mode = g * z.share + row
    degree = jnp.maximum(mode // DEG, mode % DEG)
    for k in range(MORT_OWN):
        divisor = jnp.maximum(table[z.t_count + k], 1).astype(F32)
        kept = jnp.where(degree <= table[z.t_order + k], 1.0, 0.0)
        held[k] = (total[k] / divisor * kept).astype(BF)
    held[MORT_OWN] = jnp.zeros_like(held[MORT_OWN])
    for k, o in enumerate(replies):
        for i in range(CAP):
            o[i] = held[table[z.t_arr + k * CAP + i]]
    if dense and z.near:
        s = lax.axis_index("sub")
        odd, high = s % 2 == 1, (s // 2) % 2 == 1
        inner_one, inner_two, outer_two, outer_one, own = [a[CAP:].astype(F32) for a in arrivals]
        near[...] = own + inner_one + inner_two + outer_two + outer_one
        after = jnp.where(odd, outer_one, inner_one)
        before = jnp.where(odd, inner_one, outer_one)
        after_two = jnp.where(high, outer_two, inner_two)
        behind = after * (1.0 if len(z.missing) > 0 else 0.0)
        if len(z.missing) > 1:
            behind = behind + after_two
        ahead = before * (1.0 if len(z.missing) > 2 else 0.0)
        replies[1][CAP:] = jnp.where(high, behind, ahead).astype(BF)
        replies[2][CAP:] = jnp.where(high, ahead, behind).astype(BF)


def spread_first(z, table, *refs):
    blocks, out, data = refs[:LINKS], refs[-2], refs[-1]
    for link, b in enumerate(blocks):
        data[link * CAP : (link + 1) * CAP] = b[:CAP]
    half = z.own // 2
    for f in range(z.faces):
        out[f] = data[table[z.t_slot + f], :, : z.lanes]
    for member in range(z.grps):
        for i in range(half):
            f = member * z.own + i
            left = data[table[z.t_slot + f], :, z.lanes : z.rhs]
            right = data[table[z.t_slot + f + half], :, z.lanes : z.rhs]
            out[z.faces + member * half + i] = jnp.concatenate([left, right], axis=1)
    if z.pieces > 1:
        for p in range(z.faces // z.pieces):
            ends = [data[table[z.t_slot + p * z.pieces + i], :, z.rhs : z.rhs + z.extra] for i in range(z.pieces)]
            out[z.head + p] = jnp.concatenate(ends, axis=1)
    else:
        for f in range(z.faces):
            for p in range(z.slabs):
                at = z.rhs + p * 128
                out[z.head + f * z.slabs + p] = data[table[z.t_slot + f], :, at : at + 128]


def spread_second(z, table, *refs):
    n = LINKS + (1 if z.near else 0)
    blocks, near = refs[:LINKS], refs[LINKS:n]
    outs, data = refs[n : n + z.grps], refs[-1]
    g = lax.axis_index("grp")
    for k, b in enumerate(blocks):
        data[k * CAP : (k + 1) * CAP] = b[:CAP]
    for j, o in enumerate(outs):
        for i in range(z.own):
            o[i] = data[table[z.t_slot + (g ^ j) * z.own + i]]
    if z.near:
        refs[n + z.grps][...] = near[0][...] + blocks[1][CAP:].astype(F32) + blocks[2][CAP:].astype(F32)


def to_dense(z, value):
    half = z.share // 2
    tail = jnp.concatenate([value[:half, z.lanes :], value[half:, z.lanes :]], axis=1)
    return jnp.concatenate([value[:, : z.lanes], tail], axis=0)


def from_dense(z, value):
    tail = value[z.share :]
    tail = jnp.concatenate([tail[:, : z.tail], tail[:, z.tail :]], axis=0)
    return jnp.concatenate([value[: z.share], tail], axis=1)


def second_kernel(z, table, schur, *refs):
    n = z.grps
    shares, refs = refs[:n], refs[n:]
    tables, resid, coarse, ext_in, refs = refs[0], refs[1], refs[2], refs[3], refs[4:]
    outs, refs = refs[:n], refs[n:]
    own_out, hits_out, sums_out, averages, gathered, held, coeffs, scales = refs
    g = lax.axis_index("grp")
    half = z.own // 2
    for j in range(n):
        member = g ^ j
        for i in range(z.own):
            f = member * z.own + i
            slot = j * z.own + i
            for jj, a in enumerate(shares):
                rows = share_rows(z, g ^ jj)
                averages[slot, rows, : z.lanes] = a[f]
                low = (i // half) * z.tail
                averages[slot, rows, z.lanes :] = a[z.faces + member * half + i % half, :, low : low + z.tail]
            lifted = lax.dot_general(tables[slot], averages[slot], CONTRACT_FIRST, preferred_element_type=F32)
            gathered[pl.ds(pl.multiple_of(f * FPTS, FPTS), FPTS), :] = lifted.astype(BF)
    product = jnp.dot(schur[...], gathered[...], preferred_element_type=F32)
    held[...] = (resid[...] - 0.5 * product).astype(BF)
    for f in range(z.own):
        coeffs[f] = jnp.dot(tables[f], held[f * FPTS : (f + 1) * FPTS, :], preferred_element_type=F32)
    for j, o in enumerate(outs):
        for f in range(z.own):
            o[f] = to_dense(z, coeffs[f, share_rows(z, g ^ j), :]).astype(BF)
    own_out[...] = averages[: z.own]
    for i in range(z.own):
        for jj, a in enumerate(shares):
            rows = share_rows(z, g ^ jj)
            if z.pieces > 1:
                low = (i % z.pieces) * z.extra
                scales[i, rows, :] = a[z.head + (g * z.own + i) // z.pieces, :, low : low + z.extra]
            else:
                for p in range(z.slabs):
                    scales[i, rows, p * 128 : (p + 1) * 128] = a[z.head + (g * z.own + i) * z.slabs + p]
    hits_out[...] = scales[:, :, z.vertices :]
    own_points = gathered[pl.ds(pl.multiple_of(g * z.rows, z.rows), z.rows), :]
    corner = jnp.dot(coarse[...], own_points, preferred_element_type=F32)
    sums_out[...] = jnp.zeros_like(sums_out)
    for i in range(z.corners):
        sums_out[0, pl.ds(table[z.t_corner + i], 1), : z.rhs] = corner[i : i + 1, :]
    flat = scales[:, :, : z.vertices].reshape(z.own * MODES, z.vertices)
    image = ext_in[:, :, z.vertices : z.extra].reshape(z.own * MODES, z.vertices)
    sums_out[0, :, z.rhs : z.rhs + z.vertices] = -0.5 * lax.dot_general(
        flat, image, CONTRACT_FIRST, preferred_element_type=F32
    )
    sums_out[1, :, : z.rhs] = lax.dot_general(
        flat, coeffs[...].astype(BF).reshape(z.own * MODES, z.rhs), CONTRACT_FIRST, preferred_element_type=F32
    )
    if z.near:
        one = to_dense(z, sums_out[0, :, : z.rhs]).astype(BF)
        two = to_dense(z, sums_out[1, :, : z.rhs]).astype(BF)
        blank = jnp.zeros((z.share, z.rhs - z.vertices), F32)
        between = jnp.concatenate([sums_out[0, :, z.rhs : z.rhs + z.vertices], blank], axis=1)
        between = to_dense(z, between).astype(BF)
        for o in outs:
            o[z.own] = one
            o[z.own + 1] = two
            o[z.own + 2] = between


def last_kernel(z, table, *refs):
    n = z.grps
    shares, refs = refs[:n], refs[n:]
    tables, coarse, sums, hits, earlier, start, out, averages, whole, change = refs
    g = lax.axis_index("grp")
    if z.near:
        one, two = from_dense(z, sums[0]), from_dense(z, sums[1])
        between = sums[2, : z.share, : z.vertices]
    else:
        one, two = sums[0, :, : z.rhs], sums[1, :, : z.rhs]
        between = sums[0, :, z.rhs : z.rhs + z.vertices]
    two = two + jnp.dot(between, one, precision=lax.Precision.HIGHEST, preferred_element_type=F32)
    whole[...] = one + two
    high, low = split_two(one)
    flat = hits[...].reshape(z.own * MODES, z.vertices)
    shift = jnp.dot(flat, high, preferred_element_type=F32) + jnp.dot(flat, low, preferred_element_type=F32)
    rows = [whole[pl.ds(table[z.t_corner + i], 1), :] for i in range(z.corners)]
    high, low = split_two(jnp.concatenate(rows, axis=0))
    coarse_corr = lax.dot_general(coarse[...], high, CONTRACT_FIRST, preferred_element_type=F32)
    coarse_corr = coarse_corr + lax.dot_general(coarse[...], low, CONTRACT_FIRST, preferred_element_type=F32)
    for i in range(z.own):
        for j, c in enumerate(shares):
            averages[i, share_rows(z, g ^ j), :] = from_dense(z, c[i].astype(F32))
        rows = slice(i * FPTS, (i + 1) * FPTS)
        fixed = (averages[i] - 0.5 * shift[i * MODES : (i + 1) * MODES, :]).astype(BF)
        table_i = tables_of(tables[i])
        both = lax.dot_general(
            jnp.concatenate([table_i, table_i], axis=0),
            jnp.concatenate([fixed, earlier[i]], axis=0),
            CONTRACT_FIRST,
            preferred_element_type=F32,
        )
        change[rows, :] = both + coarse_corr[rows, :]
    out[...] = start[...] - 0.5 * change[...].T


def paired(blocks):
    count = lax.axis_size("sub")
    assert count % 4 == 0
    pairs = [[], [], [], []]
    for s in range(count):
        pairs[0].append((s, s ^ 1))
        pairs[1].append((s, s ^ 2))
        pairs[2].append((s, (s + (2 if (s // 2) % 2 else -2)) % count))
        pairs[3].append((s, (s + (1 if s % 2 else -1)) % count))
    return [lax.ppermute(b, "sub", p) for b, p in zip(blocks, pairs)] + [blocks[4]]


def swapped(value, mask):
    count = lax.axis_size("grp")
    return lax.ppermute(value, "grp", [(s, s ^ mask) for s in range(count)])


def exchanged(blocks):
    return [blocks[0]] + [swapped(blocks[j], j) for j in range(1, len(blocks))]


def run(schur, rhs, start, project, coarse_basis, owner_of_face, mortar_of_face, mortar_order, subdomain_map, vertex_ids):
    subs, grps = lax.axis_size("sub"), lax.axis_size("grp")
    z = Sizes(subs, grps, schur, project, coarse_basis, rhs)
    shape = jax.ShapeDtypeStruct
    matrix, target, first = schur[0], rhs[0].T, start[0].T

    trace_b = pl.pallas_call(
        functools.partial(narrow_kernel, z),
        out_shape=pltpu.VMEM((z.rhs + z.corners, z.rows), BF),
        in_specs=[HBM] * 2,
        out_specs=VMEM,
        scratch_shapes=[
            pltpu.VMEM((z.rhs, z.rows), F32),
            pltpu.VMEM((z.corners, z.rows), BF),
            pltpu.SemaphoreType.DMA((5,)),
        ],
        compiler_params=pltpu.CompilerParams(vmem_limit_bytes=16 << 20),
    )(*[pltpu.with_memory_space_constraint(a, pltpu.HBM) for a in (first, coarse_basis[0])])
    block_two = swapped(trace_b, 2)
    block_one = swapped(trace_b, 1)

    table = pl.pallas_call(
        functools.partial(table_kernel, z),
        out_shape=pltpu.SMEM((z.t_end,), jnp.int32),
        in_specs=[SMEM] * 5,
        out_specs=SMEM,
        scratch_shapes=[pltpu.SMEM((LINKS,), jnp.int32), pltpu.SMEM((z.faces + 1,), jnp.int32), pltpu.SMEM((LINKS,), jnp.int32)],
    )(owner_of_face.transpose(0, 2, 1), mortar_of_face, mortar_order, subdomain_map, vertex_ids)
    matrix, target = pl.pallas_call(
        load_kernel,
        out_shape=[pltpu.VMEM(matrix.shape, BF), pltpu.VMEM(target.shape, F32)],
        in_specs=[HBM] * 2,
        out_specs=[VMEM] * 2,
        scratch_shapes=[pltpu.SemaphoreType.DMA((2,))],
        compiler_params=pltpu.CompilerParams(vmem_limit_bytes=16 << 20),
    )(*[pltpu.with_memory_space_constraint(a, pltpu.HBM) for a in (matrix, target)])
    pair_shape = shape((z.own, MODES // 2, 2 * FPTS), BF)
    pair_own = call(join_kernel, z, pair_shape, (project[0].reshape(z.own, MODES, FPTS),))
    block_three = swapped(block_two, 1)
    blocks = [trace_b, block_one, block_two, block_three]

    width = z.wide - z.rhs
    part = shape((z.own, z.share, z.wide), BF)
    part_more = shape((z.own + z.more, z.dense, z.lanes), BF)
    link = shape((CAP, z.share, z.wide), BF)
    thin = shape((CAP, z.dense, z.lanes), BF)
    thin_more = shape((CAP + z.more, z.dense, z.lanes), BF)
    sums_shape = shape((2, z.vertices, z.wide), F32)

    *parts, resid, ext = call(
        first_kernel,
        z,
        [part] * grps + [shape((z.rows, z.rhs), F32), shape((z.own, MODES, width), BF)],
        (table, matrix, *blocks, target, pair_own, coarse_basis[0]),
        (
            pltpu.VMEM((z.rhs + z.corners, z.all_rows), BF),
            pltpu.VMEM((z.rows, z.wide), BF),
            pltpu.VMEM((z.own, MODES, z.wide), BF),
        ),
    )
    parts = exchanged(parts)
    outgoing = call(pack_kernel, z, [link] * LINKS, (table, *parts), (pltpu.VMEM((z.faces, z.share, z.wide), BF),), (False,))
    outgoing, pair_own = lax.optimization_barrier((outgoing, pair_own))
    arrived = paired(outgoing)
    pair_two = swapped(pair_own, 2)
    arrived, pair_two = lax.optimization_barrier((arrived, pair_two))
    replies = call(
        average_kernel,
        z,
        [link] * LINKS,
        (table, *arrived),
        (pltpu.VMEM((MORT_OWN + 1, z.share, z.wide), F32), pltpu.VMEM((MORT_OWN + 1, z.share, z.wide), BF)),
        (False,),
    )
    replies, pair_own, pair_two = lax.optimization_barrier((replies, pair_own, pair_two))
    answered = paired(replies)
    pair_one, pair_three = swapped(pair_own, 1), swapped(pair_two, 1)
    answered, pair_one, pair_three = lax.optimization_barrier((answered, pair_one, pair_three))
    spread = call(
        spread_first,
        z,
        shape((z.packed, z.share, z.lanes), BF),
        (table, *answered),
        (pltpu.VMEM((SLOTS, z.share, z.wide), BF),),
    )
    spread_two = swapped(spread, 2)
    shares = [spread, swapped(spread, 1), spread_two, swapped(spread_two, 1)]
    tables = call(
        unpack_kernel, z, shape((z.faces, MODES, FPTS), BF), (pair_own, pair_one, pair_two, pair_three)
    )
    *parts, earlier, hits, sums = call(
        second_kernel,
        z,
        [part_more] * grps
        + [shape((z.own, MODES, z.rhs), BF), shape((z.own, MODES, z.vertices), BF), sums_shape],
        (table, matrix, *shares, tables, resid, coarse_basis[0], ext),
        (
            pltpu.VMEM((z.faces, MODES, z.rhs), BF),
            pltpu.VMEM((z.all_rows, z.rhs), BF),
            pltpu.VMEM((z.rows, z.rhs), BF),
            pltpu.VMEM((z.own, MODES, z.rhs), F32),
            pltpu.VMEM((z.own, MODES, z.extra), BF),
        ),
    )
    if not z.near:
        sums = lax.psum(sums, ("sub", "grp"))
    parts = exchanged(parts)
    outgoing = call(
        pack_kernel, z, [thin_more] * LINKS, (table, *parts), (pltpu.VMEM((z.faces, z.dense, z.lanes), BF),), (z.near,)
    )
    arrived = paired(outgoing)
    total_shape = [shape((z.more, z.dense, z.lanes), F32)] if z.near else []
    results = call(
        average_kernel,
        z,
        [thin, thin_more, thin_more, thin, thin] + total_shape,
        (table, *arrived),
        (pltpu.VMEM((MORT_OWN + 1, z.dense, z.lanes), F32), pltpu.VMEM((MORT_OWN + 1, z.dense, z.lanes), BF)),
        (True,),
    )
    answered = paired(results[:LINKS])
    outs = call(
        spread_second,
        z,
        [shape((z.own, z.dense, z.lanes), BF)] * grps + total_shape,
        (table, *answered, *results[LINKS:]),
        (pltpu.VMEM((SLOTS, z.dense, z.lanes), BF),),
    )
    if z.near:
        sums = outs[grps]
    shares = exchanged(outs[:grps])
    result = call(
        last_kernel,
        z,
        shape((z.rhs, z.rows), F32),
        (table, *shares, pair_own, coarse_basis[0], sums, hits, earlier, first),
        (
            pltpu.VMEM((z.own, MODES, z.rhs), F32),
            pltpu.VMEM((z.vertices, z.rhs), F32),
            pltpu.VMEM((z.rows, z.rhs), F32),
        ),
    )
    return result.T[None]


def solution(mesh):
    return jax.shard_map(
        run,
        mesh=mesh,
        in_specs=(
            P("sub", "grp", None),
            P("sub", "grp", None),
            P("sub", "grp", None),
            P("sub", "grp", None),
            P("sub", None, "grp"),
            P(),
            P(),
            P(),
            P(),
            P(),
        ),
        out_specs=P("sub", "grp", None),
        check_vma=False,
    )
```

time: 114 us -> 87.8 us (0.77)
  waiting for transfers between devices: 62.4 us -> 40.8 us
  starting transfers between devices: 38.2 us -> 33.9 us
  local copies, waits for them, and re-layouts: 3.47 us -> 1.78 us
  Pallas kernels: 9.39 us -> 10.8 us
    ppermute x22 -> x16, waiting for transfers between devices: 40.3 us -> 17.9 us  [paired(): lax.ppermute(b, 'sub', p)]
    ppermute x22 -> x16, starting transfers between devices: 25.7 us -> 23 us  [paired(): lax.ppermute(b, 'sub', p)]
    ppermute x18, starting transfers between devices: 12.6 us -> 10.8 us  [swapped(): return lax.ppermute(value, 'grp', [(s, s ^ mask) for s in range(count)])]
    unnamed x9 -> x5, local copies, waits for them, and re-layouts: 2.44 us -> 0.76 us
    pallas_call x11 -> x12, Pallas kernels: 5.85 us -> 7.32 us  [the longest x11 6.22 us: call(): pl.pallas_call(functools.partial(kernel, sizes, *static), out_shape=[pltp...]
  transfers between devices with their start and end apart: 40 -> 34, of which waited for: 19 -> 17; matrix products, arithmetic and copies ran while one was open for 1% -> 1% of each run, Pallas kernels for 4% -> 4%
where the time goes in v3:
time: 87.8 us; the launch traced here: 87.5 us
  waiting for transfers between devices  40.8 us (46%)
  starting transfers between devices  33.9 us (39%)
  Pallas kernels  10.8 us (12%)
  local copies, waits for them, and re-layouts  1.78 us (2%)
    ppermute x16, starting transfers between devices, paired(): lax.ppermute(b, 'sub', p)  23 us
    ppermute x18, waiting for transfers between devices, swapped(): return lax.ppermute(value, 'grp', [(s, s ^ mask) for s in range(count)])  22.9 us
    ppermute x16, waiting for transfers between devices, paired(): lax.ppermute(b, 'sub', p)  17.9 us
    ppermute x18, starting transfers between devices, swapped(): return lax.ppermute(value, 'grp', [(s, s ^ mask) for s in range(count)])  10.8 us
    pallas_call x11, Pallas kernels, call(): pl.pallas_call(functools.partial(kernel, sizes, *static), out_shape=[pltp...  6.22 us
    pallas_call x1, Pallas kernels, run(): pl.pallas_call(functools.partial(table_kernel, z), out_shape=pltpu.SMEM((...  1.88 us
  transfers between devices with their start and end apart: 34, of which 17 were waited for; matrix products, arithmetic and copies ran while one was open for 1% of the time, Pallas kernels for 4%

profile of v3, /device:TPU:0, one launch (start us, length us, event | category | flops | bytes accessed | tf_op | source)
XLA Modules:
  0.0 87.5 jit_solution(10908670524216127170)
XLA Ops:
  0.0 1.1 %shard_map.102.b0 = bf16[200,512]{1,0:T(8,128)(2,1)S(1)} custom-call(f32[192,512]{1,0:T(8,128)} %bitcast.13, bf16[8,512]{1,0:T(8,128)(2,1)} %bitcast.15), custom_call_target="tpu_custom_call" | custom-call | tf_op jit(solution)/shard_map/pallas_call | solution.py:434
  1.1 3.0 %collective-permute-start.1 = (bf16[200,512]{1,0:T(8,128)(2,1)S(1)}, bf16[200,512]{1,0:T(8,128)(2,1)S(1)}, u32[]{:S(2)}, u32[]{:S(2)}) collective-permute-start(bf16[200,512]{1,0:T(8,128)(2,1)S(1)} %shard_map.102.b0), channel_id=1, source_target_pairs={{0,2},{1,3},{2,0},{3,1},{4,6},{5,7},{6,4},{7,5},{8,10},{9,11},{10,... | collective-permute-start | bytes 614408 | tf_op jit(solution)/shard_map/ppermute | solution.py:421
  4.1 5.1 %collective-permute-done.1.b2 = bf16[200,512]{1,0:T(8,128)(2,1)S(1)} collective-permute-done((bf16[200,512]{1,0:T(8,128)(2,1)S(1)}, bf16[200,512]{1,0:T(8,128)(2,1)S(1)}, u32[]{:S(2)}, u32[]{:S(2)}) %collective-permute-start.1) | collective-permute-done | bytes 204832 | tf_op jit(solution)/shard_map/ppermute | solution.py:421
  9.2 1.0 %reshape_squeeze.3.tables = bf16[8,64,64]{2,1,0:T(8,128)(2,1)S(1)} reshape(bf16[1,8,4096]{2,1,0:T(8,128)(2,1)} %param.13) | data formatting | bytes 131072 | tf_op jit(solution)/shard_map/reshape;squeeze | solution.py:465
  10.3 1.6 %shard_map.101 = (bf16[512,2048]{1,0:T(8,128)(2,1)S(1)}, f32[192,512]{1,0:T(8,128)S(1)}) custom-call(bf16[512,2048]{1,0:T(8,128)(2,1)} %bitcast.19, f32[192,512]{1,0:T(8,128)} %bitcast.20), custom_call_target="tpu_custom_call" | custom-call | tf_op jit(solution)/shard_map/pallas_call | solution.py:456
  12.0 1.9 %shard_map.100.table = s32[152]{0:T(256)S(4)} custom-call(s32[8,1,32]{2,1,0:T(1,128)} %bitcast.21, s32[8,32]{1,0:T(8,128)} %mortar.1, s32[8,16]{1,0:T(8,128)} %order.1, s32[8]{0:T(128)} %smap.1, s32[8,8]{1,0:T(8,128)} %vids.1), custom_call_target="tpu_custom_call" | custom-call | tf_op jit(solution)/shard_map/pallas_call | solution.py:449
  13.9 1.7 %shard_map.104 = (bf16[8,16,256]{2,1,0:T(8,128)(2,1)S(1)}, bf16[8,16,256]{2,1,0:T(8,128)(2,1)S(1)}, bf16[8,16,256]{2,1,0:T(8,128)(2,1)S(1)}, bf16[8,16,256]{2,1,...) custom-call(s32[152]{0:T(256)S(4)} %shard_map.100.table, ...), custom_call_target="tpu_custom_call" | custom-call | tf_op jit(solution)/shard_map/pallas_call | solution.py:73
  15.6 0.6 collective-permute-start.3
  16.1 1.7 %collective-permute-start.4 = (bf16[8,16,256]{2,1,0:T(8,128)(2,1)S(1)}, bf16[8,16,256]{2,1,0:T(8,128)(2,1)S(1)}, u32[]{:S(2)}, u32[]{:S(2)}) collective-permute-start(bf16[8,16,256]{2,1,0:T(8,128)(2,1)S(1)} %get-tuple-element.75), channel_id=1, source_target_pairs={{0,2},{1,3},{2,0},{3,1},{4,6},{5,7},{6,4},{7,5},{8,10},{9,11},{10,... | collective-permute-start | bytes 196616 | tf_op jit(solution)/shard_map/ppermute | solution.py:421
  17.9 2.5 %collective-permute-done.4.c2 = bf16[8,16,256]{2,1,0:T(8,128)(2,1)S(1)} collective-permute-done((bf16[8,16,256]{2,1,0:T(8,128)(2,1)S(1)}, bf16[8,16,256]{2,1,0:T(8,128)(2,1)S(1)}, u32[]{:S(2)}, u32[]{:S(2)}) %collective-permute-start.4) | collective-permute-done | bytes 65568 | tf_op jit(solution)/shard_map/ppermute | solution.py:421
  20.4 1.8 %collective-permute-done.5.c3 = bf16[8,16,256]{2,1,0:T(8,128)(2,1)S(1)} collective-permute-done((bf16[8,16,256]{2,1,0:T(8,128)(2,1)S(1)}, bf16[8,16,256]{2,1,0:T(8,128)(2,1)S(1)}, u32[]{:S(2)}, u32[]{:S(2)}) %collective-permute-start.5) | collective-permute-done | bytes 65568 | tf_op jit(solution)/shard_map/ppermute | solution.py:421
  22.3 1.6 %collective-permute-start.6 = (bf16[8,16,256]{2,1,0:T(8,128)(2,1)S(1)}, bf16[8,16,256]{2,1,0:T(8,128)(2,1)S(1)}, u32[]{:S(2)}, u32[]{:S(2)}) collective-permute-start(bf16[8,16,256]{2,1,0:T(8,128)(2,1)S(1)} %get-tuple-element.82), channel_id=1, source_target_pairs={{0,4},{4,0},{8,12},{12,8},{16,20},{20,16},{24,28},{28,24},{1,5},{5... | collective-permute-start | bytes 196616 | tf_op jit(solution)/shard_map/ppermute | solution.py:416
  23.9 1.6 %collective-permute-start.7 = (bf16[8,16,256]{2,1,0:T(8,128)(2,1)S(1)}, bf16[8,16,256]{2,1,0:T(8,128)(2,1)S(1)}, u32[]{:S(2)}, u32[]{:S(2)}) collective-permute-start(bf16[8,16,256]{2,1,0:T(8,128)(2,1)S(1)} %get-tuple-element.83), channel_id=1, source_target_pairs={{0,8},{4,12},{8,0},{12,4},{16,24},{20,28},{24,16},{28,20},{1,9},{5... | collective-permute-start | bytes 196616 | tf_op jit(solution)/shard_map/ppermute | solution.py:416
  25.5 2.5 %collective-permute-start.8 = (bf16[8,16,256]{2,1,0:T(8,128)(2,1)S(1)}, bf16[8,16,256]{2,1,0:T(8,128)(2,1)S(1)}, u32[]{:S(2)}, u32[]{:S(2)}) collective-permute-start(bf16[8,16,256]{2,1,0:T(8,128)(2,1)S(1)} %get-tuple-element.84), channel_id=1, source_target_pairs={{0,24},{4,28},{8,16},{12,20},{16,8},{20,12},{24,0},{28,4},{1,25},{... | collective-permute-start | bytes 196616 | tf_op jit(solution)/shard_map/ppermute | solution.py:416
  27.9 1.3 %collective-permute-start.9 = (bf16[8,16,256]{2,1,0:T(8,128)(2,1)S(1)}, bf16[8,16,256]{2,1,0:T(8,128)(2,1)S(1)}, u32[]{:S(2)}, u32[]{:S(2)}) collective-permute-start(bf16[8,16,256]{2,1,0:T(8,128)(2,1)S(1)} %get-tuple-element.85), channel_id=1, source_target_pairs={{0,28},{4,8},{8,4},{12,16},{16,12},{20,24},{24,20},{28,0},{1,29},{... | collective-permute-start | bytes 196616 | tf_op jit(solution)/shard_map/ppermute | solution.py:416
  29.2 0.6 collective-permute-start.10
  29.8 2.5 %collective-permute-done.8.refs_2_ = bf16[8,16,256]{2,1,0:T(8,128)(2,1)S(1)} collective-permute-done((bf16[8,16,256]{2,1,0:T(8,128)(2,1)S(1)}, bf16[8,16,256]{2,1,0:T(8,128)(2,1)S(1)}, u32[]{:S(2)}, u32[]{:S(2)}) %collective-permute-start.8) | collective-permute-done | bytes 65568 | tf_op jit(solution)/shard_map/ppermute | solution.py:416
  32.3 2.6 %collective-permute-done.9.refs_3_ = bf16[8,16,256]{2,1,0:T(8,128)(2,1)S(1)} collective-permute-done((bf16[8,16,256]{2,1,0:T(8,128)(2,1)S(1)}, bf16[8,16,256]{2,1,0:T(8,128)(2,1)S(1)}, u32[]{:S(2)}, u32[]{:S(2)}) %collective-permute-start.9) | collective-permute-done | bytes 65568 | tf_op jit(solution)/shard_map/ppermute | solution.py:416
  34.9 0.3 shard_map.106
  35.4 2.5 %collective-permute-start.13 = (bf16[8,16,256]{2,1,0:T(8,128)(2,1)S(1)}, bf16[8,16,256]{2,1,0:T(8,128)(2,1)S(1)}, u32[]{:S(2)}, u32[]{:S(2)}) collective-permute-start(bf16[8,16,256]{2,1,0:T(8,128)(2,1)S(1)} %get-tuple-element.101), channel_id=1, source_target_pairs={{0,24},{4,28},{8,16},{12,20},{16,8},{20,12},{24,0},{28,4},{1,25},{... | collective-permute-start | bytes 196616 | tf_op jit(solution)/shard_map/ppermute | solution.py:416
  37.9 2.7 %collective-permute-start.14 = (bf16[8,16,256]{2,1,0:T(8,128)(2,1)S(1)}, bf16[8,16,256]{2,1,0:T(8,128)(2,1)S(1)}, u32[]{:S(2)}, u32[]{:S(2)}) collective-permute-start(bf16[8,16,256]{2,1,0:T(8,128)(2,1)S(1)} %get-tuple-element.102), channel_id=1, source_target_pairs={{0,28},{4,8},{8,4},{12,16},{16,12},{20,24},{24,20},{28,0},{1,29},{... | collective-permute-start | bytes 196616 | tf_op jit(solution)/shard_map/ppermute | solution.py:416
  40.6 0.5 collective-permute-start.15
  41.1 0.6 collective-permute-done.13.refs_2_
  41.6 3.2 %collective-permute-done.14.refs_3_ = bf16[8,16,256]{2,1,0:T(8,128)(2,1)S(1)} collective-permute-done((bf16[8,16,256]{2,1,0:T(8,128)(2,1)S(1)}, bf16[8,16,256]{2,1,0:T(8,128)(2,1)S(1)}, u32[]{:S(2)}, u32[]{:S(2)}) %collective-permute-start.14) | collective-permute-done | bytes 65568 | tf_op jit(solution)/shard_map/ppermute | solution.py:416
  45.0 0.6 collective-permute-start.18
  45.6 5.4 %collective-permute-done.18.refs_2_ = bf16[56,16,128]{2,1,0:T(8,128)(2,1)S(1)} collective-permute-done((bf16[56,16,128]{2,1,0:T(8,128)(2,1)S(1)}, bf16[56,16,128]{2,1,0:T(8,128)(2,1)S(1)}, u32[]{:S(2)}, u32[]{:S(2)}) %collective-permute-start.18) | collective-permute-done | bytes 229408 | tf_op jit(solution)/shard_map/ppermute | solution.py:421
  51.2 1.3 %collective-permute-done.19.refs_3_ = bf16[56,16,128]{2,1,0:T(8,128)(2,1)S(1)} collective-permute-done((bf16[56,16,128]{2,1,0:T(8,128)(2,1)S(1)}, bf16[56,16,128]{2,1,0:T(8,128)(2,1)S(1)}, u32[]{:S(2)}, u32[]{:S(2)}) %collective-permute-start.19) | collective-permute-done | bytes 229408 | tf_op jit(solution)/shard_map/ppermute | solution.py:421
  52.6 2.6 %shard_map.109 = (bf16[11,24,128]{2,1,0:T(8,128)(2,1)S(1)}, bf16[11,24,128]{2,1,0:T(8,128)(2,1)S(1)}, bf16[11,24,128]{2,1,0:T(8,128)(2,1)S(1)}, bf16[11,24,128]{...) custom-call(s32[152]{0:T(256)S(4)} %shard_map.100.table, ...), custom_call_target="tpu_custom_call" | custom-call | tf_op jit(solution)/shard_map/pallas_call | solution.py:73
  55.3 0.6 collective-permute-start.21
  55.9 1.1 %collective-permute-start.22 = (bf16[11,24,128]{2,1,0:T(8,128)(2,1)S(1)}, bf16[11,24,128]{2,1,0:T(8,128)(2,1)S(1)}, u32[]{:S(2)}, u32[]{:S(2)}) collective-permute-start(bf16[11,24,128]{2,1,0:T(8,128)(2,1)S(1)} %get-tuple-element.118), channel_id=1, source_target_pairs={{0,3},{1,2},{2,1},{3,0},{4,7},{5,6},{6,5},{7,4},{8,11},{9,10},{10,... | collective-permute-start | bytes 202760 | tf_op jit(solution)/shard_map/ppermute | solution.py:421
  57.0 3.3 %collective-permute-done.21.c2 = bf16[11,24,128]{2,1,0:T(8,128)(2,1)S(1)} collective-permute-done((bf16[11,24,128]{2,1,0:T(8,128)(2,1)S(1)}, bf16[11,24,128]{2,1,0:T(8,128)(2,1)S(1)}, u32[]{:S(2)}, u32[]{:S(2)}) %collective-permute-start.21) | collective-permute-done | bytes 67616 | tf_op jit(solution)/shard_map/ppermute | solution.py:421
  60.3 0.3 collective-permute-done.22.c3
  60.8 3.2 %collective-permute-start.25 = (bf16[11,24,128]{2,1,0:T(8,128)(2,1)S(1)}, bf16[11,24,128]{2,1,0:T(8,128)(2,1)S(1)}, u32[]{:S(2)}, u32[]{:S(2)}) collective-permute-start(bf16[11,24,128]{2,1,0:T(8,128)(2,1)S(1)} %get-tuple-element.121), channel_id=1, source_target_pairs={{0,24},{4,28},{8,16},{12,20},{16,8},{20,12},{24,0},{28,4},{1,25},{... | collective-permute-start | bytes 202760 | tf_op jit(solution)/shard_map/ppermute | solution.py:416
  64.0 2.0 %collective-permute-start.26 = (bf16[11,24,128]{2,1,0:T(8,128)(2,1)S(1)}, bf16[11,24,128]{2,1,0:T(8,128)(2,1)S(1)}, u32[]{:S(2)}, u32[]{:S(2)}) collective-permute-start(bf16[11,24,128]{2,1,0:T(8,128)(2,1)S(1)} %get-tuple-element.122), channel_id=1, source_target_pairs={{0,28},{4,8},{8,4},{12,16},{16,12},{20,24},{24,20},{28,0},{1,29},{... | collective-permute-start | bytes 202760 | tf_op jit(solution)/shard_map/ppermute | solution.py:416
  66.0 2.4 %collective-permute-done.25.refs_2_ = bf16[11,24,128]{2,1,0:T(8,128)(2,1)S(1)} collective-permute-done((bf16[11,24,128]{2,1,0:T(8,128)(2,1)S(1)}, bf16[11,24,128]{2,1,0:T(8,128)(2,1)S(1)}, u32[]{:S(2)}, u32[]{:S(2)}) %collective-permute-start.25) | collective-permute-done | bytes 67616 | tf_op jit(solution)/shard_map/ppermute | solution.py:416
  68.4 2.5 %collective-permute-done.26.refs_3_ = bf16[11,24,128]{2,1,0:T(8,128)(2,1)S(1)} collective-permute-done((bf16[11,24,128]{2,1,0:T(8,128)(2,1)S(1)}, bf16[11,24,128]{2,1,0:T(8,128)(2,1)S(1)}, u32[]{:S(2)}, u32[]{:S(2)}) %collective-permute-start.26) | collective-permute-done | bytes 67616 | tf_op jit(solution)/shard_map/ppermute | solution.py:416
  70.9 0.3 shard_map.111
  71.3 1.8 %collective-permute-start.29 = (bf16[11,24,128]{2,1,0:T(8,128)(2,1)S(1)}, bf16[11,24,128]{2,1,0:T(8,128)(2,1)S(1)}, u32[]{:S(2)}, u32[]{:S(2)}) collective-permute-start(bf16[11,24,128]{2,1,0:T(8,128)(2,1)S(1)} %get-tuple-element.126), channel_id=1, source_target_pairs={{0,24},{4,28},{8,16},{12,20},{16,8},{20,12},{24,0},{28,4},{1,25},{... | collective-permute-start | bytes 202760 | tf_op jit(solution)/shard_map/ppermute | solution.py:416
  73.1 0.8 collective-permute-start.27
  74.0 2.7 %collective-permute-start.30 = (bf16[8,24,128]{2,1,0:T(8,128)(2,1)S(1)}, bf16[8,24,128]{2,1,0:T(8,128)(2,1)S(1)}, u32[]{:S(2)}, u32[]{:S(2)}) collective-permute-start(bf16[8,24,128]{2,1,0:T(8,128)(2,1)S(1)} %get-tuple-element.127), channel_id=1, source_target_pairs={{0,28},{4,8},{8,4},{12,16},{16,12},{20,24},{24,20},{28,0},{1,29},{... | collective-permute-start | bytes 147464 | tf_op jit(solution)/shard_map/ppermute | solution.py:416
  76.6 0.6 collective-permute-done.27.refs_0_
  77.2 3.5 %collective-permute-done.30.refs_3_ = bf16[8,24,128]{2,1,0:T(8,128)(2,1)S(1)} collective-permute-done((bf16[8,24,128]{2,1,0:T(8,128)(2,1)S(1)}, bf16[8,24,128]{2,1,0:T(8,128)(2,1)S(1)}, u32[]{:S(2)}, u32[]{:S(2)}) %collective-permute-start.30) | collective-permute-done | bytes 49184 | tf_op jit(solution)/shard_map/ppermute | solution.py:416
  80.9 1.0 %collective-permute-start.32 = (bf16[8,24,128]{2,1,0:T(8,128)(2,1)S(1)}, bf16[8,24,128]{2,1,0:T(8,128)(2,1)S(1)}, u32[]{:S(2)}, u32[]{:S(2)}) collective-permute-start(bf16[8,24,128]{2,1,0:T(8,128)(2,1)S(1)} %get-tuple-element.132), channel_id=1, source_target_pairs={{0,2},{1,3},{2,0},{3,1},{4,6},{5,7},{6,4},{7,5},{8,10},{9,11},{10,... | collective-permute-start | bytes 147464 | tf_op jit(solution)/shard_map/ppermute | solution.py:421
  81.9 0.9 collective-permute-start.33
  82.7 2.5 %collective-permute-done.32.refs_2_ = bf16[8,24,128]{2,1,0:T(8,128)(2,1)S(1)} collective-permute-done((bf16[8,24,128]{2,1,0:T(8,128)(2,1)S(1)}, bf16[8,24,128]{2,1,0:T(8,128)(2,1)S(1)}, u32[]{:S(2)}, u32[]{:S(2)}) %collective-permute-start.32) | collective-permute-done | bytes 49184 | tf_op jit(solution)/shard_map/ppermute | solution.py:421
  85.2 0.7 collective-permute-done.33.refs_3_
  85.9 0.9 shard_map.113
  86.8 0.7 copy.11
  (40 shorter events, 1.2 us)
Async XLA Ops:
  0.0 13.9 %copy-start.1 = (bf16[1,8,512]{2,1,0:T(8,128)(2,1)S(1)}, bf16[1,8,512]{2,1,0:T(8,128)(2,1)}, u32[]{:S(2)}) copy-start(bf16[1,8,512]{2,1,0:T(8,128)(2,1)} %param.14) | copy-start | bytes 24580
  1.1 8.1 %collective-permute-start.1 = (bf16[200,512]{1,0:T(8,128)(2,1)S(1)}, bf16[200,512]{1,0:T(8,128)(2,1)S(1)}, u32[]{:S(2)}, u32[]{:S(2)}) collective-permute-start(bf16[200,512]{1,0:T(8,128)(2,1)S(1)} %shard_map.102.b0), channel_id=1, source_target_pairs={{0,2},{1,3},{2,0},{3,1},{4,6},{5,7},{6,4},{7,5},{8,10},{9,11},{10,... | collective-permute-start | bytes 614408 | tf_op jit(solution)/shard_map/ppermute | solution.py:421
  4.1 9.8 %collective-permute-start = (bf16[200,512]{1,0:T(8,128)(2,1)S(1)}, bf16[200,512]{1,0:T(8,128)(2,1)S(1)}, u32[]{:S(2)}, u32[]{:S(2)}) collective-permute-start(bf16[200,512]{1,0:T(8,128)(2,1)S(1)} %shard_map.102.b0), channel_id=1, source_target_pairs={{0,1},{1,0},{2,3},{3,2},{4,5},{5,4},{6,7},{7,6},{8,9},{9,8},{10,11... | collective-permute-start | bytes 614408 | tf_op jit(solution)/shard_map/ppermute | solution.py:421
  9.2 4.7 %collective-permute-start.2 = (bf16[200,512]{1,0:T(8,128)(2,1)S(1)}, bf16[200,512]{1,0:T(8,128)(2,1)S(1)}, u32[]{:S(2)}, u32[]{:S(2)}) collective-permute-start(bf16[200,512]{1,0:T(8,128)(2,1)S(1)} %collective-permute-done.1.b2), channel_id=1, source_target_pairs={{0,1},{1,0},{2,3},{3,2},{4,5},{5,4},{6,7},{7,6},{8,9},{9,8},{10,11... | collective-permute-start | bytes 614408 | tf_op jit(solution)/shard_map/ppermute | solution.py:421
  15.6 2.3 %collective-permute-start.3 = (bf16[8,16,256]{2,1,0:T(8,128)(2,1)S(1)}, bf16[8,16,256]{2,1,0:T(8,128)(2,1)S(1)}, u32[]{:S(2)}, u32[]{:S(2)}) collective-permute-start(bf16[8,16,256]{2,1,0:T(8,128)(2,1)S(1)} %get-tuple-element.74), channel_id=1, source_target_pairs={{0,1},{1,0},{2,3},{3,2},{4,5},{5,4},{6,7},{7,6},{8,9},{9,8},{10,11... | collective-permute-start | bytes 196616 | tf_op jit(solution)/shard_map/ppermute | solution.py:421
  16.1 4.3 %collective-permute-start.4 = (bf16[8,16,256]{2,1,0:T(8,128)(2,1)S(1)}, bf16[8,16,256]{2,1,0:T(8,128)(2,1)S(1)}, u32[]{:S(2)}, u32[]{:S(2)}) collective-permute-start(bf16[8,16,256]{2,1,0:T(8,128)(2,1)S(1)} %get-tuple-element.75), channel_id=1, source_target_pairs={{0,2},{1,3},{2,0},{3,1},{4,6},{5,7},{6,4},{7,5},{8,10},{9,11},{10,... | collective-permute-start | bytes 196616 | tf_op jit(solution)/shard_map/ppermute | solution.py:421
  17.9 4.4 %collective-permute-start.5 = (bf16[8,16,256]{2,1,0:T(8,128)(2,1)S(1)}, bf16[8,16,256]{2,1,0:T(8,128)(2,1)S(1)}, u32[]{:S(2)}, u32[]{:S(2)}) collective-permute-start(bf16[8,16,256]{2,1,0:T(8,128)(2,1)S(1)} %get-tuple-element.76), channel_id=1, source_target_pairs={{0,3},{1,2},{2,1},{3,0},{4,7},{5,6},{6,5},{7,4},{8,11},{9,10},{10,... | collective-permute-start | bytes 196616 | tf_op jit(solution)/shard_map/ppermute | solution.py:421
  22.3 7.5 %collective-permute-start.6 = (bf16[8,16,256]{2,1,0:T(8,128)(2,1)S(1)}, bf16[8,16,256]{2,1,0:T(8,128)(2,1)S(1)}, u32[]{:S(2)}, u32[]{:S(2)}) collective-permute-start(bf16[8,16,256]{2,1,0:T(8,128)(2,1)S(1)} %get-tuple-element.82), channel_id=1, source_target_pairs={{0,4},{4,0},{8,12},{12,8},{16,20},{20,16},{24,28},{28,24},{1,5},{5... | collective-permute-start | bytes 196616 | tf_op jit(solution)/shard_map/ppermute | solution.py:416
  23.9 5.9 %collective-permute-start.7 = (bf16[8,16,256]{2,1,0:T(8,128)(2,1)S(1)}, bf16[8,16,256]{2,1,0:T(8,128)(2,1)S(1)}, u32[]{:S(2)}, u32[]{:S(2)}) collective-permute-start(bf16[8,16,256]{2,1,0:T(8,128)(2,1)S(1)} %get-tuple-element.83), channel_id=1, source_target_pairs={{0,8},{4,12},{8,0},{12,4},{16,24},{20,28},{24,16},{28,20},{1,9},{5... | collective-permute-start | bytes 196616 | tf_op jit(solution)/shard_map/ppermute | solution.py:416
  25.5 6.8 %collective-permute-start.8 = (bf16[8,16,256]{2,1,0:T(8,128)(2,1)S(1)}, bf16[8,16,256]{2,1,0:T(8,128)(2,1)S(1)}, u32[]{:S(2)}, u32[]{:S(2)}) collective-permute-start(bf16[8,16,256]{2,1,0:T(8,128)(2,1)S(1)} %get-tuple-element.84), channel_id=1, source_target_pairs={{0,24},{4,28},{8,16},{12,20},{16,8},{20,12},{24,0},{28,4},{1,25},{... | collective-permute-start | bytes 196616 | tf_op jit(solution)/shard_map/ppermute | solution.py:416
  27.9 7.0 %collective-permute-start.9 = (bf16[8,16,256]{2,1,0:T(8,128)(2,1)S(1)}, bf16[8,16,256]{2,1,0:T(8,128)(2,1)S(1)}, u32[]{:S(2)}, u32[]{:S(2)}) collective-permute-start(bf16[8,16,256]{2,1,0:T(8,128)(2,1)S(1)} %get-tuple-element.85), channel_id=1, source_target_pairs={{0,28},{4,8},{8,4},{12,16},{16,12},{20,24},{24,20},{28,0},{1,29},{... | collective-permute-start | bytes 196616 | tf_op jit(solution)/shard_map/ppermute | solution.py:416
  29.2 5.7 %collective-permute-start.10 = (bf16[8,32,128]{2,1,0:T(8,128)(2,1)S(1)}, bf16[8,32,128]{2,1,0:T(8,128)(2,1)S(1)}, u32[]{:S(2)}, u32[]{:S(2)}) collective-permute-start(bf16[8,32,128]{2,1,0:T(8,128)(2,1)S(1)} %shard_map.103.tables.p0.refs_4_), channel_id=1, source_target_pairs={{0,2},{1,3},{2,0},{3,1},{4,6},{5,7},{6,4},{7,5},{8,10},{9,11},{10,... | collective-permute-start | bytes 196616 | tf_op jit(solution)/shard_map/ppermute | solution.py:421
  35.2 5.4 %collective-permute-start.11 = (bf16[8,16,256]{2,1,0:T(8,128)(2,1)S(1)}, bf16[8,16,256]{2,1,0:T(8,128)(2,1)S(1)}, u32[]{:S(2)}, u32[]{:S(2)}) collective-permute-start(bf16[8,16,256]{2,1,0:T(8,128)(2,1)S(1)} %get-tuple-element.99), channel_id=1, source_target_pairs={{0,4},{4,0},{8,12},{12,8},{16,20},{20,16},{24,28},{28,24},{1,5},{5... | collective-permute-start | bytes 196616 | tf_op jit(solution)/shard_map/ppermute | solution.py:416
  35.3 5.8 %collective-permute-start.12 = (bf16[8,16,256]{2,1,0:T(8,128)(2,1)S(1)}, bf16[8,16,256]{2,1,0:T(8,128)(2,1)S(1)}, u32[]{:S(2)}, u32[]{:S(2)}) collective-permute-start(bf16[8,16,256]{2,1,0:T(8,128)(2,1)S(1)} %get-tuple-element.100), channel_id=1, source_target_pairs={{0,8},{4,12},{8,0},{12,4},{16,24},{20,28},{24,16},{28,20},{1,9},{5... | collective-permute-start | bytes 196616 | tf_op jit(solution)/shard_map/ppermute | solution.py:416
  35.4 6.3 %collective-permute-start.13 = (bf16[8,16,256]{2,1,0:T(8,128)(2,1)S(1)}, bf16[8,16,256]{2,1,0:T(8,128)(2,1)S(1)}, u32[]{:S(2)}, u32[]{:S(2)}) collective-permute-start(bf16[8,16,256]{2,1,0:T(8,128)(2,1)S(1)} %get-tuple-element.101), channel_id=1, source_target_pairs={{0,24},{4,28},{8,16},{12,20},{16,8},{20,12},{24,0},{28,4},{1,25},{... | collective-permute-start | bytes 196616 | tf_op jit(solution)/shard_map/ppermute | solution.py:416
  37.9 7.0 %collective-permute-start.14 = (bf16[8,16,256]{2,1,0:T(8,128)(2,1)S(1)}, bf16[8,16,256]{2,1,0:T(8,128)(2,1)S(1)}, u32[]{:S(2)}, u32[]{:S(2)}) collective-permute-start(bf16[8,16,256]{2,1,0:T(8,128)(2,1)S(1)} %get-tuple-element.102), channel_id=1, source_target_pairs={{0,28},{4,8},{8,4},{12,16},{16,12},{20,24},{24,20},{28,0},{1,29},{... | collective-permute-start | bytes 196616 | tf_op jit(solution)/shard_map/ppermute | solution.py:416
  40.6 4.3 %collective-permute-start.16 = (bf16[8,32,128]{2,1,0:T(8,128)(2,1)S(1)}, bf16[8,32,128]{2,1,0:T(8,128)(2,1)S(1)}, u32[]{:S(2)}, u32[]{:S(2)}) collective-permute-start(bf16[8,32,128]{2,1,0:T(8,128)(2,1)S(1)} %collective-permute-done.10.p2), channel_id=1, source_target_pairs={{0,1},{1,0},{2,3},{3,2},{4,5},{5,4},{6,7},{7,6},{8,9},{9,8},{10,11... | collective-permute-start | bytes 196616 | tf_op jit(solution)/shard_map/ppermute | solution.py:421
  40.6 4.3 %collective-permute-start.15 = (bf16[8,32,128]{2,1,0:T(8,128)(2,1)S(1)}, bf16[8,32,128]{2,1,0:T(8,128)(2,1)S(1)}, u32[]{:S(2)}, u32[]{:S(2)}) collective-permute-start(bf16[8,32,128]{2,1,0:T(8,128)(2,1)S(1)} %shard_map.103.tables.p0.refs_4_), channel_id=1, source_target_pairs={{0,1},{1,0},{2,3},{3,2},{4,5},{5,4},{6,7},{7,6},{8,9},{9,8},{10,11... | collective-permute-start | bytes 196616 | tf_op jit(solution)/shard_map/ppermute | solution.py:421
  45.0 6.1 %collective-permute-start.18 = (bf16[56,16,128]{2,1,0:T(8,128)(2,1)S(1)}, bf16[56,16,128]{2,1,0:T(8,128)(2,1)S(1)}, u32[]{:S(2)}, u32[]{:S(2)}) collective-permute-start(bf16[56,16,128]{2,1,0:T(8,128)(2,1)S(1)} %shard_map.107.refs_0_), channel_id=1, source_target_pairs={{0,2},{1,3},{2,0},{3,1},{4,6},{5,7},{6,4},{7,5},{8,10},{9,11},{10,... | collective-permute-start | bytes 688136 | tf_op jit(solution)/shard_map/ppermute | solution.py:421
  45.6 5.6 %collective-permute-start.17 = (bf16[56,16,128]{2,1,0:T(8,128)(2,1)S(1)}, bf16[56,16,128]{2,1,0:T(8,128)(2,1)S(1)}, u32[]{:S(2)}, u32[]{:S(2)}) collective-permute-start(bf16[56,16,128]{2,1,0:T(8,128)(2,1)S(1)} %shard_map.107.refs_0_), channel_id=1, source_target_pairs={{0,1},{1,0},{2,3},{3,2},{4,5},{5,4},{6,7},{7,6},{8,9},{9,8},{10,11... | collective-permute-start | bytes 688136 | tf_op jit(solution)/shard_map/ppermute | solution.py:421
  51.1 1.5 %collective-permute-start.19 = (bf16[56,16,128]{2,1,0:T(8,128)(2,1)S(1)}, bf16[56,16,128]{2,1,0:T(8,128)(2,1)S(1)}, u32[]{:S(2)}, u32[]{:S(2)}) collective-permute-start(bf16[56,16,128]{2,1,0:T(8,128)(2,1)S(1)} %collective-permute-done.18.refs_2_), channel_id=1, source_target_pairs={{0,1},{1,0},{2,3},{3,2},{4,5},{5,4},{6,7},{7,6},{8,9},{9,8},{10,11... | collective-permute-start | bytes 688136 | tf_op jit(solution)/shard_map/ppermute | solution.py:421
  52.6 33.4 %copy-start = (f32[1,512,192]{1,2,0:T(8,128)S(1)}, f32[1,512,192]{1,2,0:T(8,128)}, u32[]{:S(2)}) copy-start(f32[1,512,192]{1,2,0:T(8,128)} %param.12) | copy-start | bytes 1179652
  55.2 1.9 %collective-permute-start.20 = (bf16[11,24,128]{2,1,0:T(8,128)(2,1)S(1)}, bf16[11,24,128]{2,1,0:T(8,128)(2,1)S(1)}, u32[]{:S(2)}, u32[]{:S(2)}) collective-permute-start(bf16[11,24,128]{2,1,0:T(8,128)(2,1)S(1)} %get-tuple-element.116), channel_id=1, source_target_pairs={{0,1},{1,0},{2,3},{3,2},{4,5},{5,4},{6,7},{7,6},{8,9},{9,8},{10,11... | collective-permute-start | bytes 202760 | tf_op jit(solution)/shard_map/ppermute | solution.py:421
  55.3 5.0 %collective-permute-start.21 = (bf16[11,24,128]{2,1,0:T(8,128)(2,1)S(1)}, bf16[11,24,128]{2,1,0:T(8,128)(2,1)S(1)}, u32[]{:S(2)}, u32[]{:S(2)}) collective-permute-start(bf16[11,24,128]{2,1,0:T(8,128)(2,1)S(1)} %get-tuple-element.117), channel_id=1, source_target_pairs={{0,2},{1,3},{2,0},{3,1},{4,6},{5,7},{6,4},{7,5},{8,10},{9,11},{10,... | collective-permute-start | bytes 202760 | tf_op jit(solution)/shard_map/ppermute | solution.py:421
  55.9 4.7 %collective-permute-start.22 = (bf16[11,24,128]{2,1,0:T(8,128)(2,1)S(1)}, bf16[11,24,128]{2,1,0:T(8,128)(2,1)S(1)}, u32[]{:S(2)}, u32[]{:S(2)}) collective-permute-start(bf16[11,24,128]{2,1,0:T(8,128)(2,1)S(1)} %get-tuple-element.118), channel_id=1, source_target_pairs={{0,3},{1,2},{2,1},{3,0},{4,7},{5,6},{6,5},{7,4},{8,11},{9,10},{10,... | collective-permute-start | bytes 202760 | tf_op jit(solution)/shard_map/ppermute | solution.py:421
  60.6 5.4 %collective-permute-start.23 = (bf16[11,24,128]{2,1,0:T(8,128)(2,1)S(1)}, bf16[11,24,128]{2,1,0:T(8,128)(2,1)S(1)}, u32[]{:S(2)}, u32[]{:S(2)}) collective-permute-start(bf16[11,24,128]{2,1,0:T(8,128)(2,1)S(1)} %get-tuple-element.119), channel_id=1, source_target_pairs={{0,4},{4,0},{8,12},{12,8},{16,20},{20,16},{24,28},{28,24},{1,5},{5... | collective-permute-start | bytes 202760 | tf_op jit(solution)/shard_map/ppermute | solution.py:416
  60.7 5.3 %collective-permute-start.24 = (bf16[11,24,128]{2,1,0:T(8,128)(2,1)S(1)}, bf16[11,24,128]{2,1,0:T(8,128)(2,1)S(1)}, u32[]{:S(2)}, u32[]{:S(2)}) collective-permute-start(bf16[11,24,128]{2,1,0:T(8,128)(2,1)S(1)} %get-tuple-element.120), channel_id=1, source_target_pairs={{0,8},{4,12},{8,0},{12,4},{16,24},{20,28},{24,16},{28,20},{1,9},{5... | collective-permute-start | bytes 202760 | tf_op jit(solution)/shard_map/ppermute | solution.py:416
  60.8 7.6 %collective-permute-start.25 = (bf16[11,24,128]{2,1,0:T(8,128)(2,1)S(1)}, bf16[11,24,128]{2,1,0:T(8,128)(2,1)S(1)}, u32[]{:S(2)}, u32[]{:S(2)}) collective-permute-start(bf16[11,24,128]{2,1,0:T(8,128)(2,1)S(1)} %get-tuple-element.121), channel_id=1, source_target_pairs={{0,24},{4,28},{8,16},{12,20},{16,8},{20,12},{24,0},{28,4},{1,25},{... | collective-permute-start | bytes 202760 | tf_op jit(solution)/shard_map/ppermute | solution.py:416
  64.0 7.0 %collective-permute-start.26 = (bf16[11,24,128]{2,1,0:T(8,128)(2,1)S(1)}, bf16[11,24,128]{2,1,0:T(8,128)(2,1)S(1)}, u32[]{:S(2)}, u32[]{:S(2)}) collective-permute-start(bf16[11,24,128]{2,1,0:T(8,128)(2,1)S(1)} %get-tuple-element.122), channel_id=1, source_target_pairs={{0,28},{4,8},{8,4},{12,16},{16,12},{20,24},{24,20},{28,0},{1,29},{... | collective-permute-start | bytes 202760 | tf_op jit(solution)/shard_map/ppermute | solution.py:416
  71.2 9.5 %collective-permute-start.28 = (bf16[11,24,128]{2,1,0:T(8,128)(2,1)S(1)}, bf16[11,24,128]{2,1,0:T(8,128)(2,1)S(1)}, u32[]{:S(2)}, u32[]{:S(2)}) collective-permute-start(bf16[11,24,128]{2,1,0:T(8,128)(2,1)S(1)} %get-tuple-element.125), channel_id=1, source_target_pairs={{0,8},{4,12},{8,0},{12,4},{16,24},{20,28},{24,16},{28,20},{1,9},{5... | collective-permute-start | bytes 202760 | tf_op jit(solution)/shard_map/ppermute | solution.py:416
  71.3 9.5 %collective-permute-start.29 = (bf16[11,24,128]{2,1,0:T(8,128)(2,1)S(1)}, bf16[11,24,128]{2,1,0:T(8,128)(2,1)S(1)}, u32[]{:S(2)}, u32[]{:S(2)}) collective-permute-start(bf16[11,24,128]{2,1,0:T(8,128)(2,1)S(1)} %get-tuple-element.126), channel_id=1, source_target_pairs={{0,24},{4,28},{8,16},{12,20},{16,8},{20,12},{24,0},{28,4},{1,25},{... | collective-permute-start | bytes 202760 | tf_op jit(solution)/shard_map/ppermute | solution.py:416
  73.1 4.1 %collective-permute-start.27 = (bf16[8,24,128]{2,1,0:T(8,128)(2,1)S(1)}, bf16[8,24,128]{2,1,0:T(8,128)(2,1)S(1)}, u32[]{:S(2)}, u32[]{:S(2)}) collective-permute-start(bf16[8,24,128]{2,1,0:T(8,128)(2,1)S(1)} %get-tuple-element.124), channel_id=1, source_target_pairs={{0,4},{4,0},{8,12},{12,8},{16,20},{20,16},{24,28},{28,24},{1,5},{5... | collective-permute-start | bytes 147464 | tf_op jit(solution)/shard_map/ppermute | solution.py:416
  74.0 6.8 %collective-permute-start.30 = (bf16[8,24,128]{2,1,0:T(8,128)(2,1)S(1)}, bf16[8,24,128]{2,1,0:T(8,128)(2,1)S(1)}, u32[]{:S(2)}, u32[]{:S(2)}) collective-permute-start(bf16[8,24,128]{2,1,0:T(8,128)(2,1)S(1)} %get-tuple-element.127), channel_id=1, source_target_pairs={{0,28},{4,8},{8,4},{12,16},{16,12},{20,24},{24,20},{28,0},{1,29},{... | collective-permute-start | bytes 147464 | tf_op jit(solution)/shard_map/ppermute | solution.py:416
  80.8 1.9 %collective-permute-start.31 = (bf16[8,24,128]{2,1,0:T(8,128)(2,1)S(1)}, bf16[8,24,128]{2,1,0:T(8,128)(2,1)S(1)}, u32[]{:S(2)}, u32[]{:S(2)}) collective-permute-start(bf16[8,24,128]{2,1,0:T(8,128)(2,1)S(1)} %get-tuple-element.131), channel_id=1, source_target_pairs={{0,1},{1,0},{2,3},{3,2},{4,5},{5,4},{6,7},{7,6},{8,9},{9,8},{10,11... | collective-permute-start | bytes 147464 | tf_op jit(solution)/shard_map/ppermute | solution.py:421
  80.9 4.3 %collective-permute-start.32 = (bf16[8,24,128]{2,1,0:T(8,128)(2,1)S(1)}, bf16[8,24,128]{2,1,0:T(8,128)(2,1)S(1)}, u32[]{:S(2)}, u32[]{:S(2)}) collective-permute-start(bf16[8,24,128]{2,1,0:T(8,128)(2,1)S(1)} %get-tuple-element.132), channel_id=1, source_target_pairs={{0,2},{1,3},{2,0},{3,1},{4,6},{5,7},{6,4},{7,5},{8,10},{9,11},{10,... | collective-permute-start | bytes 147464 | tf_op jit(solution)/shard_map/ppermute | solution.py:421
  81.9 4.0 %collective-permute-start.33 = (bf16[8,24,128]{2,1,0:T(8,128)(2,1)S(1)}, bf16[8,24,128]{2,1,0:T(8,128)(2,1)S(1)}, u32[]{:S(2)}, u32[]{:S(2)}) collective-permute-start(bf16[8,24,128]{2,1,0:T(8,128)(2,1)S(1)} %get-tuple-element.133), channel_id=1, source_target_pairs={{0,3},{1,2},{2,1},{3,0},{4,7},{5,6},{6,5},{7,4},{8,11},{9,10},{10,... | collective-permute-start | bytes 147464 | tf_op jit(solution)/shard_map/ppermute | solution.py:421

commit v4 on v3

--- a/solution.py
+++ b/solution.py
@@ -47,8 +47,8 @@
         self.lanes = self.rhs // 128 * 128
         self.tail = self.rhs - self.lanes
         self.missing = range(REACH + 1, subs - REACH)
-        self.near = self.vertices == self.share and LINKS <= subs and len(self.missing) <= 3
-        self.more = 3 if self.near else 0
+        self.near = self.vertices == self.share and LINKS <= subs and len(self.missing) <= 3 <= grps
+        self.more = 1 if self.near else 0
         self.dense = self.share * self.rhs // self.lanes
         self.pieces = max(1, 128 // self.extra)
         self.slabs = max(1, self.extra // 128)
@@ -141,31 +141,58 @@
     out[z.rhs :, :] = basis[...]
 
 
-def unpack_kernel(z, p0, p1, p2, p3, out):
-    for j, p in enumerate((p0, p1, p2, p3)):
-        for i in range(z.own):
-            out[j * z.own + i] = tables_of(p[i])
-
-
-def load_kernel(schur, rhs, schur_out, rhs_out, sems):
-    copies = [
-        pltpu.make_async_copy(schur, schur_out, sems.at[0]),
-        pltpu.make_async_copy(rhs, rhs_out, sems.at[1]),
-    ]
+def mode_at(place):
+    half = MODES // 2
+    return jnp.where(place < half, 2 * place, 2 * (place - half) + 1)
+
+
+def unpacked(z, raw, rows):
+    half = MODES // 2
+    value = raw[...].astype(F32)
+    for i in range(half):
+        rows[pl.ds(i, z.own, stride=half), :] = value[:, i * 2 * FPTS : (i + 1) * 2 * FPTS]
+    tables = []
+    for f in range(z.own):
+        pair = rows[f * half : (f + 1) * half, :]
+        tables.append(jnp.concatenate([pair[:, :FPTS], pair[:, FPTS:]], axis=0).astype(BF))
+    return tables
+
+
+def load_kernel(z, schur, rhs, coarse, project, schur_out, rhs_out, coarse_out, tables, raw, rows, sems):
+    pairs = ((project, raw), (rhs, rhs_out), (coarse, coarse_out), (schur, schur_out))
+    copies = [pltpu.make_async_copy(a, b, sems.at[i]) for i, (a, b) in enumerate(pairs)]
     for c in copies:
         c.start()
-    for c in copies:
+    copies[0].wait()
+    for f, value in enumerate(unpacked(z, raw, rows)):
+        tables[f] = value
+    for c in copies[1:]:
         c.wait()
 
 
-def join_kernel(z, tables, out):
-    half = MODES // 2
-    for f in range(z.own):
-        out[f] = jnp.concatenate([tables[f, :half, :], tables[f, half:, :]], axis=1)
-
-
-def tables_of(pair):
-    return jnp.concatenate([pair[:, :FPTS], pair[:, FPTS:]], axis=0)
+def two_blocks(one, two):
+    blank = jnp.zeros_like(one)
+    return jnp.concatenate(
+        [jnp.concatenate([one, blank], axis=1), jnp.concatenate([blank, two], axis=1)], axis=0
+    )
+
+
+def mix_kernel(z, schur, t0, r1, r2, r3, out, middle, rows):
+    g = lax.axis_index("grp")
+    width = 2 * FPTS
+    for j, r in enumerate((None, r1, r2, r3)):
+        t = unpacked(z, r, rows) if j else t0
+        for i in range(0, z.own, 2):
+            at = pl.ds(pl.multiple_of(((g ^ j) * z.own + i) * FPTS, width), width)
+            pair = two_blocks(t[i], t[i + 1])
+            middle[:, at] = lax.dot_general(
+                schur[:, at], pair, CONTRACT_LAST, preferred_element_type=F32
+            ).astype(BF)
+    for i in range(0, z.own, 2):
+        two = slice(i * MODES, (i + 2) * MODES)
+        out[two, :] = jnp.dot(
+            two_blocks(t0[i], t0[i + 1]), middle[two, :], preferred_element_type=F32
+        ).astype(BF)
 
 
 def share_rows(z, member):
@@ -178,13 +205,12 @@
     return jnp.concatenate(rows, axis=0).astype(BF)
 
 
-def first_kernel(z, table, schur, b0, b1, b2, b3, rhs, tables, coarse, o0, o1, o2, o3, res_out, ext_out, gathered, held, coeffs):
+def first_kernel(z, table, schur, b0, b1, b2, b3, rhs, tables, coarse, o0, o1, o2, o3, wide_out, ext_out, gathered, held, coeffs):
     g = lax.axis_index("grp")
     for j, b in enumerate((b0, b1, b2, b3)):
         gathered[:, pl.ds(pl.multiple_of((g ^ j) * z.rows, z.rows), z.rows)] = b[...]
     product = lax.dot_general(schur[...], gathered[...], CONTRACT_LAST, preferred_element_type=F32)
     residual = product[:, : z.rhs] - rhs[...].T
-    res_out[...] = residual
     held[:, : z.rhs] = residual.astype(BF)
     width = z.wide - z.rhs
     basis = lax.dot_general(coarse[...], hot_rows(z, table, width, 0), CONTRACT_FIRST, preferred_element_type=F32)
@@ -193,7 +219,9 @@
     )
     held[:, z.rhs :] = (basis + image).astype(BF)
     for f in range(z.own):
-        coeffs[f] = jnp.dot(tables_of(tables[f]), held[f * FPTS : (f + 1) * FPTS, :], preferred_element_type=F32).astype(BF)
+        value = jnp.dot(tables[f], held[f * FPTS : (f + 1) * FPTS, :], preferred_element_type=F32)
+        wide_out[f * MODES : (f + 1) * MODES, :] = value[:, : z.rhs]
+        coeffs[f] = value.astype(BF)
     ext_out[...] = coeffs[:, :, z.rhs :]
     for j, o in enumerate((o0, o1, o2, o3)):
         for f in range(z.own):
@@ -229,7 +257,7 @@
         column = lax.broadcasted_iota(jnp.int32, shape, 1)
         half = z.share // 2
         row = jnp.where(row < z.share, row, row - z.share + jnp.where(column < z.tail, 0, half))
-    mode = g * z.share + row
+    mode = mode_at(g * z.share + row)
     degree = jnp.maximum(mode // DEG, mode % DEG)
     for k in range(MORT_OWN):
         divisor = jnp.maximum(table[z.t_count + k], 1).astype(F32)
@@ -290,7 +318,9 @@
         for i in range(z.own):
             o[i] = data[table[z.t_slot + (g ^ j) * z.own + i]]
     if z.near:
-        refs[n + z.grps][...] = near[0][...] + blocks[1][CAP:].astype(F32) + blocks[2][CAP:].astype(F32)
+        value = (near[0][...] + blocks[1][CAP:].astype(F32) + blocks[2][CAP:].astype(F32)).astype(BF)
+        for o in outs:
+            o[z.own :] = value
 
 
 def to_dense(z, value):
@@ -305,103 +335,105 @@
     return jnp.concatenate([value[: z.share], tail], axis=1)
 
 
-def second_kernel(z, table, schur, *refs):
+def second_kernel(z, table, mixed, *refs):
     n = z.grps
     shares, refs = refs[:n], refs[n:]
-    tables, resid, coarse, ext_in, refs = refs[0], refs[1], refs[2], refs[3], refs[4:]
+    earlier, ext_in, refs = refs[0], refs[1], refs[2:]
     outs, refs = refs[:n], refs[n:]
-    own_out, hits_out, sums_out, averages, gathered, held, coeffs, scales = refs
+    own_out, hits_out, sums_out, averages, coeffs, scales = refs
     g = lax.axis_index("grp")
     half = z.own // 2
-    for j in range(n):
-        member = g ^ j
-        for i in range(z.own):
-            f = member * z.own + i
-            slot = j * z.own + i
-            for jj, a in enumerate(shares):
-                rows = share_rows(z, g ^ jj)
-                averages[slot, rows, : z.lanes] = a[f]
-                low = (i // half) * z.tail
-                averages[slot, rows, z.lanes :] = a[z.faces + member * half + i % half, :, low : low + z.tail]
-            lifted = lax.dot_general(tables[slot], averages[slot], CONTRACT_FIRST, preferred_element_type=F32)
-            gathered[pl.ds(pl.multiple_of(f * FPTS, FPTS), FPTS), :] = lifted.astype(BF)
-    product = jnp.dot(schur[...], gathered[...], preferred_element_type=F32)
-    held[...] = (resid[...] - 0.5 * product).astype(BF)
-    for f in range(z.own):
-        coeffs[f] = jnp.dot(tables[f], held[f * FPTS : (f + 1) * FPTS, :], preferred_element_type=F32)
+    for f in range(z.faces):
+        member, i = f // z.own, f % z.own
+        for jj, a in enumerate(shares):
+            rows = pl.ds(pl.multiple_of(f * MODES + (g ^ jj) * z.share, z.share), z.share)
+            averages[rows, : z.lanes] = a[f]
+            low = (i // half) * z.tail
+            averages[rows, z.lanes :] = a[z.faces + member * half + i % half, :, low : low + z.tail]
+    coeffs[...] = earlier[...] - 0.5 * jnp.dot(mixed[...], averages[...], preferred_element_type=F32)
     for j, o in enumerate(outs):
         for f in range(z.own):
-            o[f] = to_dense(z, coeffs[f, share_rows(z, g ^ j), :]).astype(BF)
-    own_out[...] = averages[: z.own]
+            rows = pl.ds(pl.multiple_of(f * MODES + (g ^ j) * z.share, z.share), z.share)
+            o[f] = to_dense(z, coeffs[rows, :]).astype(BF)
+    own = averages[pl.ds(pl.multiple_of(g * z.rows, z.rows), z.rows), :]
+    own_out[...] = own
     for i in range(z.own):
         for jj, a in enumerate(shares):
-            rows = share_rows(z, g ^ jj)
+            rows = pl.ds(pl.multiple_of(i * MODES + (g ^ jj) * z.share, z.share), z.share)
             if z.pieces > 1:
                 low = (i % z.pieces) * z.extra
-                scales[i, rows, :] = a[z.head + (g * z.own + i) // z.pieces, :, low : low + z.extra]
+                scales[rows, :] = a[z.head + (g * z.own + i) // z.pieces, :, low : low + z.extra]
             else:
                 for p in range(z.slabs):
-                    scales[i, rows, p * 128 : (p + 1) * 128] = a[z.head + (g * z.own + i) * z.slabs + p]
-    hits_out[...] = scales[:, :, z.vertices :]
-    own_points = gathered[pl.ds(pl.multiple_of(g * z.rows, z.rows), z.rows), :]
-    corner = jnp.dot(coarse[...], own_points, preferred_element_type=F32)
-    sums_out[...] = jnp.zeros_like(sums_out)
-    for i in range(z.corners):
-        sums_out[0, pl.ds(table[z.t_corner + i], 1), : z.rhs] = corner[i : i + 1, :]
-    flat = scales[:, :, : z.vertices].reshape(z.own * MODES, z.vertices)
-    image = ext_in[:, :, z.vertices : z.extra].reshape(z.own * MODES, z.vertices)
-    sums_out[0, :, z.rhs : z.rhs + z.vertices] = -0.5 * lax.dot_general(
-        flat, image, CONTRACT_FIRST, preferred_element_type=F32
-    )
-    sums_out[1, :, : z.rhs] = lax.dot_general(
-        flat, coeffs[...].astype(BF).reshape(z.own * MODES, z.rhs), CONTRACT_FIRST, preferred_element_type=F32
-    )
+                    scales[rows, p * 128 : (p + 1) * 128] = a[z.head + (g * z.own + i) * z.slabs + p]
+    hits_out[...] = scales[:, z.vertices :]
+    flat = scales[:, : z.vertices]
+    ext = ext_in[...].reshape(z.own * MODES, z.wide - z.rhs)
+    one = lax.dot_general(ext[:, : z.vertices], own, CONTRACT_FIRST, preferred_element_type=F32)
+    two = lax.dot_general(flat, coeffs[...].astype(BF), CONTRACT_FIRST, preferred_element_type=F32)
+    between = lax.dot_general(flat, ext[:, z.vertices : z.extra], CONTRACT_FIRST, preferred_element_type=F32)
+    between = -0.5 * between
     if z.near:
-        one = to_dense(z, sums_out[0, :, : z.rhs]).astype(BF)
-        two = to_dense(z, sums_out[1, :, : z.rhs]).astype(BF)
         blank = jnp.zeros((z.share, z.rhs - z.vertices), F32)
-        between = jnp.concatenate([sums_out[0, :, z.rhs : z.rhs + z.vertices], blank], axis=1)
-        between = to_dense(z, between).astype(BF)
-        for o in outs:
-            o[z.own] = one
-            o[z.own + 1] = two
-            o[z.own + 2] = between
+        between = jnp.concatenate([between, blank], axis=1)
+        sums_out[0] = to_dense(z, one).astype(BF)
+        sums_out[1] = to_dense(z, two).astype(BF)
+        sums_out[2] = to_dense(z, between).astype(BF)
+        for i in range(3, n):
+            sums_out[i] = jnp.zeros_like(sums_out[i])
+        for j, o in enumerate(outs):
+            o[z.own] = sums_out[g ^ j]
+    else:
+        sums_out[...] = jnp.zeros_like(sums_out)
+        sums_out[0, :, : z.rhs] = one
+        sums_out[0, :, z.rhs : z.rhs + z.vertices] = between
+        sums_out[1, :, : z.rhs] = two
 
 
 def last_kernel(z, table, *refs):
     n = z.grps
     shares, refs = refs[:n], refs[n:]
-    tables, coarse, sums, hits, earlier, start, out, averages, whole, change = refs
+    tables, coarse, sums, hits, earlier, start, out, averages, whole, gained, done, sems = refs
     g = lax.axis_index("grp")
     if z.near:
-        one, two = from_dense(z, sums[0]), from_dense(z, sums[1])
-        between = sums[2, : z.share, : z.vertices]
+        for j, c in enumerate(shares):
+            gained[g ^ j] = c[z.own]
+        one, two = from_dense(z, gained[0].astype(F32)), from_dense(z, gained[1].astype(F32))
+        between = gained[2, : z.share, : z.vertices].astype(F32)
     else:
         one, two = sums[0, :, : z.rhs], sums[1, :, : z.rhs]
         between = sums[0, :, z.rhs : z.rhs + z.vertices]
     two = two + jnp.dot(between, one, precision=lax.Precision.HIGHEST, preferred_element_type=F32)
     whole[...] = one + two
     high, low = split_two(one)
-    flat = hits[...].reshape(z.own * MODES, z.vertices)
+    flat = hits[...]
     shift = jnp.dot(flat, high, preferred_element_type=F32) + jnp.dot(flat, low, preferred_element_type=F32)
     rows = [whole[pl.ds(table[z.t_corner + i], 1), :] for i in range(z.corners)]
     high, low = split_two(jnp.concatenate(rows, axis=0))
     coarse_corr = lax.dot_general(coarse[...], high, CONTRACT_FIRST, preferred_element_type=F32)
     coarse_corr = coarse_corr + lax.dot_general(coarse[...], low, CONTRACT_FIRST, preferred_element_type=F32)
+    copies = []
+    change = []
     for i in range(z.own):
         for j, c in enumerate(shares):
             averages[i, share_rows(z, g ^ j), :] = from_dense(z, c[i].astype(F32))
-        rows = slice(i * FPTS, (i + 1) * FPTS)
-        fixed = (averages[i] - 0.5 * shift[i * MODES : (i + 1) * MODES, :]).astype(BF)
-        table_i = tables_of(tables[i])
+        rows = slice(i * MODES, (i + 1) * MODES)
+        fixed = (averages[i] - 0.5 * shift[rows, :]).astype(BF)
         both = lax.dot_general(
-            jnp.concatenate([table_i, table_i], axis=0),
-            jnp.concatenate([fixed, earlier[i]], axis=0),
+            jnp.concatenate([tables[i], tables[i]], axis=0),
+            jnp.concatenate([fixed, earlier[rows, :]], axis=0),
             CONTRACT_FIRST,
             preferred_element_type=F32,
         )
-        change[rows, :] = both + coarse_corr[rows, :]
-    out[...] = start[...] - 0.5 * change[...].T
+        change.append(both + coarse_corr[i * FPTS : (i + 1) * FPTS, :])
+        if i % 2:
+            at = pl.ds((i - 1) * FPTS, 2 * FPTS)
+            done[:, at] = start[:, at] - 0.5 * jnp.concatenate(change, axis=0).T
+            copies.append(pltpu.make_async_copy(done.at[:, at], out.at[:, at], sems.at[i // 2]))
+            copies[-1].start()
+            change = []
+    for c in copies:
+        c.wait()
 
 
 def paired(blocks):
@@ -413,12 +445,21 @@
         pairs[1].append((s, s ^ 2))
         pairs[2].append((s, (s + (2 if (s // 2) % 2 else -2)) % count))
         pairs[3].append((s, (s + (1 if s % 2 else -1)) % count))
-    return [lax.ppermute(b, "sub", p) for b, p in zip(blocks, pairs)] + [blocks[4]]
+    met = []
+    for k, p in enumerate(pairs):
+        met.append(lax.ppermute(blocks[k], "sub", p))
+    return [*met, blocks[4]]
 
 
 def swapped(value, mask):
     count = lax.axis_size("grp")
     return lax.ppermute(value, "grp", [(s, s ^ mask) for s in range(count)])
+
+
+def hypercube(value):
+    two = swapped(value, 2)
+    one = swapped(value, 1)
+    return [value, one, two, swapped(two, 1)]
 
 
 def exchanged(blocks):
@@ -444,6 +485,7 @@
         compiler_params=pltpu.CompilerParams(vmem_limit_bytes=16 << 20),
     )(*[pltpu.with_memory_space_constraint(a, pltpu.HBM) for a in (first, coarse_basis[0])])
     block_two = swapped(trace_b, 2)
+    pair_two = swapped(project[0], 2)
     block_one = swapped(trace_b, 1)
 
     table = pl.pallas_call(
@@ -453,16 +495,19 @@
         out_specs=SMEM,
         scratch_shapes=[pltpu.SMEM((LINKS,), jnp.int32), pltpu.SMEM((z.faces + 1,), jnp.int32), pltpu.SMEM((LINKS,), jnp.int32)],
     )(owner_of_face.transpose(0, 2, 1), mortar_of_face, mortar_order, subdomain_map, vertex_ids)
-    matrix, target = pl.pallas_call(
-        load_kernel,
-        out_shape=[pltpu.VMEM(matrix.shape, BF), pltpu.VMEM(target.shape, F32)],
-        in_specs=[HBM] * 2,
-        out_specs=[VMEM] * 2,
-        scratch_shapes=[pltpu.SemaphoreType.DMA((2,))],
-        compiler_params=pltpu.CompilerParams(vmem_limit_bytes=16 << 20),
-    )(*[pltpu.with_memory_space_constraint(a, pltpu.HBM) for a in (matrix, target)])
-    pair_shape = shape((z.own, MODES // 2, 2 * FPTS), BF)
-    pair_own = call(join_kernel, z, pair_shape, (project[0].reshape(z.own, MODES, FPTS),))
+    loaded = [matrix, target, coarse_basis[0]]
+    matrix, target, coarse, own_tables = pl.pallas_call(
+        functools.partial(load_kernel, z),
+        out_shape=[pltpu.VMEM(a.shape, a.dtype) for a in loaded] + [pltpu.VMEM((z.own, MODES, FPTS), BF)],
+        in_specs=[HBM] * 4,
+        out_specs=[VMEM] * 4,
+        scratch_shapes=[
+            pltpu.VMEM((z.own, MODES * FPTS), BF),
+            pltpu.VMEM((z.own * MODES // 2, 2 * FPTS), F32),
+            pltpu.SemaphoreType.DMA((4,)),
+        ],
+        compiler_params=pltpu.CompilerParams(vmem_limit_bytes=4 << 20),
+    )(*[pltpu.with_memory_space_constraint(a, pltpu.HBM) for a in (*loaded, project[0])])
     block_three = swapped(block_two, 1)
     blocks = [trace_b, block_one, block_two, block_three]
 
@@ -472,25 +517,28 @@
     link = shape((CAP, z.share, z.wide), BF)
     thin = shape((CAP, z.dense, z.lanes), BF)
     thin_more = shape((CAP + z.more, z.dense, z.lanes), BF)
-    sums_shape = shape((2, z.vertices, z.wide), F32)
-
-    *parts, resid, ext = call(
+    sums_shape = shape((grps, z.dense, z.lanes), BF) if z.near else shape((2, z.vertices, z.wide), F32)
+
+    *parts, wide, ext = call(
         first_kernel,
         z,
-        [part] * grps + [shape((z.rows, z.rhs), F32), shape((z.own, MODES, width), BF)],
-        (table, matrix, *blocks, target, pair_own, coarse_basis[0]),
+        [part] * grps + [shape((z.own * MODES, z.rhs), F32), shape((z.own, MODES, width), BF)],
+        (table, matrix, *blocks, target, own_tables, coarse),
         (
             pltpu.VMEM((z.rhs + z.corners, z.all_rows), BF),
             pltpu.VMEM((z.rows, z.wide), BF),
             pltpu.VMEM((z.own, MODES, z.wide), BF),
         ),
     )
-    parts = exchanged(parts)
+    part_one = swapped(parts[1], 1)
+    part_two = swapped(parts[2], 2)
+    part_three = swapped(parts[3], 3)
+    parts = [parts[0], part_one, part_two, part_three]
+    pair_one = swapped(project[0], 1)
+    pair_three = swapped(pair_two, 1)
     outgoing = call(pack_kernel, z, [link] * LINKS, (table, *parts), (pltpu.VMEM((z.faces, z.share, z.wide), BF),), (False,))
-    outgoing, pair_own = lax.optimization_barrier((outgoing, pair_own))
     arrived = paired(outgoing)
-    pair_two = swapped(pair_own, 2)
-    arrived, pair_two = lax.optimization_barrier((arrived, pair_two))
+    arrived, pair_one, pair_two, pair_three = lax.optimization_barrier((arrived, pair_one, pair_two, pair_three))
     replies = call(
         average_kernel,
         z,
@@ -499,10 +547,14 @@
         (pltpu.VMEM((MORT_OWN + 1, z.share, z.wide), F32), pltpu.VMEM((MORT_OWN + 1, z.share, z.wide), BF)),
         (False,),
     )
-    replies, pair_own, pair_two = lax.optimization_barrier((replies, pair_own, pair_two))
     answered = paired(replies)
-    pair_one, pair_three = swapped(pair_own, 1), swapped(pair_two, 1)
-    answered, pair_one, pair_three = lax.optimization_barrier((answered, pair_one, pair_three))
+    mixed = call(
+        mix_kernel,
+        z,
+        shape((z.rows, z.all_rows), BF),
+        (matrix, own_tables, pair_one, pair_two, pair_three),
+        (pltpu.VMEM((z.rows, z.all_rows), BF), pltpu.VMEM((z.own * MODES // 2, 2 * FPTS), F32)),
+    )
     spread = call(
         spread_first,
         z,
@@ -510,23 +562,17 @@
         (table, *answered),
         (pltpu.VMEM((SLOTS, z.share, z.wide), BF),),
     )
-    spread_two = swapped(spread, 2)
-    shares = [spread, swapped(spread, 1), spread_two, swapped(spread_two, 1)]
-    tables = call(
-        unpack_kernel, z, shape((z.faces, MODES, FPTS), BF), (pair_own, pair_one, pair_two, pair_three)
-    )
+    shares = hypercube(spread)
     *parts, earlier, hits, sums = call(
         second_kernel,
         z,
         [part_more] * grps
-        + [shape((z.own, MODES, z.rhs), BF), shape((z.own, MODES, z.vertices), BF), sums_shape],
-        (table, matrix, *shares, tables, resid, coarse_basis[0], ext),
+        + [shape((z.rows, z.rhs), BF), shape((z.own * MODES, z.vertices), BF), sums_shape],
+        (table, mixed, *shares, wide, ext),
         (
-            pltpu.VMEM((z.faces, MODES, z.rhs), BF),
             pltpu.VMEM((z.all_rows, z.rhs), BF),
-            pltpu.VMEM((z.rows, z.rhs), BF),
-            pltpu.VMEM((z.own, MODES, z.rhs), F32),
-            pltpu.VMEM((z.own, MODES, z.extra), BF),
+            pltpu.VMEM((z.rows, z.rhs), F32),
+            pltpu.VMEM((z.own * MODES, z.extra), BF),
         ),
     )
     if not z.near:
@@ -549,23 +595,30 @@
     outs = call(
         spread_second,
         z,
-        [shape((z.own, z.dense, z.lanes), BF)] * grps + total_shape,
+        [part_more] * grps,
         (table, *answered, *results[LINKS:]),
         (pltpu.VMEM((SLOTS, z.dense, z.lanes), BF),),
     )
-    if z.near:
-        sums = outs[grps]
-    shares = exchanged(outs[:grps])
-    result = call(
-        last_kernel,
-        z,
-        shape((z.rhs, z.rows), F32),
-        (table, *shares, pair_own, coarse_basis[0], sums, hits, earlier, first),
-        (
+    shares = exchanged(outs)
+    inputs = (table, *shares, own_tables, coarse, sums, hits, earlier, first)
+    result = pl.pallas_call(
+        functools.partial(last_kernel, z),
+        out_shape=pltpu.HBM((z.rhs, z.rows), F32),
+        in_specs=[SMEM] + [VMEM] * (len(inputs) - 1),
+        out_specs=HBM,
+        scratch_shapes=[
             pltpu.VMEM((z.own, MODES, z.rhs), F32),
             pltpu.VMEM((z.vertices, z.rhs), F32),
-            pltpu.VMEM((z.rows, z.rhs), F32),
-        ),
+            pltpu.VMEM((grps, z.dense, z.lanes), BF),
+            pltpu.VMEM((z.rhs, z.rows), F32),
+            pltpu.SemaphoreType.DMA((z.own // 2,)),
+        ],
+        compiler_params=pltpu.CompilerParams(vmem_limit_bytes=16 << 20),
+    )(
+        *[
+            pltpu.with_memory_space_constraint(a, pltpu.SMEM if a.dtype == jnp.int32 else pltpu.VMEM)
+            for a in inputs
+        ]
     )
     return result.T[None]
 

time: 87.8 us -> 85.9 us (0.978)
  waiting for transfers between devices: 40.8 us -> 38.1 us
  local copies, waits for them, and re-layouts: 1.78 us -> 0.01 us
  starting transfers between devices: 33.9 us -> 35.4 us
  Pallas kernels: 10.8 us -> 11.9 us
    ppermute x18, waiting for transfers between devices: 22.9 us -> 19.9 us  [swapped(): return lax.ppermute(value, 'grp', [(s, s ^ mask) for s in range(count)])]
    pallas_call x1 -> x2, Pallas kernels: 1.65 us -> 3.31 us  [the longest x1 1.81 us: run(): pl.pallas_call(functools.partial(load_kernel, z), out_shape=[pltpu.VMEM(a...]
    ppermute x18, starting transfers between devices: 10.8 us -> 12.4 us  [swapped(): return lax.ppermute(value, 'grp', [(s, s ^ mask) for s in range(count)])]
    another operation x1 -> x0, local copies, waits for them, and re-layouts: 1.03 us -> none  [run(): project[0].reshape(z.own, MODES, FPTS)]
    pallas_call x11 -> x9, Pallas kernels: 6.22 us -> 5.65 us  [call(): pl.pallas_call(functools.partial(kernel, sizes, *static), out_shape=[pltp...]
  transfers between devices with their start and end apart: 34 -> 34, of which waited for: 17 -> 15; matrix products, arithmetic and copies ran while one was open for 1% -> 0% of each run, Pallas kernels for 4% -> 8%
where the time goes in v4:
time: 85.9 us; the launch traced here: 85.7 us
  waiting for transfers between devices  38.1 us (44%)
  starting transfers between devices  35.4 us (41%)
  Pallas kernels  11.9 us (14%)
    ppermute x16, starting transfers between devices, paired(): met.append(lax.ppermute(blocks[k], 'sub', p))  23 us
    ppermute x18, waiting for transfers between devices, swapped(): return lax.ppermute(value, 'grp', [(s, s ^ mask) for s in range(count)])  19.9 us
    ppermute x16, waiting for transfers between devices, paired(): met.append(lax.ppermute(blocks[k], 'sub', p))  18.2 us
    ppermute x18, starting transfers between devices, swapped(): return lax.ppermute(value, 'grp', [(s, s ^ mask) for s in range(count)])  12.4 us
    pallas_call x9, Pallas kernels, call(): pl.pallas_call(functools.partial(kernel, sizes, *static), out_shape=[pltp...  5.65 us
    pallas_call x1, Pallas kernels, run(): pl.pallas_call(functools.partial(table_kernel, z), out_shape=pltpu.SMEM((...  1.88 us
    pallas_call x1, Pallas kernels, run(): pl.pallas_call(functools.partial(load_kernel, z), out_shape=[pltpu.VMEM(a...  1.81 us
  transfers between devices with their start and end apart: 34, of which 15 were waited for; matrix products, arithmetic and copies ran while one was open for 0% of the time, Pallas kernels for 8%

profile of v4, /device:TPU:0, one launch (start us, length us, event | category | flops | bytes accessed | tf_op | source)
XLA Modules:
  0.0 85.7 jit_solution(514205772195129337)
XLA Ops:
  0.0 1.1 %shard_map.102.b0 = bf16[200,512]{1,0:T(8,128)(2,1)S(1)} custom-call(f32[192,512]{1,0:T(8,128)} %bitcast.13, bf16[8,512]{1,0:T(8,128)(2,1)} %bitcast.20), custom_call_target="tpu_custom_call" | custom-call | tf_op jit(solution)/shard_map/pallas_call | solution.py:475
  1.1 3.0 %collective-permute-start.1 = (bf16[200,512]{1,0:T(8,128)(2,1)S(1)}, bf16[200,512]{1,0:T(8,128)(2,1)S(1)}, u32[]{:S(2)}, u32[]{:S(2)}) collective-permute-start(bf16[200,512]{1,0:T(8,128)(2,1)S(1)} %shard_map.102.b0), channel_id=1, source_target_pairs={{0,2},{1,3},{2,0},{3,1},{4,6},{5,7},{6,4},{7,5},{8,10},{9,11},{10,... | collective-permute-start | bytes 614408 | tf_op jit(solution)/shard_map/ppermute | solution.py:456
  4.1 5.1 %collective-permute-done.1.b2 = bf16[200,512]{1,0:T(8,128)(2,1)S(1)} collective-permute-done((bf16[200,512]{1,0:T(8,128)(2,1)S(1)}, bf16[200,512]{1,0:T(8,128)(2,1)S(1)}, u32[]{:S(2)}, u32[]{:S(2)}) %collective-permute-start.1) | collective-permute-done | bytes 204832 | tf_op jit(solution)/shard_map/ppermute | solution.py:456
  9.2 1.7 %collective-permute-start.11 = (bf16[8,4096]{1,0:T(8,128)(2,1)}, bf16[8,4096]{1,0:T(8,128)(2,1)S(1)}, u32[]{:S(2)}, u32[]{:S(2)}) collective-permute-start(bf16[8,4096]{1,0:T(8,128)(2,1)} %bitcast.17), channel_id=1, source_target_pairs={{0,2},{1,3},{2,0},{3,1},{4,6},{5,7},{6,4},{7,5},{8,10},{9,11},{10,... | collective-permute-start | bytes 196616 | tf_op jit(solution)/shard_map/ppermute | solution.py:456
  10.9 1.8 %shard_map.101 = (bf16[512,2048]{1,0:T(8,128)(2,1)S(1)}, f32[192,512]{1,0:T(8,128)S(1)}, bf16[8,512]{1,0:T(8,128)(2,1)S(1)}, bf16[8,64,64]{2,1,0:T(8,128)(2,1)S(1)}) custom-call(bf16[512,2048]{1,0:T(8,128)(2,1)} %bitcast.15, f32[192,512]{1,0:T(8,128)} %bitcast.16, bf16[8,512]{1,0:T(8,128)(2,1)} %bitcast.21, bf16[8,4096]{1,0:T(8,128)(2,1)} %bitcast.18), custom_call_target="tpu_custom_call" | custom-call | tf_op jit(solution)/shard_map/pallas_call | solution.py:499
  12.8 1.9 %shard_map.100.table = s32[152]{0:T(256)S(4)} custom-call(s32[8,1,32]{2,1,0:T(1,128)} %bitcast.22, s32[8,32]{1,0:T(8,128)} %mortar.1, s32[8,16]{1,0:T(8,128)} %order.1, s32[8]{0:T(128)} %smap.1, s32[8,8]{1,0:T(8,128)} %vids.1), custom_call_target="tpu_custom_call" | custom-call | tf_op jit(solution)/shard_map/pallas_call | solution.py:491
  14.7 1.6 %shard_map.103 = (bf16[8,16,256]{2,1,0:T(8,128)(2,1)S(1)}, bf16[8,16,256]{2,1,0:T(8,128)(2,1)S(1)}, bf16[8,16,256]{2,1,0:T(8,128)(2,1)S(1)}, bf16[8,16,256]{2,1,...) custom-call(s32[152]{0:T(256)S(4)} %shard_map.100.table, ...), custom_call_target="tpu_custom_call" | custom-call | tf_op jit(solution)/shard_map/pallas_call | solution.py:73
  16.3 0.3 collective-permute-start.3
  16.6 0.3 collective-permute-start.4
  16.9 1.3 %collective-permute-start.5 = (bf16[8,16,256]{2,1,0:T(8,128)(2,1)S(1)}, bf16[8,16,256]{2,1,0:T(8,128)(2,1)S(1)}, u32[]{:S(2)}, u32[]{:S(2)}) collective-permute-start(bf16[8,16,256]{2,1,0:T(8,128)(2,1)S(1)} %get-tuple-element.62), channel_id=1, source_target_pairs={{0,3},{1,2},{2,1},{3,0},{4,7},{5,6},{6,5},{7,4},{8,11},{9,10},{10,... | collective-permute-start | bytes 196616 | tf_op jit(solution)/shard_map/ppermute | solution.py:456
  18.2 0.5 collective-permute-start.10
  18.8 2.7 %collective-permute-done.4.c2 = bf16[8,16,256]{2,1,0:T(8,128)(2,1)S(1)} collective-permute-done((bf16[8,16,256]{2,1,0:T(8,128)(2,1)S(1)}, bf16[8,16,256]{2,1,0:T(8,128)(2,1)S(1)}, u32[]{:S(2)}, u32[]{:S(2)}) %collective-permute-start.4) | collective-permute-done | bytes 65568 | tf_op jit(solution)/shard_map/ppermute | solution.py:456
  21.7 1.6 %collective-permute-start.6 = (bf16[8,16,256]{2,1,0:T(8,128)(2,1)S(1)}, bf16[8,16,256]{2,1,0:T(8,128)(2,1)S(1)}, u32[]{:S(2)}, u32[]{:S(2)}) collective-permute-start(bf16[8,16,256]{2,1,0:T(8,128)(2,1)S(1)} %get-tuple-element.63), channel_id=1, source_target_pairs={{0,4},{4,0},{8,12},{12,8},{16,20},{20,16},{24,28},{28,24},{1,5},{5... | collective-permute-start | bytes 196616 | tf_op jit(solution)/shard_map/ppermute | solution.py:450
  23.2 1.6 %collective-permute-start.7 = (bf16[8,16,256]{2,1,0:T(8,128)(2,1)S(1)}, bf16[8,16,256]{2,1,0:T(8,128)(2,1)S(1)}, u32[]{:S(2)}, u32[]{:S(2)}) collective-permute-start(bf16[8,16,256]{2,1,0:T(8,128)(2,1)S(1)} %get-tuple-element.64), channel_id=1, source_target_pairs={{0,8},{4,12},{8,0},{12,4},{16,24},{20,28},{24,16},{28,20},{1,9},{5... | collective-permute-start | bytes 196616 | tf_op jit(solution)/shard_map/ppermute | solution.py:450
  24.8 2.5 %collective-permute-start.8 = (bf16[8,16,256]{2,1,0:T(8,128)(2,1)S(1)}, bf16[8,16,256]{2,1,0:T(8,128)(2,1)S(1)}, u32[]{:S(2)}, u32[]{:S(2)}) collective-permute-start(bf16[8,16,256]{2,1,0:T(8,128)(2,1)S(1)} %get-tuple-element.65), channel_id=1, source_target_pairs={{0,24},{4,28},{8,16},{12,20},{16,8},{20,12},{24,0},{28,4},{1,25},{... | collective-permute-start | bytes 196616 | tf_op jit(solution)/shard_map/ppermute | solution.py:450
  27.3 1.3 %collective-permute-start.9 = (bf16[8,16,256]{2,1,0:T(8,128)(2,1)S(1)}, bf16[8,16,256]{2,1,0:T(8,128)(2,1)S(1)}, u32[]{:S(2)}, u32[]{:S(2)}) collective-permute-start(bf16[8,16,256]{2,1,0:T(8,128)(2,1)S(1)} %get-tuple-element.66), channel_id=1, source_target_pairs={{0,28},{4,8},{8,4},{12,16},{16,12},{20,24},{24,20},{28,0},{1,29},{... | collective-permute-start | bytes 196616 | tf_op jit(solution)/shard_map/ppermute | solution.py:450
  28.6 3.0 %collective-permute-done.8.refs_2_ = bf16[8,16,256]{2,1,0:T(8,128)(2,1)S(1)} collective-permute-done((bf16[8,16,256]{2,1,0:T(8,128)(2,1)S(1)}, bf16[8,16,256]{2,1,0:T(8,128)(2,1)S(1)}, u32[]{:S(2)}, u32[]{:S(2)}) %collective-permute-start.8) | collective-permute-done | bytes 65568 | tf_op jit(solution)/shard_map/ppermute | solution.py:450
  31.6 2.7 %collective-permute-done.9.refs_3_ = bf16[8,16,256]{2,1,0:T(8,128)(2,1)S(1)} collective-permute-done((bf16[8,16,256]{2,1,0:T(8,128)(2,1)S(1)}, bf16[8,16,256]{2,1,0:T(8,128)(2,1)S(1)}, u32[]{:S(2)}, u32[]{:S(2)}) %collective-permute-start.9) | collective-permute-done | bytes 65568 | tf_op jit(solution)/shard_map/ppermute | solution.py:450
  34.3 0.3 shard_map.106
  34.8 1.8 %collective-permute-start.15 = (bf16[8,16,256]{2,1,0:T(8,128)(2,1)S(1)}, bf16[8,16,256]{2,1,0:T(8,128)(2,1)S(1)}, u32[]{:S(2)}, u32[]{:S(2)}) collective-permute-start(bf16[8,16,256]{2,1,0:T(8,128)(2,1)S(1)} %get-tuple-element.78), channel_id=1, source_target_pairs={{0,24},{4,28},{8,16},{12,20},{16,8},{20,12},{24,0},{28,4},{1,25},{... | collective-permute-start | bytes 196616 | tf_op jit(solution)/shard_map/ppermute | solution.py:450
  36.6 3.3 %collective-permute-start.16 = (bf16[8,16,256]{2,1,0:T(8,128)(2,1)S(1)}, bf16[8,16,256]{2,1,0:T(8,128)(2,1)S(1)}, u32[]{:S(2)}, u32[]{:S(2)}) collective-permute-start(bf16[8,16,256]{2,1,0:T(8,128)(2,1)S(1)} %get-tuple-element.79), channel_id=1, source_target_pairs={{0,28},{4,8},{8,4},{12,16},{16,12},{20,24},{24,20},{28,0},{1,29},{... | collective-permute-start | bytes 196616 | tf_op jit(solution)/shard_map/ppermute | solution.py:450
  39.9 0.4 collective-permute-done.14.refs_1_
  40.3 0.7 collective-permute-done.15.refs_2_
  41.0 2.5 %collective-permute-done.16.refs_3_ = bf16[8,16,256]{2,1,0:T(8,128)(2,1)S(1)} collective-permute-done((bf16[8,16,256]{2,1,0:T(8,128)(2,1)S(1)}, bf16[8,16,256]{2,1,0:T(8,128)(2,1)S(1)}, u32[]{:S(2)}, u32[]{:S(2)}) %collective-permute-start.16) | collective-permute-done | bytes 65568 | tf_op jit(solution)/shard_map/ppermute | solution.py:450
  43.7 1.2 %collective-permute-start.18 = (bf16[56,16,128]{2,1,0:T(8,128)(2,1)S(1)}, bf16[56,16,128]{2,1,0:T(8,128)(2,1)S(1)}, u32[]{:S(2)}, u32[]{:S(2)}) collective-permute-start(bf16[56,16,128]{2,1,0:T(8,128)(2,1)S(1)} %shard_map.107.refs_0_), channel_id=1, source_target_pairs={{0,2},{1,3},{2,0},{3,1},{4,6},{5,7},{6,4},{7,5},{8,10},{9,11},{10,... | collective-permute-start | bytes 688136 | tf_op jit(solution)/shard_map/ppermute | solution.py:456
  44.9 4.9 %collective-permute-done.18.refs_2_ = bf16[56,16,128]{2,1,0:T(8,128)(2,1)S(1)} collective-permute-done((bf16[56,16,128]{2,1,0:T(8,128)(2,1)S(1)}, bf16[56,16,128]{2,1,0:T(8,128)(2,1)S(1)}, u32[]{:S(2)}, u32[]{:S(2)}) %collective-permute-start.18) | collective-permute-done | bytes 229408 | tf_op jit(solution)/shard_map/ppermute | solution.py:456
  49.8 1.9 %shard_map.105.mixed = bf16[512,2048]{1,0:T(8,128)(2,1)S(1)} custom-call(bf16[512,2048]{1,0:T(8,128)(2,1)S(1)} %get-tuple-element.55.schur, bf16[8,64,64]{2,1,0:T(8,128)(2,1)S(1)} %get-tuple-element.56.tables.t0.refs_4_, bf16[8,4096]{1,0:T(8,128)(2,1)S(1)} %collective-permute-done.10.r1, bf16[8,4096]{1,0:T(8,128)(2,1)S(1)} %collective-permute-done.11.r2, ...), custom_call_target="tpu_custom_call" | custom-call | tf_op jit(solution)/shard_map/pallas_call | solution.py:73
  51.7 1.3 %shard_map.108 = (bf16[9,24,128]{2,1,0:T(8,128)(2,1)S(1)}, bf16[9,24,128]{2,1,0:T(8,128)(2,1)S(1)}, bf16[9,24,128]{2,1,0:T(8,128)(2,1)S(1)}, bf16[9,24,128]{2,1,...) custom-call(s32[152]{0:T(256)S(4)} %shard_map.100.table, ...), custom_call_target="tpu_custom_call" | custom-call | tf_op jit(solution)/shard_map/pallas_call | solution.py:73
  53.0 0.6 collective-permute-start.20
  53.6 1.1 %collective-permute-start.21 = (bf16[9,24,128]{2,1,0:T(8,128)(2,1)S(1)}, bf16[9,24,128]{2,1,0:T(8,128)(2,1)S(1)}, u32[]{:S(2)}, u32[]{:S(2)}) collective-permute-start(bf16[9,24,128]{2,1,0:T(8,128)(2,1)S(1)} %get-tuple-element.85), channel_id=1, source_target_pairs={{0,2},{1,3},{2,0},{3,1},{4,6},{5,7},{6,4},{7,5},{8,10},{9,11},{10,... | collective-permute-start | bytes 165896 | tf_op jit(solution)/shard_map/ppermute | solution.py:456
  54.7 0.3 collective-permute-start.22
  55.0 2.8 %collective-permute-done.21.c2 = bf16[9,24,128]{2,1,0:T(8,128)(2,1)S(1)} collective-permute-done((bf16[9,24,128]{2,1,0:T(8,128)(2,1)S(1)}, bf16[9,24,128]{2,1,0:T(8,128)(2,1)S(1)}, u32[]{:S(2)}, u32[]{:S(2)}) %collective-permute-start.21) | collective-permute-done | bytes 55328 | tf_op jit(solution)/shard_map/ppermute | solution.py:456
  57.7 1.1 %collective-permute-done.22.c3 = bf16[9,24,128]{2,1,0:T(8,128)(2,1)S(1)} collective-permute-done((bf16[9,24,128]{2,1,0:T(8,128)(2,1)S(1)}, bf16[9,24,128]{2,1,0:T(8,128)(2,1)S(1)}, u32[]{:S(2)}, u32[]{:S(2)}) %collective-permute-start.22) | collective-permute-done | bytes 55328 | tf_op jit(solution)/shard_map/ppermute | solution.py:456
  59.0 0.4 collective-permute-start.24
  59.4 3.6 %collective-permute-start.25 = (bf16[9,24,128]{2,1,0:T(8,128)(2,1)S(1)}, bf16[9,24,128]{2,1,0:T(8,128)(2,1)S(1)}, u32[]{:S(2)}, u32[]{:S(2)}) collective-permute-start(bf16[9,24,128]{2,1,0:T(8,128)(2,1)S(1)} %get-tuple-element.89), channel_id=1, source_target_pairs={{0,24},{4,28},{8,16},{12,20},{16,8},{20,12},{24,0},{28,4},{1,25},{... | collective-permute-start | bytes 165896 | tf_op jit(solution)/shard_map/ppermute | solution.py:450
  63.0 1.3 %collective-permute-start.26 = (bf16[9,24,128]{2,1,0:T(8,128)(2,1)S(1)}, bf16[9,24,128]{2,1,0:T(8,128)(2,1)S(1)}, u32[]{:S(2)}, u32[]{:S(2)}) collective-permute-start(bf16[9,24,128]{2,1,0:T(8,128)(2,1)S(1)} %get-tuple-element.90), channel_id=1, source_target_pairs={{0,28},{4,8},{8,4},{12,16},{16,12},{20,24},{24,20},{28,0},{1,29},{... | collective-permute-start | bytes 165896 | tf_op jit(solution)/shard_map/ppermute | solution.py:450
  64.3 2.4 %collective-permute-done.25.refs_2_ = bf16[9,24,128]{2,1,0:T(8,128)(2,1)S(1)} collective-permute-done((bf16[9,24,128]{2,1,0:T(8,128)(2,1)S(1)}, bf16[9,24,128]{2,1,0:T(8,128)(2,1)S(1)}, u32[]{:S(2)}, u32[]{:S(2)}) %collective-permute-start.25) | collective-permute-done | bytes 55328 | tf_op jit(solution)/shard_map/ppermute | solution.py:450
  66.7 3.1 %collective-permute-done.26.refs_3_ = bf16[9,24,128]{2,1,0:T(8,128)(2,1)S(1)} collective-permute-done((bf16[9,24,128]{2,1,0:T(8,128)(2,1)S(1)}, bf16[9,24,128]{2,1,0:T(8,128)(2,1)S(1)}, u32[]{:S(2)}, u32[]{:S(2)}) %collective-permute-start.26) | collective-permute-done | bytes 55328 | tf_op jit(solution)/shard_map/ppermute | solution.py:450
  69.8 0.3 shard_map.110
  70.2 1.1 %collective-permute-start.29 = (bf16[9,24,128]{2,1,0:T(8,128)(2,1)S(1)}, bf16[9,24,128]{2,1,0:T(8,128)(2,1)S(1)}, u32[]{:S(2)}, u32[]{:S(2)}) collective-permute-start(bf16[9,24,128]{2,1,0:T(8,128)(2,1)S(1)} %get-tuple-element.94), channel_id=1, source_target_pairs={{0,24},{4,28},{8,16},{12,20},{16,8},{20,12},{24,0},{28,4},{1,25},{... | collective-permute-start | bytes 165896 | tf_op jit(solution)/shard_map/ppermute | solution.py:450
  71.3 0.9 %collective-permute-start.27 = (bf16[8,24,128]{2,1,0:T(8,128)(2,1)S(1)}, bf16[8,24,128]{2,1,0:T(8,128)(2,1)S(1)}, u32[]{:S(2)}, u32[]{:S(2)}) collective-permute-start(bf16[8,24,128]{2,1,0:T(8,128)(2,1)S(1)} %get-tuple-element.92), channel_id=1, source_target_pairs={{0,4},{4,0},{8,12},{12,8},{16,20},{20,16},{24,28},{28,24},{1,5},{5... | collective-permute-start | bytes 147464 | tf_op jit(solution)/shard_map/ppermute | solution.py:450
  72.1 3.4 %collective-permute-start.30 = (bf16[8,24,128]{2,1,0:T(8,128)(2,1)S(1)}, bf16[8,24,128]{2,1,0:T(8,128)(2,1)S(1)}, u32[]{:S(2)}, u32[]{:S(2)}) collective-permute-start(bf16[8,24,128]{2,1,0:T(8,128)(2,1)S(1)} %get-tuple-element.95), channel_id=1, source_target_pairs={{0,28},{4,8},{8,4},{12,16},{16,12},{20,24},{24,20},{28,0},{1,29},{... | collective-permute-start | bytes 147464 | tf_op jit(solution)/shard_map/ppermute | solution.py:450
  75.5 3.4 %collective-permute-done.30.refs_3_ = bf16[8,24,128]{2,1,0:T(8,128)(2,1)S(1)} collective-permute-done((bf16[8,24,128]{2,1,0:T(8,128)(2,1)S(1)}, bf16[8,24,128]{2,1,0:T(8,128)(2,1)S(1)}, u32[]{:S(2)}, u32[]{:S(2)}) %collective-permute-start.30) | collective-permute-done | bytes 49184 | tf_op jit(solution)/shard_map/ppermute | solution.py:450
  79.1 1.0 %collective-permute-start.32 = (bf16[9,24,128]{2,1,0:T(8,128)(2,1)S(1)}, bf16[9,24,128]{2,1,0:T(8,128)(2,1)S(1)}, u32[]{:S(2)}, u32[]{:S(2)}) collective-permute-start(bf16[9,24,128]{2,1,0:T(8,128)(2,1)S(1)} %get-tuple-element.100), channel_id=1, source_target_pairs={{0,2},{1,3},{2,0},{3,1},{4,6},{5,7},{6,4},{7,5},{8,10},{9,11},{10,... | collective-permute-start | bytes 165896 | tf_op jit(solution)/shard_map/ppermute | solution.py:456
  80.0 0.9 %collective-permute-start.33 = (bf16[9,24,128]{2,1,0:T(8,128)(2,1)S(1)}, bf16[9,24,128]{2,1,0:T(8,128)(2,1)S(1)}, u32[]{:S(2)}, u32[]{:S(2)}) collective-permute-start(bf16[9,24,128]{2,1,0:T(8,128)(2,1)S(1)} %get-tuple-element.101), channel_id=1, source_target_pairs={{0,3},{1,2},{2,1},{3,0},{4,7},{5,6},{6,5},{7,4},{8,11},{9,10},{10,... | collective-permute-start | bytes 165896 | tf_op jit(solution)/shard_map/ppermute | solution.py:456
  80.9 2.8 %collective-permute-done.32.refs_2_ = bf16[9,24,128]{2,1,0:T(8,128)(2,1)S(1)} collective-permute-done((bf16[9,24,128]{2,1,0:T(8,128)(2,1)S(1)}, bf16[9,24,128]{2,1,0:T(8,128)(2,1)S(1)}, u32[]{:S(2)}, u32[]{:S(2)}) %collective-permute-start.32) | collective-permute-done | bytes 55328 | tf_op jit(solution)/shard_map/ppermute | solution.py:456
  83.7 0.5 collective-permute-done.33.refs_3_
  84.2 1.5 %shard_map.112 = f32[192,512]{1,0:T(8,128)} custom-call(s32[152]{0:T(256)S(4)} %shard_map.100.table, bf16[9,24,128]{2,1,0:T(8,128)(2,1)S(1)} %get-tuple-element.98.refs_0_, bf16[9,24,128]{2,1,0:T(8,128)(2,1)S(1)} %collective-permute-done.31.refs_1_, bf16[9,24,128]{2,1,0:T(8,128)(2,1)S(1)} %collective-permute-done.32.refs_2_, ...), custom_call_target="tpu_custom_call" | custom-call | tf_op jit(solution)/shard_map/pallas_call | solution.py:604
  (37 shorter events, 1.0 us)
Async XLA Ops:
  1.1 8.1 %collective-permute-start.1 = (bf16[200,512]{1,0:T(8,128)(2,1)S(1)}, bf16[200,512]{1,0:T(8,128)(2,1)S(1)}, u32[]{:S(2)}, u32[]{:S(2)}) collective-permute-start(bf16[200,512]{1,0:T(8,128)(2,1)S(1)} %shard_map.102.b0), channel_id=1, source_target_pairs={{0,2},{1,3},{2,0},{3,1},{4,6},{5,7},{6,4},{7,5},{8,10},{9,11},{10,... | collective-permute-start | bytes 614408 | tf_op jit(solution)/shard_map/ppermute | solution.py:456
  4.1 10.5 %collective-permute-start = (bf16[200,512]{1,0:T(8,128)(2,1)S(1)}, bf16[200,512]{1,0:T(8,128)(2,1)S(1)}, u32[]{:S(2)}, u32[]{:S(2)}) collective-permute-start(bf16[200,512]{1,0:T(8,128)(2,1)S(1)} %shard_map.102.b0), channel_id=1, source_target_pairs={{0,1},{1,0},{2,3},{3,2},{4,5},{5,4},{6,7},{7,6},{8,9},{9,8},{10,11... | collective-permute-start | bytes 614408 | tf_op jit(solution)/shard_map/ppermute | solution.py:456
  9.2 5.5 %collective-permute-start.2 = (bf16[200,512]{1,0:T(8,128)(2,1)S(1)}, bf16[200,512]{1,0:T(8,128)(2,1)S(1)}, u32[]{:S(2)}, u32[]{:S(2)}) collective-permute-start(bf16[200,512]{1,0:T(8,128)(2,1)S(1)} %collective-permute-done.1.b2), channel_id=1, source_target_pairs={{0,1},{1,0},{2,3},{3,2},{4,5},{5,4},{6,7},{7,6},{8,9},{9,8},{10,11... | collective-permute-start | bytes 614408 | tf_op jit(solution)/shard_map/ppermute | solution.py:456
  9.2 9.5 %collective-permute-start.11 = (bf16[8,4096]{1,0:T(8,128)(2,1)}, bf16[8,4096]{1,0:T(8,128)(2,1)S(1)}, u32[]{:S(2)}, u32[]{:S(2)}) collective-permute-start(bf16[8,4096]{1,0:T(8,128)(2,1)} %bitcast.17), channel_id=1, source_target_pairs={{0,2},{1,3},{2,0},{3,1},{4,6},{5,7},{6,4},{7,5},{8,10},{9,11},{10,... | collective-permute-start | bytes 196616 | tf_op jit(solution)/shard_map/ppermute | solution.py:456
  14.7 3.6 %copy-start.1 = (bf16[1,8,4096]{2,1,0:T(8,128)(2,1)S(1)}, bf16[1,8,4096]{2,1,0:T(8,128)(2,1)}, u32[]{:S(2)}) copy-start(bf16[1,8,4096]{2,1,0:T(8,128)(2,1)} %param.13) | copy-start | bytes 196612
  16.3 2.5 %collective-permute-start.3 = (bf16[8,16,256]{2,1,0:T(8,128)(2,1)S(1)}, bf16[8,16,256]{2,1,0:T(8,128)(2,1)S(1)}, u32[]{:S(2)}, u32[]{:S(2)}) collective-permute-start(bf16[8,16,256]{2,1,0:T(8,128)(2,1)S(1)} %get-tuple-element.60), channel_id=1, source_target_pairs={{0,1},{1,0},{2,3},{3,2},{4,5},{5,4},{6,7},{7,6},{8,9},{9,8},{10,11... | collective-permute-start | bytes 196616 | tf_op jit(solution)/shard_map/ppermute | solution.py:456
  16.6 5.0 %collective-permute-start.4 = (bf16[8,16,256]{2,1,0:T(8,128)(2,1)S(1)}, bf16[8,16,256]{2,1,0:T(8,128)(2,1)S(1)}, u32[]{:S(2)}, u32[]{:S(2)}) collective-permute-start(bf16[8,16,256]{2,1,0:T(8,128)(2,1)S(1)} %get-tuple-element.61), channel_id=1, source_target_pairs={{0,2},{1,3},{2,0},{3,1},{4,6},{5,7},{6,4},{7,5},{8,10},{9,11},{10,... | collective-permute-start | bytes 196616 | tf_op jit(solution)/shard_map/ppermute | solution.py:456
  16.9 4.7 %collective-permute-start.5 = (bf16[8,16,256]{2,1,0:T(8,128)(2,1)S(1)}, bf16[8,16,256]{2,1,0:T(8,128)(2,1)S(1)}, u32[]{:S(2)}, u32[]{:S(2)}) collective-permute-start(bf16[8,16,256]{2,1,0:T(8,128)(2,1)S(1)} %get-tuple-element.62), channel_id=1, source_target_pairs={{0,3},{1,2},{2,1},{3,0},{4,7},{5,6},{6,5},{7,4},{8,11},{9,10},{10,... | collective-permute-start | bytes 196616 | tf_op jit(solution)/shard_map/ppermute | solution.py:456
  18.2 9.1 %collective-permute-start.10 = (bf16[8,4096]{1,0:T(8,128)(2,1)S(1)}, bf16[8,4096]{1,0:T(8,128)(2,1)S(1)}, u32[]{:S(2)}, u32[]{:S(2)}) collective-permute-start(bf16[8,4096]{1,0:T(8,128)(2,1)S(1)} %bitcast.19), channel_id=1, source_target_pairs={{0,1},{1,0},{2,3},{3,2},{4,5},{5,4},{6,7},{7,6},{8,9},{9,8},{10,11... | collective-permute-start | bytes 196616 | tf_op jit(solution)/shard_map/ppermute | solution.py:456
  18.7 9.8 %collective-permute-start.12 = (bf16[8,4096]{1,0:T(8,128)(2,1)S(1)}, bf16[8,4096]{1,0:T(8,128)(2,1)S(1)}, u32[]{:S(2)}, u32[]{:S(2)}) collective-permute-start(bf16[8,4096]{1,0:T(8,128)(2,1)S(1)} %collective-permute-done.11.r2), channel_id=1, source_target_pairs={{0,1},{1,0},{2,3},{3,2},{4,5},{5,4},{6,7},{7,6},{8,9},{9,8},{10,11... | collective-permute-start | bytes 196616 | tf_op jit(solution)/shard_map/ppermute | solution.py:456
  21.7 6.9 %collective-permute-start.6 = (bf16[8,16,256]{2,1,0:T(8,128)(2,1)S(1)}, bf16[8,16,256]{2,1,0:T(8,128)(2,1)S(1)}, u32[]{:S(2)}, u32[]{:S(2)}) collective-permute-start(bf16[8,16,256]{2,1,0:T(8,128)(2,1)S(1)} %get-tuple-element.63), channel_id=1, source_target_pairs={{0,4},{4,0},{8,12},{12,8},{16,20},{20,16},{24,28},{28,24},{1,5},{5... | collective-permute-start | bytes 196616 | tf_op jit(solution)/shard_map/ppermute | solution.py:450
  23.2 5.4 %collective-permute-start.7 = (bf16[8,16,256]{2,1,0:T(8,128)(2,1)S(1)}, bf16[8,16,256]{2,1,0:T(8,128)(2,1)S(1)}, u32[]{:S(2)}, u32[]{:S(2)}) collective-permute-start(bf16[8,16,256]{2,1,0:T(8,128)(2,1)S(1)} %get-tuple-element.64), channel_id=1, source_target_pairs={{0,8},{4,12},{8,0},{12,4},{16,24},{20,28},{24,16},{28,20},{1,9},{5... | collective-permute-start | bytes 196616 | tf_op jit(solution)/shard_map/ppermute | solution.py:450
  24.8 6.8 %collective-permute-start.8 = (bf16[8,16,256]{2,1,0:T(8,128)(2,1)S(1)}, bf16[8,16,256]{2,1,0:T(8,128)(2,1)S(1)}, u32[]{:S(2)}, u32[]{:S(2)}) collective-permute-start(bf16[8,16,256]{2,1,0:T(8,128)(2,1)S(1)} %get-tuple-element.65), channel_id=1, source_target_pairs={{0,24},{4,28},{8,16},{12,20},{16,8},{20,12},{24,0},{28,4},{1,25},{... | collective-permute-start | bytes 196616 | tf_op jit(solution)/shard_map/ppermute | solution.py:450
  27.3 7.0 %collective-permute-start.9 = (bf16[8,16,256]{2,1,0:T(8,128)(2,1)S(1)}, bf16[8,16,256]{2,1,0:T(8,128)(2,1)S(1)}, u32[]{:S(2)}, u32[]{:S(2)}) collective-permute-start(bf16[8,16,256]{2,1,0:T(8,128)(2,1)S(1)} %get-tuple-element.66), channel_id=1, source_target_pairs={{0,28},{4,8},{8,4},{12,16},{16,12},{20,24},{24,20},{28,0},{1,29},{... | collective-permute-start | bytes 196616 | tf_op jit(solution)/shard_map/ppermute | solution.py:450
  34.6 5.4 %collective-permute-start.13 = (bf16[8,16,256]{2,1,0:T(8,128)(2,1)S(1)}, bf16[8,16,256]{2,1,0:T(8,128)(2,1)S(1)}, u32[]{:S(2)}, u32[]{:S(2)}) collective-permute-start(bf16[8,16,256]{2,1,0:T(8,128)(2,1)S(1)} %get-tuple-element.76), channel_id=1, source_target_pairs={{0,4},{4,0},{8,12},{12,8},{16,20},{20,16},{24,28},{28,24},{1,5},{5... | collective-permute-start | bytes 196616 | tf_op jit(solution)/shard_map/ppermute | solution.py:450
  34.6 5.7 %collective-permute-start.14 = (bf16[8,16,256]{2,1,0:T(8,128)(2,1)S(1)}, bf16[8,16,256]{2,1,0:T(8,128)(2,1)S(1)}, u32[]{:S(2)}, u32[]{:S(2)}) collective-permute-start(bf16[8,16,256]{2,1,0:T(8,128)(2,1)S(1)} %get-tuple-element.77), channel_id=1, source_target_pairs={{0,8},{4,12},{8,0},{12,4},{16,24},{20,28},{24,16},{28,20},{1,9},{5... | collective-permute-start | bytes 196616 | tf_op jit(solution)/shard_map/ppermute | solution.py:450
  34.8 6.2 %collective-permute-start.15 = (bf16[8,16,256]{2,1,0:T(8,128)(2,1)S(1)}, bf16[8,16,256]{2,1,0:T(8,128)(2,1)S(1)}, u32[]{:S(2)}, u32[]{:S(2)}) collective-permute-start(bf16[8,16,256]{2,1,0:T(8,128)(2,1)S(1)} %get-tuple-element.78), channel_id=1, source_target_pairs={{0,24},{4,28},{8,16},{12,20},{16,8},{20,12},{24,0},{28,4},{1,25},{... | collective-permute-start | bytes 196616 | tf_op jit(solution)/shard_map/ppermute | solution.py:450
  36.6 7.0 %collective-permute-start.16 = (bf16[8,16,256]{2,1,0:T(8,128)(2,1)S(1)}, bf16[8,16,256]{2,1,0:T(8,128)(2,1)S(1)}, u32[]{:S(2)}, u32[]{:S(2)}) collective-permute-start(bf16[8,16,256]{2,1,0:T(8,128)(2,1)S(1)} %get-tuple-element.79), channel_id=1, source_target_pairs={{0,28},{4,8},{8,4},{12,16},{16,12},{20,24},{24,20},{28,0},{1,29},{... | collective-permute-start | bytes 196616 | tf_op jit(solution)/shard_map/ppermute | solution.py:450
  43.7 6.1 %collective-permute-start.18 = (bf16[56,16,128]{2,1,0:T(8,128)(2,1)S(1)}, bf16[56,16,128]{2,1,0:T(8,128)(2,1)S(1)}, u32[]{:S(2)}, u32[]{:S(2)}) collective-permute-start(bf16[56,16,128]{2,1,0:T(8,128)(2,1)S(1)} %shard_map.107.refs_0_), channel_id=1, source_target_pairs={{0,2},{1,3},{2,0},{3,1},{4,6},{5,7},{6,4},{7,5},{8,10},{9,11},{10,... | collective-permute-start | bytes 688136 | tf_op jit(solution)/shard_map/ppermute | solution.py:456
  44.9 6.8 %collective-permute-start.17 = (bf16[56,16,128]{2,1,0:T(8,128)(2,1)S(1)}, bf16[56,16,128]{2,1,0:T(8,128)(2,1)S(1)}, u32[]{:S(2)}, u32[]{:S(2)}) collective-permute-start(bf16[56,16,128]{2,1,0:T(8,128)(2,1)S(1)} %shard_map.107.refs_0_), channel_id=1, source_target_pairs={{0,1},{1,0},{2,3},{3,2},{4,5},{5,4},{6,7},{7,6},{8,9},{9,8},{10,11... | collective-permute-start | bytes 688136 | tf_op jit(solution)/shard_map/ppermute | solution.py:456
  49.8 1.9 %collective-permute-start.19 = (bf16[56,16,128]{2,1,0:T(8,128)(2,1)S(1)}, bf16[56,16,128]{2,1,0:T(8,128)(2,1)S(1)}, u32[]{:S(2)}, u32[]{:S(2)}) collective-permute-start(bf16[56,16,128]{2,1,0:T(8,128)(2,1)S(1)} %collective-permute-done.18.refs_2_), channel_id=1, source_target_pairs={{0,1},{1,0},{2,3},{3,2},{4,5},{5,4},{6,7},{7,6},{8,9},{9,8},{10,11... | collective-permute-start | bytes 688136 | tf_op jit(solution)/shard_map/ppermute | solution.py:456
  51.7 32.5 %copy-start = (f32[1,512,192]{1,2,0:T(8,128)S(1)}, f32[1,512,192]{1,2,0:T(8,128)}, u32[]{:S(2)}) copy-start(f32[1,512,192]{1,2,0:T(8,128)} %param.12) | copy-start | bytes 1179652
  53.0 2.0 %collective-permute-start.20 = (bf16[9,24,128]{2,1,0:T(8,128)(2,1)S(1)}, bf16[9,24,128]{2,1,0:T(8,128)(2,1)S(1)}, u32[]{:S(2)}, u32[]{:S(2)}) collective-permute-start(bf16[9,24,128]{2,1,0:T(8,128)(2,1)S(1)} %get-tuple-element.84), channel_id=1, source_target_pairs={{0,1},{1,0},{2,3},{3,2},{4,5},{5,4},{6,7},{7,6},{8,9},{9,8},{10,11... | collective-permute-start | bytes 165896 | tf_op jit(solution)/shard_map/ppermute | solution.py:456
  53.6 4.2 %collective-permute-start.21 = (bf16[9,24,128]{2,1,0:T(8,128)(2,1)S(1)}, bf16[9,24,128]{2,1,0:T(8,128)(2,1)S(1)}, u32[]{:S(2)}, u32[]{:S(2)}) collective-permute-start(bf16[9,24,128]{2,1,0:T(8,128)(2,1)S(1)} %get-tuple-element.85), channel_id=1, source_target_pairs={{0,2},{1,3},{2,0},{3,1},{4,6},{5,7},{6,4},{7,5},{8,10},{9,11},{10,... | collective-permute-start | bytes 165896 | tf_op jit(solution)/shard_map/ppermute | solution.py:456
  54.7 4.2 %collective-permute-start.22 = (bf16[9,24,128]{2,1,0:T(8,128)(2,1)S(1)}, bf16[9,24,128]{2,1,0:T(8,128)(2,1)S(1)}, u32[]{:S(2)}, u32[]{:S(2)}) collective-permute-start(bf16[9,24,128]{2,1,0:T(8,128)(2,1)S(1)} %get-tuple-element.86), channel_id=1, source_target_pairs={{0,3},{1,2},{2,1},{3,0},{4,7},{5,6},{6,5},{7,4},{8,11},{9,10},{10,... | collective-permute-start | bytes 165896 | tf_op jit(solution)/shard_map/ppermute | solution.py:456
  58.9 5.4 %collective-permute-start.23 = (bf16[9,24,128]{2,1,0:T(8,128)(2,1)S(1)}, bf16[9,24,128]{2,1,0:T(8,128)(2,1)S(1)}, u32[]{:S(2)}, u32[]{:S(2)}) collective-permute-start(bf16[9,24,128]{2,1,0:T(8,128)(2,1)S(1)} %get-tuple-element.87), channel_id=1, source_target_pairs={{0,4},{4,0},{8,12},{12,8},{16,20},{20,16},{24,28},{28,24},{1,5},{5... | collective-permute-start | bytes 165896 | tf_op jit(solution)/shard_map/ppermute | solution.py:450
  59.0 5.3 %collective-permute-start.24 = (bf16[9,24,128]{2,1,0:T(8,128)(2,1)S(1)}, bf16[9,24,128]{2,1,0:T(8,128)(2,1)S(1)}, u32[]{:S(2)}, u32[]{:S(2)}) collective-permute-start(bf16[9,24,128]{2,1,0:T(8,128)(2,1)S(1)} %get-tuple-element.88), channel_id=1, source_target_pairs={{0,8},{4,12},{8,0},{12,4},{16,24},{20,28},{24,16},{28,20},{1,9},{5... | collective-permute-start | bytes 165896 | tf_op jit(solution)/shard_map/ppermute | solution.py:450
  59.4 7.3 %collective-permute-start.25 = (bf16[9,24,128]{2,1,0:T(8,128)(2,1)S(1)}, bf16[9,24,128]{2,1,0:T(8,128)(2,1)S(1)}, u32[]{:S(2)}, u32[]{:S(2)}) collective-permute-start(bf16[9,24,128]{2,1,0:T(8,128)(2,1)S(1)} %get-tuple-element.89), channel_id=1, source_target_pairs={{0,24},{4,28},{8,16},{12,20},{16,8},{20,12},{24,0},{28,4},{1,25},{... | collective-permute-start | bytes 165896 | tf_op jit(solution)/shard_map/ppermute | solution.py:450
  63.0 6.9 %collective-permute-start.26 = (bf16[9,24,128]{2,1,0:T(8,128)(2,1)S(1)}, bf16[9,24,128]{2,1,0:T(8,128)(2,1)S(1)}, u32[]{:S(2)}, u32[]{:S(2)}) collective-permute-start(bf16[9,24,128]{2,1,0:T(8,128)(2,1)S(1)} %get-tuple-element.90), channel_id=1, source_target_pairs={{0,28},{4,8},{8,4},{12,16},{16,12},{20,24},{24,20},{28,0},{1,29},{... | collective-permute-start | bytes 165896 | tf_op jit(solution)/shard_map/ppermute | solution.py:450
  70.1 8.8 %collective-permute-start.28 = (bf16[9,24,128]{2,1,0:T(8,128)(2,1)S(1)}, bf16[9,24,128]{2,1,0:T(8,128)(2,1)S(1)}, u32[]{:S(2)}, u32[]{:S(2)}) collective-permute-start(bf16[9,24,128]{2,1,0:T(8,128)(2,1)S(1)} %get-tuple-element.93), channel_id=1, source_target_pairs={{0,8},{4,12},{8,0},{12,4},{16,24},{20,28},{24,16},{28,20},{1,9},{5... | collective-permute-start | bytes 165896 | tf_op jit(solution)/shard_map/ppermute | solution.py:450
  70.2 8.7 %collective-permute-start.29 = (bf16[9,24,128]{2,1,0:T(8,128)(2,1)S(1)}, bf16[9,24,128]{2,1,0:T(8,128)(2,1)S(1)}, u32[]{:S(2)}, u32[]{:S(2)}) collective-permute-start(bf16[9,24,128]{2,1,0:T(8,128)(2,1)S(1)} %get-tuple-element.94), channel_id=1, source_target_pairs={{0,24},{4,28},{8,16},{12,20},{16,8},{20,12},{24,0},{28,4},{1,25},{... | collective-permute-start | bytes 165896 | tf_op jit(solution)/shard_map/ppermute | solution.py:450
  71.3 4.3 %collective-permute-start.27 = (bf16[8,24,128]{2,1,0:T(8,128)(2,1)S(1)}, bf16[8,24,128]{2,1,0:T(8,128)(2,1)S(1)}, u32[]{:S(2)}, u32[]{:S(2)}) collective-permute-start(bf16[8,24,128]{2,1,0:T(8,128)(2,1)S(1)} %get-tuple-element.92), channel_id=1, source_target_pairs={{0,4},{4,0},{8,12},{12,8},{16,20},{20,16},{24,28},{28,24},{1,5},{5... | collective-permute-start | bytes 147464 | tf_op jit(solution)/shard_map/ppermute | solution.py:450
  72.1 6.8 %collective-permute-start.30 = (bf16[8,24,128]{2,1,0:T(8,128)(2,1)S(1)}, bf16[8,24,128]{2,1,0:T(8,128)(2,1)S(1)}, u32[]{:S(2)}, u32[]{:S(2)}) collective-permute-start(bf16[8,24,128]{2,1,0:T(8,128)(2,1)S(1)} %get-tuple-element.95), channel_id=1, source_target_pairs={{0,28},{4,8},{8,4},{12,16},{16,12},{20,24},{24,20},{28,0},{1,29},{... | collective-permute-start | bytes 147464 | tf_op jit(solution)/shard_map/ppermute | solution.py:450
  79.0 1.9 %collective-permute-start.31 = (bf16[9,24,128]{2,1,0:T(8,128)(2,1)S(1)}, bf16[9,24,128]{2,1,0:T(8,128)(2,1)S(1)}, u32[]{:S(2)}, u32[]{:S(2)}) collective-permute-start(bf16[9,24,128]{2,1,0:T(8,128)(2,1)S(1)} %get-tuple-element.99), channel_id=1, source_target_pairs={{0,1},{1,0},{2,3},{3,2},{4,5},{5,4},{6,7},{7,6},{8,9},{9,8},{10,11... | collective-permute-start | bytes 165896 | tf_op jit(solution)/shard_map/ppermute | solution.py:456
  79.1 4.6 %collective-permute-start.32 = (bf16[9,24,128]{2,1,0:T(8,128)(2,1)S(1)}, bf16[9,24,128]{2,1,0:T(8,128)(2,1)S(1)}, u32[]{:S(2)}, u32[]{:S(2)}) collective-permute-start(bf16[9,24,128]{2,1,0:T(8,128)(2,1)S(1)} %get-tuple-element.100), channel_id=1, source_target_pairs={{0,2},{1,3},{2,0},{3,1},{4,6},{5,7},{6,4},{7,5},{8,10},{9,11},{10,... | collective-permute-start | bytes 165896 | tf_op jit(solution)/shard_map/ppermute | solution.py:456
  80.0 4.2 %collective-permute-start.33 = (bf16[9,24,128]{2,1,0:T(8,128)(2,1)S(1)}, bf16[9,24,128]{2,1,0:T(8,128)(2,1)S(1)}, u32[]{:S(2)}, u32[]{:S(2)}) collective-permute-start(bf16[9,24,128]{2,1,0:T(8,128)(2,1)S(1)} %get-tuple-element.101), channel_id=1, source_target_pairs={{0,3},{1,2},{2,1},{3,0},{4,7},{5,6},{6,5},{7,4},{8,11},{9,10},{10,... | collective-permute-start | bytes 165896 | tf_op jit(solution)/shard_map/ppermute | solution.py:456

commit v5 on v4

--- a/solution.py
+++ b/solution.py
@@ -205,13 +205,26 @@
     return jnp.concatenate(rows, axis=0).astype(BF)
 
 
-def first_kernel(z, table, schur, b0, b1, b2, b3, rhs, tables, coarse, o0, o1, o2, o3, wide_out, ext_out, gathered, held, coeffs):
-    g = lax.axis_index("grp")
-    for j, b in enumerate((b0, b1, b2, b3)):
-        gathered[:, pl.ds(pl.multiple_of((g ^ j) * z.rows, z.rows), z.rows)] = b[...]
-    product = lax.dot_general(schur[...], gathered[...], CONTRACT_LAST, preferred_element_type=F32)
-    residual = product[:, : z.rhs] - rhs[...].T
-    held[:, : z.rhs] = residual.astype(BF)
+def block_product(z, schur, block, j):
+    g = lax.axis_index("grp")
+    at = pl.ds(pl.multiple_of((g ^ j) * z.rows, z.rows), z.rows)
+    return lax.dot_general(schur[:, at], block[...], CONTRACT_LAST, preferred_element_type=F32)
+
+
+def early_kernel(z, schur, b0, rhs, out):
+    product = block_product(z, schur, b0, 0)
+    out[:, : z.rhs] = product[:, : z.rhs] - rhs[...].T
+    out[:, z.rhs :] = product[:, z.rhs :]
+
+
+def further_kernel(z, j, schur, block, before, out):
+    out[...] = before[...] + block_product(z, schur, block, j)
+
+
+def first_kernel(z, table, schur, b3, before, tables, coarse, o0, o1, o2, o3, wide_out, ext_out, held, coeffs):
+    g = lax.axis_index("grp")
+    product = before[...] + block_product(z, schur, b3, 3)
+    held[:, : z.rhs] = product[:, : z.rhs].astype(BF)
     width = z.wide - z.rhs
     basis = lax.dot_general(coarse[...], hot_rows(z, table, width, 0), CONTRACT_FIRST, preferred_element_type=F32)
     image = jnp.dot(
@@ -390,10 +403,20 @@
         sums_out[1, :, : z.rhs] = two
 
 
+def prior_kernel(z, tables, earlier, start, out):
+    for i in range(0, z.own, 2):
+        at = slice(i * FPTS, (i + 2) * FPTS)
+        pair = two_blocks(tables[i], tables[i + 1])
+        lifted = lax.dot_general(
+            earlier[i * MODES : (i + 2) * MODES, :], pair, CONTRACT_FIRST, preferred_element_type=F32
+        )
+        out[:, at] = start[:, at] - 0.5 * lifted
+
+
 def last_kernel(z, table, *refs):
     n = z.grps
     shares, refs = refs[:n], refs[n:]
-    tables, coarse, sums, hits, earlier, start, out, averages, whole, gained, done, sems = refs
+    tables, coarse, sums, hits, prior, out, averages, whole, gained, done, sems = refs
     g = lax.axis_index("grp")
     if z.near:
         for j, c in enumerate(shares):
@@ -410,28 +433,28 @@
     shift = jnp.dot(flat, high, preferred_element_type=F32) + jnp.dot(flat, low, preferred_element_type=F32)
     rows = [whole[pl.ds(table[z.t_corner + i], 1), :] for i in range(z.corners)]
     high, low = split_two(jnp.concatenate(rows, axis=0))
-    coarse_corr = lax.dot_general(coarse[...], high, CONTRACT_FIRST, preferred_element_type=F32)
-    coarse_corr = coarse_corr + lax.dot_general(coarse[...], low, CONTRACT_FIRST, preferred_element_type=F32)
+    both = jnp.concatenate([high.astype(F32), low.astype(F32)], axis=0).astype(BF)
+    basis = coarse[...].astype(F32)
+    basis = jnp.concatenate([basis, basis], axis=0).astype(BF)
+    coarse_corr = lax.dot_general(both, basis, CONTRACT_FIRST, preferred_element_type=F32)
     copies = []
-    change = []
-    for i in range(z.own):
-        for j, c in enumerate(shares):
-            averages[i, share_rows(z, g ^ j), :] = from_dense(z, c[i].astype(F32))
-        rows = slice(i * MODES, (i + 1) * MODES)
-        fixed = (averages[i] - 0.5 * shift[rows, :]).astype(BF)
-        both = lax.dot_general(
-            jnp.concatenate([tables[i], tables[i]], axis=0),
-            jnp.concatenate([fixed, earlier[rows, :]], axis=0),
+    for i in range(0, z.own, 2):
+        fixed = []
+        for f in (i, i + 1):
+            for j, c in enumerate(shares):
+                averages[f, share_rows(z, g ^ j), :] = from_dense(z, c[f].astype(F32))
+            fixed.append(averages[f] - 0.5 * shift[f * MODES : (f + 1) * MODES, :])
+        lifted = lax.dot_general(
+            jnp.concatenate(fixed, axis=0).astype(BF),
+            two_blocks(tables[i], tables[i + 1]),
             CONTRACT_FIRST,
             preferred_element_type=F32,
         )
-        change.append(both + coarse_corr[i * FPTS : (i + 1) * FPTS, :])
-        if i % 2:
-            at = pl.ds((i - 1) * FPTS, 2 * FPTS)
-            done[:, at] = start[:, at] - 0.5 * jnp.concatenate(change, axis=0).T
-            copies.append(pltpu.make_async_copy(done.at[:, at], out.at[:, at], sems.at[i // 2]))
-            copies[-1].start()
-            change = []
+        at = slice(i * FPTS, (i + 2) * FPTS)
+        done[:, at] = prior[:, at] - 0.5 * (lifted + coarse_corr[:, at])
+        at = pl.ds(i * FPTS, 2 * FPTS)
+        copies.append(pltpu.make_async_copy(done.at[:, at], out.at[:, at], sems.at[i // 2]))
+        copies[-1].start()
     for c in copies:
         c.wait()
 
@@ -456,12 +479,6 @@
     return lax.ppermute(value, "grp", [(s, s ^ mask) for s in range(count)])
 
 
-def hypercube(value):
-    two = swapped(value, 2)
-    one = swapped(value, 1)
-    return [value, one, two, swapped(two, 1)]
-
-
 def exchanged(blocks):
     return [blocks[0]] + [swapped(blocks[j], j) for j in range(1, len(blocks))]
 
@@ -485,7 +502,6 @@
         compiler_params=pltpu.CompilerParams(vmem_limit_bytes=16 << 20),
     )(*[pltpu.with_memory_space_constraint(a, pltpu.HBM) for a in (first, coarse_basis[0])])
     block_two = swapped(trace_b, 2)
-    pair_two = swapped(project[0], 2)
     block_one = swapped(trace_b, 1)
 
     table = pl.pallas_call(
@@ -509,7 +525,12 @@
         compiler_params=pltpu.CompilerParams(vmem_limit_bytes=4 << 20),
     )(*[pltpu.with_memory_space_constraint(a, pltpu.HBM) for a in (*loaded, project[0])])
     block_three = swapped(block_two, 1)
-    blocks = [trace_b, block_one, block_two, block_three]
+    begun_shape = shape((z.rows, z.rhs + z.corners), F32)
+    begun = call(early_kernel, z, begun_shape, (matrix, trace_b, target))
+    begun, table, raw = lax.optimization_barrier((begun, table, project[0]))
+    pair_two = swapped(raw, 2)
+    begun = call(further_kernel, z, begun_shape, (matrix, block_one, begun), (), (1,))
+    begun = call(further_kernel, z, begun_shape, (matrix, block_two, begun), (), (2,))
 
     width = z.wide - z.rhs
     part = shape((z.own, z.share, z.wide), BF)
@@ -523,9 +544,8 @@
         first_kernel,
         z,
         [part] * grps + [shape((z.own * MODES, z.rhs), F32), shape((z.own, MODES, width), BF)],
-        (table, matrix, *blocks, target, own_tables, coarse),
+        (table, matrix, block_three, begun, own_tables, coarse),
         (
-            pltpu.VMEM((z.rhs + z.corners, z.all_rows), BF),
             pltpu.VMEM((z.rows, z.wide), BF),
             pltpu.VMEM((z.own, MODES, z.wide), BF),
         ),
@@ -534,11 +554,10 @@
     part_two = swapped(parts[2], 2)
     part_three = swapped(parts[3], 3)
     parts = [parts[0], part_one, part_two, part_three]
-    pair_one = swapped(project[0], 1)
-    pair_three = swapped(pair_two, 1)
     outgoing = call(pack_kernel, z, [link] * LINKS, (table, *parts), (pltpu.VMEM((z.faces, z.share, z.wide), BF),), (False,))
     arrived = paired(outgoing)
-    arrived, pair_one, pair_two, pair_three = lax.optimization_barrier((arrived, pair_one, pair_two, pair_three))
+    pair_one = swapped(raw, 1)
+    arrived, pair_one, pair_two = lax.optimization_barrier((arrived, pair_one, pair_two))
     replies = call(
         average_kernel,
         z,
@@ -548,6 +567,17 @@
         (False,),
     )
     answered = paired(replies)
+    pair_three = swapped(pair_two, 1)
+    answered, pair_three = lax.optimization_barrier((answered, pair_three))
+    spread = call(
+        spread_first,
+        z,
+        shape((z.packed, z.share, z.lanes), BF),
+        (table, *answered),
+        (pltpu.VMEM((SLOTS, z.share, z.wide), BF),),
+    )
+    spread_two = swapped(spread, 2)
+    shares = [spread, swapped(spread, 1), spread_two, swapped(spread_two, 1)]
     mixed = call(
         mix_kernel,
         z,
@@ -555,14 +585,6 @@
         (matrix, own_tables, pair_one, pair_two, pair_three),
         (pltpu.VMEM((z.rows, z.all_rows), BF), pltpu.VMEM((z.own * MODES // 2, 2 * FPTS), F32)),
     )
-    spread = call(
-        spread_first,
-        z,
-        shape((z.packed, z.share, z.lanes), BF),
-        (table, *answered),
-        (pltpu.VMEM((SLOTS, z.share, z.wide), BF),),
-    )
-    shares = hypercube(spread)
     *parts, earlier, hits, sums = call(
         second_kernel,
         z,
@@ -599,8 +621,10 @@
         (table, *answered, *results[LINKS:]),
         (pltpu.VMEM((SLOTS, z.dense, z.lanes), BF),),
     )
-    shares = exchanged(outs)
-    inputs = (table, *shares, own_tables, coarse, sums, hits, earlier, first)
+    last_two = swapped(outs[2], 2)
+    shares = [outs[0], swapped(outs[1], 1), last_two, swapped(outs[3], 3)]
+    prior = call(prior_kernel, z, shape((z.rhs, z.rows), F32), (own_tables, earlier, first))
+    inputs = (table, *shares, own_tables, coarse, sums, hits, prior)
     result = pl.pallas_call(
         functools.partial(last_kernel, z),
         out_shape=pltpu.HBM((z.rhs, z.rows), F32),

time: 85.9 us -> 87.6 us (1.020)
  Pallas kernels: 11.9 us -> 13.5 us
    pallas_call x9 -> x13, Pallas kernels: 5.65 us -> 7.34 us  [call(): pl.pallas_call(functools.partial(kernel, sizes, *static), out_shape=[pltp...]
where the time goes in v5:
time: 87.6 us; the launch traced here: 87.3 us
  waiting for transfers between devices  38.3 us (44%)
  starting transfers between devices  35.3 us (40%)
  Pallas kernels  13.5 us (15%)
    ppermute x16, starting transfers between devices, paired(): met.append(lax.ppermute(blocks[k], 'sub', p))  23.1 us
    ppermute x18, waiting for transfers between devices, swapped(): return lax.ppermute(value, 'grp', [(s, s ^ mask) for s in range(count)])  20 us
    ppermute x16, waiting for transfers between devices, paired(): met.append(lax.ppermute(blocks[k], 'sub', p))  18.3 us
    ppermute x18, starting transfers between devices, swapped(): return lax.ppermute(value, 'grp', [(s, s ^ mask) for s in range(count)])  12.1 us
    pallas_call x13, Pallas kernels, call(): pl.pallas_call(functools.partial(kernel, sizes, *static), out_shape=[pltp...  7.34 us
    pallas_call x1, Pallas kernels, run(): pl.pallas_call(functools.partial(table_kernel, z), out_shape=pltpu.SMEM((...  1.88 us
    pallas_call x1, Pallas kernels, run(): pl.pallas_call(functools.partial(load_kernel, z), out_shape=[pltpu.VMEM(a...  1.81 us
  transfers between devices with their start and end apart: 34, of which 15 were waited for; matrix products, arithmetic and copies ran while one was open for 0% of the time, Pallas kernels for 8%

profile of v5, /device:TPU:0, one launch (start us, length us, event | category | flops | bytes accessed | tf_op | source)
XLA Modules:
  0.0 87.3 jit_solution(2992385342507300727)
XLA Ops:
  0.0 1.1 %shard_map.101.b0 = bf16[200,512]{1,0:T(8,128)(2,1)S(1)} custom-call(f32[192,512]{1,0:T(8,128)} %bitcast.13, bf16[8,512]{1,0:T(8,128)(2,1)} %bitcast.20), custom_call_target="tpu_custom_call" | custom-call | tf_op jit(solution)/shard_map/pallas_call | solution.py:492
  1.1 3.0 %collective-permute-start = (bf16[200,512]{1,0:T(8,128)(2,1)S(1)}, bf16[200,512]{1,0:T(8,128)(2,1)S(1)}, u32[]{:S(2)}, u32[]{:S(2)}) collective-permute-start(bf16[200,512]{1,0:T(8,128)(2,1)S(1)} %shard_map.101.b0), channel_id=1, source_target_pairs={{0,2},{1,3},{2,0},{3,1},{4,6},{5,7},{6,4},{7,5},{8,10},{9,11},{10,... | collective-permute-start | bytes 614408 | tf_op jit(solution)/shard_map/ppermute | solution.py:479
  4.1 5.1 %collective-permute-done.block = bf16[200,512]{1,0:T(8,128)(2,1)S(1)} collective-permute-done((bf16[200,512]{1,0:T(8,128)(2,1)S(1)}, bf16[200,512]{1,0:T(8,128)(2,1)S(1)}, u32[]{:S(2)}, u32[]{:S(2)}) %collective-permute-start) | collective-permute-done | bytes 204832 | tf_op jit(solution)/shard_map/ppermute | solution.py:479
  9.2 1.8 %shard_map.100 = (bf16[512,2048]{1,0:T(8,128)(2,1)S(1)}, f32[192,512]{1,0:T(8,128)S(1)}, bf16[8,512]{1,0:T(8,128)(2,1)S(1)}, bf16[8,64,64]{2,1,0:T(8,128)(2,1)S(1)}) custom-call(bf16[512,2048]{1,0:T(8,128)(2,1)} %bitcast.15, f32[192,512]{1,0:T(8,128)} %bitcast.16, bf16[8,512]{1,0:T(8,128)(2,1)} %bitcast.21, bf16[8,4096]{1,0:T(8,128)(2,1)} %bitcast.17), custom_call_target="tpu_custom_call" | custom-call | tf_op jit(solution)/shard_map/pallas_call | solution.py:515
  11.0 0.3 shard_map.102.before
  11.4 1.9 %shard_map.103.table = s32[152]{0:T(256)S(4)} custom-call(s32[8,1,32]{2,1,0:T(1,128)} %bitcast.22, s32[8,32]{1,0:T(8,128)} %mortar.1, s32[8,16]{1,0:T(8,128)} %order.1, s32[8]{0:T(128)} %smap.1, s32[8,8]{1,0:T(8,128)} %vids.1), custom_call_target="tpu_custom_call" | custom-call | tf_op jit(solution)/shard_map/pallas_call | solution.py:507
  13.3 0.3 shard_map.104.before
  13.6 0.3 shard_map.105.before
  13.9 2.1 %shard_map.106 = (bf16[8,16,256]{2,1,0:T(8,128)(2,1)S(1)}, bf16[8,16,256]{2,1,0:T(8,128)(2,1)S(1)}, bf16[8,16,256]{2,1,0:T(8,128)(2,1)S(1)}, bf16[8,16,256]{2,1,...) custom-call(s32[152]{0:T(256)S(4)} %shard_map.103.table, ...), custom_call_target="tpu_custom_call" | custom-call | tf_op jit(solution)/shard_map/pallas_call | solution.py:73
  16.0 0.5 collective-permute-start.3
  16.6 1.7 %collective-permute-start.4 = (bf16[8,16,256]{2,1,0:T(8,128)(2,1)S(1)}, bf16[8,16,256]{2,1,0:T(8,128)(2,1)S(1)}, u32[]{:S(2)}, u32[]{:S(2)}) collective-permute-start(bf16[8,16,256]{2,1,0:T(8,128)(2,1)S(1)} %get-tuple-element.71), channel_id=1, source_target_pairs={{0,2},{1,3},{2,0},{3,1},{4,6},{5,7},{6,4},{7,5},{8,10},{9,11},{10,... | collective-permute-start | bytes 196616 | tf_op jit(solution)/shard_map/ppermute | solution.py:479
  18.3 1.4 %collective-permute-start.11 = (bf16[8,4096]{1,0:T(8,128)(2,1)S(1)}, bf16[8,4096]{1,0:T(8,128)(2,1)S(1)}, u32[]{:S(2)}, u32[]{:S(2)}) collective-permute-start(bf16[8,4096]{1,0:T(8,128)(2,1)S(1)} %bitcast.18), channel_id=1, source_target_pairs={{0,2},{1,3},{2,0},{3,1},{4,6},{5,7},{6,4},{7,5},{8,10},{9,11},{10,... | collective-permute-start | bytes 196616 | tf_op jit(solution)/shard_map/ppermute | solution.py:479
  19.7 0.4 collective-permute-start.10
  20.2 0.6 collective-permute-done.4.c2
  20.8 1.9 %collective-permute-done.5.c3 = bf16[8,16,256]{2,1,0:T(8,128)(2,1)S(1)} collective-permute-done((bf16[8,16,256]{2,1,0:T(8,128)(2,1)S(1)}, bf16[8,16,256]{2,1,0:T(8,128)(2,1)S(1)}, u32[]{:S(2)}, u32[]{:S(2)}) %collective-permute-start.5) | collective-permute-done | bytes 65568 | tf_op jit(solution)/shard_map/ppermute | solution.py:479
  22.8 1.6 %collective-permute-start.6 = (bf16[8,16,256]{2,1,0:T(8,128)(2,1)S(1)}, bf16[8,16,256]{2,1,0:T(8,128)(2,1)S(1)}, u32[]{:S(2)}, u32[]{:S(2)}) collective-permute-start(bf16[8,16,256]{2,1,0:T(8,128)(2,1)S(1)} %get-tuple-element.73), channel_id=1, source_target_pairs={{0,4},{4,0},{8,12},{12,8},{16,20},{20,16},{24,28},{28,24},{1,5},{5... | collective-permute-start | bytes 196616 | tf_op jit(solution)/shard_map/ppermute | solution.py:473
  24.3 1.6 %collective-permute-start.7 = (bf16[8,16,256]{2,1,0:T(8,128)(2,1)S(1)}, bf16[8,16,256]{2,1,0:T(8,128)(2,1)S(1)}, u32[]{:S(2)}, u32[]{:S(2)}) collective-permute-start(bf16[8,16,256]{2,1,0:T(8,128)(2,1)S(1)} %get-tuple-element.74), channel_id=1, source_target_pairs={{0,8},{4,12},{8,0},{12,4},{16,24},{20,28},{24,16},{28,20},{1,9},{5... | collective-permute-start | bytes 196616 | tf_op jit(solution)/shard_map/ppermute | solution.py:473
  25.9 2.5 %collective-permute-start.8 = (bf16[8,16,256]{2,1,0:T(8,128)(2,1)S(1)}, bf16[8,16,256]{2,1,0:T(8,128)(2,1)S(1)}, u32[]{:S(2)}, u32[]{:S(2)}) collective-permute-start(bf16[8,16,256]{2,1,0:T(8,128)(2,1)S(1)} %get-tuple-element.75), channel_id=1, source_target_pairs={{0,24},{4,28},{8,16},{12,20},{16,8},{20,12},{24,0},{28,4},{1,25},{... | collective-permute-start | bytes 196616 | tf_op jit(solution)/shard_map/ppermute | solution.py:473
  28.4 1.3 %collective-permute-start.9 = (bf16[8,16,256]{2,1,0:T(8,128)(2,1)S(1)}, bf16[8,16,256]{2,1,0:T(8,128)(2,1)S(1)}, u32[]{:S(2)}, u32[]{:S(2)}) collective-permute-start(bf16[8,16,256]{2,1,0:T(8,128)(2,1)S(1)} %get-tuple-element.76), channel_id=1, source_target_pairs={{0,28},{4,8},{8,4},{12,16},{16,12},{20,24},{24,20},{28,0},{1,29},{... | collective-permute-start | bytes 196616 | tf_op jit(solution)/shard_map/ppermute | solution.py:473
  29.7 3.0 %collective-permute-done.8.refs_2_ = bf16[8,16,256]{2,1,0:T(8,128)(2,1)S(1)} collective-permute-done((bf16[8,16,256]{2,1,0:T(8,128)(2,1)S(1)}, bf16[8,16,256]{2,1,0:T(8,128)(2,1)S(1)}, u32[]{:S(2)}, u32[]{:S(2)}) %collective-permute-start.8) | collective-permute-done | bytes 65568 | tf_op jit(solution)/shard_map/ppermute | solution.py:473
  32.7 2.6 %collective-permute-done.9.refs_3_ = bf16[8,16,256]{2,1,0:T(8,128)(2,1)S(1)} collective-permute-done((bf16[8,16,256]{2,1,0:T(8,128)(2,1)S(1)}, bf16[8,16,256]{2,1,0:T(8,128)(2,1)S(1)}, u32[]{:S(2)}, u32[]{:S(2)}) %collective-permute-start.9) | collective-permute-done | bytes 65568 | tf_op jit(solution)/shard_map/ppermute | solution.py:473
  35.4 0.3 shard_map.108
  35.8 1.8 %collective-permute-start.14 = (bf16[8,16,256]{2,1,0:T(8,128)(2,1)S(1)}, bf16[8,16,256]{2,1,0:T(8,128)(2,1)S(1)}, u32[]{:S(2)}, u32[]{:S(2)}) collective-permute-start(bf16[8,16,256]{2,1,0:T(8,128)(2,1)S(1)} %get-tuple-element.88), channel_id=1, source_target_pairs={{0,24},{4,28},{8,16},{12,20},{16,8},{20,12},{24,0},{28,4},{1,25},{... | collective-permute-start | bytes 196616 | tf_op jit(solution)/shard_map/ppermute | solution.py:473
  37.6 3.4 %collective-permute-start.15 = (bf16[8,16,256]{2,1,0:T(8,128)(2,1)S(1)}, bf16[8,16,256]{2,1,0:T(8,128)(2,1)S(1)}, u32[]{:S(2)}, u32[]{:S(2)}) collective-permute-start(bf16[8,16,256]{2,1,0:T(8,128)(2,1)S(1)} %get-tuple-element.89), channel_id=1, source_target_pairs={{0,28},{4,8},{8,4},{12,16},{16,12},{20,24},{24,20},{28,0},{1,29},{... | collective-permute-start | bytes 196616 | tf_op jit(solution)/shard_map/ppermute | solution.py:473
  41.0 1.3 %collective-permute-done.14.refs_2_ = bf16[8,16,256]{2,1,0:T(8,128)(2,1)S(1)} collective-permute-done((bf16[8,16,256]{2,1,0:T(8,128)(2,1)S(1)}, bf16[8,16,256]{2,1,0:T(8,128)(2,1)S(1)}, u32[]{:S(2)}, u32[]{:S(2)}) %collective-permute-start.14) | collective-permute-done | bytes 65568 | tf_op jit(solution)/shard_map/ppermute | solution.py:473
  42.3 2.4 %collective-permute-done.15.refs_3_ = bf16[8,16,256]{2,1,0:T(8,128)(2,1)S(1)} collective-permute-done((bf16[8,16,256]{2,1,0:T(8,128)(2,1)S(1)}, bf16[8,16,256]{2,1,0:T(8,128)(2,1)S(1)}, u32[]{:S(2)}, u32[]{:S(2)}) %collective-permute-start.15) | collective-permute-done | bytes 65568 | tf_op jit(solution)/shard_map/ppermute | solution.py:473
  44.9 1.0 %collective-permute-start.18 = (bf16[56,16,128]{2,1,0:T(8,128)(2,1)S(1)}, bf16[56,16,128]{2,1,0:T(8,128)(2,1)S(1)}, u32[]{:S(2)}, u32[]{:S(2)}) collective-permute-start(bf16[56,16,128]{2,1,0:T(8,128)(2,1)S(1)} %shard_map.110.refs_0_), channel_id=1, source_target_pairs={{0,2},{1,3},{2,0},{3,1},{4,6},{5,7},{6,4},{7,5},{8,10},{9,11},{10,... | collective-permute-start | bytes 688136 | tf_op jit(solution)/shard_map/ppermute | solution.py:479
  45.9 6.0 %collective-permute-done.18.refs_2_ = bf16[56,16,128]{2,1,0:T(8,128)(2,1)S(1)} collective-permute-done((bf16[56,16,128]{2,1,0:T(8,128)(2,1)S(1)}, bf16[56,16,128]{2,1,0:T(8,128)(2,1)S(1)}, u32[]{:S(2)}, u32[]{:S(2)}) %collective-permute-start.18) | collective-permute-done | bytes 229408 | tf_op jit(solution)/shard_map/ppermute | solution.py:479
  51.9 1.9 %shard_map.109.mixed = bf16[512,2048]{1,0:T(8,128)(2,1)S(1)} custom-call(bf16[512,2048]{1,0:T(8,128)(2,1)S(1)} %get-tuple-element.63.schur, bf16[8,64,64]{2,1,0:T(8,128)(2,1)S(1)} %get-tuple-element.66.tables.t0.refs_4_, bf16[8,4096]{1,0:T(8,128)(2,1)S(1)} %collective-permute-done.10.r1, bf16[8,4096]{1,0:T(8,128)(2,1)S(1)} %collective-permute-done.11.r2, ...), custom_call_target="tpu_custom_call" | custom-call | tf_op jit(solution)/shard_map/pallas_call | solution.py:73
  53.8 1.3 %shard_map.111 = (bf16[9,24,128]{2,1,0:T(8,128)(2,1)S(1)}, bf16[9,24,128]{2,1,0:T(8,128)(2,1)S(1)}, bf16[9,24,128]{2,1,0:T(8,128)(2,1)S(1)}, bf16[9,24,128]{2,1,...) custom-call(s32[152]{0:T(256)S(4)} %shard_map.103.table, ...), custom_call_target="tpu_custom_call" | custom-call | tf_op jit(solution)/shard_map/pallas_call | solution.py:73
  55.1 0.6 collective-permute-start.20
  55.7 0.3 collective-permute-start.21
  56.0 1.1 %collective-permute-start.22 = (bf16[9,24,128]{2,1,0:T(8,128)(2,1)S(1)}, bf16[9,24,128]{2,1,0:T(8,128)(2,1)S(1)}, u32[]{:S(2)}, u32[]{:S(2)}) collective-permute-start(bf16[9,24,128]{2,1,0:T(8,128)(2,1)S(1)} %get-tuple-element.102), channel_id=1, source_target_pairs={{0,3},{1,2},{2,1},{3,0},{4,7},{5,6},{6,5},{7,4},{8,11},{9,10},{10,... | collective-permute-start | bytes 165896 | tf_op jit(solution)/shard_map/ppermute | solution.py:479
  57.1 3.1 %collective-permute-done.21.c2 = bf16[9,24,128]{2,1,0:T(8,128)(2,1)S(1)} collective-permute-done((bf16[9,24,128]{2,1,0:T(8,128)(2,1)S(1)}, bf16[9,24,128]{2,1,0:T(8,128)(2,1)S(1)}, u32[]{:S(2)}, u32[]{:S(2)}) %collective-permute-start.21) | collective-permute-done | bytes 55328 | tf_op jit(solution)/shard_map/ppermute | solution.py:479
  60.2 1.1 %collective-permute-start.23 = (bf16[9,24,128]{2,1,0:T(8,128)(2,1)S(1)}, bf16[9,24,128]{2,1,0:T(8,128)(2,1)S(1)}, u32[]{:S(2)}, u32[]{:S(2)}) collective-permute-start(bf16[9,24,128]{2,1,0:T(8,128)(2,1)S(1)} %get-tuple-element.103), channel_id=1, source_target_pairs={{0,4},{4,0},{8,12},{12,8},{16,20},{20,16},{24,28},{28,24},{1,5},{5... | collective-permute-start | bytes 165896 | tf_op jit(solution)/shard_map/ppermute | solution.py:473
  61.4 1.0 %collective-permute-start.24 = (bf16[9,24,128]{2,1,0:T(8,128)(2,1)S(1)}, bf16[9,24,128]{2,1,0:T(8,128)(2,1)S(1)}, u32[]{:S(2)}, u32[]{:S(2)}) collective-permute-start(bf16[9,24,128]{2,1,0:T(8,128)(2,1)S(1)} %get-tuple-element.104), channel_id=1, source_target_pairs={{0,8},{4,12},{8,0},{12,4},{16,24},{20,28},{24,16},{28,20},{1,9},{5... | collective-permute-start | bytes 165896 | tf_op jit(solution)/shard_map/ppermute | solution.py:473
  62.4 1.4 %collective-permute-start.25 = (bf16[9,24,128]{2,1,0:T(8,128)(2,1)S(1)}, bf16[9,24,128]{2,1,0:T(8,128)(2,1)S(1)}, u32[]{:S(2)}, u32[]{:S(2)}) collective-permute-start(bf16[9,24,128]{2,1,0:T(8,128)(2,1)S(1)} %get-tuple-element.105), channel_id=1, source_target_pairs={{0,24},{4,28},{8,16},{12,20},{16,8},{20,12},{24,0},{28,4},{1,25},{... | collective-permute-start | bytes 165896 | tf_op jit(solution)/shard_map/ppermute | solution.py:473
  63.8 1.9 %collective-permute-start.26 = (bf16[9,24,128]{2,1,0:T(8,128)(2,1)S(1)}, bf16[9,24,128]{2,1,0:T(8,128)(2,1)S(1)}, u32[]{:S(2)}, u32[]{:S(2)}) collective-permute-start(bf16[9,24,128]{2,1,0:T(8,128)(2,1)S(1)} %get-tuple-element.106), channel_id=1, source_target_pairs={{0,28},{4,8},{8,4},{12,16},{16,12},{20,24},{24,20},{28,0},{1,29},{... | collective-permute-start | bytes 165896 | tf_op jit(solution)/shard_map/ppermute | solution.py:473
  65.7 2.7 %collective-permute-done.25.refs_2_ = bf16[9,24,128]{2,1,0:T(8,128)(2,1)S(1)} collective-permute-done((bf16[9,24,128]{2,1,0:T(8,128)(2,1)S(1)}, bf16[9,24,128]{2,1,0:T(8,128)(2,1)S(1)}, u32[]{:S(2)}, u32[]{:S(2)}) %collective-permute-start.25) | collective-permute-done | bytes 55328 | tf_op jit(solution)/shard_map/ppermute | solution.py:473
  68.4 2.2 %collective-permute-done.26.refs_3_ = bf16[9,24,128]{2,1,0:T(8,128)(2,1)S(1)} collective-permute-done((bf16[9,24,128]{2,1,0:T(8,128)(2,1)S(1)}, bf16[9,24,128]{2,1,0:T(8,128)(2,1)S(1)}, u32[]{:S(2)}, u32[]{:S(2)}) %collective-permute-start.26) | collective-permute-done | bytes 55328 | tf_op jit(solution)/shard_map/ppermute | solution.py:473
  71.0 1.4 %collective-permute-start.29 = (bf16[9,24,128]{2,1,0:T(8,128)(2,1)S(1)}, bf16[9,24,128]{2,1,0:T(8,128)(2,1)S(1)}, u32[]{:S(2)}, u32[]{:S(2)}) collective-permute-start(bf16[9,24,128]{2,1,0:T(8,128)(2,1)S(1)} %get-tuple-element.110), channel_id=1, source_target_pairs={{0,24},{4,28},{8,16},{12,20},{16,8},{20,12},{24,0},{28,4},{1,25},{... | collective-permute-start | bytes 165896 | tf_op jit(solution)/shard_map/ppermute | solution.py:473
  72.4 1.1 %collective-permute-start.27 = (bf16[8,24,128]{2,1,0:T(8,128)(2,1)S(1)}, bf16[8,24,128]{2,1,0:T(8,128)(2,1)S(1)}, u32[]{:S(2)}, u32[]{:S(2)}) collective-permute-start(bf16[8,24,128]{2,1,0:T(8,128)(2,1)S(1)} %get-tuple-element.108), channel_id=1, source_target_pairs={{0,4},{4,0},{8,12},{12,8},{16,20},{20,16},{24,28},{28,24},{1,5},{5... | collective-permute-start | bytes 147464 | tf_op jit(solution)/shard_map/ppermute | solution.py:473
  73.5 2.8 %collective-permute-start.30 = (bf16[8,24,128]{2,1,0:T(8,128)(2,1)S(1)}, bf16[8,24,128]{2,1,0:T(8,128)(2,1)S(1)}, u32[]{:S(2)}, u32[]{:S(2)}) collective-permute-start(bf16[8,24,128]{2,1,0:T(8,128)(2,1)S(1)} %get-tuple-element.111), channel_id=1, source_target_pairs={{0,28},{4,8},{8,4},{12,16},{16,12},{20,24},{24,20},{28,0},{1,29},{... | collective-permute-start | bytes 147464 | tf_op jit(solution)/shard_map/ppermute | solution.py:473
  76.5 3.8 %collective-permute-done.30.refs_3_ = bf16[8,24,128]{2,1,0:T(8,128)(2,1)S(1)} collective-permute-done((bf16[8,24,128]{2,1,0:T(8,128)(2,1)S(1)}, bf16[8,24,128]{2,1,0:T(8,128)(2,1)S(1)}, u32[]{:S(2)}, u32[]{:S(2)}) %collective-permute-start.30) | collective-permute-done | bytes 49184 | tf_op jit(solution)/shard_map/ppermute | solution.py:473
  80.5 1.7 %collective-permute-start.32 = (bf16[9,24,128]{2,1,0:T(8,128)(2,1)S(1)}, bf16[9,24,128]{2,1,0:T(8,128)(2,1)S(1)}, u32[]{:S(2)}, u32[]{:S(2)}) collective-permute-start(bf16[9,24,128]{2,1,0:T(8,128)(2,1)S(1)} %get-tuple-element.116), channel_id=1, source_target_pairs={{0,2},{1,3},{2,0},{3,1},{4,6},{5,7},{6,4},{7,5},{8,10},{9,11},{10,... | collective-permute-start | bytes 165896 | tf_op jit(solution)/shard_map/ppermute | solution.py:479
  82.6 2.1 %collective-permute-done.32.refs_2_ = bf16[9,24,128]{2,1,0:T(8,128)(2,1)S(1)} collective-permute-done((bf16[9,24,128]{2,1,0:T(8,128)(2,1)S(1)}, bf16[9,24,128]{2,1,0:T(8,128)(2,1)S(1)}, u32[]{:S(2)}, u32[]{:S(2)}) %collective-permute-start.32) | collective-permute-done | bytes 55328 | tf_op jit(solution)/shard_map/ppermute | solution.py:479
  84.7 1.2 %collective-permute-done.33.refs_3_ = bf16[9,24,128]{2,1,0:T(8,128)(2,1)S(1)} collective-permute-done((bf16[9,24,128]{2,1,0:T(8,128)(2,1)S(1)}, bf16[9,24,128]{2,1,0:T(8,128)(2,1)S(1)}, u32[]{:S(2)}, u32[]{:S(2)}) %collective-permute-start.33) | collective-permute-done | bytes 55328 | tf_op jit(solution)/shard_map/ppermute | solution.py:479
  86.0 1.4 %shard_map.116 = f32[192,512]{1,0:T(8,128)} custom-call(s32[152]{0:T(256)S(4)} %shard_map.103.table, bf16[9,24,128]{2,1,0:T(8,128)(2,1)S(1)} %get-tuple-element.114.refs_0_, bf16[9,24,128]{2,1,0:T(8,128)(2,1)S(1)} %collective-permute-done.31.refs_1_, bf16[9,24,128]{2,1,0:T(8,128)(2,1)S(1)} %collective-permute-done.32.refs_2_, ...), custom_call_target="tpu_custom_call" | custom-call | tf_op jit(solution)/shard_map/pallas_call | solution.py:628
  (41 shorter events, 1.5 us)
Async XLA Ops:
  1.1 8.1 %collective-permute-start = (bf16[200,512]{1,0:T(8,128)(2,1)S(1)}, bf16[200,512]{1,0:T(8,128)(2,1)S(1)}, u32[]{:S(2)}, u32[]{:S(2)}) collective-permute-start(bf16[200,512]{1,0:T(8,128)(2,1)S(1)} %shard_map.101.b0), channel_id=1, source_target_pairs={{0,2},{1,3},{2,0},{3,1},{4,6},{5,7},{6,4},{7,5},{8,10},{9,11},{10,... | collective-permute-start | bytes 614408 | tf_op jit(solution)/shard_map/ppermute | solution.py:479
  4.1 9.1 %collective-permute-start.2 = (bf16[200,512]{1,0:T(8,128)(2,1)S(1)}, bf16[200,512]{1,0:T(8,128)(2,1)S(1)}, u32[]{:S(2)}, u32[]{:S(2)}) collective-permute-start(bf16[200,512]{1,0:T(8,128)(2,1)S(1)} %shard_map.101.b0), channel_id=1, source_target_pairs={{0,1},{1,0},{2,3},{3,2},{4,5},{5,4},{6,7},{7,6},{8,9},{9,8},{10,11... | collective-permute-start | bytes 614408 | tf_op jit(solution)/shard_map/ppermute | solution.py:479
  9.2 4.7 %collective-permute-start.1 = (bf16[200,512]{1,0:T(8,128)(2,1)S(1)}, bf16[200,512]{1,0:T(8,128)(2,1)}, u32[]{:S(2)}, u32[]{:S(2)}) collective-permute-start(bf16[200,512]{1,0:T(8,128)(2,1)S(1)} %collective-permute-done.block), channel_id=1, source_target_pairs={{0,1},{1,0},{2,3},{3,2},{4,5},{5,4},{6,7},{7,6},{8,9},{9,8},{10,11... | collective-permute-start | bytes 614408 | tf_op jit(solution)/shard_map/ppermute | solution.py:479
  13.9 4.4 %copy-start.1 = (bf16[1,8,4096]{2,1,0:T(8,128)(2,1)S(1)}, bf16[1,8,4096]{2,1,0:T(8,128)(2,1)}, u32[]{:S(2)}) copy-start(bf16[1,8,4096]{2,1,0:T(8,128)(2,1)} %param.13) | copy-start | bytes 196612
  16.0 4.2 %collective-permute-start.3 = (bf16[8,16,256]{2,1,0:T(8,128)(2,1)S(1)}, bf16[8,16,256]{2,1,0:T(8,128)(2,1)S(1)}, u32[]{:S(2)}, u32[]{:S(2)}) collective-permute-start(bf16[8,16,256]{2,1,0:T(8,128)(2,1)S(1)} %get-tuple-element.70), channel_id=1, source_target_pairs={{0,1},{1,0},{2,3},{3,2},{4,5},{5,4},{6,7},{7,6},{8,9},{9,8},{10,11... | collective-permute-start | bytes 196616 | tf_op jit(solution)/shard_map/ppermute | solution.py:479
  16.6 4.3 %collective-permute-start.4 = (bf16[8,16,256]{2,1,0:T(8,128)(2,1)S(1)}, bf16[8,16,256]{2,1,0:T(8,128)(2,1)S(1)}, u32[]{:S(2)}, u32[]{:S(2)}) collective-permute-start(bf16[8,16,256]{2,1,0:T(8,128)(2,1)S(1)} %get-tuple-element.71), channel_id=1, source_target_pairs={{0,2},{1,3},{2,0},{3,1},{4,6},{5,7},{6,4},{7,5},{8,10},{9,11},{10,... | collective-permute-start | bytes 196616 | tf_op jit(solution)/shard_map/ppermute | solution.py:479
  18.3 4.4 %collective-permute-start.5 = (bf16[8,16,256]{2,1,0:T(8,128)(2,1)S(1)}, bf16[8,16,256]{2,1,0:T(8,128)(2,1)S(1)}, u32[]{:S(2)}, u32[]{:S(2)}) collective-permute-start(bf16[8,16,256]{2,1,0:T(8,128)(2,1)S(1)} %get-tuple-element.72), channel_id=1, source_target_pairs={{0,3},{1,2},{2,1},{3,0},{4,7},{5,6},{6,5},{7,4},{8,11},{9,10},{10,... | collective-permute-start | bytes 196616 | tf_op jit(solution)/shard_map/ppermute | solution.py:479
  18.3 10.1 %collective-permute-start.11 = (bf16[8,4096]{1,0:T(8,128)(2,1)S(1)}, bf16[8,4096]{1,0:T(8,128)(2,1)S(1)}, u32[]{:S(2)}, u32[]{:S(2)}) collective-permute-start(bf16[8,4096]{1,0:T(8,128)(2,1)S(1)} %bitcast.18), channel_id=1, source_target_pairs={{0,2},{1,3},{2,0},{3,1},{4,6},{5,7},{6,4},{7,5},{8,10},{9,11},{10,... | collective-permute-start | bytes 196616 | tf_op jit(solution)/shard_map/ppermute | solution.py:479
  19.7 10.0 %collective-permute-start.10 = (bf16[8,4096]{1,0:T(8,128)(2,1)S(1)}, bf16[8,4096]{1,0:T(8,128)(2,1)S(1)}, u32[]{:S(2)}, u32[]{:S(2)}) collective-permute-start(bf16[8,4096]{1,0:T(8,128)(2,1)S(1)} %bitcast.19), channel_id=1, source_target_pairs={{0,1},{1,0},{2,3},{3,2},{4,5},{5,4},{6,7},{7,6},{8,9},{9,8},{10,11... | collective-permute-start | bytes 196616 | tf_op jit(solution)/shard_map/ppermute | solution.py:479
  22.8 6.9 %collective-permute-start.6 = (bf16[8,16,256]{2,1,0:T(8,128)(2,1)S(1)}, bf16[8,16,256]{2,1,0:T(8,128)(2,1)S(1)}, u32[]{:S(2)}, u32[]{:S(2)}) collective-permute-start(bf16[8,16,256]{2,1,0:T(8,128)(2,1)S(1)} %get-tuple-element.73), channel_id=1, source_target_pairs={{0,4},{4,0},{8,12},{12,8},{16,20},{20,16},{24,28},{28,24},{1,5},{5... | collective-permute-start | bytes 196616 | tf_op jit(solution)/shard_map/ppermute | solution.py:473
  24.3 5.4 %collective-permute-start.7 = (bf16[8,16,256]{2,1,0:T(8,128)(2,1)S(1)}, bf16[8,16,256]{2,1,0:T(8,128)(2,1)S(1)}, u32[]{:S(2)}, u32[]{:S(2)}) collective-permute-start(bf16[8,16,256]{2,1,0:T(8,128)(2,1)S(1)} %get-tuple-element.74), channel_id=1, source_target_pairs={{0,8},{4,12},{8,0},{12,4},{16,24},{20,28},{24,16},{28,20},{1,9},{5... | collective-permute-start | bytes 196616 | tf_op jit(solution)/shard_map/ppermute | solution.py:473
  25.9 6.8 %collective-permute-start.8 = (bf16[8,16,256]{2,1,0:T(8,128)(2,1)S(1)}, bf16[8,16,256]{2,1,0:T(8,128)(2,1)S(1)}, u32[]{:S(2)}, u32[]{:S(2)}) collective-permute-start(bf16[8,16,256]{2,1,0:T(8,128)(2,1)S(1)} %get-tuple-element.75), channel_id=1, source_target_pairs={{0,24},{4,28},{8,16},{12,20},{16,8},{20,12},{24,0},{28,4},{1,25},{... | collective-permute-start | bytes 196616 | tf_op jit(solution)/shard_map/ppermute | solution.py:473
  28.4 7.0 %collective-permute-start.9 = (bf16[8,16,256]{2,1,0:T(8,128)(2,1)S(1)}, bf16[8,16,256]{2,1,0:T(8,128)(2,1)S(1)}, u32[]{:S(2)}, u32[]{:S(2)}) collective-permute-start(bf16[8,16,256]{2,1,0:T(8,128)(2,1)S(1)} %get-tuple-element.76), channel_id=1, source_target_pairs={{0,28},{4,8},{8,4},{12,16},{16,12},{20,24},{24,20},{28,0},{1,29},{... | collective-permute-start | bytes 196616 | tf_op jit(solution)/shard_map/ppermute | solution.py:473
  35.4 5.7 %collective-permute-start.16 = (bf16[8,4096]{1,0:T(8,128)(2,1)S(1)}, bf16[8,4096]{1,0:T(8,128)(2,1)S(1)}, u32[]{:S(2)}, u32[]{:S(2)}) collective-permute-start(bf16[8,4096]{1,0:T(8,128)(2,1)S(1)} %collective-permute-done.11.r2), channel_id=1, source_target_pairs={{0,1},{1,0},{2,3},{3,2},{4,5},{5,4},{6,7},{7,6},{8,9},{9,8},{10,11... | collective-permute-start | bytes 196616 | tf_op jit(solution)/shard_map/ppermute | solution.py:479
  35.7 5.4 %collective-permute-start.12 = (bf16[8,16,256]{2,1,0:T(8,128)(2,1)S(1)}, bf16[8,16,256]{2,1,0:T(8,128)(2,1)S(1)}, u32[]{:S(2)}, u32[]{:S(2)}) collective-permute-start(bf16[8,16,256]{2,1,0:T(8,128)(2,1)S(1)} %get-tuple-element.86), channel_id=1, source_target_pairs={{0,4},{4,0},{8,12},{12,8},{16,20},{20,16},{24,28},{28,24},{1,5},{5... | collective-permute-start | bytes 196616 | tf_op jit(solution)/shard_map/ppermute | solution.py:473
  35.7 5.3 %collective-permute-start.13 = (bf16[8,16,256]{2,1,0:T(8,128)(2,1)S(1)}, bf16[8,16,256]{2,1,0:T(8,128)(2,1)S(1)}, u32[]{:S(2)}, u32[]{:S(2)}) collective-permute-start(bf16[8,16,256]{2,1,0:T(8,128)(2,1)S(1)} %get-tuple-element.87), channel_id=1, source_target_pairs={{0,8},{4,12},{8,0},{12,4},{16,24},{20,28},{24,16},{28,20},{1,9},{5... | collective-permute-start | bytes 196616 | tf_op jit(solution)/shard_map/ppermute | solution.py:473
  35.8 6.5 %collective-permute-start.14 = (bf16[8,16,256]{2,1,0:T(8,128)(2,1)S(1)}, bf16[8,16,256]{2,1,0:T(8,128)(2,1)S(1)}, u32[]{:S(2)}, u32[]{:S(2)}) collective-permute-start(bf16[8,16,256]{2,1,0:T(8,128)(2,1)S(1)} %get-tuple-element.88), channel_id=1, source_target_pairs={{0,24},{4,28},{8,16},{12,20},{16,8},{20,12},{24,0},{28,4},{1,25},{... | collective-permute-start | bytes 196616 | tf_op jit(solution)/shard_map/ppermute | solution.py:473
  37.6 7.1 %collective-permute-start.15 = (bf16[8,16,256]{2,1,0:T(8,128)(2,1)S(1)}, bf16[8,16,256]{2,1,0:T(8,128)(2,1)S(1)}, u32[]{:S(2)}, u32[]{:S(2)}) collective-permute-start(bf16[8,16,256]{2,1,0:T(8,128)(2,1)S(1)} %get-tuple-element.89), channel_id=1, source_target_pairs={{0,28},{4,8},{8,4},{12,16},{16,12},{20,24},{24,20},{28,0},{1,29},{... | collective-permute-start | bytes 196616 | tf_op jit(solution)/shard_map/ppermute | solution.py:473
  44.9 7.0 %collective-permute-start.18 = (bf16[56,16,128]{2,1,0:T(8,128)(2,1)S(1)}, bf16[56,16,128]{2,1,0:T(8,128)(2,1)S(1)}, u32[]{:S(2)}, u32[]{:S(2)}) collective-permute-start(bf16[56,16,128]{2,1,0:T(8,128)(2,1)S(1)} %shard_map.110.refs_0_), channel_id=1, source_target_pairs={{0,2},{1,3},{2,0},{3,1},{4,6},{5,7},{6,4},{7,5},{8,10},{9,11},{10,... | collective-permute-start | bytes 688136 | tf_op jit(solution)/shard_map/ppermute | solution.py:479
  45.9 7.9 %collective-permute-start.17 = (bf16[56,16,128]{2,1,0:T(8,128)(2,1)S(1)}, bf16[56,16,128]{2,1,0:T(8,128)(2,1)S(1)}, u32[]{:S(2)}, u32[]{:S(2)}) collective-permute-start(bf16[56,16,128]{2,1,0:T(8,128)(2,1)S(1)} %shard_map.110.refs_0_), channel_id=1, source_target_pairs={{0,1},{1,0},{2,3},{3,2},{4,5},{5,4},{6,7},{7,6},{8,9},{9,8},{10,11... | collective-permute-start | bytes 688136 | tf_op jit(solution)/shard_map/ppermute | solution.py:479
  51.9 1.9 %collective-permute-start.19 = (bf16[56,16,128]{2,1,0:T(8,128)(2,1)S(1)}, bf16[56,16,128]{2,1,0:T(8,128)(2,1)S(1)}, u32[]{:S(2)}, u32[]{:S(2)}) collective-permute-start(bf16[56,16,128]{2,1,0:T(8,128)(2,1)S(1)} %collective-permute-done.18.refs_2_), channel_id=1, source_target_pairs={{0,1},{1,0},{2,3},{3,2},{4,5},{5,4},{6,7},{7,6},{8,9},{9,8},{10,11... | collective-permute-start | bytes 688136 | tf_op jit(solution)/shard_map/ppermute | solution.py:479
  53.8 28.5 %copy-start = (f32[1,512,192]{1,2,0:T(8,128)S(1)}, f32[1,512,192]{1,2,0:T(8,128)}, u32[]{:S(2)}) copy-start(f32[1,512,192]{1,2,0:T(8,128)} %param.12) | copy-start | bytes 1179652
  55.1 2.0 %collective-permute-start.20 = (bf16[9,24,128]{2,1,0:T(8,128)(2,1)S(1)}, bf16[9,24,128]{2,1,0:T(8,128)(2,1)S(1)}, u32[]{:S(2)}, u32[]{:S(2)}) collective-permute-start(bf16[9,24,128]{2,1,0:T(8,128)(2,1)S(1)} %get-tuple-element.100), channel_id=1, source_target_pairs={{0,1},{1,0},{2,3},{3,2},{4,5},{5,4},{6,7},{7,6},{8,9},{9,8},{10,11... | collective-permute-start | bytes 165896 | tf_op jit(solution)/shard_map/ppermute | solution.py:479
  55.7 4.5 %collective-permute-start.21 = (bf16[9,24,128]{2,1,0:T(8,128)(2,1)S(1)}, bf16[9,24,128]{2,1,0:T(8,128)(2,1)S(1)}, u32[]{:S(2)}, u32[]{:S(2)}) collective-permute-start(bf16[9,24,128]{2,1,0:T(8,128)(2,1)S(1)} %get-tuple-element.101), channel_id=1, source_target_pairs={{0,2},{1,3},{2,0},{3,1},{4,6},{5,7},{6,4},{7,5},{8,10},{9,11},{10,... | collective-permute-start | bytes 165896 | tf_op jit(solution)/shard_map/ppermute | solution.py:479
  56.0 4.2 %collective-permute-start.22 = (bf16[9,24,128]{2,1,0:T(8,128)(2,1)S(1)}, bf16[9,24,128]{2,1,0:T(8,128)(2,1)S(1)}, u32[]{:S(2)}, u32[]{:S(2)}) collective-permute-start(bf16[9,24,128]{2,1,0:T(8,128)(2,1)S(1)} %get-tuple-element.102), channel_id=1, source_target_pairs={{0,3},{1,2},{2,1},{3,0},{4,7},{5,6},{6,5},{7,4},{8,11},{9,10},{10,... | collective-permute-start | bytes 165896 | tf_op jit(solution)/shard_map/ppermute | solution.py:479
  60.2 5.4 %collective-permute-start.23 = (bf16[9,24,128]{2,1,0:T(8,128)(2,1)S(1)}, bf16[9,24,128]{2,1,0:T(8,128)(2,1)S(1)}, u32[]{:S(2)}, u32[]{:S(2)}) collective-permute-start(bf16[9,24,128]{2,1,0:T(8,128)(2,1)S(1)} %get-tuple-element.103), channel_id=1, source_target_pairs={{0,4},{4,0},{8,12},{12,8},{16,20},{20,16},{24,28},{28,24},{1,5},{5... | collective-permute-start | bytes 165896 | tf_op jit(solution)/shard_map/ppermute | solution.py:473
  61.4 4.3 %collective-permute-start.24 = (bf16[9,24,128]{2,1,0:T(8,128)(2,1)S(1)}, bf16[9,24,128]{2,1,0:T(8,128)(2,1)S(1)}, u32[]{:S(2)}, u32[]{:S(2)}) collective-permute-start(bf16[9,24,128]{2,1,0:T(8,128)(2,1)S(1)} %get-tuple-element.104), channel_id=1, source_target_pairs={{0,8},{4,12},{8,0},{12,4},{16,24},{20,28},{24,16},{28,20},{1,9},{5... | collective-permute-start | bytes 165896 | tf_op jit(solution)/shard_map/ppermute | solution.py:473
  62.4 6.1 %collective-permute-start.25 = (bf16[9,24,128]{2,1,0:T(8,128)(2,1)S(1)}, bf16[9,24,128]{2,1,0:T(8,128)(2,1)S(1)}, u32[]{:S(2)}, u32[]{:S(2)}) collective-permute-start(bf16[9,24,128]{2,1,0:T(8,128)(2,1)S(1)} %get-tuple-element.105), channel_id=1, source_target_pairs={{0,24},{4,28},{8,16},{12,20},{16,8},{20,12},{24,0},{28,4},{1,25},{... | collective-permute-start | bytes 165896 | tf_op jit(solution)/shard_map/ppermute | solution.py:473
  63.8 6.9 %collective-permute-start.26 = (bf16[9,24,128]{2,1,0:T(8,128)(2,1)S(1)}, bf16[9,24,128]{2,1,0:T(8,128)(2,1)S(1)}, u32[]{:S(2)}, u32[]{:S(2)}) collective-permute-start(bf16[9,24,128]{2,1,0:T(8,128)(2,1)S(1)} %get-tuple-element.106), channel_id=1, source_target_pairs={{0,28},{4,8},{8,4},{12,16},{16,12},{20,24},{24,20},{28,0},{1,29},{... | collective-permute-start | bytes 165896 | tf_op jit(solution)/shard_map/ppermute | solution.py:473
  70.9 9.4 %collective-permute-start.28 = (bf16[9,24,128]{2,1,0:T(8,128)(2,1)S(1)}, bf16[9,24,128]{2,1,0:T(8,128)(2,1)S(1)}, u32[]{:S(2)}, u32[]{:S(2)}) collective-permute-start(bf16[9,24,128]{2,1,0:T(8,128)(2,1)S(1)} %get-tuple-element.109), channel_id=1, source_target_pairs={{0,8},{4,12},{8,0},{12,4},{16,24},{20,28},{24,16},{28,20},{1,9},{5... | collective-permute-start | bytes 165896 | tf_op jit(solution)/shard_map/ppermute | solution.py:473
  71.0 9.3 %collective-permute-start.29 = (bf16[9,24,128]{2,1,0:T(8,128)(2,1)S(1)}, bf16[9,24,128]{2,1,0:T(8,128)(2,1)S(1)}, u32[]{:S(2)}, u32[]{:S(2)}) collective-permute-start(bf16[9,24,128]{2,1,0:T(8,128)(2,1)S(1)} %get-tuple-element.110), channel_id=1, source_target_pairs={{0,24},{4,28},{8,16},{12,20},{16,8},{20,12},{24,0},{28,4},{1,25},{... | collective-permute-start | bytes 165896 | tf_op jit(solution)/shard_map/ppermute | solution.py:473
  72.4 4.1 %collective-permute-start.27 = (bf16[8,24,128]{2,1,0:T(8,128)(2,1)S(1)}, bf16[8,24,128]{2,1,0:T(8,128)(2,1)S(1)}, u32[]{:S(2)}, u32[]{:S(2)}) collective-permute-start(bf16[8,24,128]{2,1,0:T(8,128)(2,1)S(1)} %get-tuple-element.108), channel_id=1, source_target_pairs={{0,4},{4,0},{8,12},{12,8},{16,20},{20,16},{24,28},{28,24},{1,5},{5... | collective-permute-start | bytes 147464 | tf_op jit(solution)/shard_map/ppermute | solution.py:473
  73.5 6.8 %collective-permute-start.30 = (bf16[8,24,128]{2,1,0:T(8,128)(2,1)S(1)}, bf16[8,24,128]{2,1,0:T(8,128)(2,1)S(1)}, u32[]{:S(2)}, u32[]{:S(2)}) collective-permute-start(bf16[8,24,128]{2,1,0:T(8,128)(2,1)S(1)} %get-tuple-element.111), channel_id=1, source_target_pairs={{0,28},{4,8},{8,4},{12,16},{16,12},{20,24},{24,20},{28,0},{1,29},{... | collective-permute-start | bytes 147464 | tf_op jit(solution)/shard_map/ppermute | solution.py:473
  80.4 2.2 %collective-permute-start.31 = (bf16[9,24,128]{2,1,0:T(8,128)(2,1)S(1)}, bf16[9,24,128]{2,1,0:T(8,128)(2,1)S(1)}, u32[]{:S(2)}, u32[]{:S(2)}) collective-permute-start(bf16[9,24,128]{2,1,0:T(8,128)(2,1)S(1)} %get-tuple-element.115), channel_id=1, source_target_pairs={{0,1},{1,0},{2,3},{3,2},{4,5},{5,4},{6,7},{7,6},{8,9},{9,8},{10,11... | collective-permute-start | bytes 165896 | tf_op jit(solution)/shard_map/ppermute | solution.py:479
  80.5 4.3 %collective-permute-start.32 = (bf16[9,24,128]{2,1,0:T(8,128)(2,1)S(1)}, bf16[9,24,128]{2,1,0:T(8,128)(2,1)S(1)}, u32[]{:S(2)}, u32[]{:S(2)}) collective-permute-start(bf16[9,24,128]{2,1,0:T(8,128)(2,1)S(1)} %get-tuple-element.116), channel_id=1, source_target_pairs={{0,2},{1,3},{2,0},{3,1},{4,6},{5,7},{6,4},{7,5},{8,10},{9,11},{10,... | collective-permute-start | bytes 165896 | tf_op jit(solution)/shard_map/ppermute | solution.py:479
  82.1 3.8 %collective-permute-start.33 = (bf16[9,24,128]{2,1,0:T(8,128)(2,1)S(1)}, bf16[9,24,128]{2,1,0:T(8,128)(2,1)S(1)}, u32[]{:S(2)}, u32[]{:S(2)}) collective-permute-start(bf16[9,24,128]{2,1,0:T(8,128)(2,1)S(1)} %get-tuple-element.117), channel_id=1, source_target_pairs={{0,3},{1,2},{2,1},{3,0},{4,7},{5,6},{6,5},{7,4},{8,11},{9,10},{10,... | collective-permute-start | bytes 165896 | tf_op jit(solution)/shard_map/ppermute | solution.py:479

commit v6 on v5

--- a/solution.py
+++ b/solution.py
@@ -63,7 +63,7 @@
         self.t_end = self.t_corner + self.corners
 
 
-def call(kernel, sizes, outs, args, scratch=(), static=()):
+def call(kernel, sizes, outs, args, scratch=(), static=(), aliases=None):
     single = not isinstance(outs, list)
     outs = [outs] if single else outs
     ins = [SMEM if a.dtype == jnp.int32 else VMEM for a in args]
@@ -76,6 +76,7 @@
         in_specs=ins,
         out_specs=[VMEM for _ in outs],
         scratch_shapes=list(scratch),
+        input_output_aliases=aliases or {},
         compiler_params=pltpu.CompilerParams(vmem_limit_bytes=16 << 20),
     )(*args)
     return results[0] if single else results
@@ -348,21 +349,34 @@
     return jnp.concatenate([value[: z.share], tail], axis=1)
 
 
+def lay_out(z, jj, a, averages):
+    g = lax.axis_index("grp")
+    half = z.own // 2
+    for f in range(z.faces):
+        member, i = f // z.own, f % z.own
+        rows = pl.ds(pl.multiple_of(f * MODES + (g ^ jj) * z.share, z.share), z.share)
+        averages[rows, : z.lanes] = a[f]
+        low = (i // half) * z.tail
+        averages[rows, z.lanes :] = a[z.faces + member * half + i % half, :, low : low + z.tail]
+
+
+def begin_kernel(z, a0, a1, averages):
+    lay_out(z, 0, a0, averages)
+    lay_out(z, 1, a1, averages)
+
+
+def add_kernel(z, a2, before, averages):
+    lay_out(z, 2, a2, averages)
+
+
 def second_kernel(z, table, mixed, *refs):
     n = z.grps
     shares, refs = refs[:n], refs[n:]
-    earlier, ext_in, refs = refs[0], refs[1], refs[2:]
+    earlier, ext_in, refs = refs[0], refs[1], refs[3:]
     outs, refs = refs[:n], refs[n:]
     own_out, hits_out, sums_out, averages, coeffs, scales = refs
     g = lax.axis_index("grp")
-    half = z.own // 2
-    for f in range(z.faces):
-        member, i = f // z.own, f % z.own
-        for jj, a in enumerate(shares):
-            rows = pl.ds(pl.multiple_of(f * MODES + (g ^ jj) * z.share, z.share), z.share)
-            averages[rows, : z.lanes] = a[f]
-            low = (i // half) * z.tail
-            averages[rows, z.lanes :] = a[z.faces + member * half + i % half, :, low : low + z.tail]
+    lay_out(z, 3, shares[3], averages)
     coeffs[...] = earlier[...] - 0.5 * jnp.dot(mixed[...], averages[...], preferred_element_type=F32)
     for j, o in enumerate(outs):
         for f in range(z.own):
@@ -480,7 +494,10 @@
 
 
 def exchanged(blocks):
-    return [blocks[0]] + [swapped(blocks[j], j) for j in range(1, len(blocks))]
+    met = [blocks[0]]
+    for j in range(1, len(blocks)):
+        met.append(swapped(blocks[j], j))
+    return met
 
 
 def run(schur, rhs, start, project, coarse_basis, owner_of_face, mortar_of_face, mortar_order, subdomain_map, vertex_ids):
@@ -550,10 +567,7 @@
             pltpu.VMEM((z.own, MODES, z.wide), BF),
         ),
     )
-    part_one = swapped(parts[1], 1)
-    part_two = swapped(parts[2], 2)
-    part_three = swapped(parts[3], 3)
-    parts = [parts[0], part_one, part_two, part_three]
+    parts = exchanged(parts)
     outgoing = call(pack_kernel, z, [link] * LINKS, (table, *parts), (pltpu.VMEM((z.faces, z.share, z.wide), BF),), (False,))
     arrived = paired(outgoing)
     pair_one = swapped(raw, 1)
@@ -577,7 +591,12 @@
         (pltpu.VMEM((SLOTS, z.share, z.wide), BF),),
     )
     spread_two = swapped(spread, 2)
-    shares = [spread, swapped(spread, 1), spread_two, swapped(spread_two, 1)]
+    spread_one = swapped(spread, 1)
+    spread_three = swapped(spread_two, 1)
+    shares = [spread, spread_one, spread_two, spread_three]
+    laid_shape = shape((z.all_rows, z.rhs), BF)
+    laid = call(begin_kernel, z, laid_shape, (spread, spread_one))
+    laid = call(add_kernel, z, laid_shape, (spread_two, laid), aliases={1: 0})
     mixed = call(
         mix_kernel,
         z,
@@ -585,17 +604,17 @@
         (matrix, own_tables, pair_one, pair_two, pair_three),
         (pltpu.VMEM((z.rows, z.all_rows), BF), pltpu.VMEM((z.own * MODES // 2, 2 * FPTS), F32)),
     )
-    *parts, earlier, hits, sums = call(
+    *parts, earlier, hits, sums, _ = call(
         second_kernel,
         z,
         [part_more] * grps
-        + [shape((z.rows, z.rhs), BF), shape((z.own * MODES, z.vertices), BF), sums_shape],
-        (table, mixed, *shares, wide, ext),
+        + [shape((z.rows, z.rhs), BF), shape((z.own * MODES, z.vertices), BF), sums_shape, laid_shape],
+        (table, mixed, *shares, wide, ext, laid),
         (
-            pltpu.VMEM((z.all_rows, z.rhs), BF),
             pltpu.VMEM((z.rows, z.rhs), F32),
             pltpu.VMEM((z.own * MODES, z.extra), BF),
         ),
+        aliases={4 + grps: grps + 3},
     )
     if not z.near:
         sums = lax.psum(sums, ("sub", "grp"))
@@ -621,8 +640,7 @@
         (table, *answered, *results[LINKS:]),
         (pltpu.VMEM((SLOTS, z.dense, z.lanes), BF),),
     )
-    last_two = swapped(outs[2], 2)
-    shares = [outs[0], swapped(outs[1], 1), last_two, swapped(outs[3], 3)]
+    shares = exchanged(outs)
     prior = call(prior_kernel, z, shape((z.rhs, z.rows), F32), (own_tables, earlier, first))
     inputs = (table, *shares, own_tables, coarse, sums, hits, prior)
     result = pl.pallas_call(

time: 87.6 us -> 87.7 us (level)
    pallas_call x13 -> x15, Pallas kernels: 7.34 us -> 7.45 us  [call(): pl.pallas_call(functools.partial(kernel, sizes, *static), out_shape=[pltp...]
where the time goes in v6:
time: 87.7 us; the launch traced here: 87.4 us
  waiting for transfers between devices  38.3 us (44%)
  starting transfers between devices  35.3 us (40%)
  Pallas kernels  13.6 us (16%)
    ppermute x16, starting transfers between devices, paired(): met.append(lax.ppermute(blocks[k], 'sub', p))  23.1 us
    ppermute x18, waiting for transfers between devices, swapped(): return lax.ppermute(value, 'grp', [(s, s ^ mask) for s in range(count)])  20 us
    ppermute x16, waiting for transfers between devices, paired(): met.append(lax.ppermute(blocks[k], 'sub', p))  18.3 us
    ppermute x18, starting transfers between devices, swapped(): return lax.ppermute(value, 'grp', [(s, s ^ mask) for s in range(count)])  12.1 us
    pallas_call x15, Pallas kernels, call(): pl.pallas_call(functools.partial(kernel, sizes, *static), out_shape=[pltp...  7.45 us
    pallas_call x1, Pallas kernels, run(): pl.pallas_call(functools.partial(table_kernel, z), out_shape=pltpu.SMEM((...  1.88 us
    pallas_call x1, Pallas kernels, run(): pl.pallas_call(functools.partial(load_kernel, z), out_shape=[pltpu.VMEM(a...  1.81 us
  transfers between devices with their start and end apart: 34, of which 15 were waited for; matrix products, arithmetic and copies ran while one was open for 0% of the time, Pallas kernels for 8%

profile of v6, /device:TPU:0, one launch (start us, length us, event | category | flops | bytes accessed | tf_op | source)
XLA Modules:
  0.0 87.4 jit_solution(13694048121800511590)
XLA Ops:
  0.0 1.1 %shard_map.101.b0 = bf16[200,512]{1,0:T(8,128)(2,1)S(1)} custom-call(f32[192,512]{1,0:T(8,128)} %bitcast.13, bf16[8,512]{1,0:T(8,128)(2,1)} %bitcast.20), custom_call_target="tpu_custom_call" | custom-call | tf_op jit(solution)/shard_map/pallas_call | solution.py:509
  1.1 3.0 %collective-permute-start = (bf16[200,512]{1,0:T(8,128)(2,1)S(1)}, bf16[200,512]{1,0:T(8,128)(2,1)S(1)}, u32[]{:S(2)}, u32[]{:S(2)}) collective-permute-start(bf16[200,512]{1,0:T(8,128)(2,1)S(1)} %shard_map.101.b0), channel_id=1, source_target_pairs={{0,2},{1,3},{2,0},{3,1},{4,6},{5,7},{6,4},{7,5},{8,10},{9,11},{10,... | collective-permute-start | bytes 614408 | tf_op jit(solution)/shard_map/ppermute | solution.py:493
  4.1 5.1 %collective-permute-done.block = bf16[200,512]{1,0:T(8,128)(2,1)S(1)} collective-permute-done((bf16[200,512]{1,0:T(8,128)(2,1)S(1)}, bf16[200,512]{1,0:T(8,128)(2,1)S(1)}, u32[]{:S(2)}, u32[]{:S(2)}) %collective-permute-start) | collective-permute-done | bytes 204832 | tf_op jit(solution)/shard_map/ppermute | solution.py:493
  9.2 1.8 %shard_map.100 = (bf16[512,2048]{1,0:T(8,128)(2,1)S(1)}, f32[192,512]{1,0:T(8,128)S(1)}, bf16[8,512]{1,0:T(8,128)(2,1)S(1)}, bf16[8,64,64]{2,1,0:T(8,128)(2,1)S(1)}) custom-call(bf16[512,2048]{1,0:T(8,128)(2,1)} %bitcast.15, f32[192,512]{1,0:T(8,128)} %bitcast.16, bf16[8,512]{1,0:T(8,128)(2,1)} %bitcast.21, bf16[8,4096]{1,0:T(8,128)(2,1)} %bitcast.17), custom_call_target="tpu_custom_call" | custom-call | tf_op jit(solution)/shard_map/pallas_call | solution.py:532
  11.0 0.3 shard_map.102.before
  11.4 1.9 %shard_map.103.table = s32[152]{0:T(256)S(4)} custom-call(s32[8,1,32]{2,1,0:T(1,128)} %bitcast.22, s32[8,32]{1,0:T(8,128)} %mortar.1, s32[8,16]{1,0:T(8,128)} %order.1, s32[8]{0:T(128)} %smap.1, s32[8,8]{1,0:T(8,128)} %vids.1), custom_call_target="tpu_custom_call" | custom-call | tf_op jit(solution)/shard_map/pallas_call | solution.py:524
  13.3 0.3 shard_map.104.before
  13.6 0.3 shard_map.105.before
  13.9 2.1 %shard_map.106 = (bf16[8,16,256]{2,1,0:T(8,128)(2,1)S(1)}, bf16[8,16,256]{2,1,0:T(8,128)(2,1)S(1)}, bf16[8,16,256]{2,1,0:T(8,128)(2,1)S(1)}, bf16[8,16,256]{2,1,...) custom-call(s32[152]{0:T(256)S(4)} %shard_map.103.table, ...), custom_call_target="tpu_custom_call" | custom-call | tf_op jit(solution)/shard_map/pallas_call | solution.py:73
  16.0 0.5 collective-permute-start.3
  16.6 1.7 %collective-permute-start.4 = (bf16[8,16,256]{2,1,0:T(8,128)(2,1)S(1)}, bf16[8,16,256]{2,1,0:T(8,128)(2,1)S(1)}, u32[]{:S(2)}, u32[]{:S(2)}) collective-permute-start(bf16[8,16,256]{2,1,0:T(8,128)(2,1)S(1)} %get-tuple-element.71), channel_id=1, source_target_pairs={{0,2},{1,3},{2,0},{3,1},{4,6},{5,7},{6,4},{7,5},{8,10},{9,11},{10,... | collective-permute-start | bytes 196616 | tf_op jit(solution)/shard_map/ppermute | solution.py:493
  18.3 1.4 %collective-permute-start.11 = (bf16[8,4096]{1,0:T(8,128)(2,1)S(1)}, bf16[8,4096]{1,0:T(8,128)(2,1)S(1)}, u32[]{:S(2)}, u32[]{:S(2)}) collective-permute-start(bf16[8,4096]{1,0:T(8,128)(2,1)S(1)} %bitcast.18), channel_id=1, source_target_pairs={{0,2},{1,3},{2,0},{3,1},{4,6},{5,7},{6,4},{7,5},{8,10},{9,11},{10,... | collective-permute-start | bytes 196616 | tf_op jit(solution)/shard_map/ppermute | solution.py:493
  19.7 0.4 collective-permute-start.10
  20.2 0.6 collective-permute-done.4.c2
  20.8 1.9 %collective-permute-done.5.c3 = bf16[8,16,256]{2,1,0:T(8,128)(2,1)S(1)} collective-permute-done((bf16[8,16,256]{2,1,0:T(8,128)(2,1)S(1)}, bf16[8,16,256]{2,1,0:T(8,128)(2,1)S(1)}, u32[]{:S(2)}, u32[]{:S(2)}) %collective-permute-start.5) | collective-permute-done | bytes 65568 | tf_op jit(solution)/shard_map/ppermute | solution.py:493
  22.8 1.6 %collective-permute-start.6 = (bf16[8,16,256]{2,1,0:T(8,128)(2,1)S(1)}, bf16[8,16,256]{2,1,0:T(8,128)(2,1)S(1)}, u32[]{:S(2)}, u32[]{:S(2)}) collective-permute-start(bf16[8,16,256]{2,1,0:T(8,128)(2,1)S(1)} %get-tuple-element.73), channel_id=1, source_target_pairs={{0,4},{4,0},{8,12},{12,8},{16,20},{20,16},{24,28},{28,24},{1,5},{5... | collective-permute-start | bytes 196616 | tf_op jit(solution)/shard_map/ppermute | solution.py:487
  24.3 1.6 %collective-permute-start.7 = (bf16[8,16,256]{2,1,0:T(8,128)(2,1)S(1)}, bf16[8,16,256]{2,1,0:T(8,128)(2,1)S(1)}, u32[]{:S(2)}, u32[]{:S(2)}) collective-permute-start(bf16[8,16,256]{2,1,0:T(8,128)(2,1)S(1)} %get-tuple-element.74), channel_id=1, source_target_pairs={{0,8},{4,12},{8,0},{12,4},{16,24},{20,28},{24,16},{28,20},{1,9},{5... | collective-permute-start | bytes 196616 | tf_op jit(solution)/shard_map/ppermute | solution.py:487
  25.9 2.5 %collective-permute-start.8 = (bf16[8,16,256]{2,1,0:T(8,128)(2,1)S(1)}, bf16[8,16,256]{2,1,0:T(8,128)(2,1)S(1)}, u32[]{:S(2)}, u32[]{:S(2)}) collective-permute-start(bf16[8,16,256]{2,1,0:T(8,128)(2,1)S(1)} %get-tuple-element.75), channel_id=1, source_target_pairs={{0,24},{4,28},{8,16},{12,20},{16,8},{20,12},{24,0},{28,4},{1,25},{... | collective-permute-start | bytes 196616 | tf_op jit(solution)/shard_map/ppermute | solution.py:487
  28.4 1.3 %collective-permute-start.9 = (bf16[8,16,256]{2,1,0:T(8,128)(2,1)S(1)}, bf16[8,16,256]{2,1,0:T(8,128)(2,1)S(1)}, u32[]{:S(2)}, u32[]{:S(2)}) collective-permute-start(bf16[8,16,256]{2,1,0:T(8,128)(2,1)S(1)} %get-tuple-element.76), channel_id=1, source_target_pairs={{0,28},{4,8},{8,4},{12,16},{16,12},{20,24},{24,20},{28,0},{1,29},{... | collective-permute-start | bytes 196616 | tf_op jit(solution)/shard_map/ppermute | solution.py:487
  29.7 3.0 %collective-permute-done.8.refs_2_ = bf16[8,16,256]{2,1,0:T(8,128)(2,1)S(1)} collective-permute-done((bf16[8,16,256]{2,1,0:T(8,128)(2,1)S(1)}, bf16[8,16,256]{2,1,0:T(8,128)(2,1)S(1)}, u32[]{:S(2)}, u32[]{:S(2)}) %collective-permute-start.8) | collective-permute-done | bytes 65568 | tf_op jit(solution)/shard_map/ppermute | solution.py:487
  32.7 2.6 %collective-permute-done.9.refs_3_ = bf16[8,16,256]{2,1,0:T(8,128)(2,1)S(1)} collective-permute-done((bf16[8,16,256]{2,1,0:T(8,128)(2,1)S(1)}, bf16[8,16,256]{2,1,0:T(8,128)(2,1)S(1)}, u32[]{:S(2)}, u32[]{:S(2)}) %collective-permute-start.9) | collective-permute-done | bytes 65568 | tf_op jit(solution)/shard_map/ppermute | solution.py:487
  35.4 0.3 shard_map.108
  35.8 1.8 %collective-permute-start.14 = (bf16[8,16,256]{2,1,0:T(8,128)(2,1)S(1)}, bf16[8,16,256]{2,1,0:T(8,128)(2,1)S(1)}, u32[]{:S(2)}, u32[]{:S(2)}) collective-permute-start(bf16[8,16,256]{2,1,0:T(8,128)(2,1)S(1)} %get-tuple-element.88), channel_id=1, source_target_pairs={{0,24},{4,28},{8,16},{12,20},{16,8},{20,12},{24,0},{28,4},{1,25},{... | collective-permute-start | bytes 196616 | tf_op jit(solution)/shard_map/ppermute | solution.py:487
  37.6 3.4 %collective-permute-start.15 = (bf16[8,16,256]{2,1,0:T(8,128)(2,1)S(1)}, bf16[8,16,256]{2,1,0:T(8,128)(2,1)S(1)}, u32[]{:S(2)}, u32[]{:S(2)}) collective-permute-start(bf16[8,16,256]{2,1,0:T(8,128)(2,1)S(1)} %get-tuple-element.89), channel_id=1, source_target_pairs={{0,28},{4,8},{8,4},{12,16},{16,12},{20,24},{24,20},{28,0},{1,29},{... | collective-permute-start | bytes 196616 | tf_op jit(solution)/shard_map/ppermute | solution.py:487
  41.0 1.3 %collective-permute-done.14.refs_2_ = bf16[8,16,256]{2,1,0:T(8,128)(2,1)S(1)} collective-permute-done((bf16[8,16,256]{2,1,0:T(8,128)(2,1)S(1)}, bf16[8,16,256]{2,1,0:T(8,128)(2,1)S(1)}, u32[]{:S(2)}, u32[]{:S(2)}) %collective-permute-start.14) | collective-permute-done | bytes 65568 | tf_op jit(solution)/shard_map/ppermute | solution.py:487
  42.3 2.4 %collective-permute-done.15.refs_3_ = bf16[8,16,256]{2,1,0:T(8,128)(2,1)S(1)} collective-permute-done((bf16[8,16,256]{2,1,0:T(8,128)(2,1)S(1)}, bf16[8,16,256]{2,1,0:T(8,128)(2,1)S(1)}, u32[]{:S(2)}, u32[]{:S(2)}) %collective-permute-start.15) | collective-permute-done | bytes 65568 | tf_op jit(solution)/shard_map/ppermute | solution.py:487
  44.9 1.0 %collective-permute-start.18 = (bf16[56,16,128]{2,1,0:T(8,128)(2,1)S(1)}, bf16[56,16,128]{2,1,0:T(8,128)(2,1)S(1)}, u32[]{:S(2)}, u32[]{:S(2)}) collective-permute-start(bf16[56,16,128]{2,1,0:T(8,128)(2,1)S(1)} %shard_map.110.a0.refs_0_), channel_id=1, source_target_pairs={{0,2},{1,3},{2,0},{3,1},{4,6},{5,7},{6,4},{7,5},{8,10},{9,11},{10,... | collective-permute-start | bytes 688136 | tf_op jit(solution)/shard_map/ppermute | solution.py:493
  45.9 6.0 %collective-permute-done.18.a2.refs_2_ = bf16[56,16,128]{2,1,0:T(8,128)(2,1)S(1)} collective-permute-done((bf16[56,16,128]{2,1,0:T(8,128)(2,1)S(1)}, bf16[56,16,128]{2,1,0:T(8,128)(2,1)S(1)}, u32[]{:S(2)}, u32[]{:S(2)}) %collective-permute-start.18) | collective-permute-done | bytes 229408 | tf_op jit(solution)/shard_map/ppermute | solution.py:493
  51.9 1.9 %shard_map.109.mixed = bf16[512,2048]{1,0:T(8,128)(2,1)S(1)} custom-call(bf16[512,2048]{1,0:T(8,128)(2,1)S(1)} %get-tuple-element.63.schur, bf16[8,64,64]{2,1,0:T(8,128)(2,1)S(1)} %get-tuple-element.66.tables.t0.refs_4_, bf16[8,4096]{1,0:T(8,128)(2,1)S(1)} %collective-permute-done.10.r1, bf16[8,4096]{1,0:T(8,128)(2,1)S(1)} %collective-permute-done.11.r2, ...), custom_call_target="tpu_custom_call" | custom-call | tf_op jit(solution)/shard_map/pallas_call | solution.py:73
  54.1 1.2 %shard_map.113 = (bf16[9,24,128]{2,1,0:T(8,128)(2,1)S(1)}, bf16[9,24,128]{2,1,0:T(8,128)(2,1)S(1)}, bf16[9,24,128]{2,1,0:T(8,128)(2,1)S(1)}, bf16[9,24,128]{2,1,...) custom-call(s32[152]{0:T(256)S(4)} %shard_map.103.table, ...), custom_call_target="tpu_custom_call", output_to_operand_aliasing={{7}: (8, {})} | custom-call | tf_op jit(solution)/shard_map/pallas_call | solution.py:73
  55.2 0.6 collective-permute-start.20
  55.8 0.3 collective-permute-start.21
  56.1 1.1 %collective-permute-start.22 = (bf16[9,24,128]{2,1,0:T(8,128)(2,1)S(1)}, bf16[9,24,128]{2,1,0:T(8,128)(2,1)S(1)}, u32[]{:S(2)}, u32[]{:S(2)}) collective-permute-start(bf16[9,24,128]{2,1,0:T(8,128)(2,1)S(1)} %get-tuple-element.102), channel_id=1, source_target_pairs={{0,3},{1,2},{2,1},{3,0},{4,7},{5,6},{6,5},{7,4},{8,11},{9,10},{10,... | collective-permute-start | bytes 165896 | tf_op jit(solution)/shard_map/ppermute | solution.py:493
  57.2 3.1 %collective-permute-done.21.c2 = bf16[9,24,128]{2,1,0:T(8,128)(2,1)S(1)} collective-permute-done((bf16[9,24,128]{2,1,0:T(8,128)(2,1)S(1)}, bf16[9,24,128]{2,1,0:T(8,128)(2,1)S(1)}, u32[]{:S(2)}, u32[]{:S(2)}) %collective-permute-start.21) | collective-permute-done | bytes 55328 | tf_op jit(solution)/shard_map/ppermute | solution.py:493
  60.4 1.1 %collective-permute-start.23 = (bf16[9,24,128]{2,1,0:T(8,128)(2,1)S(1)}, bf16[9,24,128]{2,1,0:T(8,128)(2,1)S(1)}, u32[]{:S(2)}, u32[]{:S(2)}) collective-permute-start(bf16[9,24,128]{2,1,0:T(8,128)(2,1)S(1)} %get-tuple-element.103), channel_id=1, source_target_pairs={{0,4},{4,0},{8,12},{12,8},{16,20},{20,16},{24,28},{28,24},{1,5},{5... | collective-permute-start | bytes 165896 | tf_op jit(solution)/shard_map/ppermute | solution.py:487
  61.5 1.0 %collective-permute-start.24 = (bf16[9,24,128]{2,1,0:T(8,128)(2,1)S(1)}, bf16[9,24,128]{2,1,0:T(8,128)(2,1)S(1)}, u32[]{:S(2)}, u32[]{:S(2)}) collective-permute-start(bf16[9,24,128]{2,1,0:T(8,128)(2,1)S(1)} %get-tuple-element.104), channel_id=1, source_target_pairs={{0,8},{4,12},{8,0},{12,4},{16,24},{20,28},{24,16},{28,20},{1,9},{5... | collective-permute-start | bytes 165896 | tf_op jit(solution)/shard_map/ppermute | solution.py:487
  62.5 1.4 %collective-permute-start.25 = (bf16[9,24,128]{2,1,0:T(8,128)(2,1)S(1)}, bf16[9,24,128]{2,1,0:T(8,128)(2,1)S(1)}, u32[]{:S(2)}, u32[]{:S(2)}) collective-permute-start(bf16[9,24,128]{2,1,0:T(8,128)(2,1)S(1)} %get-tuple-element.105), channel_id=1, source_target_pairs={{0,24},{4,28},{8,16},{12,20},{16,8},{20,12},{24,0},{28,4},{1,25},{... | collective-permute-start | bytes 165896 | tf_op jit(solution)/shard_map/ppermute | solution.py:487
  63.9 1.9 %collective-permute-start.26 = (bf16[9,24,128]{2,1,0:T(8,128)(2,1)S(1)}, bf16[9,24,128]{2,1,0:T(8,128)(2,1)S(1)}, u32[]{:S(2)}, u32[]{:S(2)}) collective-permute-start(bf16[9,24,128]{2,1,0:T(8,128)(2,1)S(1)} %get-tuple-element.106), channel_id=1, source_target_pairs={{0,28},{4,8},{8,4},{12,16},{16,12},{20,24},{24,20},{28,0},{1,29},{... | collective-permute-start | bytes 165896 | tf_op jit(solution)/shard_map/ppermute | solution.py:487
  65.8 2.7 %collective-permute-done.25.refs_2_ = bf16[9,24,128]{2,1,0:T(8,128)(2,1)S(1)} collective-permute-done((bf16[9,24,128]{2,1,0:T(8,128)(2,1)S(1)}, bf16[9,24,128]{2,1,0:T(8,128)(2,1)S(1)}, u32[]{:S(2)}, u32[]{:S(2)}) %collective-permute-start.25) | collective-permute-done | bytes 55328 | tf_op jit(solution)/shard_map/ppermute | solution.py:487
  68.5 2.2 %collective-permute-done.26.refs_3_ = bf16[9,24,128]{2,1,0:T(8,128)(2,1)S(1)} collective-permute-done((bf16[9,24,128]{2,1,0:T(8,128)(2,1)S(1)}, bf16[9,24,128]{2,1,0:T(8,128)(2,1)S(1)}, u32[]{:S(2)}, u32[]{:S(2)}) %collective-permute-start.26) | collective-permute-done | bytes 55328 | tf_op jit(solution)/shard_map/ppermute | solution.py:487
  71.1 1.4 %collective-permute-start.29 = (bf16[9,24,128]{2,1,0:T(8,128)(2,1)S(1)}, bf16[9,24,128]{2,1,0:T(8,128)(2,1)S(1)}, u32[]{:S(2)}, u32[]{:S(2)}) collective-permute-start(bf16[9,24,128]{2,1,0:T(8,128)(2,1)S(1)} %get-tuple-element.110), channel_id=1, source_target_pairs={{0,24},{4,28},{8,16},{12,20},{16,8},{20,12},{24,0},{28,4},{1,25},{... | collective-permute-start | bytes 165896 | tf_op jit(solution)/shard_map/ppermute | solution.py:487
  72.5 1.1 %collective-permute-start.27 = (bf16[8,24,128]{2,1,0:T(8,128)(2,1)S(1)}, bf16[8,24,128]{2,1,0:T(8,128)(2,1)S(1)}, u32[]{:S(2)}, u32[]{:S(2)}) collective-permute-start(bf16[8,24,128]{2,1,0:T(8,128)(2,1)S(1)} %get-tuple-element.108), channel_id=1, source_target_pairs={{0,4},{4,0},{8,12},{12,8},{16,20},{20,16},{24,28},{28,24},{1,5},{5... | collective-permute-start | bytes 147464 | tf_op jit(solution)/shard_map/ppermute | solution.py:487
  73.6 2.8 %collective-permute-start.30 = (bf16[8,24,128]{2,1,0:T(8,128)(2,1)S(1)}, bf16[8,24,128]{2,1,0:T(8,128)(2,1)S(1)}, u32[]{:S(2)}, u32[]{:S(2)}) collective-permute-start(bf16[8,24,128]{2,1,0:T(8,128)(2,1)S(1)} %get-tuple-element.111), channel_id=1, source_target_pairs={{0,28},{4,8},{8,4},{12,16},{16,12},{20,24},{24,20},{28,0},{1,29},{... | collective-permute-start | bytes 147464 | tf_op jit(solution)/shard_map/ppermute | solution.py:487
  76.6 3.8 %collective-permute-done.30.refs_3_ = bf16[8,24,128]{2,1,0:T(8,128)(2,1)S(1)} collective-permute-done((bf16[8,24,128]{2,1,0:T(8,128)(2,1)S(1)}, bf16[8,24,128]{2,1,0:T(8,128)(2,1)S(1)}, u32[]{:S(2)}, u32[]{:S(2)}) %collective-permute-start.30) | collective-permute-done | bytes 49184 | tf_op jit(solution)/shard_map/ppermute | solution.py:487
  80.6 1.7 %collective-permute-start.32 = (bf16[9,24,128]{2,1,0:T(8,128)(2,1)S(1)}, bf16[9,24,128]{2,1,0:T(8,128)(2,1)S(1)}, u32[]{:S(2)}, u32[]{:S(2)}) collective-permute-start(bf16[9,24,128]{2,1,0:T(8,128)(2,1)S(1)} %get-tuple-element.116), channel_id=1, source_target_pairs={{0,2},{1,3},{2,0},{3,1},{4,6},{5,7},{6,4},{7,5},{8,10},{9,11},{10,... | collective-permute-start | bytes 165896 | tf_op jit(solution)/shard_map/ppermute | solution.py:493
  82.7 2.1 %collective-permute-done.32.refs_2_ = bf16[9,24,128]{2,1,0:T(8,128)(2,1)S(1)} collective-permute-done((bf16[9,24,128]{2,1,0:T(8,128)(2,1)S(1)}, bf16[9,24,128]{2,1,0:T(8,128)(2,1)S(1)}, u32[]{:S(2)}, u32[]{:S(2)}) %collective-permute-start.32) | collective-permute-done | bytes 55328 | tf_op jit(solution)/shard_map/ppermute | solution.py:493
  84.8 1.2 %collective-permute-done.33.refs_3_ = bf16[9,24,128]{2,1,0:T(8,128)(2,1)S(1)} collective-permute-done((bf16[9,24,128]{2,1,0:T(8,128)(2,1)S(1)}, bf16[9,24,128]{2,1,0:T(8,128)(2,1)S(1)}, u32[]{:S(2)}, u32[]{:S(2)}) %collective-permute-start.33) | collective-permute-done | bytes 55328 | tf_op jit(solution)/shard_map/ppermute | solution.py:493
  86.1 1.4 %shard_map.118 = f32[192,512]{1,0:T(8,128)} custom-call(s32[152]{0:T(256)S(4)} %shard_map.103.table, bf16[9,24,128]{2,1,0:T(8,128)(2,1)S(1)} %get-tuple-element.114.refs_0_, bf16[9,24,128]{2,1,0:T(8,128)(2,1)S(1)} %collective-permute-done.31.refs_1_, bf16[9,24,128]{2,1,0:T(8,128)(2,1)S(1)} %collective-permute-done.32.refs_2_, ...), custom_call_target="tpu_custom_call" | custom-call | tf_op jit(solution)/shard_map/pallas_call | solution.py:646
  (43 shorter events, 1.8 us)
Async XLA Ops:
  1.1 8.1 %collective-permute-start = (bf16[200,512]{1,0:T(8,128)(2,1)S(1)}, bf16[200,512]{1,0:T(8,128)(2,1)S(1)}, u32[]{:S(2)}, u32[]{:S(2)}) collective-permute-start(bf16[200,512]{1,0:T(8,128)(2,1)S(1)} %shard_map.101.b0), channel_id=1, source_target_pairs={{0,2},{1,3},{2,0},{3,1},{4,6},{5,7},{6,4},{7,5},{8,10},{9,11},{10,... | collective-permute-start | bytes 614408 | tf_op jit(solution)/shard_map/ppermute | solution.py:493
  4.1 9.1 %collective-permute-start.2 = (bf16[200,512]{1,0:T(8,128)(2,1)S(1)}, bf16[200,512]{1,0:T(8,128)(2,1)S(1)}, u32[]{:S(2)}, u32[]{:S(2)}) collective-permute-start(bf16[200,512]{1,0:T(8,128)(2,1)S(1)} %shard_map.101.b0), channel_id=1, source_target_pairs={{0,1},{1,0},{2,3},{3,2},{4,5},{5,4},{6,7},{7,6},{8,9},{9,8},{10,11... | collective-permute-start | bytes 614408 | tf_op jit(solution)/shard_map/ppermute | solution.py:493
  9.2 4.7 %collective-permute-start.1 = (bf16[200,512]{1,0:T(8,128)(2,1)S(1)}, bf16[200,512]{1,0:T(8,128)(2,1)}, u32[]{:S(2)}, u32[]{:S(2)}) collective-permute-start(bf16[200,512]{1,0:T(8,128)(2,1)S(1)} %collective-permute-done.block), channel_id=1, source_target_pairs={{0,1},{1,0},{2,3},{3,2},{4,5},{5,4},{6,7},{7,6},{8,9},{9,8},{10,11... | collective-permute-start | bytes 614408 | tf_op jit(solution)/shard_map/ppermute | solution.py:493
  13.9 4.4 %copy-start.1 = (bf16[1,8,4096]{2,1,0:T(8,128)(2,1)S(1)}, bf16[1,8,4096]{2,1,0:T(8,128)(2,1)}, u32[]{:S(2)}) copy-start(bf16[1,8,4096]{2,1,0:T(8,128)(2,1)} %param.13) | copy-start | bytes 196612
  16.0 4.2 %collective-permute-start.3 = (bf16[8,16,256]{2,1,0:T(8,128)(2,1)S(1)}, bf16[8,16,256]{2,1,0:T(8,128)(2,1)S(1)}, u32[]{:S(2)}, u32[]{:S(2)}) collective-permute-start(bf16[8,16,256]{2,1,0:T(8,128)(2,1)S(1)} %get-tuple-element.70), channel_id=1, source_target_pairs={{0,1},{1,0},{2,3},{3,2},{4,5},{5,4},{6,7},{7,6},{8,9},{9,8},{10,11... | collective-permute-start | bytes 196616 | tf_op jit(solution)/shard_map/ppermute | solution.py:493
  16.6 4.3 %collective-permute-start.4 = (bf16[8,16,256]{2,1,0:T(8,128)(2,1)S(1)}, bf16[8,16,256]{2,1,0:T(8,128)(2,1)S(1)}, u32[]{:S(2)}, u32[]{:S(2)}) collective-permute-start(bf16[8,16,256]{2,1,0:T(8,128)(2,1)S(1)} %get-tuple-element.71), channel_id=1, source_target_pairs={{0,2},{1,3},{2,0},{3,1},{4,6},{5,7},{6,4},{7,5},{8,10},{9,11},{10,... | collective-permute-start | bytes 196616 | tf_op jit(solution)/shard_map/ppermute | solution.py:493
  18.3 4.4 %collective-permute-start.5 = (bf16[8,16,256]{2,1,0:T(8,128)(2,1)S(1)}, bf16[8,16,256]{2,1,0:T(8,128)(2,1)S(1)}, u32[]{:S(2)}, u32[]{:S(2)}) collective-permute-start(bf16[8,16,256]{2,1,0:T(8,128)(2,1)S(1)} %get-tuple-element.72), channel_id=1, source_target_pairs={{0,3},{1,2},{2,1},{3,0},{4,7},{5,6},{6,5},{7,4},{8,11},{9,10},{10,... | collective-permute-start | bytes 196616 | tf_op jit(solution)/shard_map/ppermute | solution.py:493
  18.3 10.1 %collective-permute-start.11 = (bf16[8,4096]{1,0:T(8,128)(2,1)S(1)}, bf16[8,4096]{1,0:T(8,128)(2,1)S(1)}, u32[]{:S(2)}, u32[]{:S(2)}) collective-permute-start(bf16[8,4096]{1,0:T(8,128)(2,1)S(1)} %bitcast.18), channel_id=1, source_target_pairs={{0,2},{1,3},{2,0},{3,1},{4,6},{5,7},{6,4},{7,5},{8,10},{9,11},{10,... | collective-permute-start | bytes 196616 | tf_op jit(solution)/shard_map/ppermute | solution.py:493
  19.7 10.0 %collective-permute-start.10 = (bf16[8,4096]{1,0:T(8,128)(2,1)S(1)}, bf16[8,4096]{1,0:T(8,128)(2,1)S(1)}, u32[]{:S(2)}, u32[]{:S(2)}) collective-permute-start(bf16[8,4096]{1,0:T(8,128)(2,1)S(1)} %bitcast.19), channel_id=1, source_target_pairs={{0,1},{1,0},{2,3},{3,2},{4,5},{5,4},{6,7},{7,6},{8,9},{9,8},{10,11... | collective-permute-start | bytes 196616 | tf_op jit(solution)/shard_map/ppermute | solution.py:493
  22.8 6.9 %collective-permute-start.6 = (bf16[8,16,256]{2,1,0:T(8,128)(2,1)S(1)}, bf16[8,16,256]{2,1,0:T(8,128)(2,1)S(1)}, u32[]{:S(2)}, u32[]{:S(2)}) collective-permute-start(bf16[8,16,256]{2,1,0:T(8,128)(2,1)S(1)} %get-tuple-element.73), channel_id=1, source_target_pairs={{0,4},{4,0},{8,12},{12,8},{16,20},{20,16},{24,28},{28,24},{1,5},{5... | collective-permute-start | bytes 196616 | tf_op jit(solution)/shard_map/ppermute | solution.py:487
  24.3 5.4 %collective-permute-start.7 = (bf16[8,16,256]{2,1,0:T(8,128)(2,1)S(1)}, bf16[8,16,256]{2,1,0:T(8,128)(2,1)S(1)}, u32[]{:S(2)}, u32[]{:S(2)}) collective-permute-start(bf16[8,16,256]{2,1,0:T(8,128)(2,1)S(1)} %get-tuple-element.74), channel_id=1, source_target_pairs={{0,8},{4,12},{8,0},{12,4},{16,24},{20,28},{24,16},{28,20},{1,9},{5... | collective-permute-start | bytes 196616 | tf_op jit(solution)/shard_map/ppermute | solution.py:487
  25.9 6.8 %collective-permute-start.8 = (bf16[8,16,256]{2,1,0:T(8,128)(2,1)S(1)}, bf16[8,16,256]{2,1,0:T(8,128)(2,1)S(1)}, u32[]{:S(2)}, u32[]{:S(2)}) collective-permute-start(bf16[8,16,256]{2,1,0:T(8,128)(2,1)S(1)} %get-tuple-element.75), channel_id=1, source_target_pairs={{0,24},{4,28},{8,16},{12,20},{16,8},{20,12},{24,0},{28,4},{1,25},{... | collective-permute-start | bytes 196616 | tf_op jit(solution)/shard_map/ppermute | solution.py:487
  28.4 7.0 %collective-permute-start.9 = (bf16[8,16,256]{2,1,0:T(8,128)(2,1)S(1)}, bf16[8,16,256]{2,1,0:T(8,128)(2,1)S(1)}, u32[]{:S(2)}, u32[]{:S(2)}) collective-permute-start(bf16[8,16,256]{2,1,0:T(8,128)(2,1)S(1)} %get-tuple-element.76), channel_id=1, source_target_pairs={{0,28},{4,8},{8,4},{12,16},{16,12},{20,24},{24,20},{28,0},{1,29},{... | collective-permute-start | bytes 196616 | tf_op jit(solution)/shard_map/ppermute | solution.py:487
  35.4 5.7 %collective-permute-start.16 = (bf16[8,4096]{1,0:T(8,128)(2,1)S(1)}, bf16[8,4096]{1,0:T(8,128)(2,1)S(1)}, u32[]{:S(2)}, u32[]{:S(2)}) collective-permute-start(bf16[8,4096]{1,0:T(8,128)(2,1)S(1)} %collective-permute-done.11.r2), channel_id=1, source_target_pairs={{0,1},{1,0},{2,3},{3,2},{4,5},{5,4},{6,7},{7,6},{8,9},{9,8},{10,11... | collective-permute-start | bytes 196616 | tf_op jit(solution)/shard_map/ppermute | solution.py:493
  35.7 5.4 %collective-permute-start.12 = (bf16[8,16,256]{2,1,0:T(8,128)(2,1)S(1)}, bf16[8,16,256]{2,1,0:T(8,128)(2,1)S(1)}, u32[]{:S(2)}, u32[]{:S(2)}) collective-permute-start(bf16[8,16,256]{2,1,0:T(8,128)(2,1)S(1)} %get-tuple-element.86), channel_id=1, source_target_pairs={{0,4},{4,0},{8,12},{12,8},{16,20},{20,16},{24,28},{28,24},{1,5},{5... | collective-permute-start | bytes 196616 | tf_op jit(solution)/shard_map/ppermute | solution.py:487
  35.7 5.3 %collective-permute-start.13 = (bf16[8,16,256]{2,1,0:T(8,128)(2,1)S(1)}, bf16[8,16,256]{2,1,0:T(8,128)(2,1)S(1)}, u32[]{:S(2)}, u32[]{:S(2)}) collective-permute-start(bf16[8,16,256]{2,1,0:T(8,128)(2,1)S(1)} %get-tuple-element.87), channel_id=1, source_target_pairs={{0,8},{4,12},{8,0},{12,4},{16,24},{20,28},{24,16},{28,20},{1,9},{5... | collective-permute-start | bytes 196616 | tf_op jit(solution)/shard_map/ppermute | solution.py:487
  35.8 6.5 %collective-permute-start.14 = (bf16[8,16,256]{2,1,0:T(8,128)(2,1)S(1)}, bf16[8,16,256]{2,1,0:T(8,128)(2,1)S(1)}, u32[]{:S(2)}, u32[]{:S(2)}) collective-permute-start(bf16[8,16,256]{2,1,0:T(8,128)(2,1)S(1)} %get-tuple-element.88), channel_id=1, source_target_pairs={{0,24},{4,28},{8,16},{12,20},{16,8},{20,12},{24,0},{28,4},{1,25},{... | collective-permute-start | bytes 196616 | tf_op jit(solution)/shard_map/ppermute | solution.py:487
  37.6 7.1 %collective-permute-start.15 = (bf16[8,16,256]{2,1,0:T(8,128)(2,1)S(1)}, bf16[8,16,256]{2,1,0:T(8,128)(2,1)S(1)}, u32[]{:S(2)}, u32[]{:S(2)}) collective-permute-start(bf16[8,16,256]{2,1,0:T(8,128)(2,1)S(1)} %get-tuple-element.89), channel_id=1, source_target_pairs={{0,28},{4,8},{8,4},{12,16},{16,12},{20,24},{24,20},{28,0},{1,29},{... | collective-permute-start | bytes 196616 | tf_op jit(solution)/shard_map/ppermute | solution.py:487
  44.9 7.0 %collective-permute-start.18 = (bf16[56,16,128]{2,1,0:T(8,128)(2,1)S(1)}, bf16[56,16,128]{2,1,0:T(8,128)(2,1)S(1)}, u32[]{:S(2)}, u32[]{:S(2)}) collective-permute-start(bf16[56,16,128]{2,1,0:T(8,128)(2,1)S(1)} %shard_map.110.a0.refs_0_), channel_id=1, source_target_pairs={{0,2},{1,3},{2,0},{3,1},{4,6},{5,7},{6,4},{7,5},{8,10},{9,11},{10,... | collective-permute-start | bytes 688136 | tf_op jit(solution)/shard_map/ppermute | solution.py:493
  45.9 7.9 %collective-permute-start.17 = (bf16[56,16,128]{2,1,0:T(8,128)(2,1)S(1)}, bf16[56,16,128]{2,1,0:T(8,128)(2,1)S(1)}, u32[]{:S(2)}, u32[]{:S(2)}) collective-permute-start(bf16[56,16,128]{2,1,0:T(8,128)(2,1)S(1)} %shard_map.110.a0.refs_0_), channel_id=1, source_target_pairs={{0,1},{1,0},{2,3},{3,2},{4,5},{5,4},{6,7},{7,6},{8,9},{9,8},{10,11... | collective-permute-start | bytes 688136 | tf_op jit(solution)/shard_map/ppermute | solution.py:493
  51.9 2.2 %collective-permute-start.19 = (bf16[56,16,128]{2,1,0:T(8,128)(2,1)S(1)}, bf16[56,16,128]{2,1,0:T(8,128)(2,1)S(1)}, u32[]{:S(2)}, u32[]{:S(2)}) collective-permute-start(bf16[56,16,128]{2,1,0:T(8,128)(2,1)S(1)} %collective-permute-done.18.a2.refs_2_), channel_id=1, source_target_pairs={{0,1},{1,0},{2,3},{3,2},{4,5},{5,4},{6,7},{7,6},{8,9},{9,8},{10,11... | collective-permute-start | bytes 688136 | tf_op jit(solution)/shard_map/ppermute | solution.py:493
  54.1 28.3 %copy-start = (f32[1,512,192]{1,2,0:T(8,128)S(1)}, f32[1,512,192]{1,2,0:T(8,128)}, u32[]{:S(2)}) copy-start(f32[1,512,192]{1,2,0:T(8,128)} %param.12) | copy-start | bytes 1179652
  55.2 2.0 %collective-permute-start.20 = (bf16[9,24,128]{2,1,0:T(8,128)(2,1)S(1)}, bf16[9,24,128]{2,1,0:T(8,128)(2,1)S(1)}, u32[]{:S(2)}, u32[]{:S(2)}) collective-permute-start(bf16[9,24,128]{2,1,0:T(8,128)(2,1)S(1)} %get-tuple-element.100), channel_id=1, source_target_pairs={{0,1},{1,0},{2,3},{3,2},{4,5},{5,4},{6,7},{7,6},{8,9},{9,8},{10,11... | collective-permute-start | bytes 165896 | tf_op jit(solution)/shard_map/ppermute | solution.py:493
  55.8 4.5 %collective-permute-start.21 = (bf16[9,24,128]{2,1,0:T(8,128)(2,1)S(1)}, bf16[9,24,128]{2,1,0:T(8,128)(2,1)S(1)}, u32[]{:S(2)}, u32[]{:S(2)}) collective-permute-start(bf16[9,24,128]{2,1,0:T(8,128)(2,1)S(1)} %get-tuple-element.101), channel_id=1, source_target_pairs={{0,2},{1,3},{2,0},{3,1},{4,6},{5,7},{6,4},{7,5},{8,10},{9,11},{10,... | collective-permute-start | bytes 165896 | tf_op jit(solution)/shard_map/ppermute | solution.py:493
  56.1 4.2 %collective-permute-start.22 = (bf16[9,24,128]{2,1,0:T(8,128)(2,1)S(1)}, bf16[9,24,128]{2,1,0:T(8,128)(2,1)S(1)}, u32[]{:S(2)}, u32[]{:S(2)}) collective-permute-start(bf16[9,24,128]{2,1,0:T(8,128)(2,1)S(1)} %get-tuple-element.102), channel_id=1, source_target_pairs={{0,3},{1,2},{2,1},{3,0},{4,7},{5,6},{6,5},{7,4},{8,11},{9,10},{10,... | collective-permute-start | bytes 165896 | tf_op jit(solution)/shard_map/ppermute | solution.py:493
  60.4 5.4 %collective-permute-start.23 = (bf16[9,24,128]{2,1,0:T(8,128)(2,1)S(1)}, bf16[9,24,128]{2,1,0:T(8,128)(2,1)S(1)}, u32[]{:S(2)}, u32[]{:S(2)}) collective-permute-start(bf16[9,24,128]{2,1,0:T(8,128)(2,1)S(1)} %get-tuple-element.103), channel_id=1, source_target_pairs={{0,4},{4,0},{8,12},{12,8},{16,20},{20,16},{24,28},{28,24},{1,5},{5... | collective-permute-start | bytes 165896 | tf_op jit(solution)/shard_map/ppermute | solution.py:487
  61.5 4.3 %collective-permute-start.24 = (bf16[9,24,128]{2,1,0:T(8,128)(2,1)S(1)}, bf16[9,24,128]{2,1,0:T(8,128)(2,1)S(1)}, u32[]{:S(2)}, u32[]{:S(2)}) collective-permute-start(bf16[9,24,128]{2,1,0:T(8,128)(2,1)S(1)} %get-tuple-element.104), channel_id=1, source_target_pairs={{0,8},{4,12},{8,0},{12,4},{16,24},{20,28},{24,16},{28,20},{1,9},{5... | collective-permute-start | bytes 165896 | tf_op jit(solution)/shard_map/ppermute | solution.py:487
  62.5 6.1 %collective-permute-start.25 = (bf16[9,24,128]{2,1,0:T(8,128)(2,1)S(1)}, bf16[9,24,128]{2,1,0:T(8,128)(2,1)S(1)}, u32[]{:S(2)}, u32[]{:S(2)}) collective-permute-start(bf16[9,24,128]{2,1,0:T(8,128)(2,1)S(1)} %get-tuple-element.105), channel_id=1, source_target_pairs={{0,24},{4,28},{8,16},{12,20},{16,8},{20,12},{24,0},{28,4},{1,25},{... | collective-permute-start | bytes 165896 | tf_op jit(solution)/shard_map/ppermute | solution.py:487
  63.9 6.9 %collective-permute-start.26 = (bf16[9,24,128]{2,1,0:T(8,128)(2,1)S(1)}, bf16[9,24,128]{2,1,0:T(8,128)(2,1)S(1)}, u32[]{:S(2)}, u32[]{:S(2)}) collective-permute-start(bf16[9,24,128]{2,1,0:T(8,128)(2,1)S(1)} %get-tuple-element.106), channel_id=1, source_target_pairs={{0,28},{4,8},{8,4},{12,16},{16,12},{20,24},{24,20},{28,0},{1,29},{... | collective-permute-start | bytes 165896 | tf_op jit(solution)/shard_map/ppermute | solution.py:487
  71.0 9.4 %collective-permute-start.28 = (bf16[9,24,128]{2,1,0:T(8,128)(2,1)S(1)}, bf16[9,24,128]{2,1,0:T(8,128)(2,1)S(1)}, u32[]{:S(2)}, u32[]{:S(2)}) collective-permute-start(bf16[9,24,128]{2,1,0:T(8,128)(2,1)S(1)} %get-tuple-element.109), channel_id=1, source_target_pairs={{0,8},{4,12},{8,0},{12,4},{16,24},{20,28},{24,16},{28,20},{1,9},{5... | collective-permute-start | bytes 165896 | tf_op jit(solution)/shard_map/ppermute | solution.py:487
  71.1 9.3 %collective-permute-start.29 = (bf16[9,24,128]{2,1,0:T(8,128)(2,1)S(1)}, bf16[9,24,128]{2,1,0:T(8,128)(2,1)S(1)}, u32[]{:S(2)}, u32[]{:S(2)}) collective-permute-start(bf16[9,24,128]{2,1,0:T(8,128)(2,1)S(1)} %get-tuple-element.110), channel_id=1, source_target_pairs={{0,24},{4,28},{8,16},{12,20},{16,8},{20,12},{24,0},{28,4},{1,25},{... | collective-permute-start | bytes 165896 | tf_op jit(solution)/shard_map/ppermute | solution.py:487
  72.5 4.1 %collective-permute-start.27 = (bf16[8,24,128]{2,1,0:T(8,128)(2,1)S(1)}, bf16[8,24,128]{2,1,0:T(8,128)(2,1)S(1)}, u32[]{:S(2)}, u32[]{:S(2)}) collective-permute-start(bf16[8,24,128]{2,1,0:T(8,128)(2,1)S(1)} %get-tuple-element.108), channel_id=1, source_target_pairs={{0,4},{4,0},{8,12},{12,8},{16,20},{20,16},{24,28},{28,24},{1,5},{5... | collective-permute-start | bytes 147464 | tf_op jit(solution)/shard_map/ppermute | solution.py:487
  73.6 6.8 %collective-permute-start.30 = (bf16[8,24,128]{2,1,0:T(8,128)(2,1)S(1)}, bf16[8,24,128]{2,1,0:T(8,128)(2,1)S(1)}, u32[]{:S(2)}, u32[]{:S(2)}) collective-permute-start(bf16[8,24,128]{2,1,0:T(8,128)(2,1)S(1)} %get-tuple-element.111), channel_id=1, source_target_pairs={{0,28},{4,8},{8,4},{12,16},{16,12},{20,24},{24,20},{28,0},{1,29},{... | collective-permute-start | bytes 147464 | tf_op jit(solution)/shard_map/ppermute | solution.py:487
  80.5 2.2 %collective-permute-start.31 = (bf16[9,24,128]{2,1,0:T(8,128)(2,1)S(1)}, bf16[9,24,128]{2,1,0:T(8,128)(2,1)S(1)}, u32[]{:S(2)}, u32[]{:S(2)}) collective-permute-start(bf16[9,24,128]{2,1,0:T(8,128)(2,1)S(1)} %get-tuple-element.115), channel_id=1, source_target_pairs={{0,1},{1,0},{2,3},{3,2},{4,5},{5,4},{6,7},{7,6},{8,9},{9,8},{10,11... | collective-permute-start | bytes 165896 | tf_op jit(solution)/shard_map/ppermute | solution.py:493
  80.6 4.3 %collective-permute-start.32 = (bf16[9,24,128]{2,1,0:T(8,128)(2,1)S(1)}, bf16[9,24,128]{2,1,0:T(8,128)(2,1)S(1)}, u32[]{:S(2)}, u32[]{:S(2)}) collective-permute-start(bf16[9,24,128]{2,1,0:T(8,128)(2,1)S(1)} %get-tuple-element.116), channel_id=1, source_target_pairs={{0,2},{1,3},{2,0},{3,1},{4,6},{5,7},{6,4},{7,5},{8,10},{9,11},{10,... | collective-permute-start | bytes 165896 | tf_op jit(solution)/shard_map/ppermute | solution.py:493
  82.2 3.8 %collective-permute-start.33 = (bf16[9,24,128]{2,1,0:T(8,128)(2,1)S(1)}, bf16[9,24,128]{2,1,0:T(8,128)(2,1)S(1)}, u32[]{:S(2)}, u32[]{:S(2)}) collective-permute-start(bf16[9,24,128]{2,1,0:T(8,128)(2,1)S(1)} %get-tuple-element.117), channel_id=1, source_target_pairs={{0,3},{1,2},{2,1},{3,0},{4,7},{5,6},{6,5},{7,4},{8,11},{9,10},{10,... | collective-permute-start | bytes 165896 | tf_op jit(solution)/shard_map/ppermute | solution.py:493

commit v7 on v6

--- a/solution.py
+++ b/solution.py
@@ -53,7 +53,8 @@
         self.pieces = max(1, 128 // self.extra)
         self.slabs = max(1, self.extra // 128)
         self.head = self.faces + self.faces * self.tail // self.lanes
-        self.packed = self.head + self.faces * self.slabs // self.pieces
+        self.each = self.own * self.slabs // self.pieces
+        self.packed = self.head + 2 * self.each
         self.t_src = 0
         self.t_arr = SLOTS
         self.t_slot = 2 * SLOTS
@@ -126,7 +127,7 @@
 
 
 def narrow_kernel(z, start, coarse, out, held, basis, sems):
-    pieces = 4
+    pieces = 2
     size = z.rhs // pieces
     copies = [
         pltpu.make_async_copy(start.at[pl.ds(i * size, size)], held.at[pl.ds(i * size, size)], sems.at[i])
@@ -297,7 +298,8 @@
         replies[2][CAP:] = jnp.where(high, ahead, behind).astype(BF)
 
 
-def spread_first(z, table, *refs):
+def spread_first(z, mask, table, *refs):
+    g = lax.axis_index("grp")
     blocks, out, data = refs[:LINKS], refs[-2], refs[-1]
     for link, b in enumerate(blocks):
         data[link * CAP : (link + 1) * CAP] = b[:CAP]
@@ -310,15 +312,18 @@
             left = data[table[z.t_slot + f], :, z.lanes : z.rhs]
             right = data[table[z.t_slot + f + half], :, z.lanes : z.rhs]
             out[z.faces + member * half + i] = jnp.concatenate([left, right], axis=1)
-    if z.pieces > 1:
-        for p in range(z.faces // z.pieces):
-            ends = [data[table[z.t_slot + p * z.pieces + i], :, z.rhs : z.rhs + z.extra] for i in range(z.pieces)]
-            out[z.head + p] = jnp.concatenate(ends, axis=1)
-    else:
-        for f in range(z.faces):
-            for p in range(z.slabs):
-                at = z.rhs + p * 128
-                out[z.head + f * z.slabs + p] = data[table[z.t_slot + f], :, at : at + 128]
+    for order, target in enumerate((mask, mask ^ 1)):
+        slots = [table[z.t_slot + (g ^ target) * z.own + i] for i in range(z.own)]
+        at = z.head + order * z.each
+        if z.pieces > 1:
+            for p in range(z.each):
+                mine = slots[p * z.pieces : (p + 1) * z.pieces]
+                out[at + p] = jnp.concatenate([data[k, :, z.rhs : z.rhs + z.extra] for k in mine], axis=1)
+        else:
+            for f in range(z.own):
+                for p in range(z.slabs):
+                    low = z.rhs + p * 128
+                    out[at + f * z.slabs + p] = data[slots[f], :, low : low + 128]
 
 
 def spread_second(z, table, *refs):
@@ -389,10 +394,10 @@
             rows = pl.ds(pl.multiple_of(i * MODES + (g ^ jj) * z.share, z.share), z.share)
             if z.pieces > 1:
                 low = (i % z.pieces) * z.extra
-                scales[rows, :] = a[z.head + (g * z.own + i) // z.pieces, :, low : low + z.extra]
+                scales[rows, :] = a[z.head + jj % 2 * z.each + i // z.pieces, :, low : low + z.extra]
             else:
                 for p in range(z.slabs):
-                    scales[rows, p * 128 : (p + 1) * 128] = a[z.head + (g * z.own + i) * z.slabs + p]
+                    scales[rows, p * 128 : (p + 1) * 128] = a[z.head + jj % 2 * z.each + i * z.slabs + p]
     hits_out[...] = scales[:, z.vertices :]
     flat = scales[:, : z.vertices]
     ext = ext_in[...].reshape(z.own * MODES, z.wide - z.rhs)
@@ -514,7 +519,7 @@
         scratch_shapes=[
             pltpu.VMEM((z.rhs, z.rows), F32),
             pltpu.VMEM((z.corners, z.rows), BF),
-            pltpu.SemaphoreType.DMA((5,)),
+            pltpu.SemaphoreType.DMA((3,)),
         ],
         compiler_params=pltpu.CompilerParams(vmem_limit_bytes=16 << 20),
     )(*[pltpu.with_memory_space_constraint(a, pltpu.HBM) for a in (first, coarse_basis[0])])
@@ -583,14 +588,19 @@
     answered = paired(replies)
     pair_three = swapped(pair_two, 1)
     answered, pair_three = lax.optimization_barrier((answered, pair_three))
-    spread = call(
-        spread_first,
-        z,
-        shape((z.packed, z.share, z.lanes), BF),
-        (table, *answered),
-        (pltpu.VMEM((SLOTS, z.share, z.wide), BF),),
-    )
-    spread_two = swapped(spread, 2)
+    def spread_for(mask):
+        return call(
+            spread_first,
+            z,
+            shape((z.packed, z.share, z.lanes), BF),
+            (table, *answered),
+            (pltpu.VMEM((SLOTS, z.share, z.wide), BF),),
+            (mask,),
+        )
+
+    spread_far = spread_for(2)
+    spread = spread_for(0)
+    spread_two = swapped(spread_far, 2)
     spread_one = swapped(spread, 1)
     spread_three = swapped(spread_two, 1)
     shares = [spread, spread_one, spread_two, spread_three]

time: 87.7 us -> 87.3 us (level)
    pallas_call x15 -> x16, Pallas kernels: 7.45 us -> 7.56 us  [call(): pl.pallas_call(functools.partial(kernel, sizes, *static), out_shape=[pltp...]
  transfers between devices with their start and end apart: 34 -> 34, of which waited for: 15 -> 15; matrix products, arithmetic and copies ran while one was open for 0% -> 0% of each run, Pallas kernels for 8% -> 9%
where the time goes in v7:
time: 87.3 us; the launch traced here: 87 us
  waiting for transfers between devices  37.7 us (43%)
  starting transfers between devices  35.3 us (40%)
  Pallas kernels  13.7 us (16%)
    ppermute x16, starting transfers between devices, paired(): met.append(lax.ppermute(blocks[k], 'sub', p))  23.1 us
    ppermute x18, waiting for transfers between devices, swapped(): return lax.ppermute(value, 'grp', [(s, s ^ mask) for s in range(count)])  19.5 us
    ppermute x16, waiting for transfers between devices, paired(): met.append(lax.ppermute(blocks[k], 'sub', p))  18.3 us
    ppermute x18, starting transfers between devices, swapped(): return lax.ppermute(value, 'grp', [(s, s ^ mask) for s in range(count)])  12.2 us
    pallas_call x16, Pallas kernels, call(): pl.pallas_call(functools.partial(kernel, sizes, *static), out_shape=[pltp...  7.56 us
    pallas_call x1, Pallas kernels, run(): pl.pallas_call(functools.partial(table_kernel, z), out_shape=pltpu.SMEM((...  1.88 us
    pallas_call x1, Pallas kernels, run(): pl.pallas_call(functools.partial(load_kernel, z), out_shape=[pltpu.VMEM(a...  1.81 us
  transfers between devices with their start and end apart: 34, of which 15 were waited for; matrix products, arithmetic and copies ran while one was open for 0% of the time, Pallas kernels for 9%

profile of v7, /device:TPU:0, one launch (start us, length us, event | category | flops | bytes accessed | tf_op | source)
XLA Modules:
  0.0 87.0 jit_solution(7389510306455648271)
XLA Ops:
  0.0 1.1 %shard_map.101.b0 = bf16[200,512]{1,0:T(8,128)(2,1)S(1)} custom-call(f32[192,512]{1,0:T(8,128)} %bitcast.13, bf16[8,512]{1,0:T(8,128)(2,1)} %bitcast.20), custom_call_target="tpu_custom_call" | custom-call | tf_op jit(solution)/shard_map/pallas_call | solution.py:514
  1.1 3.0 %collective-permute-start = (bf16[200,512]{1,0:T(8,128)(2,1)S(1)}, bf16[200,512]{1,0:T(8,128)(2,1)S(1)}, u32[]{:S(2)}, u32[]{:S(2)}) collective-permute-start(bf16[200,512]{1,0:T(8,128)(2,1)S(1)} %shard_map.101.b0), channel_id=1, source_target_pairs={{0,2},{1,3},{2,0},{3,1},{4,6},{5,7},{6,4},{7,5},{8,10},{9,11},{10,... | collective-permute-start | bytes 614408 | tf_op jit(solution)/shard_map/ppermute | solution.py:498
  4.1 5.1 %collective-permute-done.block = bf16[200,512]{1,0:T(8,128)(2,1)S(1)} collective-permute-done((bf16[200,512]{1,0:T(8,128)(2,1)S(1)}, bf16[200,512]{1,0:T(8,128)(2,1)S(1)}, u32[]{:S(2)}, u32[]{:S(2)}) %collective-permute-start) | collective-permute-done | bytes 204832 | tf_op jit(solution)/shard_map/ppermute | solution.py:498
  9.2 1.8 %shard_map.100 = (bf16[512,2048]{1,0:T(8,128)(2,1)S(1)}, f32[192,512]{1,0:T(8,128)S(1)}, bf16[8,512]{1,0:T(8,128)(2,1)S(1)}, bf16[8,64,64]{2,1,0:T(8,128)(2,1)S(1)}) custom-call(bf16[512,2048]{1,0:T(8,128)(2,1)} %bitcast.15, f32[192,512]{1,0:T(8,128)} %bitcast.16, bf16[8,512]{1,0:T(8,128)(2,1)} %bitcast.21, bf16[8,4096]{1,0:T(8,128)(2,1)} %bitcast.17), custom_call_target="tpu_custom_call" | custom-call | tf_op jit(solution)/shard_map/pallas_call | solution.py:537
  11.0 0.3 shard_map.102.before
  11.3 1.9 %shard_map.103.table = s32[152]{0:T(256)S(4)} custom-call(s32[8,1,32]{2,1,0:T(1,128)} %bitcast.22, s32[8,32]{1,0:T(8,128)} %mortar.1, s32[8,16]{1,0:T(8,128)} %order.1, s32[8]{0:T(128)} %smap.1, s32[8,8]{1,0:T(8,128)} %vids.1), custom_call_target="tpu_custom_call" | custom-call | tf_op jit(solution)/shard_map/pallas_call | solution.py:529
  13.2 0.3 shard_map.104.before
  13.6 0.3 shard_map.105.before
  13.9 2.1 %shard_map.106 = (bf16[8,16,256]{2,1,0:T(8,128)(2,1)S(1)}, bf16[8,16,256]{2,1,0:T(8,128)(2,1)S(1)}, bf16[8,16,256]{2,1,0:T(8,128)(2,1)S(1)}, bf16[8,16,256]{2,1,...) custom-call(s32[152]{0:T(256)S(4)} %shard_map.103.table, ...), custom_call_target="tpu_custom_call" | custom-call | tf_op jit(solution)/shard_map/pallas_call | solution.py:74
  16.0 0.6 collective-permute-start.3
  16.6 1.7 %collective-permute-start.4 = (bf16[8,16,256]{2,1,0:T(8,128)(2,1)S(1)}, bf16[8,16,256]{2,1,0:T(8,128)(2,1)S(1)}, u32[]{:S(2)}, u32[]{:S(2)}) collective-permute-start(bf16[8,16,256]{2,1,0:T(8,128)(2,1)S(1)} %get-tuple-element.71), channel_id=1, source_target_pairs={{0,2},{1,3},{2,0},{3,1},{4,6},{5,7},{6,4},{7,5},{8,10},{9,11},{10,... | collective-permute-start | bytes 196616 | tf_op jit(solution)/shard_map/ppermute | solution.py:498
  18.3 1.4 %collective-permute-start.11 = (bf16[8,4096]{1,0:T(8,128)(2,1)S(1)}, bf16[8,4096]{1,0:T(8,128)(2,1)S(1)}, u32[]{:S(2)}, u32[]{:S(2)}) collective-permute-start(bf16[8,4096]{1,0:T(8,128)(2,1)S(1)} %bitcast.18), channel_id=1, source_target_pairs={{0,2},{1,3},{2,0},{3,1},{4,6},{5,7},{6,4},{7,5},{8,10},{9,11},{10,... | collective-permute-start | bytes 196616 | tf_op jit(solution)/shard_map/ppermute | solution.py:498
  19.7 0.4 collective-permute-start.10
  20.2 0.7 collective-permute-done.4.c2
  20.8 1.9 %collective-permute-done.5.c3 = bf16[8,16,256]{2,1,0:T(8,128)(2,1)S(1)} collective-permute-done((bf16[8,16,256]{2,1,0:T(8,128)(2,1)S(1)}, bf16[8,16,256]{2,1,0:T(8,128)(2,1)S(1)}, u32[]{:S(2)}, u32[]{:S(2)}) %collective-permute-start.5) | collective-permute-done | bytes 65568 | tf_op jit(solution)/shard_map/ppermute | solution.py:498
  22.7 1.6 %collective-permute-start.6 = (bf16[8,16,256]{2,1,0:T(8,128)(2,1)S(1)}, bf16[8,16,256]{2,1,0:T(8,128)(2,1)S(1)}, u32[]{:S(2)}, u32[]{:S(2)}) collective-permute-start(bf16[8,16,256]{2,1,0:T(8,128)(2,1)S(1)} %get-tuple-element.73), channel_id=1, source_target_pairs={{0,4},{4,0},{8,12},{12,8},{16,20},{20,16},{24,28},{28,24},{1,5},{5... | collective-permute-start | bytes 196616 | tf_op jit(solution)/shard_map/ppermute | solution.py:492
  24.3 1.6 %collective-permute-start.7 = (bf16[8,16,256]{2,1,0:T(8,128)(2,1)S(1)}, bf16[8,16,256]{2,1,0:T(8,128)(2,1)S(1)}, u32[]{:S(2)}, u32[]{:S(2)}) collective-permute-start(bf16[8,16,256]{2,1,0:T(8,128)(2,1)S(1)} %get-tuple-element.74), channel_id=1, source_target_pairs={{0,8},{4,12},{8,0},{12,4},{16,24},{20,28},{24,16},{28,20},{1,9},{5... | collective-permute-start | bytes 196616 | tf_op jit(solution)/shard_map/ppermute | solution.py:492
  25.9 2.5 %collective-permute-start.8 = (bf16[8,16,256]{2,1,0:T(8,128)(2,1)S(1)}, bf16[8,16,256]{2,1,0:T(8,128)(2,1)S(1)}, u32[]{:S(2)}, u32[]{:S(2)}) collective-permute-start(bf16[8,16,256]{2,1,0:T(8,128)(2,1)S(1)} %get-tuple-element.75), channel_id=1, source_target_pairs={{0,24},{4,28},{8,16},{12,20},{16,8},{20,12},{24,0},{28,4},{1,25},{... | collective-permute-start | bytes 196616 | tf_op jit(solution)/shard_map/ppermute | solution.py:492
  28.4 1.3 %collective-permute-start.9 = (bf16[8,16,256]{2,1,0:T(8,128)(2,1)S(1)}, bf16[8,16,256]{2,1,0:T(8,128)(2,1)S(1)}, u32[]{:S(2)}, u32[]{:S(2)}) collective-permute-start(bf16[8,16,256]{2,1,0:T(8,128)(2,1)S(1)} %get-tuple-element.76), channel_id=1, source_target_pairs={{0,28},{4,8},{8,4},{12,16},{16,12},{20,24},{24,20},{28,0},{1,29},{... | collective-permute-start | bytes 196616 | tf_op jit(solution)/shard_map/ppermute | solution.py:492
  29.7 3.0 %collective-permute-done.8.refs_2_ = bf16[8,16,256]{2,1,0:T(8,128)(2,1)S(1)} collective-permute-done((bf16[8,16,256]{2,1,0:T(8,128)(2,1)S(1)}, bf16[8,16,256]{2,1,0:T(8,128)(2,1)S(1)}, u32[]{:S(2)}, u32[]{:S(2)}) %collective-permute-start.8) | collective-permute-done | bytes 65568 | tf_op jit(solution)/shard_map/ppermute | solution.py:492
  32.7 2.6 %collective-permute-done.9.refs_3_ = bf16[8,16,256]{2,1,0:T(8,128)(2,1)S(1)} collective-permute-done((bf16[8,16,256]{2,1,0:T(8,128)(2,1)S(1)}, bf16[8,16,256]{2,1,0:T(8,128)(2,1)S(1)}, u32[]{:S(2)}, u32[]{:S(2)}) %collective-permute-start.9) | collective-permute-done | bytes 65568 | tf_op jit(solution)/shard_map/ppermute | solution.py:492
  35.3 0.3 shard_map.108
  35.8 1.8 %collective-permute-start.14 = (bf16[8,16,256]{2,1,0:T(8,128)(2,1)S(1)}, bf16[8,16,256]{2,1,0:T(8,128)(2,1)S(1)}, u32[]{:S(2)}, u32[]{:S(2)}) collective-permute-start(bf16[8,16,256]{2,1,0:T(8,128)(2,1)S(1)} %get-tuple-element.88), channel_id=1, source_target_pairs={{0,24},{4,28},{8,16},{12,20},{16,8},{20,12},{24,0},{28,4},{1,25},{... | collective-permute-start | bytes 196616 | tf_op jit(solution)/shard_map/ppermute | solution.py:492
  37.6 3.4 %collective-permute-start.15 = (bf16[8,16,256]{2,1,0:T(8,128)(2,1)S(1)}, bf16[8,16,256]{2,1,0:T(8,128)(2,1)S(1)}, u32[]{:S(2)}, u32[]{:S(2)}) collective-permute-start(bf16[8,16,256]{2,1,0:T(8,128)(2,1)S(1)} %get-tuple-element.89), channel_id=1, source_target_pairs={{0,28},{4,8},{8,4},{12,16},{16,12},{20,24},{24,20},{28,0},{1,29},{... | collective-permute-start | bytes 196616 | tf_op jit(solution)/shard_map/ppermute | solution.py:492
  41.0 1.3 %collective-permute-done.14.refs_2_ = bf16[8,16,256]{2,1,0:T(8,128)(2,1)S(1)} collective-permute-done((bf16[8,16,256]{2,1,0:T(8,128)(2,1)S(1)}, bf16[8,16,256]{2,1,0:T(8,128)(2,1)S(1)}, u32[]{:S(2)}, u32[]{:S(2)}) %collective-permute-start.14) | collective-permute-done | bytes 65568 | tf_op jit(solution)/shard_map/ppermute | solution.py:492
  42.3 2.4 %collective-permute-done.15.refs_3_ = bf16[8,16,256]{2,1,0:T(8,128)(2,1)S(1)} collective-permute-done((bf16[8,16,256]{2,1,0:T(8,128)(2,1)S(1)}, bf16[8,16,256]{2,1,0:T(8,128)(2,1)S(1)}, u32[]{:S(2)}, u32[]{:S(2)}) %collective-permute-start.15) | collective-permute-done | bytes 65568 | tf_op jit(solution)/shard_map/ppermute | solution.py:492
  44.8 1.0 %collective-permute-start.18 = (bf16[52,16,128]{2,1,0:T(8,128)(2,1)S(1)}, bf16[52,16,128]{2,1,0:T(8,128)(2,1)S(1)}, u32[]{:S(2)}, u32[]{:S(2)}) collective-permute-start(bf16[52,16,128]{2,1,0:T(8,128)(2,1)S(1)} %shard_map.111), channel_id=1, source_target_pairs={{0,2},{1,3},{2,0},{3,1},{4,6},{5,7},{6,4},{7,5},{8,10},{9,11},{10,... | collective-permute-start | bytes 638984 | tf_op jit(solution)/shard_map/ppermute | solution.py:498
  46.1 5.4 %collective-permute-done.18.a2.refs_2_ = bf16[52,16,128]{2,1,0:T(8,128)(2,1)S(1)} collective-permute-done((bf16[52,16,128]{2,1,0:T(8,128)(2,1)S(1)}, bf16[52,16,128]{2,1,0:T(8,128)(2,1)S(1)}, u32[]{:S(2)}, u32[]{:S(2)}) %collective-permute-start.18) | collective-permute-done | bytes 213024 | tf_op jit(solution)/shard_map/ppermute | solution.py:498
  51.5 1.9 %shard_map.109.mixed = bf16[512,2048]{1,0:T(8,128)(2,1)S(1)} custom-call(bf16[512,2048]{1,0:T(8,128)(2,1)S(1)} %get-tuple-element.63.schur, bf16[8,64,64]{2,1,0:T(8,128)(2,1)S(1)} %get-tuple-element.66.tables.t0.refs_4_, bf16[8,4096]{1,0:T(8,128)(2,1)S(1)} %collective-permute-done.10.r1, bf16[8,4096]{1,0:T(8,128)(2,1)S(1)} %collective-permute-done.11.r2, ...), custom_call_target="tpu_custom_call" | custom-call | tf_op jit(solution)/shard_map/pallas_call | solution.py:74
  53.7 1.1 %shard_map.114 = (bf16[9,24,128]{2,1,0:T(8,128)(2,1)S(1)}, bf16[9,24,128]{2,1,0:T(8,128)(2,1)S(1)}, bf16[9,24,128]{2,1,0:T(8,128)(2,1)S(1)}, bf16[9,24,128]{2,1,...) custom-call(s32[152]{0:T(256)S(4)} %shard_map.103.table, ...), custom_call_target="tpu_custom_call", output_to_operand_aliasing={{7}: (8, {})} | custom-call | tf_op jit(solution)/shard_map/pallas_call | solution.py:74
  54.8 0.6 collective-permute-start.20
  55.4 0.3 collective-permute-start.21
  55.7 1.1 %collective-permute-start.22 = (bf16[9,24,128]{2,1,0:T(8,128)(2,1)S(1)}, bf16[9,24,128]{2,1,0:T(8,128)(2,1)S(1)}, u32[]{:S(2)}, u32[]{:S(2)}) collective-permute-start(bf16[9,24,128]{2,1,0:T(8,128)(2,1)S(1)} %get-tuple-element.102), channel_id=1, source_target_pairs={{0,3},{1,2},{2,1},{3,0},{4,7},{5,6},{6,5},{7,4},{8,11},{9,10},{10,... | collective-permute-start | bytes 165896 | tf_op jit(solution)/shard_map/ppermute | solution.py:498
  56.8 3.0 %collective-permute-done.21.c2 = bf16[9,24,128]{2,1,0:T(8,128)(2,1)S(1)} collective-permute-done((bf16[9,24,128]{2,1,0:T(8,128)(2,1)S(1)}, bf16[9,24,128]{2,1,0:T(8,128)(2,1)S(1)}, u32[]{:S(2)}, u32[]{:S(2)}) %collective-permute-start.21) | collective-permute-done | bytes 55328 | tf_op jit(solution)/shard_map/ppermute | solution.py:498
  59.9 1.1 %collective-permute-start.23 = (bf16[9,24,128]{2,1,0:T(8,128)(2,1)S(1)}, bf16[9,24,128]{2,1,0:T(8,128)(2,1)S(1)}, u32[]{:S(2)}, u32[]{:S(2)}) collective-permute-start(bf16[9,24,128]{2,1,0:T(8,128)(2,1)S(1)} %get-tuple-element.103), channel_id=1, source_target_pairs={{0,4},{4,0},{8,12},{12,8},{16,20},{20,16},{24,28},{28,24},{1,5},{5... | collective-permute-start | bytes 165896 | tf_op jit(solution)/shard_map/ppermute | solution.py:492
  61.1 1.0 %collective-permute-start.24 = (bf16[9,24,128]{2,1,0:T(8,128)(2,1)S(1)}, bf16[9,24,128]{2,1,0:T(8,128)(2,1)S(1)}, u32[]{:S(2)}, u32[]{:S(2)}) collective-permute-start(bf16[9,24,128]{2,1,0:T(8,128)(2,1)S(1)} %get-tuple-element.104), channel_id=1, source_target_pairs={{0,8},{4,12},{8,0},{12,4},{16,24},{20,28},{24,16},{28,20},{1,9},{5... | collective-permute-start | bytes 165896 | tf_op jit(solution)/shard_map/ppermute | solution.py:492
  62.1 1.4 %collective-permute-start.25 = (bf16[9,24,128]{2,1,0:T(8,128)(2,1)S(1)}, bf16[9,24,128]{2,1,0:T(8,128)(2,1)S(1)}, u32[]{:S(2)}, u32[]{:S(2)}) collective-permute-start(bf16[9,24,128]{2,1,0:T(8,128)(2,1)S(1)} %get-tuple-element.105), channel_id=1, source_target_pairs={{0,24},{4,28},{8,16},{12,20},{16,8},{20,12},{24,0},{28,4},{1,25},{... | collective-permute-start | bytes 165896 | tf_op jit(solution)/shard_map/ppermute | solution.py:492
  63.5 1.9 %collective-permute-start.26 = (bf16[9,24,128]{2,1,0:T(8,128)(2,1)S(1)}, bf16[9,24,128]{2,1,0:T(8,128)(2,1)S(1)}, u32[]{:S(2)}, u32[]{:S(2)}) collective-permute-start(bf16[9,24,128]{2,1,0:T(8,128)(2,1)S(1)} %get-tuple-element.106), channel_id=1, source_target_pairs={{0,28},{4,8},{8,4},{12,16},{16,12},{20,24},{24,20},{28,0},{1,29},{... | collective-permute-start | bytes 165896 | tf_op jit(solution)/shard_map/ppermute | solution.py:492
  65.4 2.7 %collective-permute-done.25.refs_2_ = bf16[9,24,128]{2,1,0:T(8,128)(2,1)S(1)} collective-permute-done((bf16[9,24,128]{2,1,0:T(8,128)(2,1)S(1)}, bf16[9,24,128]{2,1,0:T(8,128)(2,1)S(1)}, u32[]{:S(2)}, u32[]{:S(2)}) %collective-permute-start.25) | collective-permute-done | bytes 55328 | tf_op jit(solution)/shard_map/ppermute | solution.py:492
  68.1 2.2 %collective-permute-done.26.refs_3_ = bf16[9,24,128]{2,1,0:T(8,128)(2,1)S(1)} collective-permute-done((bf16[9,24,128]{2,1,0:T(8,128)(2,1)S(1)}, bf16[9,24,128]{2,1,0:T(8,128)(2,1)S(1)}, u32[]{:S(2)}, u32[]{:S(2)}) %collective-permute-start.26) | collective-permute-done | bytes 55328 | tf_op jit(solution)/shard_map/ppermute | solution.py:492
  70.7 1.4 %collective-permute-start.29 = (bf16[9,24,128]{2,1,0:T(8,128)(2,1)S(1)}, bf16[9,24,128]{2,1,0:T(8,128)(2,1)S(1)}, u32[]{:S(2)}, u32[]{:S(2)}) collective-permute-start(bf16[9,24,128]{2,1,0:T(8,128)(2,1)S(1)} %get-tuple-element.110), channel_id=1, source_target_pairs={{0,24},{4,28},{8,16},{12,20},{16,8},{20,12},{24,0},{28,4},{1,25},{... | collective-permute-start | bytes 165896 | tf_op jit(solution)/shard_map/ppermute | solution.py:492
  72.1 1.1 %collective-permute-start.27 = (bf16[8,24,128]{2,1,0:T(8,128)(2,1)S(1)}, bf16[8,24,128]{2,1,0:T(8,128)(2,1)S(1)}, u32[]{:S(2)}, u32[]{:S(2)}) collective-permute-start(bf16[8,24,128]{2,1,0:T(8,128)(2,1)S(1)} %get-tuple-element.108), channel_id=1, source_target_pairs={{0,4},{4,0},{8,12},{12,8},{16,20},{20,16},{24,28},{28,24},{1,5},{5... | collective-permute-start | bytes 147464 | tf_op jit(solution)/shard_map/ppermute | solution.py:492
  73.2 2.8 %collective-permute-start.30 = (bf16[8,24,128]{2,1,0:T(8,128)(2,1)S(1)}, bf16[8,24,128]{2,1,0:T(8,128)(2,1)S(1)}, u32[]{:S(2)}, u32[]{:S(2)}) collective-permute-start(bf16[8,24,128]{2,1,0:T(8,128)(2,1)S(1)} %get-tuple-element.111), channel_id=1, source_target_pairs={{0,28},{4,8},{8,4},{12,16},{16,12},{20,24},{24,20},{28,0},{1,29},{... | collective-permute-start | bytes 147464 | tf_op jit(solution)/shard_map/ppermute | solution.py:492
  76.2 3.8 %collective-permute-done.30.refs_3_ = bf16[8,24,128]{2,1,0:T(8,128)(2,1)S(1)} collective-permute-done((bf16[8,24,128]{2,1,0:T(8,128)(2,1)S(1)}, bf16[8,24,128]{2,1,0:T(8,128)(2,1)S(1)}, u32[]{:S(2)}, u32[]{:S(2)}) %collective-permute-start.30) | collective-permute-done | bytes 49184 | tf_op jit(solution)/shard_map/ppermute | solution.py:492
  80.2 1.7 %collective-permute-start.32 = (bf16[9,24,128]{2,1,0:T(8,128)(2,1)S(1)}, bf16[9,24,128]{2,1,0:T(8,128)(2,1)S(1)}, u32[]{:S(2)}, u32[]{:S(2)}) collective-permute-start(bf16[9,24,128]{2,1,0:T(8,128)(2,1)S(1)} %get-tuple-element.116), channel_id=1, source_target_pairs={{0,2},{1,3},{2,0},{3,1},{4,6},{5,7},{6,4},{7,5},{8,10},{9,11},{10,... | collective-permute-start | bytes 165896 | tf_op jit(solution)/shard_map/ppermute | solution.py:498
  82.3 2.1 %collective-permute-done.32.refs_2_ = bf16[9,24,128]{2,1,0:T(8,128)(2,1)S(1)} collective-permute-done((bf16[9,24,128]{2,1,0:T(8,128)(2,1)S(1)}, bf16[9,24,128]{2,1,0:T(8,128)(2,1)S(1)}, u32[]{:S(2)}, u32[]{:S(2)}) %collective-permute-start.32) | collective-permute-done | bytes 55328 | tf_op jit(solution)/shard_map/ppermute | solution.py:498
  84.4 1.2 %collective-permute-done.33.refs_3_ = bf16[9,24,128]{2,1,0:T(8,128)(2,1)S(1)} collective-permute-done((bf16[9,24,128]{2,1,0:T(8,128)(2,1)S(1)}, bf16[9,24,128]{2,1,0:T(8,128)(2,1)S(1)}, u32[]{:S(2)}, u32[]{:S(2)}) %collective-permute-start.33) | collective-permute-done | bytes 55328 | tf_op jit(solution)/shard_map/ppermute | solution.py:498
  85.7 1.4 %shard_map.119 = f32[192,512]{1,0:T(8,128)} custom-call(s32[152]{0:T(256)S(4)} %shard_map.103.table, bf16[9,24,128]{2,1,0:T(8,128)(2,1)S(1)} %get-tuple-element.114.refs_0_, bf16[9,24,128]{2,1,0:T(8,128)(2,1)S(1)} %collective-permute-done.31.refs_1_, bf16[9,24,128]{2,1,0:T(8,128)(2,1)S(1)} %collective-permute-done.32.refs_2_, ...), custom_call_target="tpu_custom_call" | custom-call | tf_op jit(solution)/shard_map/pallas_call | solution.py:656
  (44 shorter events, 2.0 us)
Async XLA Ops:
  1.1 8.1 %collective-permute-start = (bf16[200,512]{1,0:T(8,128)(2,1)S(1)}, bf16[200,512]{1,0:T(8,128)(2,1)S(1)}, u32[]{:S(2)}, u32[]{:S(2)}) collective-permute-start(bf16[200,512]{1,0:T(8,128)(2,1)S(1)} %shard_map.101.b0), channel_id=1, source_target_pairs={{0,2},{1,3},{2,0},{3,1},{4,6},{5,7},{6,4},{7,5},{8,10},{9,11},{10,... | collective-permute-start | bytes 614408 | tf_op jit(solution)/shard_map/ppermute | solution.py:498
  4.1 9.1 %collective-permute-start.2 = (bf16[200,512]{1,0:T(8,128)(2,1)S(1)}, bf16[200,512]{1,0:T(8,128)(2,1)S(1)}, u32[]{:S(2)}, u32[]{:S(2)}) collective-permute-start(bf16[200,512]{1,0:T(8,128)(2,1)S(1)} %shard_map.101.b0), channel_id=1, source_target_pairs={{0,1},{1,0},{2,3},{3,2},{4,5},{5,4},{6,7},{7,6},{8,9},{9,8},{10,11... | collective-permute-start | bytes 614408 | tf_op jit(solution)/shard_map/ppermute | solution.py:498
  9.2 4.7 %collective-permute-start.1 = (bf16[200,512]{1,0:T(8,128)(2,1)S(1)}, bf16[200,512]{1,0:T(8,128)(2,1)}, u32[]{:S(2)}, u32[]{:S(2)}) collective-permute-start(bf16[200,512]{1,0:T(8,128)(2,1)S(1)} %collective-permute-done.block), channel_id=1, source_target_pairs={{0,1},{1,0},{2,3},{3,2},{4,5},{5,4},{6,7},{7,6},{8,9},{9,8},{10,11... | collective-permute-start | bytes 614408 | tf_op jit(solution)/shard_map/ppermute | solution.py:498
  13.9 4.4 %copy-start.1 = (bf16[1,8,4096]{2,1,0:T(8,128)(2,1)S(1)}, bf16[1,8,4096]{2,1,0:T(8,128)(2,1)}, u32[]{:S(2)}) copy-start(bf16[1,8,4096]{2,1,0:T(8,128)(2,1)} %param.13) | copy-start | bytes 196612
  16.0 4.2 %collective-permute-start.3 = (bf16[8,16,256]{2,1,0:T(8,128)(2,1)S(1)}, bf16[8,16,256]{2,1,0:T(8,128)(2,1)S(1)}, u32[]{:S(2)}, u32[]{:S(2)}) collective-permute-start(bf16[8,16,256]{2,1,0:T(8,128)(2,1)S(1)} %get-tuple-element.70), channel_id=1, source_target_pairs={{0,1},{1,0},{2,3},{3,2},{4,5},{5,4},{6,7},{7,6},{8,9},{9,8},{10,11... | collective-permute-start | bytes 196616 | tf_op jit(solution)/shard_map/ppermute | solution.py:498
  16.6 4.3 %collective-permute-start.4 = (bf16[8,16,256]{2,1,0:T(8,128)(2,1)S(1)}, bf16[8,16,256]{2,1,0:T(8,128)(2,1)S(1)}, u32[]{:S(2)}, u32[]{:S(2)}) collective-permute-start(bf16[8,16,256]{2,1,0:T(8,128)(2,1)S(1)} %get-tuple-element.71), channel_id=1, source_target_pairs={{0,2},{1,3},{2,0},{3,1},{4,6},{5,7},{6,4},{7,5},{8,10},{9,11},{10,... | collective-permute-start | bytes 196616 | tf_op jit(solution)/shard_map/ppermute | solution.py:498
  18.3 4.4 %collective-permute-start.5 = (bf16[8,16,256]{2,1,0:T(8,128)(2,1)S(1)}, bf16[8,16,256]{2,1,0:T(8,128)(2,1)S(1)}, u32[]{:S(2)}, u32[]{:S(2)}) collective-permute-start(bf16[8,16,256]{2,1,0:T(8,128)(2,1)S(1)} %get-tuple-element.72), channel_id=1, source_target_pairs={{0,3},{1,2},{2,1},{3,0},{4,7},{5,6},{6,5},{7,4},{8,11},{9,10},{10,... | collective-permute-start | bytes 196616 | tf_op jit(solution)/shard_map/ppermute | solution.py:498
  18.3 10.1 %collective-permute-start.11 = (bf16[8,4096]{1,0:T(8,128)(2,1)S(1)}, bf16[8,4096]{1,0:T(8,128)(2,1)S(1)}, u32[]{:S(2)}, u32[]{:S(2)}) collective-permute-start(bf16[8,4096]{1,0:T(8,128)(2,1)S(1)} %bitcast.18), channel_id=1, source_target_pairs={{0,2},{1,3},{2,0},{3,1},{4,6},{5,7},{6,4},{7,5},{8,10},{9,11},{10,... | collective-permute-start | bytes 196616 | tf_op jit(solution)/shard_map/ppermute | solution.py:498
  19.7 9.9 %collective-permute-start.10 = (bf16[8,4096]{1,0:T(8,128)(2,1)S(1)}, bf16[8,4096]{1,0:T(8,128)(2,1)S(1)}, u32[]{:S(2)}, u32[]{:S(2)}) collective-permute-start(bf16[8,4096]{1,0:T(8,128)(2,1)S(1)} %bitcast.19), channel_id=1, source_target_pairs={{0,1},{1,0},{2,3},{3,2},{4,5},{5,4},{6,7},{7,6},{8,9},{9,8},{10,11... | collective-permute-start | bytes 196616 | tf_op jit(solution)/shard_map/ppermute | solution.py:498
  22.7 6.9 %collective-permute-start.6 = (bf16[8,16,256]{2,1,0:T(8,128)(2,1)S(1)}, bf16[8,16,256]{2,1,0:T(8,128)(2,1)S(1)}, u32[]{:S(2)}, u32[]{:S(2)}) collective-permute-start(bf16[8,16,256]{2,1,0:T(8,128)(2,1)S(1)} %get-tuple-element.73), channel_id=1, source_target_pairs={{0,4},{4,0},{8,12},{12,8},{16,20},{20,16},{24,28},{28,24},{1,5},{5... | collective-permute-start | bytes 196616 | tf_op jit(solution)/shard_map/ppermute | solution.py:492
  24.3 5.4 %collective-permute-start.7 = (bf16[8,16,256]{2,1,0:T(8,128)(2,1)S(1)}, bf16[8,16,256]{2,1,0:T(8,128)(2,1)S(1)}, u32[]{:S(2)}, u32[]{:S(2)}) collective-permute-start(bf16[8,16,256]{2,1,0:T(8,128)(2,1)S(1)} %get-tuple-element.74), channel_id=1, source_target_pairs={{0,8},{4,12},{8,0},{12,4},{16,24},{20,28},{24,16},{28,20},{1,9},{5... | collective-permute-start | bytes 196616 | tf_op jit(solution)/shard_map/ppermute | solution.py:492
  25.9 6.8 %collective-permute-start.8 = (bf16[8,16,256]{2,1,0:T(8,128)(2,1)S(1)}, bf16[8,16,256]{2,1,0:T(8,128)(2,1)S(1)}, u32[]{:S(2)}, u32[]{:S(2)}) collective-permute-start(bf16[8,16,256]{2,1,0:T(8,128)(2,1)S(1)} %get-tuple-element.75), channel_id=1, source_target_pairs={{0,24},{4,28},{8,16},{12,20},{16,8},{20,12},{24,0},{28,4},{1,25},{... | collective-permute-start | bytes 196616 | tf_op jit(solution)/shard_map/ppermute | solution.py:492
  28.4 7.0 %collective-permute-start.9 = (bf16[8,16,256]{2,1,0:T(8,128)(2,1)S(1)}, bf16[8,16,256]{2,1,0:T(8,128)(2,1)S(1)}, u32[]{:S(2)}, u32[]{:S(2)}) collective-permute-start(bf16[8,16,256]{2,1,0:T(8,128)(2,1)S(1)} %get-tuple-element.76), channel_id=1, source_target_pairs={{0,28},{4,8},{8,4},{12,16},{16,12},{20,24},{24,20},{28,0},{1,29},{... | collective-permute-start | bytes 196616 | tf_op jit(solution)/shard_map/ppermute | solution.py:492
  35.3 5.7 %collective-permute-start.16 = (bf16[8,4096]{1,0:T(8,128)(2,1)S(1)}, bf16[8,4096]{1,0:T(8,128)(2,1)S(1)}, u32[]{:S(2)}, u32[]{:S(2)}) collective-permute-start(bf16[8,4096]{1,0:T(8,128)(2,1)S(1)} %collective-permute-done.11.r2), channel_id=1, source_target_pairs={{0,1},{1,0},{2,3},{3,2},{4,5},{5,4},{6,7},{7,6},{8,9},{9,8},{10,11... | collective-permute-start | bytes 196616 | tf_op jit(solution)/shard_map/ppermute | solution.py:498
  35.6 5.4 %collective-permute-start.12 = (bf16[8,16,256]{2,1,0:T(8,128)(2,1)S(1)}, bf16[8,16,256]{2,1,0:T(8,128)(2,1)S(1)}, u32[]{:S(2)}, u32[]{:S(2)}) collective-permute-start(bf16[8,16,256]{2,1,0:T(8,128)(2,1)S(1)} %get-tuple-element.86), channel_id=1, source_target_pairs={{0,4},{4,0},{8,12},{12,8},{16,20},{20,16},{24,28},{28,24},{1,5},{5... | collective-permute-start | bytes 196616 | tf_op jit(solution)/shard_map/ppermute | solution.py:492
  35.7 5.3 %collective-permute-start.13 = (bf16[8,16,256]{2,1,0:T(8,128)(2,1)S(1)}, bf16[8,16,256]{2,1,0:T(8,128)(2,1)S(1)}, u32[]{:S(2)}, u32[]{:S(2)}) collective-permute-start(bf16[8,16,256]{2,1,0:T(8,128)(2,1)S(1)} %get-tuple-element.87), channel_id=1, source_target_pairs={{0,8},{4,12},{8,0},{12,4},{16,24},{20,28},{24,16},{28,20},{1,9},{5... | collective-permute-start | bytes 196616 | tf_op jit(solution)/shard_map/ppermute | solution.py:492
  35.8 6.5 %collective-permute-start.14 = (bf16[8,16,256]{2,1,0:T(8,128)(2,1)S(1)}, bf16[8,16,256]{2,1,0:T(8,128)(2,1)S(1)}, u32[]{:S(2)}, u32[]{:S(2)}) collective-permute-start(bf16[8,16,256]{2,1,0:T(8,128)(2,1)S(1)} %get-tuple-element.88), channel_id=1, source_target_pairs={{0,24},{4,28},{8,16},{12,20},{16,8},{20,12},{24,0},{28,4},{1,25},{... | collective-permute-start | bytes 196616 | tf_op jit(solution)/shard_map/ppermute | solution.py:492
  37.6 7.1 %collective-permute-start.15 = (bf16[8,16,256]{2,1,0:T(8,128)(2,1)S(1)}, bf16[8,16,256]{2,1,0:T(8,128)(2,1)S(1)}, u32[]{:S(2)}, u32[]{:S(2)}) collective-permute-start(bf16[8,16,256]{2,1,0:T(8,128)(2,1)S(1)} %get-tuple-element.89), channel_id=1, source_target_pairs={{0,28},{4,8},{8,4},{12,16},{16,12},{20,24},{24,20},{28,0},{1,29},{... | collective-permute-start | bytes 196616 | tf_op jit(solution)/shard_map/ppermute | solution.py:492
  44.8 6.7 %collective-permute-start.18 = (bf16[52,16,128]{2,1,0:T(8,128)(2,1)S(1)}, bf16[52,16,128]{2,1,0:T(8,128)(2,1)S(1)}, u32[]{:S(2)}, u32[]{:S(2)}) collective-permute-start(bf16[52,16,128]{2,1,0:T(8,128)(2,1)S(1)} %shard_map.111), channel_id=1, source_target_pairs={{0,2},{1,3},{2,0},{3,1},{4,6},{5,7},{6,4},{7,5},{8,10},{9,11},{10,... | collective-permute-start | bytes 638984 | tf_op jit(solution)/shard_map/ppermute | solution.py:498
  46.0 7.4 %collective-permute-start.17 = (bf16[52,16,128]{2,1,0:T(8,128)(2,1)S(1)}, bf16[52,16,128]{2,1,0:T(8,128)(2,1)S(1)}, u32[]{:S(2)}, u32[]{:S(2)}) collective-permute-start(bf16[52,16,128]{2,1,0:T(8,128)(2,1)S(1)} %shard_map.110.a0.refs_0_), channel_id=1, source_target_pairs={{0,1},{1,0},{2,3},{3,2},{4,5},{5,4},{6,7},{7,6},{8,9},{9,8},{10,11... | collective-permute-start | bytes 638984 | tf_op jit(solution)/shard_map/ppermute | solution.py:498
  51.5 2.2 %collective-permute-start.19 = (bf16[52,16,128]{2,1,0:T(8,128)(2,1)S(1)}, bf16[52,16,128]{2,1,0:T(8,128)(2,1)S(1)}, u32[]{:S(2)}, u32[]{:S(2)}) collective-permute-start(bf16[52,16,128]{2,1,0:T(8,128)(2,1)S(1)} %collective-permute-done.18.a2.refs_2_), channel_id=1, source_target_pairs={{0,1},{1,0},{2,3},{3,2},{4,5},{5,4},{6,7},{7,6},{8,9},{9,8},{10,11... | collective-permute-start | bytes 638984 | tf_op jit(solution)/shard_map/ppermute | solution.py:498
  53.7 28.3 %copy-start = (f32[1,512,192]{1,2,0:T(8,128)S(1)}, f32[1,512,192]{1,2,0:T(8,128)}, u32[]{:S(2)}) copy-start(f32[1,512,192]{1,2,0:T(8,128)} %param.12) | copy-start | bytes 1179652
  54.8 2.0 %collective-permute-start.20 = (bf16[9,24,128]{2,1,0:T(8,128)(2,1)S(1)}, bf16[9,24,128]{2,1,0:T(8,128)(2,1)S(1)}, u32[]{:S(2)}, u32[]{:S(2)}) collective-permute-start(bf16[9,24,128]{2,1,0:T(8,128)(2,1)S(1)} %get-tuple-element.100), channel_id=1, source_target_pairs={{0,1},{1,0},{2,3},{3,2},{4,5},{5,4},{6,7},{7,6},{8,9},{9,8},{10,11... | collective-permute-start | bytes 165896 | tf_op jit(solution)/shard_map/ppermute | solution.py:498
  55.4 4.5 %collective-permute-start.21 = (bf16[9,24,128]{2,1,0:T(8,128)(2,1)S(1)}, bf16[9,24,128]{2,1,0:T(8,128)(2,1)S(1)}, u32[]{:S(2)}, u32[]{:S(2)}) collective-permute-start(bf16[9,24,128]{2,1,0:T(8,128)(2,1)S(1)} %get-tuple-element.101), channel_id=1, source_target_pairs={{0,2},{1,3},{2,0},{3,1},{4,6},{5,7},{6,4},{7,5},{8,10},{9,11},{10,... | collective-permute-start | bytes 165896 | tf_op jit(solution)/shard_map/ppermute | solution.py:498
  55.7 4.2 %collective-permute-start.22 = (bf16[9,24,128]{2,1,0:T(8,128)(2,1)S(1)}, bf16[9,24,128]{2,1,0:T(8,128)(2,1)S(1)}, u32[]{:S(2)}, u32[]{:S(2)}) collective-permute-start(bf16[9,24,128]{2,1,0:T(8,128)(2,1)S(1)} %get-tuple-element.102), channel_id=1, source_target_pairs={{0,3},{1,2},{2,1},{3,0},{4,7},{5,6},{6,5},{7,4},{8,11},{9,10},{10,... | collective-permute-start | bytes 165896 | tf_op jit(solution)/shard_map/ppermute | solution.py:498
  59.9 5.5 %collective-permute-start.23 = (bf16[9,24,128]{2,1,0:T(8,128)(2,1)S(1)}, bf16[9,24,128]{2,1,0:T(8,128)(2,1)S(1)}, u32[]{:S(2)}, u32[]{:S(2)}) collective-permute-start(bf16[9,24,128]{2,1,0:T(8,128)(2,1)S(1)} %get-tuple-element.103), channel_id=1, source_target_pairs={{0,4},{4,0},{8,12},{12,8},{16,20},{20,16},{24,28},{28,24},{1,5},{5... | collective-permute-start | bytes 165896 | tf_op jit(solution)/shard_map/ppermute | solution.py:492
  61.1 4.3 %collective-permute-start.24 = (bf16[9,24,128]{2,1,0:T(8,128)(2,1)S(1)}, bf16[9,24,128]{2,1,0:T(8,128)(2,1)S(1)}, u32[]{:S(2)}, u32[]{:S(2)}) collective-permute-start(bf16[9,24,128]{2,1,0:T(8,128)(2,1)S(1)} %get-tuple-element.104), channel_id=1, source_target_pairs={{0,8},{4,12},{8,0},{12,4},{16,24},{20,28},{24,16},{28,20},{1,9},{5... | collective-permute-start | bytes 165896 | tf_op jit(solution)/shard_map/ppermute | solution.py:492
  62.1 6.1 %collective-permute-start.25 = (bf16[9,24,128]{2,1,0:T(8,128)(2,1)S(1)}, bf16[9,24,128]{2,1,0:T(8,128)(2,1)S(1)}, u32[]{:S(2)}, u32[]{:S(2)}) collective-permute-start(bf16[9,24,128]{2,1,0:T(8,128)(2,1)S(1)} %get-tuple-element.105), channel_id=1, source_target_pairs={{0,24},{4,28},{8,16},{12,20},{16,8},{20,12},{24,0},{28,4},{1,25},{... | collective-permute-start | bytes 165896 | tf_op jit(solution)/shard_map/ppermute | solution.py:492
  63.5 6.9 %collective-permute-start.26 = (bf16[9,24,128]{2,1,0:T(8,128)(2,1)S(1)}, bf16[9,24,128]{2,1,0:T(8,128)(2,1)S(1)}, u32[]{:S(2)}, u32[]{:S(2)}) collective-permute-start(bf16[9,24,128]{2,1,0:T(8,128)(2,1)S(1)} %get-tuple-element.106), channel_id=1, source_target_pairs={{0,28},{4,8},{8,4},{12,16},{16,12},{20,24},{24,20},{28,0},{1,29},{... | collective-permute-start | bytes 165896 | tf_op jit(solution)/shard_map/ppermute | solution.py:492
  70.6 9.4 %collective-permute-start.28 = (bf16[9,24,128]{2,1,0:T(8,128)(2,1)S(1)}, bf16[9,24,128]{2,1,0:T(8,128)(2,1)S(1)}, u32[]{:S(2)}, u32[]{:S(2)}) collective-permute-start(bf16[9,24,128]{2,1,0:T(8,128)(2,1)S(1)} %get-tuple-element.109), channel_id=1, source_target_pairs={{0,8},{4,12},{8,0},{12,4},{16,24},{20,28},{24,16},{28,20},{1,9},{5... | collective-permute-start | bytes 165896 | tf_op jit(solution)/shard_map/ppermute | solution.py:492
  70.7 9.3 %collective-permute-start.29 = (bf16[9,24,128]{2,1,0:T(8,128)(2,1)S(1)}, bf16[9,24,128]{2,1,0:T(8,128)(2,1)S(1)}, u32[]{:S(2)}, u32[]{:S(2)}) collective-permute-start(bf16[9,24,128]{2,1,0:T(8,128)(2,1)S(1)} %get-tuple-element.110), channel_id=1, source_target_pairs={{0,24},{4,28},{8,16},{12,20},{16,8},{20,12},{24,0},{28,4},{1,25},{... | collective-permute-start | bytes 165896 | tf_op jit(solution)/shard_map/ppermute | solution.py:492
  72.1 4.1 %collective-permute-start.27 = (bf16[8,24,128]{2,1,0:T(8,128)(2,1)S(1)}, bf16[8,24,128]{2,1,0:T(8,128)(2,1)S(1)}, u32[]{:S(2)}, u32[]{:S(2)}) collective-permute-start(bf16[8,24,128]{2,1,0:T(8,128)(2,1)S(1)} %get-tuple-element.108), channel_id=1, source_target_pairs={{0,4},{4,0},{8,12},{12,8},{16,20},{20,16},{24,28},{28,24},{1,5},{5... | collective-permute-start | bytes 147464 | tf_op jit(solution)/shard_map/ppermute | solution.py:492
  73.2 6.8 %collective-permute-start.30 = (bf16[8,24,128]{2,1,0:T(8,128)(2,1)S(1)}, bf16[8,24,128]{2,1,0:T(8,128)(2,1)S(1)}, u32[]{:S(2)}, u32[]{:S(2)}) collective-permute-start(bf16[8,24,128]{2,1,0:T(8,128)(2,1)S(1)} %get-tuple-element.111), channel_id=1, source_target_pairs={{0,28},{4,8},{8,4},{12,16},{16,12},{20,24},{24,20},{28,0},{1,29},{... | collective-permute-start | bytes 147464 | tf_op jit(solution)/shard_map/ppermute | solution.py:492
  80.1 2.2 %collective-permute-start.31 = (bf16[9,24,128]{2,1,0:T(8,128)(2,1)S(1)}, bf16[9,24,128]{2,1,0:T(8,128)(2,1)S(1)}, u32[]{:S(2)}, u32[]{:S(2)}) collective-permute-start(bf16[9,24,128]{2,1,0:T(8,128)(2,1)S(1)} %get-tuple-element.115), channel_id=1, source_target_pairs={{0,1},{1,0},{2,3},{3,2},{4,5},{5,4},{6,7},{7,6},{8,9},{9,8},{10,11... | collective-permute-start | bytes 165896 | tf_op jit(solution)/shard_map/ppermute | solution.py:498
  80.2 4.3 %collective-permute-start.32 = (bf16[9,24,128]{2,1,0:T(8,128)(2,1)S(1)}, bf16[9,24,128]{2,1,0:T(8,128)(2,1)S(1)}, u32[]{:S(2)}, u32[]{:S(2)}) collective-permute-start(bf16[9,24,128]{2,1,0:T(8,128)(2,1)S(1)} %get-tuple-element.116), channel_id=1, source_target_pairs={{0,2},{1,3},{2,0},{3,1},{4,6},{5,7},{6,4},{7,5},{8,10},{9,11},{10,... | collective-permute-start | bytes 165896 | tf_op jit(solution)/shard_map/ppermute | solution.py:498
  81.8 3.8 %collective-permute-start.33 = (bf16[9,24,128]{2,1,0:T(8,128)(2,1)S(1)}, bf16[9,24,128]{2,1,0:T(8,128)(2,1)S(1)}, u32[]{:S(2)}, u32[]{:S(2)}) collective-permute-start(bf16[9,24,128]{2,1,0:T(8,128)(2,1)S(1)} %get-tuple-element.117), channel_id=1, source_target_pairs={{0,3},{1,2},{2,1},{3,0},{4,7},{5,6},{6,5},{7,4},{8,11},{9,10},{10,... | collective-permute-start | bytes 165896 | tf_op jit(solution)/shard_map/ppermute | solution.py:498
